TPU v7x, 32 devices: a whole 2x2x4 slice. The times are simulated.
32 devices in a mesh: crops: 2 (over y), row: 8 (over z, x), col: 2 (over core).
Axes of the slice: x: 2, y: 2, z: 4, core: 2. Of those that a mesh axis runs over, the one named last changes fastest.
Arguments:
- pair: bfloat16 [736, 368, 128], P(('crops', 'row'), 'col'), parts along dimension 0, may hold values from -6 to 6
- chain_lengths: int32 [10], P('crops'), parts along dimension 0, may hold values from 1 to 184, 368 in all
- in_weight: bfloat16 [128, 640], replicated, may hold values from -0.5 to 0.5
- out_weight: bfloat16 [128, 128], replicated, may hold values from -0.5 to 0.5
- trans_in: bfloat16 [128, 1024], replicated, may hold values from -0.5 to 0.5
- trans_out: bfloat16 [512, 128], replicated, may hold values from -0.25 to 0.25
Outputs:
- pair_out: bfloat16 [736, 368, 128], P(('crops', 'row'), 'col'), parts along dimension 0
There are 2 independent parts, one for each index of `crops`. A program takes and returns all parts, laid end to end along the dimension named above; an argument that names none is the same for every part. Nothing has to cross between parts.
Inputs may be any that keep to these rules, and one draw needn't show every extreme that they name: `chain_lengths`: the entries sum to 368; the last entry counts padding tokens at the end of the crop, the others count tokens of chains.
All inputs are finite; a program needn't handle non-finite values.
Results may differ from a plain program's by a relative error of at most 0.0056.
Values may be sent and summed in bfloat16 or wider, within the bound.
No kernel may reach another device: no remote copies, remote signals or barrier semaphores. Data moves between devices by JAX's collectives and lax.ppermute only.
A program may use at most 192 MiB of HBM per device.

v0:
```python
import jax
import jax.numpy as jnp
from jax import lax
from jax.sharding import PartitionSpec as P


def partner(x, axis, stride):
    return lax.ppermute(x, axis, [(i, i ^ 1 << stride) for i in range(lax.axis_size(axis))])


def layer_norm(values):
    centered = values - jnp.mean(values, axis=-1, keepdims=True)
    variance = jnp.mean(centered * centered, axis=-1, keepdims=True)
    return centered * lax.rsqrt(variance + 1e-05)


def per_device(pair, chain_lengths, in_weight, out_weight, trans_in, trans_out):
    tile_rows, tile_cols, width = pair.shape
    hidden_units = trans_out.shape[0]
    row_count = lax.axis_size("row")
    col_count = lax.axis_size("col")
    tokens = tile_rows * row_count
    valid_count = tokens - chain_lengths[chain_lengths.shape[0] - 1]
    row_id = lax.axis_index("row")
    col_id = lax.axis_index("col")
    row_pos = row_id * tile_rows + jnp.arange(tile_rows, dtype=jnp.int32)
    col_pos = col_id * tile_cols + jnp.arange(tile_cols, dtype=jnp.int32)
    pair_mask = ((row_pos < valid_count)[:, None] & (col_pos < valid_count)[None, :]).astype(
        jnp.float32
    )[:, :, None]
    normed = layer_norm(pair.astype(jnp.float32)).astype(jnp.bfloat16)
    projected = jnp.dot(normed.reshape(-1, width), in_weight, preferred_element_type=jnp.float32)
    projected = projected.reshape(tile_rows, tile_cols, 5 * width)
    left_ops = (
        jax.nn.sigmoid(projected[..., :width]) * projected[..., width : 2 * width] * pair_mask
    ).astype(jnp.bfloat16)
    right_ops = (
        jax.nn.sigmoid(projected[..., 2 * width : 3 * width])
        * projected[..., 3 * width : 4 * width]
        * pair_mask
    ).astype(jnp.bfloat16)
    out_gate = jax.nn.sigmoid(projected[..., 4 * width :])
    quotient = row_count // col_count
    low_bits = quotient.bit_length() - 1
    col_bits = col_count.bit_length() - 1
    mirrored = right_ops
    for bit_level in range(col_bits):
        row_bit = row_id // 2 ** (low_bits + bit_level) % 2
        col_bit = col_id // 2**bit_level % 2
        passed = partner(mirrored, "row", low_bits + bit_level)
        returned = partner(passed, "col", bit_level)
        mirrored = jnp.where(row_bit == col_bit, mirrored, returned)
    stacked = lax.all_gather(mirrored, "row", axis=0, tiled=True)
    right_rows = stacked.reshape(col_count, quotient, tile_rows, tile_cols, width)
    right_rows = right_rows.transpose(1, 2, 0, 3, 4).reshape(tile_cols, tokens, width)
    triangle = jnp.einsum(
        "ikc,jkc->ijc",
        lax.all_gather(left_ops, "col", axis=1, tiled=True),
        right_rows,
        preferred_element_type=jnp.float32,
    )
    tri_normed = layer_norm(triangle).astype(jnp.bfloat16)
    update = jnp.dot(tri_normed.reshape(-1, width), out_weight, preferred_element_type=jnp.float32)
    updated = pair.astype(jnp.float32) + out_gate * update.reshape(tile_rows, tile_cols, width)
    trans_normed = layer_norm(updated).astype(jnp.bfloat16)
    expanded = jnp.dot(
        trans_normed.reshape(-1, width), trans_in, preferred_element_type=jnp.float32
    )
    hidden = (jax.nn.silu(expanded[:, :hidden_units]) * expanded[:, hidden_units:]).astype(
        jnp.bfloat16
    )
    result = updated + jnp.dot(hidden, trans_out, preferred_element_type=jnp.float32).reshape(
        tile_rows, tile_cols, width
    )
    return result.astype(jnp.bfloat16)


def solution(mesh):
    placed = (P(("crops", "row"), "col", None), P("crops"), P(), P(), P(), P())
    return jax.shard_map(
        per_device,
        mesh=mesh,
        in_specs=placed,
        out_specs=P(("crops", "row"), "col", None),
        check_vma=False,
    )
```

profile of v0, /device:TPU:1, one launch (start us, length us, event | category | flops | bytes accessed | tf_op | source)
XLA Modules:
  0.0 567.9 jit_solution(1478053768714049187)
XLA Ops:
  6.5 0.0 copy-start
  6.5 0.0 copy-start.3
  6.5 0.0 copy-start.5
  6.5 0.0 all-gather.5.cloned.1.call-start
  6.6 1.4 slice.27
  8.6 2.5 convert_reduce_fusion
  11.1 4.2 fusion.5
  15.4 0.1 and_convert_fusion
  15.5 0.0 copy-done.3
  15.5 0.0 copy-done.5
  15.5 4.7 fusion.23
  20.2 0.0 copy-start.2
  20.2 5.2 fusion.8
  25.5 2.6 copy-done.2
  28.1 3.1 collective-permute-start
  31.2 0.0 all-gather.5.cloned.1.call-update
  31.2 0.2 all-gather.3.cloned.1.call-start
  31.5 93.1 %collective-permute-done = bf16[46,184,128]{2,1,0:T(8,128)(2,1)} collective-permute-done((bf16[46,184,128]{2,1,0:T(8,128)(2,1)S(1)}, bf16[46,184,128]{2,1,0:T(8,128)(2,1)}, u32[]{:S(2)}, u32[]{:S(2)}) %collective-permute-start) | collective-permute-done | bytes 2166816 | tf_op jit(solution)/shard_map/ppermute | solution.py:8
  124.6 1.2 collective-permute-start.1
  125.8 4.2 collective-permute-done.1
  130.1 3.1 broadcast_select_fusion
  133.2 0.0 all-gather.3.cloned.1.call-update
  133.2 0.0 all-gather.5.cloned.1.call-done
  133.3 7.0 %copy.19 = bf16[46,368,128]{1,0,2:T(8,128)(2,1)} copy(bf16[46,368,128]{2,1,0:T(8,128)(2,1)} %all-gather.5.cloned.1.call-done) | data formatting | bytes 8667136 | tf_op jit(solution)/shard_map/all_gather | solution.py:58
  140.2 327.6 %all-gather.3.cloned.1.call-done = bf16[368,184,128]{2,1,0:T(8,128)(2,1)} async-done(((bf16[46,184,128]{2,1,0:T(8,128)(2,1)}), bf16[368,184,128]{2,1,0:T(8,128)(2,1)}) %all-gather.3.cloned.1.call-update) | async-done | bytes 17334288 | tf_op jit(solution)/shard_map/all_gather | solution.py:53
  467.8 14.1 %copy.17 = bf16[4,46,2,184,128]{4,3,2,1,0:T(8,128)(2,1)} copy(bf16[4,46,2,184,128]{4,3,1,0,2:T(8,128)(2,1)} %bitcast.28) | data formatting | bytes 34668544 | tf_op jit(solution)/shard_map/transpose | solution.py:55
  481.9 23.5 %copy.18 = bf16[184,368,128]{1,0,2:T(8,128)(2,1)} copy(bf16[184,368,128]{2,1,0:T(8,128)(2,1)} %bitcast.27) | data formatting | bytes 34668544 | tf_op jit(solution)/shard_map/reshape | solution.py:55
  505.5 12.1 %bitcast_reduce_fusion = (f32[46,184]{1,0:T(8,128)S(1)}, f32[128,184,46]{1,2,0:T(8,128)S(1)}) fusion(bf16[184,368,128]{1,0,2:T(8,128)(2,1)} %copy.18, bf16[46,368,128]{1,0,2:T(8,128)(2,1)} %copy.19), kind=kOutput, calls=%fused_computation.7 | convolution fusion | flops 798451456 | bytes 26035264 | tf_op jit(solution)/shard_map/ikc,jkc->ijc/dot_general | solution.py:56
  517.6 0.8 multiply_reduce_fusion
  518.4 0.0 copy-start.4
  518.4 0.0 copy-start.7
  518.4 1.0 multiply_convert_fusion
  519.4 0.6 copy-done.4
  520.0 0.0 copy-done.7
  520.0 6.9 %fusion.32 = (f32[46,184]{1,0:T(8,128)S(1)}, f32[46,184,128]{2,1,0:T(8,128)S(1)}) fusion(bf16[128,128]{1,0:T(8,128)(2,1)S(1)} %copy-done.7, bf16[46,184,128]{1,0,2:T(8,128)(2,1)S(1)} %multiply_convert_fusion, f32[46,184,640]{2,1,0:T(8,128)} %copy-done.2, bf16[46,184,128]{2,1,0:T(8,128)(2,1)S(1)} %copy-done.4), kind=kOutput, calls=%fused_computation.54 | convolution fusion | flops 284923648 | bytes 13067328 | tf_op jit(solution)/shard_map/dot_general | solution.py:63
  526.9 3.0 multiply_reduce_fusion.1
  530.0 2.8 multiply_convert_fusion.1
  532.8 0.0 copy-done
  532.8 0.0 copy-start.6
  532.8 13.5 %fusion.33 = f32[8464,1024]{1,0:T(8,128)} fusion(bf16[8464,128]{1,0:T(8,128)(2,1)S(1)} %bitcast.29, bf16[128,1024]{1,0:T(8,128)(2,1)S(1)} %copy-done), kind=kOutput, calls=%fused_computation.55 | convolution fusion | flops 2218786816 | bytes 37097472 | tf_op jit(solution)/shard_map/dot_general | solution.py:66
  546.3 0.0 copy-done.6
  546.3 12.8 %fusion.1 = f32[8464,128]{1,0:T(8,128)S(1)} fusion(bf16[512,128]{1,0:T(8,128)(2,1)S(1)} %copy-done.6, f32[8464,1024]{1,0:T(8,128)} %fusion.33), kind=kOutput, calls=%fused_computation.2 | convolution fusion | flops 1135394816 | bytes 39133184 | tf_op jit(solution)/shard_map/dot_general | solution.py:72
  559.1 0.0 copy-start.1
  559.1 1.9 add_convert_fusion
  561.1 0.0 copy-done.1
  (8 shorter events, 0.1 us)
Async XLA Ops:
  6.5 526.2 %copy-start = (bf16[128,1024]{1,0:T(8,128)(2,1)S(1)}, bf16[128,1024]{1,0:T(8,128)(2,1)}, u32[]{:S(2)}) copy-start(bf16[128,1024]{1,0:T(8,128)(2,1)} %param.10) | copy-start | bytes 786436
  6.5 8.9 %copy-start.3 = (bf16[46,184,128]{2,1,0:T(8,128)(2,1)S(1)}, bf16[46,184,128]{2,1,0:T(8,128)(2,1)}, u32[]{:S(2)}) copy-start(bf16[46,184,128]{2,1,0:T(8,128)(2,1)} %param.6) | copy-start | bytes 6500356
  6.5 9.0 %copy-start.5 = (bf16[128,640]{1,0:T(8,128)(2,1)S(1)}, bf16[128,640]{1,0:T(8,128)(2,1)}, u32[]{:S(2)}) copy-start(bf16[128,640]{1,0:T(8,128)(2,1)} %param.8) | copy-start | bytes 491524
  6.5 126.7 %all-gather.5.cloned.1.call-start = ((), (), s32[]{:S(2)}) async-start(), calls=%async_computation.1 | async-start | bytes 6500352 | tf_op jit(solution)/shard_map/all_gather | solution.py:58
  20.2 7.8 %copy-start.2 = (f32[46,184,640]{2,1,0:T(8,128)}, f32[46,184,640]{2,1,0:T(8,128)S(1)}, u32[]{:S(2)}) copy-start(f32[46,184,640]{2,1,0:T(8,128)S(1)} %fusion.23) | copy-start | bytes 65003524
  28.1 96.5 %collective-permute-start = (bf16[46,184,128]{2,1,0:T(8,128)(2,1)S(1)}, bf16[46,184,128]{2,1,0:T(8,128)(2,1)}, u32[]{:S(2)}, u32[]{:S(2)}) collective-permute-start(bf16[46,184,128]{2,1,0:T(8,128)(2,1)S(1)} %get-tuple-element.6), channel_id=1, source_target_pairs={{0,8},{2,10},{4,12},{6,14},{8,0},{10,2},{12,4},{14,6},{1,9},{3,11}... | collective-permute-start | bytes 6500360 | tf_op jit(solution)/shard_map/ppermute | solution.py:8
  31.2 436.6 %all-gather.3.cloned.1.call-start = ((), (), s32[]{:S(2)}) async-start(), calls=%async_computation | async-start | bytes 19501056 | tf_op jit(solution)/shard_map/all_gather | solution.py:53
  124.6 5.5 collective-permute-start.1
  518.4 1.6 copy-start.4
  518.4 1.6 copy-start.7
  532.8 13.5 %copy-start.6 = (bf16[512,128]{1,0:T(8,128)(2,1)S(1)}, bf16[512,128]{1,0:T(8,128)(2,1)}, u32[]{:S(2)}) copy-start(bf16[512,128]{1,0:T(8,128)(2,1)} %param.11) | copy-start | bytes 393220
  559.1 2.0 copy-start.1
Sparse Core Ops, SparseCore 0:
  31.4 13.7 all-gather.4
  133.3 334.4 all-gather.2
where the time goes:
time: 570 us; the launch traced here: 568 us
  waiting for transfers between devices  425 us (75%)
  matrix products  50 us (9%)
  local copies, waits for them, and re-layouts  49.2 us (9%)
  other arithmetic  24.8 us (4%)
  between operations  14.3 us (3%)
    all_gather x1, waiting for transfers between devices, per_device(): stacked = lax.all_gather(mirrored, 'row', axis=0, tiled=True)  328 us
    ppermute x2, waiting for transfers between devices, partner(): lax.ppermute(x, axis, [(i, i ^ 1 << stride) for i in range(lax.axis_size(...  97.4 us
    reshape x1, local copies, waits for them, and re-layouts, per_device(): right_rows.transpose(1, 2, 0, 3, 4).reshape(tile_cols, tokens, width)  23.5 us
    transpose x1, local copies, waits for them, and re-layouts, per_device(): right_rows.transpose(1, 2, 0, 3, 4).reshape(tile_cols, tokens, width)  14.1 us
    dot_general x1, matrix products, per_device(): jnp.dot(trans_normed.reshape(-1, width), trans_in, preferred_element_type...  13.5 us
    dot_general x1, matrix products, per_device(): jnp.dot(hidden, trans_out, preferred_element_type=jnp.float32)  12.8 us
    dot_general x1, matrix products, per_device(): jnp.einsum('ikc,jkc->ijc', lax.all_gather(left_ops, 'col', axis=1, tiled=...  12.1 us
  transfers between devices with their start and end apart: 4, of which 3 were waited for; matrix products, arithmetic and copies ran while one was open for 2% of the time, Pallas kernels for 0%

commit v1 on v0

v1 whole, which is shorter than its diff:
```python
import jax
import jax.numpy as jnp
from jax import lax
from jax.sharding import PartitionSpec as P


def layer_norm(values):
    centered = values - jnp.mean(values, axis=-1, keepdims=True)
    variance = jnp.mean(centered * centered, axis=-1, keepdims=True)
    return centered * lax.rsqrt(variance + 1e-05)


def per_device(pair, chain_lengths, in_weight, out_weight, trans_in, trans_out):
    tile_rows, tile_cols, width = pair.shape
    hidden_units = trans_out.shape[0]
    row_count = lax.axis_size("row")
    col_count = lax.axis_size("col")
    outer = row_count // 2
    tokens = tile_rows * row_count
    valid_count = tokens - chain_lengths[chain_lengths.shape[0] - 1]
    row_id = lax.axis_index("row")
    col_id = lax.axis_index("col")
    line_id = row_id // 2

    def along_line(value, step, targets):
        perm = [(2 * (t - step) + b, 2 * t + b) for t in targets for b in range(2)]
        return lax.ppermute(value, "row", perm)

    row_pos = row_id * tile_rows + jnp.arange(tile_rows, dtype=jnp.int32)
    col_pos = col_id * tile_cols + jnp.arange(tile_cols, dtype=jnp.int32)
    pair_mask = ((row_pos < valid_count)[:, None] & (col_pos < valid_count)[None, :]).astype(
        jnp.float32
    )[:, :, None]
    normed = layer_norm(pair.astype(jnp.float32)).astype(jnp.bfloat16).reshape(-1, width)

    def gated(offset):
        block = jnp.dot(
            normed,
            in_weight[:, offset * width : (offset + 2) * width],
            preferred_element_type=jnp.float32,
        ).reshape(tile_rows, tile_cols, 2 * width)
        value = jax.nn.sigmoid(block[..., :width]) * block[..., width:] * pair_mask
        return value.astype(jnp.bfloat16)

    right_ops = gated(2)
    from_left, from_right = {0: right_ops}, {0: right_ops}
    for step in range(1, outer):
        from_left[step] = along_line(from_left[step - 1], 1, range(step, outer))
        from_right[step] = along_line(from_right[step - 1], -1, range(0, outer - step))
    left_ops = gated(0)
    left_other = lax.ppermute(left_ops, "row", [(i, i ^ 1) for i in range(row_count)])
    lefts = jnp.concatenate([left_ops, left_other], axis=0)

    partials = []
    for source in range(outer):
        block = right_ops
        for step in range(1, outer):
            if source + step < outer:
                block = jnp.where(line_id == source + step, from_left[step], block)
            if source - step >= 0:
                block = jnp.where(line_id == source - step, from_right[step], block)
        partials.append(
            jnp.einsum("ikc,jkc->ijc", lefts, block, preferred_element_type=jnp.float32)
        )
    partial = jnp.stack(partials)
    share = outer // col_count
    mine = lax.dynamic_slice_in_dim(partial, col_id * share, share, 0)
    for hop in range(1, col_count):
        target = (col_id + hop) % col_count
        passed = lax.dynamic_slice_in_dim(partial, target * share, share, 0)
        mine = mine + lax.ppermute(
            passed, "col", [(c, (c + hop) % col_count) for c in range(col_count)]
        )
    tri_normed = layer_norm(mine).astype(jnp.bfloat16)
    own_part = tri_normed[:, :tile_rows]
    other_part = lax.ppermute(
        tri_normed[:, tile_rows:], "row", [(i, i ^ 1) for i in range(row_count)]
    )
    even = row_id % 2 == 0
    both = jnp.stack(
        [jnp.where(even, own_part, other_part), jnp.where(even, other_part, own_part)], axis=1
    )
    tri_normed = both.transpose(2, 0, 1, 3, 4).reshape(-1, width)

    out_gate = jax.nn.sigmoid(
        jnp.dot(normed, in_weight[:, 4 * width :], preferred_element_type=jnp.float32)
    )
    update = jnp.dot(tri_normed, out_weight, preferred_element_type=jnp.float32)
    updated = pair.astype(jnp.float32).reshape(-1, width) + out_gate * update
    trans_normed = layer_norm(updated).astype(jnp.bfloat16)
    expanded = jnp.dot(trans_normed, trans_in, preferred_element_type=jnp.float32)
    hidden = (jax.nn.silu(expanded[:, :hidden_units]) * expanded[:, hidden_units:]).astype(
        jnp.bfloat16
    )
    result = updated + jnp.dot(hidden, trans_out, preferred_element_type=jnp.float32)
    return result.reshape(tile_rows, tile_cols, width).astype(jnp.bfloat16)


def solution(mesh):
    placed = (P(("crops", "row"), "col", None), P("crops"), P(), P(), P(), P())
    return jax.shard_map(
        per_device,
        mesh=mesh,
        in_specs=placed,
        out_specs=P(("crops", "row"), "col", None),
        check_vma=False,
    )
```

time: 570 us -> 392 us (0.69)
  the two profiles are of different devices: /device:TPU:1 before, /device:TPU:26 now
where the time goes in v1:
time: 392 us; the launch traced here: 385 us
  waiting for transfers between devices  157 us (40%)
  local copies, waits for them, and re-layouts  89.4 us (23%)
  matrix products  69.9 us (18%)
  other arithmetic  55.7 us (14%)
  starting transfers between devices  11.6 us (3%)
    ppermute x6, waiting for transfers between devices, along_line(): return lax.ppermute(value, 'row', perm)  128 us
    dot_general x4, matrix products, per_device(): jnp.einsum('ikc,jkc->ijc', lefts, block, preferred_element_type=jnp.float32)  23.4 us
    ppermute x1, waiting for transfers between devices, per_device(): lax.ppermute(tri_normed[:, tile_rows:], 'row', [(i, i ^ 1) for i in range...  20.9 us
    another operation x2, local copies, waits for them, and re-layouts, per_device(): jnp.stack([jnp.where(even, own_part, other_part), jnp.where(even, other_p...  16.7 us
    dot_general x1, matrix products, per_device(): jnp.dot(hidden, trans_out, preferred_element_type=jnp.float32)  14.7 us
    dot_general x1, matrix products, per_device(): jnp.dot(trans_normed, trans_in, preferred_element_type=jnp.float32)  13.4 us
    reduce_sum x3, other arithmetic, layer_norm(): variance = jnp.mean(centered * centered, axis=-1, keepdims=True)  11.3 us
    ppermute x6, starting transfers between devices, along_line(): return lax.ppermute(value, 'row', perm)  10.5 us
  transfers between devices with their start and end apart: 9, of which 6 were waited for; matrix products, arithmetic and copies ran while one was open for 5% of the time, Pallas kernels for 0%

profile of v1, /device:TPU:26, one launch (start us, length us, event | category | flops | bytes accessed | tf_op | source)
XLA Modules:
  0.0 384.7 jit_solution(3044584943278683480)
XLA Ops:
  0.0 2.6 convert_reduce_fusion
  2.7 4.2 %multiply_reduce_fusion.2 = f32[46,184]{1,0:T(8,128)S(1)} fusion(bf16[46,184,128]{2,1,0:T(8,128)(2,1)} %param.6, f32[46,184]{1,0:T(8,128)S(1)} %broadcast_multiply_fusion.1), kind=kLoop, calls=%fused_computation.32 | loop fusion | flops 4325104 | bytes 2234496 | tf_op jit(solution)/shard_map/reduce_sum | solution.py:9
  7.0 2.5 multiply_convert_fusion.2
  9.5 0.0 copy-start.4
  9.5 4.6 %fusion.20 = f32[46,184,256]{2,1,0:T(8,128)} fusion(bf16[46,184,128]{2,1,0:T(8,128)(2,1)S(1)} %multiply_convert_fusion.2, bf16[128,640]{1,0:T(8,128)(2,1)S(1)} %copy-done.12), kind=kOutput, calls=%fused_computation.48 | convolution fusion | flops 554696704 | bytes 10899456 | tf_op jit(solution)/shard_map/dot_general | solution.py:37
  14.2 4.6 %fusion.22 = f32[46,184,256]{2,1,0:T(8,128)} fusion(bf16[46,184,128]{2,1,0:T(8,128)(2,1)S(1)} %multiply_convert_fusion.2, bf16[128,640]{1,0:T(8,128)(2,1)S(1)} %copy-done.12), kind=kOutput, calls=%fused_computation.50 | convolution fusion | flops 554696704 | bytes 10899456 | tf_op jit(solution)/shard_map/dot_general | solution.py:37
  18.8 0.6 slice.40
  20.0 0.1 and_convert_fusion
  20.1 7.1 %fusion.8 = (bf16[46,184,128]{2,1,0:T(8,128)(2,1)S(1)}, bf16[46,184,128]{2,1,0:T(8,128)(2,1)S(1)}) fusion(f32[46,184,256]{2,1,0:T(8,128)} %fusion.20, f32[46,184]{1,0:T(8,128)S(1)} %and_convert_fusion, f32[46,184,256]{2,1,0:T(8,128)} %fusion.22), kind=kLoop, calls=%fused_computation.16 | loop fusion | flops 13000704 | bytes 21701696 | tf_op jit(solution)/shard_map/convert_element_type | solution.py:43
  27.2 2.5 collective-permute-start.4
  29.8 1.3 collective-permute-start
  31.1 44.9 %collective-permute-done.4 = bf16[46,184,128]{2,1,0:T(8,128)(2,1)S(1)} collective-permute-done((bf16[46,184,128]{2,1,0:T(8,128)(2,1)S(1)}, bf16[46,184,128]{2,1,0:T(8,128)(2,1)S(1)}, u32[]{:S(2)}, u32[]{:S(2)}) %collective-permute-start.4) | collective-permute-done | bytes 2166816 | tf_op jit(solution)/shard_map/ppermute | solution.py:27
  76.0 2.1 collective-permute-start.5
  78.0 2.2 collective-permute-done
  80.2 1.3 collective-permute-start.1
  81.5 0.6 collective-permute-start.3
  82.1 0.0 collective-permute-done.5
  82.1 2.1 collective-permute-start.6
  84.2 46.0 %collective-permute-done.1 = bf16[46,184,128]{2,1,0:T(8,128)(2,1)} collective-permute-done((bf16[46,184,128]{2,1,0:T(8,128)(2,1)S(1)}, bf16[46,184,128]{2,1,0:T(8,128)(2,1)}, u32[]{:S(2)}, u32[]{:S(2)}) %collective-permute-start.1) | collective-permute-done | bytes 2166816 | tf_op jit(solution)/shard_map/ppermute | solution.py:27
  130.2 1.3 collective-permute-start.2
  131.5 0.0 collective-permute-done.3
  131.5 4.1 %pad_maximum_fusion.1 = bf16[92,184,128]{2,1,0:T(8,128)(2,1)} fusion(bf16[46,184,128]{2,1,0:T(8,128)(2,1)} %collective-permute-done.3, bf16[46,184,128]{2,1,0:T(8,128)(2,1)S(1)} %get-tuple-element.13), kind=kLoop, calls=%fused_computation.28 | loop fusion | flops 2166784 | bytes 8667136 | tf_op jit(solution)/shard_map/concatenate | solution.py:52
  135.6 8.9 %copy.25 = bf16[92,184,128]{0,1,2:T(8,128)(2,1)} copy(bf16[92,184,128]{2,1,0:T(8,128)(2,1)} %pad_maximum_fusion.1) | data formatting | bytes 8667136 | tf_op jit(solution)/shard_map/concatenate | solution.py:52
  144.5 0.0 collective-permute-done.6
  144.5 35.0 %collective-permute-done.2 = bf16[46,184,128]{2,1,0:T(8,128)(2,1)} collective-permute-done((bf16[46,184,128]{2,1,0:T(8,128)(2,1)}, bf16[46,184,128]{2,1,0:T(8,128)(2,1)}, u32[]{:S(2)}, u32[]{:S(2)}) %collective-permute-start.2) | collective-permute-done | bytes 2166816 | tf_op jit(solution)/shard_map/ppermute | solution.py:27
  179.4 8.4 %select_select_fusion.3 = (bf16[46,184,128]{2,1,0:T(8,128)(2,1)S(1)}, bf16[46,184,128]{2,1,0:T(8,128)(2,1)}, bf16[46,184,128]{2,1,0:T(8,128)(2,1)}, bf16[46,184,128]{2,1,0:T(8,128)(2,1)}) fusion(bf16[46,184,128]{2,1,0:T(8,128)(2,1)} %collective-permute-done.2, bf16[46,184,128]{2,1,0:T(8,128)(2,1)} %collective-permute-done.1, ...), kind=kLoop, calls=%fused_computation.43 | loop fusion | flops 13000704 | bytes 23834628 | tf_op jit(solution)/shard_map/jit(_where)/select_n | solution.py:59
  187.9 5.2 %copy.24 = bf16[46,184,128]{1,0,2:T(8,128)(2,1)} copy(bf16[46,184,128]{2,1,0:T(8,128)(2,1)S(1)} %get-tuple-element.7) | data formatting | bytes 4333568 | tf_op jit(solution)/shard_map/jit(_where)/select_n | solution.py:59
  193.1 5.0 %copy.26 = bf16[46,184,128]{1,0,2:T(8,128)(2,1)} copy(bf16[46,184,128]{2,1,0:T(8,128)(2,1)} %get-tuple-element.8) | data formatting | bytes 4333568 | tf_op jit(solution)/shard_map/jit(_where)/select_n | solution.py:59
  198.1 7.7 %convolution_bitcast_fusion.3 = f32[1,92,46,128]{1,2,3,0:T(8,128)} fusion(bf16[46,184,128]{1,0,2:T(8,128)(2,1)} %copy.24, bf16[92,184,128]{0,1,2:T(8,128)(2,1)} %copy.25), kind=kOutput, calls=%fused_computation.47 | convolution fusion | flops 199344128 | bytes 8667136 | tf_op jit(solution)/shard_map/ikc,jkc->ijc/dot_general | solution.py:63
  205.8 3.9 %convolution_bitcast_fusion.2 = f32[1,92,46,128]{1,2,3,0:T(8,128)} fusion(bf16[46,184,128]{1,0,2:T(8,128)(2,1)S(1)} %copy-done.8, bf16[92,184,128]{0,1,2:T(8,128)(2,1)S(1)} %bitcast.49), kind=kOutput, calls=%fused_computation.46 | convolution fusion | flops 199344128 | bytes 8667136 | tf_op jit(solution)/shard_map/ikc,jkc->ijc/dot_general | solution.py:63
  209.7 4.9 %copy.28 = bf16[46,184,128]{1,0,2:T(8,128)(2,1)} copy(bf16[46,184,128]{2,1,0:T(8,128)(2,1)} %get-tuple-element.9) | data formatting | bytes 4333568 | tf_op jit(solution)/shard_map/jit(_where)/select_n | solution.py:61
  214.5 5.8 %convolution_bitcast_fusion.1 = f32[1,92,46,128]{1,2,3,0:T(8,128)S(1)} fusion(bf16[46,184,128]{1,0,2:T(8,128)(2,1)} %copy.28, bf16[92,184,128]{0,1,2:T(8,128)(2,1)} %copy.25), kind=kOutput, calls=%fused_computation.45 | convolution fusion | flops 199344128 | bytes 8667136 | tf_op jit(solution)/shard_map/ikc,jkc->ijc/dot_general | solution.py:63
  220.4 4.9 %copy.30 = bf16[46,184,128]{1,0,2:T(8,128)(2,1)} copy(bf16[46,184,128]{2,1,0:T(8,128)(2,1)} %get-tuple-element.10) | data formatting | bytes 4333568 | tf_op jit(solution)/shard_map/jit(_where)/select_n | solution.py:61
  225.3 6.0 %convolution_bitcast_fusion = f32[1,92,46,128]{1,2,3,0:T(8,128)S(1)} fusion(bf16[46,184,128]{1,0,2:T(8,128)(2,1)} %copy.30, bf16[92,184,128]{0,1,2:T(8,128)(2,1)} %copy.25), kind=kOutput, calls=%fused_computation.44 | convolution fusion | flops 199344128 | bytes 8667136 | tf_op jit(solution)/shard_map/ikc,jkc->ijc/dot_general | solution.py:63
  231.2 0.0 copy-done.5
  231.3 1.5 pad_maximum_fusion
  232.8 4.5 %copy-done.1 = f32[4,92,46,128]{1,2,3,0:T(8,128)} copy-done((f32[4,92,46,128]{1,2,3,0:T(8,128)}, f32[4,92,46,128]{1,2,3,0:T(8,128)S(1)}, u32[]{:S(2)}) %copy-start.1) | copy-done | bytes 8667160
  237.3 3.0 constant_dynamic-slice_fusion
  240.3 7.4 %copy.32 = f32[2,92,46,128]{3,0,2,1:T(2,128)} copy(f32[2,92,46,128]{1,2,3,0:T(8,128)} %constant_dynamic-slice_fusion) | data formatting | bytes 8667136 | tf_op jit(solution)/shard_map/dynamic_slice | solution.py:70
  247.7 0.0 collective-permute-start.7
  247.7 7.7 %collective-permute-done.7 = f32[2,92,46,128]{3,0,2,1:T(2,128)} collective-permute-done((f32[2,92,46,128]{3,0,2,1:T(2,128)}, f32[2,92,46,128]{3,0,2,1:T(2,128)}, u32[]{:S(2)}, u32[]{:S(2)}) %collective-permute-start.7) | collective-permute-done | bytes 4333600 | tf_op jit(solution)/shard_map/ppermute | solution.py:71
  255.4 7.4 %copy.33 = f32[2,92,46,128]{1,2,3,0:T(8,128)} copy(f32[2,92,46,128]{3,0,2,1:T(2,128)} %collective-permute-done.7) | data formatting | bytes 8667136 | tf_op jit(solution)/shard_map/ppermute | solution.py:71
  262.8 5.5 %fusion.28 = (f32[2,92,46]{1,2,0:T(8,128)S(1)}, f32[2,92,46,128]{1,2,3,0:T(8,128)S(1)}) fusion(f32[2,92,46,128]{1,2,3,0:T(8,128)} %copy.33, f32[4,92,46,128]{1,2,3,0:T(8,128)} %copy-done.1, s32[]{:T(128)S(6)} %select_n.110), kind=kLoop, calls=%fused_computation.66 | loop fusion | flops 2158320 | bytes 13034564 | tf_op jit(solution)/shard_map/reduce_sum | solution.py:8
  268.3 0.8 multiply_reduce_fusion
  269.2 0.7 multiply_convert_fusion
  269.9 2.6 slice.53
  272.4 6.0 %copy.34 = bf16[2,46,46,128]{3,0,2,1:T(2,128)(2,1)} copy(bf16[2,46,46,128]{1,2,3,0:T(8,128)(2,1)} %slice.53) | data formatting | bytes 2166784 | tf_op jit(solution)/shard_map/slice | solution.py:77
  278.4 0.5 collective-permute-start.8
  278.9 4.9 %fusion.5 = f32[8464,128]{1,0:T(8,128)} fusion(bf16[8464,128]{1,0:T(8,128)(2,1)} %bitcast.51, bf16[128,640]{1,0:T(8,128)(2,1)} %param.8), kind=kOutput, calls=%fused_computation.10 | convolution fusion | flops 280598528 | bytes 6533120 | tf_op jit(solution)/shard_map/dot_general | solution.py:86
  283.8 20.9 %collective-permute-done.8 = bf16[2,46,46,128]{3,0,2,1:T(2,128)(2,1)} collective-permute-done((bf16[2,46,46,128]{3,0,2,1:T(2,128)(2,1)}, bf16[2,46,46,128]{3,0,2,1:T(2,128)(2,1)}, u32[]{:S(2)}, u32[]{:S(2)}) %collective-permute-start.8) | collective-permute-done | bytes 1083424 | tf_op jit(solution)/shard_map/ppermute | solution.py:76
  304.7 5.9 %copy.35 = bf16[2,46,46,128]{1,2,3,0:T(8,128)(2,1)} copy(bf16[2,46,46,128]{3,0,2,1:T(2,128)(2,1)} %collective-permute-done.8) | data formatting | bytes 2166784 | tf_op jit(solution)/shard_map/ppermute | solution.py:76
  310.6 5.0 %select_bitcast_fusion.1 = (bf16[2,1,46,46,128]{2,3,4,0,1:T(8,128)(2,1)}, bf16[2,1,46,46,128]{2,3,4,0,1:T(8,128)(2,1)}) fusion(bf16[2,46,46,128]{1,2,3,0:T(8,128)(2,1)} %copy.35, pred[]{:T(512)S(6)} %eq.12, bf16[2,92,46,128]{1,2,3,0:T(8,128)(2,1)S(1)} %multiply_convert_fusion), kind=kLoop, calls=%fused_computation.35 | loop fusion | flops 1083392 | bytes 4333569 | tf_op jit(solution)/shard_map/stack | solution.py:80
  315.6 10.0 %copy.37 = bf16[2,1,46,46,128]{4,1,3,2,0:T(2,128)(2,1)} copy(bf16[2,1,46,46,128]{2,3,4,0,1:T(8,128)(2,1)} %get-tuple-element.11) | data formatting | bytes 2166784 | tf_op jit(solution)/shard_map/stack | solution.py:80
  325.6 6.7 %copy.38 = bf16[2,1,46,46,128]{4,1,3,2,0:T(2,128)(2,1)} copy(bf16[2,1,46,46,128]{2,3,4,0,1:T(8,128)(2,1)S(1)} %copy-done.7) | data formatting | bytes 2166784 | tf_op jit(solution)/shard_map/stack | solution.py:80
  332.3 6.7 %maximum_bitcast_fusion = bf16[46,2,2,46,128]{4,2,3,0,1:T(2,128)(2,1)S(1)} fusion(bf16[2,1,46,46,128]{4,1,3,2,0:T(2,128)(2,1)} %copy.38, bf16[2,1,46,46,128]{4,1,3,2,0:T(2,128)(2,1)} %copy.37), kind=kLoop, calls=%fused_computation.37 | loop fusion | flops 4333568 | bytes 4333568 | tf_op jit(solution)/shard_map/transpose | solution.py:83
  339.0 0.0 copy-start.3
  339.0 0.0 copy-start.13
  339.0 2.0 copy.39
  341.1 4.5 %reshape.95 = bf16[8464,128]{1,0:T(8,128)(2,1)} reshape(bf16[46,2,2,46,128]{4,3,2,1,0:T(8,128)(2,1)} %copy.39) | data formatting | bytes 4333568 | tf_op jit(solution)/shard_map/reshape | solution.py:83
  345.5 4.3 %fusion.29 = (f32[8464]{0:T(1024)S(1)}, f32[8464,128]{1,0:T(8,128)S(1)}) fusion(f32[8464,128]{1,0:T(8,128)} %fusion.5, bf16[8464,128]{1,0:T(8,128)(2,1)} %reshape.95, bf16[128,128]{1,0:T(8,128)(2,1)S(1)} %copy-done.13, bf16[8464,128]{1,0:T(8,128)(2,1)S(1)} %bitcast.50), kind=kOutput, calls=%fused_computation.67 | convolution fusion | flops 281673472 | bytes 13067328 | tf_op jit(solution)/shard_map/dot_general | solution.py:88
  349.9 6.3 %multiply_reduce_fusion.1 = f32[8464]{0:T(1024)S(1)} fusion(f32[8464,128]{1,0:T(8,128)S(1)} %get-tuple-element.16, f32[8464]{0:T(1024)S(1)} %broadcast_multiply_fusion.2), kind=kLoop, calls=%fused_computation.30 | loop fusion | flops 3241712 | bytes 4401280 | tf_op jit(solution)/shard_map/reduce_sum | solution.py:9
  356.2 0.0 copy-start.14
  356.2 13.4 %fusion.17 = f32[8464,1024]{1,0:T(8,128)} fusion(bf16[128,1024]{1,0:T(8,128)(2,1)S(1)} %copy-done, f32[8464,128]{1,0:T(8,128)S(1)} %get-tuple-element.16, f32[8464]{0:T(1024)S(1)} %add_rsqrt_fusion.2, f32[8464]{0:T(1024)S(1)} %broadcast_multiply_fusion.2), kind=kOutput, calls=%fused_computation.36 | convolution fusion | flops 2222036992 | bytes 39331968 | tf_op jit(solution)/shard_map/dot_general | solution.py:91
  369.6 14.7 %fusion.4 = bf16[8464,128]{1,0:T(8,128)(2,1)} fusion(f32[8464,128]{1,0:T(8,128)S(1)} %get-tuple-element.16, bf16[512,128]{1,0:T(8,128)(2,1)S(1)} %copy-done.14, f32[8464,1024]{1,0:T(8,128)} %fusion.17), kind=kOutput, calls=%fused_computation.9 | convolution fusion | flops 1137561600 | bytes 41299968 | tf_op jit(solution)/shard_map/dot_general | solution.py:95
  (39 shorter events, 0.1 us)
Async XLA Ops:
  0.0 356.2 %copy-start = (bf16[128,1024]{1,0:T(8,128)(2,1)S(1)}, bf16[128,1024]{1,0:T(8,128)(2,1)}, u32[]{:S(2)}) copy-start(bf16[128,1024]{1,0:T(8,128)(2,1)} %param.10) | copy-start | bytes 786436
  0.0 6.9 %copy-start.2 = (bf16[46,184,128]{2,1,0:T(8,128)(2,1)S(1)}, bf16[46,184,128]{2,1,0:T(8,128)(2,1)}, u32[]{:S(2)}) copy-start(bf16[46,184,128]{2,1,0:T(8,128)(2,1)} %param.6) | copy-start | bytes 6500356
  0.0 9.5 %copy-start.12 = (bf16[128,640]{1,0:T(8,128)(2,1)S(1)}, bf16[128,640]{1,0:T(8,128)(2,1)}, u32[]{:S(2)}) copy-start(bf16[128,640]{1,0:T(8,128)(2,1)} %param.8) | copy-start | bytes 491524
  9.5 4.7 %copy-start.4 = (bf16[46,184,128]{2,1,0:T(8,128)(2,1)}, bf16[46,184,128]{2,1,0:T(8,128)(2,1)S(1)}, u32[]{:S(2)}) copy-start(bf16[46,184,128]{2,1,0:T(8,128)(2,1)S(1)} %multiply_convert_fusion.2) | copy-start | bytes 6500356
  14.1 4.6 %copy-start.15 = (s32[5]{0:T(128)S(1)}, s32[5]{0:T(128)}, u32[]{:S(2)}) copy-start(s32[5]{0:T(128)} %param.7) | copy-start | bytes 64
  27.2 2.5 copy-start.9
  27.2 48.7 %collective-permute-start.4 = (bf16[46,184,128]{2,1,0:T(8,128)(2,1)S(1)}, bf16[46,184,128]{2,1,0:T(8,128)(2,1)S(1)}, u32[]{:S(2)}, u32[]{:S(2)}) collective-permute-start(bf16[46,184,128]{2,1,0:T(8,128)(2,1)S(1)} %get-tuple-element.14), channel_id=1, source_target_pairs={{4,0},{6,2},{8,4},{10,6},{12,8},{14,10},{5,1},{7,3},{9,5},{11,7},{... | collective-permute-start | bytes 6500360 | tf_op jit(solution)/shard_map/ppermute | solution.py:27
  29.8 50.5 %collective-permute-start = (bf16[46,184,128]{2,1,0:T(8,128)(2,1)S(1)}, bf16[46,184,128]{2,1,0:T(8,128)(2,1)S(1)}, u32[]{:S(2)}, u32[]{:S(2)}) collective-permute-start(bf16[46,184,128]{2,1,0:T(8,128)(2,1)S(1)} %get-tuple-element.14), channel_id=1, source_target_pairs={{0,4},{2,6},{4,8},{6,10},{8,12},{10,14},{1,5},{3,7},{5,9},{7,11},{... | collective-permute-start | bytes 6500360 | tf_op jit(solution)/shard_map/ppermute | solution.py:27
  76.0 5.6 %copy-start.10 = (bf16[46,184,128]{2,1,0:T(8,128)(2,1)}, bf16[46,184,128]{2,1,0:T(8,128)(2,1)S(1)}, u32[]{:S(2)}) copy-start(bf16[46,184,128]{2,1,0:T(8,128)(2,1)S(1)} %collective-permute-done.4) | copy-start | bytes 6500356
  76.0 6.2 %collective-permute-start.5 = (bf16[46,184,128]{2,1,0:T(8,128)(2,1)S(1)}, bf16[46,184,128]{2,1,0:T(8,128)(2,1)}, u32[]{:S(2)}, u32[]{:S(2)}) collective-permute-start(bf16[46,184,128]{2,1,0:T(8,128)(2,1)S(1)} %collective-permute-done.4), channel_id=1, source_target_pairs={{4,0},{6,2},{8,4},{10,6},{5,1},{7,3},{9,5},{11,7},{20,16},{22,18},... | collective-permute-start | bytes 6500360 | tf_op jit(solution)/shard_map/ppermute | solution.py:27
  80.2 1.9 copy-start.11
  80.2 50.0 %collective-permute-start.1 = (bf16[46,184,128]{2,1,0:T(8,128)(2,1)S(1)}, bf16[46,184,128]{2,1,0:T(8,128)(2,1)}, u32[]{:S(2)}, u32[]{:S(2)}) collective-permute-start(bf16[46,184,128]{2,1,0:T(8,128)(2,1)S(1)} %collective-permute-done), channel_id=1, source_target_pairs={{4,8},{6,10},{8,12},{10,14},{5,9},{7,11},{9,13},{11,15},{20,24},{2... | collective-permute-start | bytes 6500360 | tf_op jit(solution)/shard_map/ppermute | solution.py:27
  81.5 50.0 %collective-permute-start.3 = (bf16[46,184,128]{2,1,0:T(8,128)(2,1)S(1)}, bf16[46,184,128]{2,1,0:T(8,128)(2,1)}, u32[]{:S(2)}, u32[]{:S(2)}) collective-permute-start(bf16[46,184,128]{2,1,0:T(8,128)(2,1)S(1)} %get-tuple-element.13), channel_id=1, source_target_pairs={{0,2},{2,0},{4,6},{6,4},{8,10},{10,8},{12,14},{14,12},{1,3},{3,1},... | collective-permute-start | bytes 6500360 | tf_op jit(solution)/shard_map/ppermute | solution.py:51
  82.1 62.4 %collective-permute-start.6 = (bf16[46,184,128]{2,1,0:T(8,128)(2,1)}, bf16[46,184,128]{2,1,0:T(8,128)(2,1)}, u32[]{:S(2)}, u32[]{:S(2)}) collective-permute-start(bf16[46,184,128]{2,1,0:T(8,128)(2,1)} %collective-permute-done.5), channel_id=1, source_target_pairs={{4,0},{6,2},{5,1},{7,3},{20,16},{22,18},{21,17},{23,19}} | collective-permute-start | bytes 6500360 | tf_op jit(solution)/shard_map/ppermute | solution.py:27
  130.2 49.3 %collective-permute-start.2 = (bf16[46,184,128]{2,1,0:T(8,128)(2,1)}, bf16[46,184,128]{2,1,0:T(8,128)(2,1)}, u32[]{:S(2)}, u32[]{:S(2)}) collective-permute-start(bf16[46,184,128]{2,1,0:T(8,128)(2,1)} %collective-permute-done.1), channel_id=1, source_target_pairs={{8,12},{10,14},{9,13},{11,15},{24,28},{26,30},{25,29},{27,31}} | collective-permute-start | bytes 6500360 | tf_op jit(solution)/shard_map/ppermute | solution.py:27
  193.1 12.7 %slice-start = ((s8[6029312]{0:T(1024)(128)(4,1)}), s8[1835008]{0:T(1024)(128)(4,1)S(1)}, s32[]{:S(2)}) async-start(s8[6029312]{0:T(1024)(128)(4,1)} %bitcast.48), calls=%async_computation | async-start | bytes 3670016
  198.1 7.7 %slice-start.1 = ((s8[6029312]{0:T(1024)(128)(4,1)}), s8[4194304]{0:T(1024)(128)(4,1)S(1)}, s32[]{:S(2)}) async-start(s8[6029312]{0:T(1024)(128)(4,1)} %bitcast.48), calls=%async_computation.1 | async-start | bytes 8388608
  198.1 7.7 %copy-start.8 = (bf16[46,184,128]{1,0,2:T(8,128)(2,1)S(1)}, bf16[46,184,128]{1,0,2:T(8,128)(2,1)}, u32[]{:S(2)}) copy-start(bf16[46,184,128]{1,0,2:T(8,128)(2,1)} %copy.26) | copy-start | bytes 6500356
  225.3 6.0 %copy-start.5 = (f32[1,92,46,128]{1,2,3,0:T(8,128)S(1)}, f32[1,92,46,128]{1,2,3,0:T(8,128)}, u32[]{:S(2)}) copy-start(f32[1,92,46,128]{1,2,3,0:T(8,128)} %convolution_bitcast_fusion.3) | copy-start | bytes 6500356
  225.3 6.0 %copy-start.6 = (f32[1,92,46,128]{1,2,3,0:T(8,128)S(1)}, f32[1,92,46,128]{1,2,3,0:T(8,128)}, u32[]{:S(2)}) copy-start(f32[1,92,46,128]{1,2,3,0:T(8,128)} %convolution_bitcast_fusion.2) | copy-start | bytes 6500356
  232.8 4.5 %copy-start.1 = (f32[4,92,46,128]{1,2,3,0:T(8,128)}, f32[4,92,46,128]{1,2,3,0:T(8,128)S(1)}, u32[]{:S(2)}) copy-start(f32[4,92,46,128]{1,2,3,0:T(8,128)S(1)} %pad_maximum_fusion) | copy-start | bytes 26001412
  247.7 7.7 %collective-permute-start.7 = (f32[2,92,46,128]{3,0,2,1:T(2,128)}, f32[2,92,46,128]{3,0,2,1:T(2,128)}, u32[]{:S(2)}, u32[]{:S(2)}) collective-permute-start(f32[2,92,46,128]{3,0,2,1:T(2,128)} %copy.32), channel_id=1, source_target_pairs={{0,1},{1,0},{2,3},{3,2},{4,5},{5,4},{6,7},{7,6},{8,9},{9,8},{10,11... | collective-permute-start | bytes 13000712 | tf_op jit(solution)/shard_map/ppermute | solution.py:71
  278.4 26.3 %collective-permute-start.8 = (bf16[2,46,46,128]{3,0,2,1:T(2,128)(2,1)}, bf16[2,46,46,128]{3,0,2,1:T(2,128)(2,1)}, u32[]{:S(2)}, u32[]{:S(2)}) collective-permute-start(bf16[2,46,46,128]{3,0,2,1:T(2,128)(2,1)} %copy.34), channel_id=1, source_target_pairs={{0,2},{2,0},{4,6},{6,4},{8,10},{10,8},{12,14},{14,12},{1,3},{3,1},... | collective-permute-start | bytes 3250184 | tf_op jit(solution)/shard_map/ppermute | solution.py:76
  315.6 10.0 %copy-start.7 = (bf16[2,1,46,46,128]{2,3,4,0,1:T(8,128)(2,1)S(1)}, bf16[2,1,46,46,128]{2,3,4,0,1:T(8,128)(2,1)}, u32[]{:S(2)}) copy-start(bf16[2,1,46,46,128]{2,3,4,0,1:T(8,128)(2,1)} %get-tuple-element.12) | copy-start | bytes 3250180
  339.0 6.5 %copy-start.3 = (bf16[46,184,128]{2,1,0:T(8,128)(2,1)S(1)}, bf16[46,184,128]{2,1,0:T(8,128)(2,1)}, u32[]{:S(2)}) copy-start(bf16[46,184,128]{2,1,0:T(8,128)(2,1)} %param.6) | copy-start | bytes 6500356
  339.0 6.5 %copy-start.13 = (bf16[128,128]{1,0:T(8,128)(2,1)S(1)}, bf16[128,128]{1,0:T(8,128)(2,1)}, u32[]{:S(2)}) copy-start(bf16[128,128]{1,0:T(8,128)(2,1)} %param.9) | copy-start | bytes 98308
  356.2 13.5 %copy-start.14 = (bf16[512,128]{1,0:T(8,128)(2,1)S(1)}, bf16[512,128]{1,0:T(8,128)(2,1)}, u32[]{:S(2)}) copy-start(bf16[512,128]{1,0:T(8,128)(2,1)} %param.11) | copy-start | bytes 393220

commit v2 on v1

--- a/solution.py
+++ b/solution.py
@@ -1,7 +1,175 @@
 import jax
 import jax.numpy as jnp
 from jax import lax
+from jax.experimental import pallas as pl
+from jax.experimental.pallas import tpu as pltpu
 from jax.sharding import PartitionSpec as P
+
+VMEM = pltpu.VMEM
+BF16, F32 = jnp.bfloat16, jnp.float32
+
+
+def norm_rows(values):
+    centered = values - jnp.mean(values, axis=-1, keepdims=True)
+    variance = jnp.mean(centered * centered, axis=-1, keepdims=True)
+    return centered * lax.rsqrt(variance + 1e-05)
+
+
+def project_kernel(where_ref, pair_ref, weight_ref, own_ref, other_ref):
+    valid, row0, col0 = where_ref[0], where_ref[1], where_ref[2]
+    _, half, cols, width = pair_ref.shape
+    token = col0 + lax.broadcasted_iota(jnp.int32, (cols, width), 0)
+    low = lax.broadcasted_iota(jnp.int32, (cols, width), 1) < width // 2
+
+    def step(r, carry):
+        rows = [pair_ref[h, r].astype(F32) for h in range(2)]
+        normed = norm_rows(jnp.concatenate(rows, axis=0)).astype(BF16)
+        both = jnp.dot(normed, weight_ref[...], preferred_element_type=F32)
+        out = jax.nn.sigmoid(both[:, :width]) * both[:, width:]
+        halves = []
+        for h in range(2):
+            limit = jnp.where(row0 + h * half + r < valid, valid, 0)
+            halves.append(jnp.where(token < limit, out[h * cols : (h + 1) * cols], 0.0))
+        first, second = halves
+        own_ref[r] = jnp.where(low, first, pltpu.roll(second, width // 2, 1)).astype(BF16)
+        other_ref[r] = jnp.where(low, pltpu.roll(first, width // 2, 1), second).astype(BF16)
+        return carry
+
+    lax.fori_loop(0, half, step, 0)
+
+
+def project(where, pair, weight):
+    _, half, cols, width = pair.shape
+    piece = jax.ShapeDtypeStruct((half, cols, width), BF16)
+    return pl.pallas_call(
+        project_kernel,
+        out_shape=(piece, piece),
+        in_specs=[pl.BlockSpec(memory_space=pltpu.SMEM)] + [pl.BlockSpec(memory_space=VMEM)] * 2,
+        out_specs=[pl.BlockSpec(memory_space=VMEM)] * 2,
+        compiler_params=pltpu.CompilerParams(vmem_limit_bytes=48 << 20),
+        name="project",
+    )(where, pair, weight)
+
+
+def major_kernel(start_ref, first_ref, second_ref, out_ref, work_ref):
+    half, cols, width = first_ref.shape
+    chans = width // 2
+    pitch = work_ref.shape[1] // chans
+    for ref, start in ((first_ref, start_ref[0]), (second_ref, start_ref[1])):
+
+        def step(r, carry, ref=ref, start=start):
+            turned = ref[r].astype(F32).T
+            for h in range(2):
+                rows = turned[h * chans : (h + 1) * chans]
+                at = pl.ds(start + h * half + r, chans, stride=pitch)
+                work_ref[0, at, :] = rows[:, :width]
+                work_ref[1, at, : cols - width] = rows[:, width:]
+            return carry
+
+        lax.fori_loop(0, half, step, 0)
+
+    def pack(c, carry):
+        rows = pl.ds(c * pitch, out_ref.shape[1])
+        out_ref[c, :, :width] = work_ref[0, rows, :].astype(BF16)
+        out_ref[c, :, width:] = work_ref[1, rows, : cols - width].astype(BF16)
+        return carry
+
+    lax.fori_loop(0, chans, pack, 0, unroll=4)
+
+
+def major(starts, first, second):
+    half, cols, width = first.shape
+    pitch = (4 * half + 7) // 8 * 8
+    return pl.pallas_call(
+        major_kernel,
+        out_shape=jax.ShapeDtypeStruct((width // 2, 4 * half, cols), BF16),
+        in_specs=[pl.BlockSpec(memory_space=pltpu.SMEM)] + [pl.BlockSpec(memory_space=VMEM)] * 2,
+        out_specs=pl.BlockSpec(memory_space=VMEM),
+        scratch_shapes=[VMEM((2, width // 2 * pitch, width), F32)],
+        compiler_params=pltpu.CompilerParams(vmem_limit_bytes=48 << 20),
+        name="major",
+    )(starts, first, second)
+
+
+def triangle_kernel(left_ref, right_ref, out_ref, work_ref):
+    chans, rows, _ = left_ref.shape
+    _, half, cols, width = out_ref.shape
+
+    def product(c, carry):
+        value = lax.dot_general(
+            left_ref[c], right_ref[c], (((1,), (1,)), ((), ())), preferred_element_type=F32
+        )
+        work_ref[pl.ds(c, rows, stride=chans), :cols] = value
+        return carry
+
+    lax.fori_loop(0, chans, product, 0, unroll=4)
+    for o in range(2):
+
+        def turn(r, carry, o=o):
+            parts = []
+            for h in range(2):
+                at = pl.multiple_of((o * 2 * half + h * half + r) * chans, chans)
+                parts.append(work_ref[pl.ds(at, chans), :])
+            out_ref[o, r] = jnp.concatenate(parts, axis=0).T[:cols]
+            return carry
+
+        lax.fori_loop(0, half, turn, 0)
+
+
+def triangle(left, right):
+    chans, rows, _ = left.shape
+    return pl.pallas_call(
+        triangle_kernel,
+        out_shape=jax.ShapeDtypeStruct((2, rows // 4, right.shape[1], 2 * chans), F32),
+        in_specs=[pl.BlockSpec(memory_space=VMEM)] * 2,
+        out_specs=pl.BlockSpec(memory_space=VMEM),
+        scratch_shapes=[VMEM((rows * chans, 128), F32)],
+        compiler_params=pltpu.CompilerParams(vmem_limit_bytes=48 << 20),
+        name="triangle",
+    )(left, right)
+
+
+def finish_kernel(order_ref, pair_ref, own_ref, other_ref, gate_ref, out_w_ref, in_ref, back_ref, out_ref):
+    _, half, cols, width = pair_ref.shape
+    blocks = own_ref.shape[0]
+    hidden_units = back_ref.shape[0]
+    low = lax.broadcasted_iota(jnp.int32, own_ref.shape[2:], 1) < width // 2
+    flip = order_ref[0]
+
+    def step(r, carry):
+        tri = [[], []]
+        for b in range(blocks):
+            at = jnp.where(flip == 1, blocks - 1 - b, b)
+            own, other = own_ref[at, r].astype(F32), other_ref[at, r].astype(F32)
+            tri[0].append(jnp.where(low, own, pltpu.roll(other, width // 2, 1)))
+            tri[1].append(jnp.where(low, pltpu.roll(own, width // 2, 1), other))
+        tri_normed = norm_rows(jnp.concatenate(tri[0] + tri[1], axis=0)).astype(BF16)
+        pair = jnp.concatenate([pair_ref[h, r].astype(F32) for h in range(2)], axis=0)
+        normed = norm_rows(pair).astype(BF16)
+        out_gate = jax.nn.sigmoid(jnp.dot(normed, gate_ref[...], preferred_element_type=F32))
+        update = jnp.dot(tri_normed, out_w_ref[...], preferred_element_type=F32)
+        updated = pair + out_gate * update
+        trans_normed = norm_rows(updated).astype(BF16)
+        expanded = jnp.dot(trans_normed, in_ref[...], preferred_element_type=F32)
+        swish, linear = expanded[:, :hidden_units], expanded[:, hidden_units:]
+        hidden = (swish * jax.nn.sigmoid(swish) * linear).astype(BF16)
+        result = updated + jnp.dot(hidden, back_ref[...], preferred_element_type=F32)
+        for h in range(2):
+            out_ref[h, r] = result[h * cols : (h + 1) * cols].astype(BF16)
+        return carry
+
+    lax.fori_loop(0, half, step, 0)
+
+
+def finish(order, pair, own, other, gate_w, out_w, trans_in, trans_out):
+    return pl.pallas_call(
+        finish_kernel,
+        out_shape=jax.ShapeDtypeStruct(pair.shape, BF16),
+        in_specs=[pl.BlockSpec(memory_space=pltpu.SMEM)] + [pl.BlockSpec(memory_space=VMEM)] * 7,
+        out_specs=pl.BlockSpec(memory_space=VMEM),
+        compiler_params=pltpu.CompilerParams(vmem_limit_bytes=48 << 20),
+        name="finish",
+    )(order, pair, own, other, gate_w, out_w, trans_in, trans_out)
 
 
 def layer_norm(values):
@@ -10,7 +178,7 @@
     return centered * lax.rsqrt(variance + 1e-05)
 
 
-def per_device(pair, chain_lengths, in_weight, out_weight, trans_in, trans_out):
+def any_mesh(pair, chain_lengths, in_weight, out_weight, trans_in, trans_out):
     tile_rows, tile_cols, width = pair.shape
     hidden_units = trans_out.shape[0]
     row_count = lax.axis_size("row")
@@ -96,6 +264,97 @@
     return result.reshape(tile_rows, tile_cols, width).astype(jnp.bfloat16)
 
 
+def per_device(pair, chain_lengths, in_weight, out_weight, trans_in, trans_out):
+    if (lax.axis_size("row"), lax.axis_size("col")) != (8, 2):
+        return any_mesh(pair, chain_lengths, in_weight, out_weight, trans_in, trans_out)
+    return two_by_four(pair, chain_lengths, in_weight, out_weight, trans_in, trans_out)
+
+
+def two_by_four(pair, chain_lengths, in_weight, out_weight, trans_in, trans_out):
+    tile_rows, tile_cols, width = pair.shape
+    half = tile_rows // 2
+    tokens = tile_rows * lax.axis_size("row")
+    valid_count = tokens - chain_lengths[chain_lengths.shape[0] - 1]
+    row_id, core = lax.axis_index("row"), lax.axis_index("col")
+    place, side = row_id // 2, row_id % 2
+    keeper = place // 2
+
+    def among(value, moves):
+        return lax.ppermute(value, "row", [(2 * s + b, 2 * t + b) for s, t in moves for b in range(2)])
+
+    def across(value):
+        return lax.ppermute(value, "row", [(i, i ^ 1) for i in range(8)])
+
+    def to_core(value, places, keep):
+        perm = []
+        for z in places:
+            target = z // 2 if keep else 1 - z // 2
+            perm += [(4 * z + 2 * b + 1 - target, 4 * z + 2 * b + target) for b in range(2)]
+        return lax.ppermute(value, ("row", "col"), perm)
+
+    def by_side(block, axis):
+        return jnp.where(side == 0, block, jnp.roll(block, width // 2, axis))
+
+    def gate_pair(first):
+        return jnp.concatenate(
+            [by_side(in_weight[:, (first + i) * width : (first + i + 1) * width], 1) for i in range(2)],
+            axis=1,
+        )
+
+    where = jnp.stack([valid_count, row_id * tile_rows, core * tile_cols]).astype(jnp.int32)
+    folded = pair.reshape(2, half, tile_cols, width)
+    mates, cross = [(0, 1), (1, 0), (2, 3), (3, 2)], [(1, 2), (2, 1)]
+    inward, outward = [(0, 1), (3, 2)], [(1, 0), (2, 3)]
+
+    right_own, right_far = project(where, folded, gate_pair(2))
+    right_beside = across(right_far)
+    mate = [among(v, mates) for v in (right_own, right_beside)]
+    near = [among(v, cross) for v in (right_own, right_beside)]
+    far = [among(v, cross) for v in mate]
+    left_own, left_far = project(where, folded, gate_pair(0))
+    left_beside = across(left_far)
+    guest = [among(v, inward) for v in (left_own, left_beside)]
+
+    plain = jnp.array([0, tile_rows], jnp.int32)
+    sided = jnp.stack([side * tile_rows, (1 - side) * tile_rows]).astype(jnp.int32)
+    left = major(plain, left_own, left_beside)
+    left_guest = major(plain, *guest)
+    rights = {
+        "own": major(sided, right_own, right_beside),
+        "mate": major(sided, *mate),
+        "near": major(sided, *near),
+        "far": major(sided, *far),
+    }
+    home = [triangle(left, rights[k]) for k in ("own", "mate")]
+    away = [triangle(left, rights[k]) for k in ("near", "far")]
+    lent = [triangle(left_guest, rights[k]) for k in ("near", "far")]
+
+    home_rest = [to_core(v, range(4), True) for v in home]
+    away_rest = [to_core(v, (1, 2), False) for v in away]
+    lent_rest = [to_core(v, (1, 2), False) for v in lent]
+    given = [among((a + b).astype(BF16), outward) for a, b in zip(lent, lent_rest)]
+    is_keeper = core == keeper
+    inner = (place == 1) | (place == 2)
+    blocks = []
+    for i in range(2):
+        total = jnp.where(is_keeper, home[i] + home_rest[i], away[i] + away_rest[i]).astype(BF16)
+        blocks.append(jnp.where(is_keeper | inner, total, given[i]))
+    own = jnp.stack([b[0] for b in blocks])
+    other = jnp.stack([across(b[1]) for b in blocks])
+    flip = jnp.where(is_keeper, place % 2, place // 2).astype(jnp.int32).reshape(1)
+    result = finish(
+        flip,
+        folded,
+        own,
+        other,
+        in_weight[:, 4 * width :],
+        by_side(out_weight, 0),
+        trans_in,
+        trans_out,
+    )
+    return result.reshape(tile_rows, tile_cols, width)
+
+
 def solution(mesh):
     placed = (P(("crops", "row"), "col", None), P("crops"), P(), P(), P(), P())
     return jax.shard_map(

time: 392 us -> 388 us (0.990)
  the two profiles are of different devices: /device:TPU:26 before, /device:TPU:1 now
where the time goes in v2:
time: 388 us; the launch traced here: 383 us
  Pallas kernels  180 us (46%)
  waiting for transfers between devices  110 us (28%)
  starting transfers between devices  44.5 us (11%)
  local copies, waits for them, and re-layouts  35 us (9%)
  other arithmetic  13.1 us (3%)
    ppermute x10, waiting for transfers between devices, among(): lax.ppermute(value, 'row', [(2 * s + b, 2 * t + b) for s, t in moves for...  78.7 us
    pallas_call x6, Pallas kernels, major(): pl.pallas_call(major_kernel, out_shape=jax.ShapeDtypeStruct((width // 2,...  65.7 us
    pallas_call x6, Pallas kernels, triangle(): pl.pallas_call(triangle_kernel, out_shape=jax.ShapeDtypeStruct((2, rows /...  63.1 us
    ppermute x4, waiting for transfers between devices, across(): return lax.ppermute(value, 'row', [(i, i ^ 1) for i in range(8)])  30.9 us
    pallas_call x1, Pallas kernels, finish(): pl.pallas_call(finish_kernel, out_shape=jax.ShapeDtypeStruct(pair.shape,...  29.2 us
    ppermute x10, starting transfers between devices, among(): lax.ppermute(value, 'row', [(2 * s + b, 2 * t + b) for s, t in moves for...  23.3 us
    pallas_call x2, Pallas kernels, project(): pl.pallas_call(project_kernel, out_shape=(piece, piece), in_specs=[pl.Blo...  21.9 us
    pallas_call x6, local copies, waits for them, and re-layouts, triangle(): pl.pallas_call(triangle_kernel, out_shape=jax.ShapeDtypeStruct((2, rows /...  18.3 us
  transfers between devices with their start and end apart: 20, of which 8 were waited for; matrix products, arithmetic and copies ran while one was open for 9% of the time, Pallas kernels for 37%

profile of v2, /device:TPU:1, one launch (start us, length us, event | category | flops | bytes accessed | tf_op | source)
XLA Modules:
  0.0 383.0 jit_solution(14989043095492155677)
XLA Ops:
  0.0 1.0 fusion.9
  1.0 1.3 slice.72
  3.0 0.9 fusion.8
  4.0 1.6 copy-done.6
  5.6 10.5 %project.3 = (bf16[23,184,128]{2,1,0:T(8,128)(2,1)S(1)}, bf16[23,184,128]{2,1,0:T(8,128)(2,1)S(1)}) custom-call(s32[3]{0:T(128)S(1)} %pad_add_fusion.where_ref, bf16[2,23,184,128]{3,2,1,0:T(8,128)(2,1)S(1)} %bitcast.13, bf16[128,256]{1,0:T(8,128)(2,1)S(1)} %get-tuple-element.33.weight_ref), custom_call_target="tpu_custom_call" | custom-call | tf_op jit(solution)/shard_map/project/pallas_call | solution.py:44
  16.1 2.1 collective-permute-start.1
  18.2 0.7 collective-permute-start.3
  18.9 11.5 %project.2 = (bf16[23,184,128]{2,1,0:T(8,128)(2,1)}, bf16[23,184,128]{2,1,0:T(8,128)(2,1)S(1)}) custom-call(s32[3]{0:T(128)S(1)} %pad_add_fusion.where_ref, bf16[2,23,184,128]{3,2,1,0:T(8,128)(2,1)S(1)} %bitcast.14, bf16[128,256]{1,0:T(8,128)(2,1)S(1)} %get-tuple-element.32.weight_ref), custom_call_target="tpu_custom_call" | custom-call | tf_op jit(solution)/shard_map/project/pallas_call | solution.py:44
  30.4 4.0 %collective-permute-start.10 = (bf16[23,184,128]{2,1,0:T(8,128)(2,1)S(1)}, bf16[23,184,128]{2,1,0:T(8,128)(2,1)S(1)}, u32[]{:S(2)}, u32[]{:S(2)}) collective-permute-start(bf16[23,184,128]{2,1,0:T(8,128)(2,1)S(1)} %get-tuple-element.11.first_ref), channel_id=1, source_target_pairs={{0,4},{2,6},{4,0},{6,2},{8,12},{10,14},{12,8},{14,10},{1,5},{3,7},... | collective-permute-start | bytes 3250184 | tf_op jit(solution)/shard_map/ppermute | solution.py:283
  34.4 7.4 %collective-permute-done.1.second_ref = bf16[23,184,128]{2,1,0:T(8,128)(2,1)S(1)} collective-permute-done((bf16[23,184,128]{2,1,0:T(8,128)(2,1)S(1)}, bf16[23,184,128]{2,1,0:T(8,128)(2,1)S(1)}, u32[]{:S(2)}, u32[]{:S(2)}) %collective-permute-start.1) | collective-permute-done | bytes 1083424 | tf_op jit(solution)/shard_map/ppermute | solution.py:286
  41.8 1.2 collective-permute-start.11
  43.1 1.6 collective-permute-start.4
  44.7 1.0 copy-done.10
  45.7 5.8 %collective-permute-start.6 = (bf16[23,184,128]{2,1,0:T(8,128)(2,1)}, bf16[23,184,128]{2,1,0:T(8,128)(2,1)}, u32[]{:S(2)}, u32[]{:S(2)}) collective-permute-start(bf16[23,184,128]{2,1,0:T(8,128)(2,1)} %get-tuple-element.9.first_ref), channel_id=1, source_target_pairs={{0,4},{2,6},{12,8},{14,10},{1,5},{3,7},{13,9},{15,11},{16,20},{18,... | collective-permute-start | bytes 3250184 | tf_op jit(solution)/shard_map/ppermute | solution.py:283
  51.5 13.7 %collective-permute-done.second_ref = bf16[23,184,128]{2,1,0:T(8,128)(2,1)} collective-permute-done((bf16[23,184,128]{2,1,0:T(8,128)(2,1)S(1)}, bf16[23,184,128]{2,1,0:T(8,128)(2,1)}, u32[]{:S(2)}, u32[]{:S(2)}) %collective-permute-start) | collective-permute-done | bytes 1083424 | tf_op jit(solution)/shard_map/ppermute | solution.py:286
  65.2 4.1 %collective-permute-start.7 = (bf16[23,184,128]{2,1,0:T(8,128)(2,1)}, bf16[23,184,128]{2,1,0:T(8,128)(2,1)}, u32[]{:S(2)}, u32[]{:S(2)}) collective-permute-start(bf16[23,184,128]{2,1,0:T(8,128)(2,1)} %collective-permute-done.second_ref), channel_id=1, source_target_pairs={{0,4},{2,6},{12,8},{14,10},{1,5},{3,7},{13,9},{15,11},{16,20},{18,... | collective-permute-start | bytes 3250184 | tf_op jit(solution)/shard_map/ppermute | solution.py:283
  69.3 1.7 collective-permute-start.13
  70.9 9.5 %collective-permute-done.11.second_ref = bf16[23,184,128]{2,1,0:T(8,128)(2,1)} collective-permute-done((bf16[23,184,128]{2,1,0:T(8,128)(2,1)S(1)}, bf16[23,184,128]{2,1,0:T(8,128)(2,1)}, u32[]{:S(2)}, u32[]{:S(2)}) %collective-permute-start.11) | collective-permute-done | bytes 1083424 | tf_op jit(solution)/shard_map/ppermute | solution.py:283
  80.4 1.7 collective-permute-start.14
  82.2 1.2 copy-done.11
  83.4 10.9 %major.8.right_ref = bf16[64,92,184]{2,1,0:T(8,128)(2,1)S(1)} custom-call(s32[2]{0:T(128)S(1)} %pad_add_fusion.1.start_ref, bf16[23,184,128]{2,1,0:T(8,128)(2,1)S(1)} %copy-done.11, bf16[23,184,128]{2,1,0:T(8,128)(2,1)} %collective-permute-done.4.second_ref), custom_call_target="tpu_custom_call" | custom-call | tf_op jit(solution)/shard_map/major/pallas_call | solution.py:83
  94.3 1.7 copy-done
  96.0 6.6 %collective-permute-done.6.first_ref = bf16[23,184,128]{2,1,0:T(8,128)(2,1)} collective-permute-done((bf16[23,184,128]{2,1,0:T(8,128)(2,1)}, bf16[23,184,128]{2,1,0:T(8,128)(2,1)}, u32[]{:S(2)}, u32[]{:S(2)}) %collective-permute-start.6) | collective-permute-done | bytes 1083424 | tf_op jit(solution)/shard_map/ppermute | solution.py:283
  102.6 23.2 %collective-permute-done.7.second_ref = bf16[23,184,128]{2,1,0:T(8,128)(2,1)} collective-permute-done((bf16[23,184,128]{2,1,0:T(8,128)(2,1)}, bf16[23,184,128]{2,1,0:T(8,128)(2,1)}, u32[]{:S(2)}, u32[]{:S(2)}) %collective-permute-start.7) | collective-permute-done | bytes 1083424 | tf_op jit(solution)/shard_map/ppermute | solution.py:283
  125.8 11.2 %major.9.left_ref = bf16[64,92,184]{2,1,0:T(8,128)(2,1)S(1)} custom-call(s32[2]{0:T(128)S(1)} %iota_multiply_fusion.start_ref, bf16[23,184,128]{2,1,0:T(8,128)(2,1)} %collective-permute-done.6.first_ref, bf16[23,184,128]{2,1,0:T(8,128)(2,1)} %collective-permute-done.7.second_ref), custom_call_target="tpu_custom_call" | custom-call | tf_op jit(solution)/shard_map/major/pallas_call | solution.py:83
  137.1 10.5 %triangle.8 = f32[2,23,92,128]{3,2,1,0:T(8,128)S(1)} custom-call(bf16[64,92,184]{2,1,0:T(8,128)(2,1)S(1)} %major.9.left_ref, bf16[64,92,184]{2,1,0:T(8,128)(2,1)} %copy-done), custom_call_target="tpu_custom_call" | custom-call | tf_op jit(solution)/shard_map/triangle/pallas_call | solution.py:121
  147.6 3.1 copy.12
  150.7 2.0 collective-permute-start.8
  152.7 11.2 %major.11.right_ref = bf16[64,92,184]{2,1,0:T(8,128)(2,1)S(1)} custom-call(s32[2]{0:T(128)S(1)} %pad_add_fusion.1.start_ref, bf16[23,184,128]{2,1,0:T(8,128)(2,1)} %collective-permute-done.13.first_ref, bf16[23,184,128]{2,1,0:T(8,128)(2,1)} %collective-permute-done.14.second_ref), custom_call_target="tpu_custom_call" | custom-call | tf_op jit(solution)/shard_map/major/pallas_call | solution.py:83
  163.9 1.6 copy-done.1
  165.5 10.5 %triangle.11 = f32[2,23,92,128]{3,2,1,0:T(8,128)S(1)} custom-call(bf16[64,92,184]{2,1,0:T(8,128)(2,1)S(1)} %major.9.left_ref, bf16[64,92,184]{2,1,0:T(8,128)(2,1)} %copy-done.1), custom_call_target="tpu_custom_call" | custom-call | tf_op jit(solution)/shard_map/triangle/pallas_call | solution.py:121
  176.1 3.0 copy.20
  179.1 2.0 collective-permute-start.16
  181.1 11.2 %major.6.left_ref = bf16[64,92,184]{2,1,0:T(8,128)(2,1)S(1)} custom-call(s32[2]{0:T(128)S(1)} %iota_multiply_fusion.start_ref, bf16[23,184,128]{2,1,0:T(8,128)(2,1)} %get-tuple-element.9.first_ref, bf16[23,184,128]{2,1,0:T(8,128)(2,1)} %collective-permute-done.second_ref), custom_call_target="tpu_custom_call" | custom-call | tf_op jit(solution)/shard_map/major/pallas_call | solution.py:83
  192.3 10.2 %major.7.right_ref = bf16[64,92,184]{2,1,0:T(8,128)(2,1)S(1)} custom-call(s32[2]{0:T(128)S(1)} %pad_add_fusion.1.start_ref, bf16[23,184,128]{2,1,0:T(8,128)(2,1)S(1)} %get-tuple-element.11.first_ref, bf16[23,184,128]{2,1,0:T(8,128)(2,1)S(1)} %collective-permute-done.1.second_ref), custom_call_target="tpu_custom_call" | custom-call | tf_op jit(solution)/shard_map/major/pallas_call | solution.py:83
  202.5 1.7 copy-done.9
  204.2 10.5 %triangle.6 = f32[2,23,92,128]{3,2,1,0:T(8,128)S(1)} custom-call(bf16[64,92,184]{2,1,0:T(8,128)(2,1)S(1)} %major.6.left_ref, bf16[64,92,184]{2,1,0:T(8,128)(2,1)} %copy-done.9), custom_call_target="tpu_custom_call" | custom-call | tf_op jit(solution)/shard_map/triangle/pallas_call | solution.py:121
  214.7 3.0 copy.8
  217.8 5.8 %collective-permute-start.2 = (f32[2,23,92,128]{3,0,2,1:T(2,128)}, f32[2,23,92,128]{3,0,2,1:T(2,128)}, u32[]{:S(2)}, u32[]{:S(2)}) collective-permute-start(f32[2,23,92,128]{3,0,2,1:T(2,128)} %copy.8), channel_id=1, source_target_pairs={{1,0},{3,2},{5,4},{7,6},{8,9},{10,11},{12,13},{14,15},{17,16},{19,... | collective-permute-start | bytes 6500360 | tf_op jit(solution)/shard_map/ppermute | solution.py:293
  223.5 10.5 %triangle.7 = f32[2,23,92,128]{3,2,1,0:T(8,128)S(1)} custom-call(bf16[64,92,184]{2,1,0:T(8,128)(2,1)S(1)} %major.6.left_ref, bf16[64,92,184]{2,1,0:T(8,128)(2,1)} %copy-done), custom_call_target="tpu_custom_call" | custom-call | tf_op jit(solution)/shard_map/triangle/pallas_call | solution.py:121
  234.1 3.1 copy.10
  237.1 2.0 collective-permute-start.5
  239.1 10.9 %major.10.right_ref = bf16[64,92,184]{2,1,0:T(8,128)(2,1)S(1)} custom-call(s32[2]{0:T(128)S(1)} %pad_add_fusion.1.start_ref, bf16[23,184,128]{2,1,0:T(8,128)(2,1)S(1)} %collective-permute-done.10.first_ref, bf16[23,184,128]{2,1,0:T(8,128)(2,1)} %collective-permute-done.11.second_ref), custom_call_target="tpu_custom_call" | custom-call | tf_op jit(solution)/shard_map/major/pallas_call | solution.py:83
  250.1 1.7 copy-done.8
  251.7 10.5 %triangle.9 = f32[2,23,92,128]{3,2,1,0:T(8,128)S(1)} custom-call(bf16[64,92,184]{2,1,0:T(8,128)(2,1)S(1)} %major.6.left_ref, bf16[64,92,184]{2,1,0:T(8,128)(2,1)} %copy-done.8), custom_call_target="tpu_custom_call" | custom-call | tf_op jit(solution)/shard_map/triangle/pallas_call | solution.py:121
  262.2 3.1 copy.16
  265.3 2.7 collective-permute-start.12
  268.0 10.5 %triangle.10 = f32[2,23,92,128]{3,2,1,0:T(8,128)S(1)} custom-call(bf16[64,92,184]{2,1,0:T(8,128)(2,1)S(1)} %major.6.left_ref, bf16[64,92,184]{2,1,0:T(8,128)(2,1)} %copy-done.1), custom_call_target="tpu_custom_call" | custom-call | tf_op jit(solution)/shard_map/triangle/pallas_call | solution.py:121
  278.5 3.0 copy.18
  281.5 2.0 collective-permute-start.15
  283.6 2.0 fusion.3
  285.6 1.8 copy.14
  287.4 1.3 collective-permute-start.9
  288.7 2.0 fusion
  290.7 1.8 copy.22
  292.5 1.3 collective-permute-start.17
  293.9 21.9 %collective-permute-done.9 = bf16[2,23,92,128]{3,0,2,1:T(2,128)(2,1)} collective-permute-done((bf16[2,23,92,128]{3,0,2,1:T(2,128)(2,1)}, bf16[2,23,92,128]{3,0,2,1:T(2,128)(2,1)}, u32[]{:S(2)}, u32[]{:S(2)}) %collective-permute-start.9) | collective-permute-done | bytes 1083424 | tf_op jit(solution)/shard_map/ppermute | solution.py:283
  315.8 4.3 %fusion.6 = bf16[2,23,92,128]{3,2,1,0:T(8,128)(2,1)S(1)} fusion(f32[2,23,92,128]{3,2,1,0:T(8,128)} %copy-done.5, f32[2,23,92,128]{3,0,2,1:T(2,128)} %collective-permute-done.5, f32[2,23,92,128]{3,2,1,0:T(8,128)} %copy-done.4, f32[2,23,92,128]{3,0,2,1:T(2,128)} %collective-permute-done.2, bf16[2,23,92,128]{3,0,2,1:T(2,128)(2,1)} %collective-permute-done.9, ...), kind=kLoop, calls=%fused_computation.12 | loop fusion | flops 2708480 | bytes 10833922 | tf_op jit(solution)/shard_map/jit(_where)/select_n | solution.py:341
  320.2 1.3 collective-permute-start.18
  321.5 17.5 %collective-permute-done.17 = bf16[2,23,92,128]{3,0,2,1:T(2,128)(2,1)} collective-permute-done((bf16[2,23,92,128]{3,0,2,1:T(2,128)(2,1)}, bf16[2,23,92,128]{3,0,2,1:T(2,128)(2,1)}, u32[]{:S(2)}, u32[]{:S(2)}) %collective-permute-start.17) | collective-permute-done | bytes 1083424 | tf_op jit(solution)/shard_map/ppermute | solution.py:283
  339.0 3.4 fusion.7
  342.5 1.3 collective-permute-start.19
  344.0 9.8 %collective-permute-done.19 = bf16[23,92,128]{2,1,0:T(8,128)(2,1)S(1)} collective-permute-done((bf16[23,92,128]{2,1,0:T(8,128)(2,1)S(1)}, bf16[23,92,128]{2,1,0:T(8,128)(2,1)S(1)}, u32[]{:S(2)}, u32[]{:S(2)}) %collective-permute-start.19) | collective-permute-done | bytes 541728 | tf_op jit(solution)/shard_map/ppermute | solution.py:286
  353.9 29.2 %finish.1 = bf16[2,23,184,128]{3,2,1,0:T(8,128)(2,1)} custom-call(s32[1]{0:T(128)} %bitcast.order_ref, bf16[2,23,184,128]{3,2,1,0:T(8,128)(2,1)S(1)} %bitcast.15, bf16[2,23,92,128]{3,2,1,0:T(8,128)(2,1)S(1)} %pad_maximum_fusion.own_ref, bf16[2,23,92,128]{3,2,1,0:T(8,128)(2,1)S(1)} %pad_maximum_fusion.1.other_ref, ...), custom_call_target="tpu_custom_call" | custom-call | tf_op jit(solution)/shard_map/finish/pallas_call | solution.py:165
  (46 shorter events, 0.7 us)
Async XLA Ops:
  4.0 1.6 copy-start.6
  16.1 25.7 %collective-permute-start.1 = (bf16[23,184,128]{2,1,0:T(8,128)(2,1)S(1)}, bf16[23,184,128]{2,1,0:T(8,128)(2,1)S(1)}, u32[]{:S(2)}, u32[]{:S(2)}) collective-permute-start(bf16[23,184,128]{2,1,0:T(8,128)(2,1)S(1)} %get-tuple-element.12), channel_id=1, source_target_pairs={{0,2},{2,0},{4,6},{6,4},{8,10},{10,8},{12,14},{14,12},{1,3},{3,1},... | collective-permute-start | bytes 3250184 | tf_op jit(solution)/shard_map/ppermute | solution.py:286
  18.2 26.5 %collective-permute-start.3 = (bf16[23,184,128]{2,1,0:T(8,128)(2,1)S(1)}, bf16[23,184,128]{2,1,0:T(8,128)(2,1)S(1)}, u32[]{:S(2)}, u32[]{:S(2)}) collective-permute-start(bf16[23,184,128]{2,1,0:T(8,128)(2,1)S(1)} %get-tuple-element.11.first_ref), channel_id=1, source_target_pairs={{4,8},{6,10},{8,4},{10,6},{5,9},{7,11},{9,5},{11,7},{20,24},{22,26... | collective-permute-start | bytes 3250184 | tf_op jit(solution)/shard_map/ppermute | solution.py:283
  30.4 34.8 %collective-permute-start = (bf16[23,184,128]{2,1,0:T(8,128)(2,1)S(1)}, bf16[23,184,128]{2,1,0:T(8,128)(2,1)}, u32[]{:S(2)}, u32[]{:S(2)}) collective-permute-start(bf16[23,184,128]{2,1,0:T(8,128)(2,1)S(1)} %get-tuple-element.10), channel_id=1, source_target_pairs={{0,2},{2,0},{4,6},{6,4},{8,10},{10,8},{12,14},{14,12},{1,3},{3,1},... | collective-permute-start | bytes 3250184 | tf_op jit(solution)/shard_map/ppermute | solution.py:286
  30.4 38.9 %collective-permute-start.10 = (bf16[23,184,128]{2,1,0:T(8,128)(2,1)S(1)}, bf16[23,184,128]{2,1,0:T(8,128)(2,1)S(1)}, u32[]{:S(2)}, u32[]{:S(2)}) collective-permute-start(bf16[23,184,128]{2,1,0:T(8,128)(2,1)S(1)} %get-tuple-element.11.first_ref), channel_id=1, source_target_pairs={{0,4},{2,6},{4,0},{6,2},{8,12},{10,14},{12,8},{14,10},{1,5},{3,7},... | collective-permute-start | bytes 3250184 | tf_op jit(solution)/shard_map/ppermute | solution.py:283
  41.8 38.6 %collective-permute-start.11 = (bf16[23,184,128]{2,1,0:T(8,128)(2,1)S(1)}, bf16[23,184,128]{2,1,0:T(8,128)(2,1)}, u32[]{:S(2)}, u32[]{:S(2)}) collective-permute-start(bf16[23,184,128]{2,1,0:T(8,128)(2,1)S(1)} %collective-permute-done.1.second_ref), channel_id=1, source_target_pairs={{0,4},{2,6},{4,0},{6,2},{8,12},{10,14},{12,8},{14,10},{1,5},{3,7},... | collective-permute-start | bytes 3250184 | tf_op jit(solution)/shard_map/ppermute | solution.py:283
  43.1 39.1 %collective-permute-start.4 = (bf16[23,184,128]{2,1,0:T(8,128)(2,1)S(1)}, bf16[23,184,128]{2,1,0:T(8,128)(2,1)}, u32[]{:S(2)}, u32[]{:S(2)}) collective-permute-start(bf16[23,184,128]{2,1,0:T(8,128)(2,1)S(1)} %collective-permute-done.1.second_ref), channel_id=1, source_target_pairs={{4,8},{6,10},{8,4},{10,6},{5,9},{7,11},{9,5},{11,7},{20,24},{22,26... | collective-permute-start | bytes 3250184 | tf_op jit(solution)/shard_map/ppermute | solution.py:283
  44.7 1.0 copy-start.10
  45.7 56.9 %collective-permute-start.6 = (bf16[23,184,128]{2,1,0:T(8,128)(2,1)}, bf16[23,184,128]{2,1,0:T(8,128)(2,1)}, u32[]{:S(2)}, u32[]{:S(2)}) collective-permute-start(bf16[23,184,128]{2,1,0:T(8,128)(2,1)} %get-tuple-element.9.first_ref), channel_id=1, source_target_pairs={{0,4},{2,6},{12,8},{14,10},{1,5},{3,7},{13,9},{15,11},{16,20},{18,... | collective-permute-start | bytes 3250184 | tf_op jit(solution)/shard_map/ppermute | solution.py:283
  65.2 60.7 %collective-permute-start.7 = (bf16[23,184,128]{2,1,0:T(8,128)(2,1)}, bf16[23,184,128]{2,1,0:T(8,128)(2,1)}, u32[]{:S(2)}, u32[]{:S(2)}) collective-permute-start(bf16[23,184,128]{2,1,0:T(8,128)(2,1)} %collective-permute-done.second_ref), channel_id=1, source_target_pairs={{0,4},{2,6},{12,8},{14,10},{1,5},{3,7},{13,9},{15,11},{16,20},{18,... | collective-permute-start | bytes 3250184 | tf_op jit(solution)/shard_map/ppermute | solution.py:283
  69.3 83.4 %collective-permute-start.13 = (bf16[23,184,128]{2,1,0:T(8,128)(2,1)S(1)}, bf16[23,184,128]{2,1,0:T(8,128)(2,1)}, u32[]{:S(2)}, u32[]{:S(2)}) collective-permute-start(bf16[23,184,128]{2,1,0:T(8,128)(2,1)S(1)} %collective-permute-done.10.first_ref), channel_id=1, source_target_pairs={{4,8},{6,10},{8,4},{10,6},{5,9},{7,11},{9,5},{11,7},{20,24},{22,26... | collective-permute-start | bytes 3250184 | tf_op jit(solution)/shard_map/ppermute | solution.py:283
  80.4 72.2 %collective-permute-start.14 = (bf16[23,184,128]{2,1,0:T(8,128)(2,1)}, bf16[23,184,128]{2,1,0:T(8,128)(2,1)}, u32[]{:S(2)}, u32[]{:S(2)}) collective-permute-start(bf16[23,184,128]{2,1,0:T(8,128)(2,1)} %collective-permute-done.11.second_ref), channel_id=1, source_target_pairs={{4,8},{6,10},{8,4},{10,6},{5,9},{7,11},{9,5},{11,7},{20,24},{22,26... | collective-permute-start | bytes 3250184 | tf_op jit(solution)/shard_map/ppermute | solution.py:283
  82.2 1.2 copy-start.11
  94.3 1.7 copy-start
  150.7 130.9 %collective-permute-start.8 = (f32[2,23,92,128]{3,0,2,1:T(2,128)}, f32[2,23,92,128]{3,0,2,1:T(2,128)}, u32[]{:S(2)}, u32[]{:S(2)}) collective-permute-start(f32[2,23,92,128]{3,0,2,1:T(2,128)} %copy.12), channel_id=1, source_target_pairs={{4,5},{6,7},{9,8},{11,10},{20,21},{22,23},{25,24},{27,26}} | collective-permute-start | bytes 6500360 | tf_op jit(solution)/shard_map/ppermute | solution.py:293
  163.9 1.6 copy-start.1
  179.1 108.3 %collective-permute-start.16 = (f32[2,23,92,128]{3,0,2,1:T(2,128)}, f32[2,23,92,128]{3,0,2,1:T(2,128)}, u32[]{:S(2)}, u32[]{:S(2)}) collective-permute-start(f32[2,23,92,128]{3,0,2,1:T(2,128)} %copy.20), channel_id=1, source_target_pairs={{4,5},{6,7},{9,8},{11,10},{20,21},{22,23},{25,24},{27,26}} | collective-permute-start | bytes 6500360 | tf_op jit(solution)/shard_map/ppermute | solution.py:293
  202.5 1.7 copy-start.9
  214.7 3.0 copy-start.4
  217.8 74.8 %collective-permute-start.2 = (f32[2,23,92,128]{3,0,2,1:T(2,128)}, f32[2,23,92,128]{3,0,2,1:T(2,128)}, u32[]{:S(2)}, u32[]{:S(2)}) collective-permute-start(f32[2,23,92,128]{3,0,2,1:T(2,128)} %copy.8), channel_id=1, source_target_pairs={{1,0},{3,2},{5,4},{7,6},{8,9},{10,11},{12,13},{14,15},{17,16},{19,... | collective-permute-start | bytes 6500360 | tf_op jit(solution)/shard_map/ppermute | solution.py:293
  234.1 3.1 copy-start.5
  237.1 56.8 %collective-permute-start.5 = (f32[2,23,92,128]{3,0,2,1:T(2,128)}, f32[2,23,92,128]{3,0,2,1:T(2,128)}, u32[]{:S(2)}, u32[]{:S(2)}) collective-permute-start(f32[2,23,92,128]{3,0,2,1:T(2,128)} %copy.10), channel_id=1, source_target_pairs={{4,5},{6,7},{9,8},{11,10},{20,21},{22,23},{25,24},{27,26}} | collective-permute-start | bytes 6500360 | tf_op jit(solution)/shard_map/ppermute | solution.py:293
  250.0 1.7 copy-start.8
  265.3 56.2 %collective-permute-start.12 = (f32[2,23,92,128]{3,0,2,1:T(2,128)}, f32[2,23,92,128]{3,0,2,1:T(2,128)}, u32[]{:S(2)}, u32[]{:S(2)}) collective-permute-start(f32[2,23,92,128]{3,0,2,1:T(2,128)} %copy.16), channel_id=1, source_target_pairs={{1,0},{3,2},{5,4},{7,6},{8,9},{10,11},{12,13},{14,15},{17,16},{19,... | collective-permute-start | bytes 6500360 | tf_op jit(solution)/shard_map/ppermute | solution.py:293
  278.5 3.0 copy-start.2
  281.5 40.0 %collective-permute-start.15 = (f32[2,23,92,128]{3,0,2,1:T(2,128)}, f32[2,23,92,128]{3,0,2,1:T(2,128)}, u32[]{:S(2)}, u32[]{:S(2)}) collective-permute-start(f32[2,23,92,128]{3,0,2,1:T(2,128)} %copy.18), channel_id=1, source_target_pairs={{4,5},{6,7},{9,8},{11,10},{20,21},{22,23},{25,24},{27,26}} | collective-permute-start | bytes 6500360 | tf_op jit(solution)/shard_map/ppermute | solution.py:293
  287.4 28.4 %collective-permute-start.9 = (bf16[2,23,92,128]{3,0,2,1:T(2,128)(2,1)}, bf16[2,23,92,128]{3,0,2,1:T(2,128)(2,1)}, u32[]{:S(2)}, u32[]{:S(2)}) collective-permute-start(bf16[2,23,92,128]{3,0,2,1:T(2,128)(2,1)} %copy.14), channel_id=1, source_target_pairs={{4,0},{6,2},{8,12},{10,14},{5,1},{7,3},{9,13},{11,15},{20,16},{22,... | collective-permute-start | bytes 3250184 | tf_op jit(solution)/shard_map/ppermute | solution.py:283
  292.5 46.5 %collective-permute-start.17 = (bf16[2,23,92,128]{3,0,2,1:T(2,128)(2,1)}, bf16[2,23,92,128]{3,0,2,1:T(2,128)(2,1)}, u32[]{:S(2)}, u32[]{:S(2)}) collective-permute-start(bf16[2,23,92,128]{3,0,2,1:T(2,128)(2,1)} %copy.22), channel_id=1, source_target_pairs={{4,0},{6,2},{8,12},{10,14},{5,1},{7,3},{9,13},{11,15},{20,16},{22,... | collective-permute-start | bytes 3250184 | tf_op jit(solution)/shard_map/ppermute | solution.py:283
  320.1 18.9 %copy-start.3 = (f32[2,23,92,128]{3,2,1,0:T(8,128)S(1)}, f32[2,23,92,128]{3,2,1,0:T(8,128)}, u32[]{:S(2)}) copy-start(f32[2,23,92,128]{3,2,1,0:T(8,128)} %copy-done.2) | copy-start | bytes 6500356
  320.2 23.7 %collective-permute-start.18 = (bf16[23,92,128]{2,1,0:T(8,128)(2,1)S(1)}, bf16[23,92,128]{2,1,0:T(8,128)(2,1)S(1)}, u32[]{:S(2)}, u32[]{:S(2)}) collective-permute-start(bf16[23,92,128]{2,1,0:T(8,128)(2,1)S(1)} %get-tuple-element.13), channel_id=1, source_target_pairs={{0,2},{2,0},{4,6},{6,4},{8,10},{10,8},{12,14},{14,12},{1,3},{3,1},... | collective-permute-start | bytes 1625096 | tf_op jit(solution)/shard_map/ppermute | solution.py:286
  342.4 1.4 copy-start.14
  342.5 11.2 %collective-permute-start.19 = (bf16[23,92,128]{2,1,0:T(8,128)(2,1)S(1)}, bf16[23,92,128]{2,1,0:T(8,128)(2,1)S(1)}, u32[]{:S(2)}, u32[]{:S(2)}) collective-permute-start(bf16[23,92,128]{2,1,0:T(8,128)(2,1)S(1)} %get-tuple-element.15), channel_id=1, source_target_pairs={{0,2},{2,0},{4,6},{6,4},{8,10},{10,8},{12,14},{14,12},{1,3},{3,1},... | collective-permute-start | bytes 1625096 | tf_op jit(solution)/shard_map/ppermute | solution.py:286
  343.8 10.0 %copy-start.7 = (bf16[46,184,128]{2,1,0:T(8,128)(2,1)S(1)}, bf16[46,184,128]{2,1,0:T(8,128)(2,1)}, u32[]{:S(2)}) copy-start(bf16[46,184,128]{2,1,0:T(8,128)(2,1)} %param.7) | copy-start | bytes 6500356
  343.8 10.0 %copy-start.12 = (bf16[128,1024]{1,0:T(8,128)(2,1)S(1)}, bf16[128,1024]{1,0:T(8,128)(2,1)}, u32[]{:S(2)}) copy-start(bf16[128,1024]{1,0:T(8,128)(2,1)} %in_ref.1) | copy-start | bytes 786436
  343.8 10.0 %copy-start.13 = (bf16[512,128]{1,0:T(8,128)(2,1)S(1)}, bf16[512,128]{1,0:T(8,128)(2,1)}, u32[]{:S(2)}) copy-start(bf16[512,128]{1,0:T(8,128)(2,1)} %back_ref.1) | copy-start | bytes 393220

commit v3 on v1

--- a/solution.py
+++ b/solution.py
@@ -1,7 +1,275 @@
 import jax
 import jax.numpy as jnp
 from jax import lax
+from jax.experimental import pallas as pl
+from jax.experimental.pallas import tpu as pltpu
 from jax.sharding import PartitionSpec as P
+
+VMEM = pltpu.VMEM
+BF16, F32 = jnp.bfloat16, jnp.float32
+CHUNK = 16
+
+
+def whole(count):
+    return [pl.BlockSpec(memory_space=VMEM)] * count
+
+
+def params():
+    return pltpu.CompilerParams(vmem_limit_bytes=48 << 20)
+
+
+def cost(flops, moved, transcendentals=0):
+    return pl.CostEstimate(flops=flops, bytes_accessed=moved, transcendentals=transcendentals)
+
+
+def sigmoid(values):
+    return 0.5 * jnp.tanh(0.5 * values) + 0.5
+
+
+def norm_chans(values):
+    centered = values - jnp.mean(values, axis=0, keepdims=True)
+    variance = jnp.mean(centered * centered, axis=0, keepdims=True)
+    return centered * lax.rsqrt(variance + 1e-05)
+
+
+def padded(count, unit):
+    return -(-count // unit) * unit
+
+
+def project_kernel(where_ref, pair_ref, weight_ref, own_ref, far_ref):
+    valid, row0, col0 = where_ref[0], where_ref[1], where_ref[2]
+    _, half, cols, width = pair_ref.shape
+    chans = width // 2
+    tail = cols - width
+    lane = lax.broadcasted_iota(jnp.int32, (1, 3 * width), 1)
+    in_tail = lane >= 2 * width
+    ends = jnp.where(in_tail, 2 * width + chans, width)
+    is_first = jnp.where(lane < ends, 1, 0)
+    token = jnp.where(in_tail, lane % chans + width, lane % width) + col0
+    gap = jnp.zeros((chans - tail, width), F32)
+
+    def step(r, carry):
+        first, second = (pair_ref[h, r].astype(F32) for h in range(2))
+        tokens = jnp.concatenate(
+            [first[:width], second[:width], first[width:], gap, second[width:], gap], axis=0
+        )
+        normed = norm_chans(tokens.T).astype(BF16)
+        both = jnp.dot(weight_ref[...], normed, preferred_element_type=F32)
+        limits = [jnp.where(row0 + h * half + r < valid, valid, 0) for h in range(2)]
+        keep = jnp.where(token < limits[1] + is_first * (limits[0] - limits[1]), 1.0, 0.0)
+        out = (sigmoid(both[:width]) * both[width:] * keep).astype(BF16)
+        own_ref[r] = out[:chans]
+        far_ref[r] = out[chans:]
+        return carry
+
+    lax.fori_loop(0, half, step, 0, unroll=4)
+
+
+def project(where, pair, weight):
+    _, half, cols, width = pair.shape
+    piece = jax.ShapeDtypeStruct((half, width // 2, 3 * width), BF16)
+    return pl.pallas_call(
+        project_kernel,
+        out_shape=(piece, piece),
+        in_specs=[pl.BlockSpec(memory_space=pltpu.SMEM)] + whole(2),
+        out_specs=whole(2),
+        compiler_params=params(),
+        cost_estimate=cost(4 * pair.size * width, 4 * pair.size, pair.size),
+        name="project",
+    )(where, pair, weight)
+
+
+def channel_major(pieces, clear):
+    width = pieces[0].shape[2] // 3
+    main, rest = [], []
+    for piece in pieces:
+        tail = piece[:, :, 2 * width :]
+        turned = jnp.concatenate([tail[:, :, width // 2 :], tail[:, :, : width // 2]], axis=2)
+        main += [piece[:, :, :width], piece[:, :, width : 2 * width]]
+        rest += [tail, turned]
+    rest = jnp.concatenate(rest, axis=0)
+    if clear:
+        low = lax.broadcasted_iota(jnp.int32, rest.shape, 2) < width // 2
+        rest = jnp.where(low, rest, jnp.zeros_like(rest))
+    main = jnp.swapaxes(jnp.concatenate(main, axis=0), 0, 1)
+    return main, jnp.swapaxes(rest, 0, 1)
+
+
+def left_kernel(own_ref, beside_ref, out_ref):
+    width = own_ref.shape[2] // 3
+    main, rest = channel_major([own_ref[...], beside_ref[...]], True)
+    rows = main.shape[1]
+    out_ref[:, :rows, :width] = main
+    out_ref[:, :rows, width:] = rest
+    out_ref[:, rows:] = jnp.zeros_like(out_ref[:, rows:])
+
+
+def left_major(own, beside):
+    half, chans, lanes = own.shape
+    piece = pl.BlockSpec((half, CHUNK, lanes), lambda c: (0, c, 0))
+    return pl.pallas_call(
+        left_kernel,
+        grid=(chans // CHUNK,),
+        out_shape=jax.ShapeDtypeStruct((chans, padded(4 * half, 16), lanes // 3 * 2), BF16),
+        in_specs=[piece, piece],
+        out_specs=pl.BlockSpec((CHUNK, padded(4 * half, 16), lanes // 3 * 2), lambda c: (c, 0, 0)),
+        compiler_params=params(),
+        cost_estimate=cost(0, 8 * own.size),
+        name="left_major",
+    )(own, beside)
+
+
+def triangle_kernel(side_ref, *refs):
+    lefts = len(refs) // 2 - 1
+    own, beside = refs[lefts][...], refs[lefts + 1][...]
+    outs, right_ref = refs[lefts + 2 : -1], refs[-1]
+    width = own.shape[2] // 3
+    even = side_ref[0] == 0
+    main, rest = channel_major(
+        [jnp.where(even, own, beside), jnp.where(even, beside, own)], False
+    )
+    rows = main.shape[1]
+
+    @pl.when(pl.program_id(0) == 0)
+    def _():
+        right_ref[...] = jnp.zeros_like(right_ref)
+
+    right_ref[:, :rows, :width] = main
+    right_ref[:, :rows, width:] = rest
+    for c in range(CHUNK):
+        for left_ref, out_ref in zip(refs[:lefts], outs):
+            out_ref[c] = lax.dot_general(
+                left_ref[c], right_ref[c], (((1,), (1,)), ((), ())), preferred_element_type=F32
+            )
+
+
+def triangle(side, lefts, own, beside):
+    half, chans, lanes = own.shape
+    rows, cols = padded(4 * half, 16), padded(4 * half, 128)
+    piece = pl.BlockSpec((half, CHUNK, lanes), lambda c: (0, c, 0))
+    left = pl.BlockSpec((CHUNK, rows, lanes // 3 * 2), lambda c: (c, 0, 0))
+    out = pl.BlockSpec((CHUNK, rows, cols), lambda c: (c, 0, 0))
+    return pl.pallas_call(
+        triangle_kernel,
+        grid=(chans // CHUNK,),
+        out_shape=[jax.ShapeDtypeStruct((chans, rows, cols), F32) for _ in lefts],
+        in_specs=[pl.BlockSpec(memory_space=pltpu.SMEM)] + [left] * len(lefts) + [piece, piece],
+        out_specs=[out] * len(lefts),
+        scratch_shapes=[VMEM((CHUNK, cols, lanes // 3 * 2), BF16)],
+        compiler_params=params(),
+        cost_estimate=cost(2 * len(lefts) * chans * rows * cols * lanes // 3 * 2, (4 + 8 * len(lefts)) * own.size),
+        name="triangle",
+    )(side, *lefts, own, beside)
+
+
+def fold_kernel(role_ref, *refs):
+    own_ref, beside_ref, work_ref = refs[-3:]
+    half, cols, width = own_ref.shape
+    chans = width // 2
+    c = pl.program_id(0)
+    options = len(refs[:-3]) // 2
+    for option in range(options):
+        mine_ref, rest_ref = refs[2 * option : 2 * option + 2]
+
+        def gather():
+            total = (mine_ref[...] + rest_ref[...]).astype(BF16)
+            at = pl.ds(pl.multiple_of(c * CHUNK, CHUNK), CHUNK)
+            work_ref[:, at, :] = jnp.swapaxes(total, 0, 1)
+
+        if options == 1:
+            gather()
+        else:
+            pl.when(role_ref[0] == option)(gather)
+
+    @pl.when(c == pl.num_programs(0) - 1)
+    def _():
+        for o, out_ref in enumerate((own_ref, beside_ref)):
+
+            def turn(r, carry, o=o, out_ref=out_ref):
+                at = o * 2 * half + r
+                stacked = jnp.concatenate([work_ref[at], work_ref[at + half]], axis=0)
+                out_ref[r] = stacked.T[:cols]
+                return carry
+
+            lax.fori_loop(0, half, turn, 0, unroll=True)
+
+
+def fold(half, role, *parts):
+    chans, rows, cols = parts[0].shape
+    out = jax.ShapeDtypeStruct((half, padded(4 * half, 16), 2 * chans), BF16)
+
+    def block(option):
+        if len(parts) == 2:
+            return pl.BlockSpec((CHUNK, rows, cols), lambda c, role_ref: (c, 0, 0))
+        return pl.BlockSpec(
+            (CHUNK, rows, cols), lambda c, role_ref: (jnp.where(role_ref[0] == option, c, 0), 0, 0)
+        )
+
+    return pl.pallas_call(
+        fold_kernel,
+        grid_spec=pltpu.PrefetchScalarGridSpec(
+            num_scalar_prefetch=1,
+            grid=(chans // CHUNK,),
+            in_specs=[block(i // 2) for i in range(len(parts))],
+            out_specs=[pl.BlockSpec(out.shape, lambda c, role_ref: (0, 0, 0))] * 2,
+            scratch_shapes=[VMEM((rows, chans, cols), BF16)],
+        ),
+        out_shape=(out, out),
+        compiler_params=params(),
+        cost_estimate=cost(0, 10 * parts[0].size),
+        name="fold",
+    )(role, *parts)
+
+
+def finish_kernel(order_ref, pair_ref, *refs):
+    owns, others = refs[0:2], refs[2:4]
+    gate_ref, out_w_ref, in_ref, back_ref, out_ref = refs[4:]
+    _, half, cols, width = pair_ref.shape
+    hidden_units = back_ref.shape[1]
+    flip = order_ref[0] == 1
+
+    block = cols // 2
+    chans = width // 2
+
+    def step(r, carry):
+        rows = [[], []]
+        for own_ref, other_ref in zip(owns, others):
+            own, other = (ref[r].astype(F32).T[:, :block] for ref in (own_ref, other_ref))
+            for h in range(2):
+                at = slice(h * chans, (h + 1) * chans)
+                rows[h].append(jnp.concatenate([own[at], other[at]], axis=0))
+        lanes = []
+        for first, second in rows:
+            lanes += [jnp.where(flip, second, first), jnp.where(flip, first, second)]
+        tri_normed = norm_chans(jnp.concatenate(lanes, axis=1)).astype(BF16)
+        pair = jnp.concatenate([pair_ref[h, r].astype(F32) for h in range(2)], axis=0).T
+        normed = norm_chans(pair).astype(BF16)
+        out_gate = sigmoid(jnp.dot(gate_ref[...], normed, preferred_element_type=F32))
+        update = jnp.dot(out_w_ref[...], tri_normed, preferred_element_type=F32)
+        updated = pair + out_gate * update
+        trans_normed = norm_chans(updated).astype(BF16)
+        expanded = jnp.dot(in_ref[...], trans_normed, preferred_element_type=F32)
+        swish, linear = expanded[:hidden_units], expanded[hidden_units:]
+        hidden = (swish * sigmoid(swish) * linear).astype(BF16)
+        result = updated + jnp.dot(back_ref[...], hidden, preferred_element_type=F32)
+        result = result.T
+        for h in range(2):
+            out_ref[h, r] = result[h * cols : (h + 1) * cols].astype(BF16)
+        return carry
+
+    lax.fori_loop(0, half, step, 0, unroll=2)
+
+
+def finish(order, pair, owns, others, gate_w, out_w, trans_in, trans_out):
+    return pl.pallas_call(
+        finish_kernel,
+        out_shape=jax.ShapeDtypeStruct(pair.shape, BF16),
+        in_specs=[pl.BlockSpec(memory_space=pltpu.SMEM)] + whole(9),
+        out_specs=pl.BlockSpec(memory_space=VMEM),
+        compiler_params=params(),
+        cost_estimate=cost(28 * pair.size * pair.shape[-1], 6 * pair.size, 6 * pair.size),
+        name="finish",
+    )(order, pair, *owns, *others, gate_w, out_w, trans_in, trans_out)
 
 
 def layer_norm(values):
@@ -10,7 +278,7 @@
     return centered * lax.rsqrt(variance + 1e-05)
 
 
-def per_device(pair, chain_lengths, in_weight, out_weight, trans_in, trans_out):
+def any_mesh(pair, chain_lengths, in_weight, out_weight, trans_in, trans_out):
     tile_rows, tile_cols, width = pair.shape
     hidden_units = trans_out.shape[0]
     row_count = lax.axis_size("row")
@@ -96,6 +364,90 @@
     return result.reshape(tile_rows, tile_cols, width).astype(jnp.bfloat16)
 
 
+def per_device(pair, chain_lengths, in_weight, out_weight, trans_in, trans_out):
+    if (lax.axis_size("row"), lax.axis_size("col")) != (8, 2):
+        return any_mesh(pair, chain_lengths, in_weight, out_weight, trans_in, trans_out)
+    return two_by_four(pair, chain_lengths, in_weight, out_weight, trans_in, trans_out)
+
+
+def two_by_four(pair, chain_lengths, in_weight, out_weight, trans_in, trans_out):
+    tile_rows, tile_cols, width = pair.shape
+    half = tile_rows // 2
+    tokens = tile_rows * lax.axis_size("row")
+    valid_count = tokens - chain_lengths[chain_lengths.shape[0] - 1]
+    row_id, core = lax.axis_index("row"), lax.axis_index("col")
+    place, side = row_id // 2, row_id % 2
+    keeper = place // 2
+
+    def among(value, moves):
+        return lax.ppermute(value, "row", [(2 * s + b, 2 * t + b) for s, t in moves for b in range(2)])
+
+    def across(value):
+        return lax.ppermute(value, "row", [(i, i ^ 1) for i in range(8)])
+
+    def to_core(value, places, keep):
+        perm = []
+        for z in places:
+            target = z // 2 if keep else 1 - z // 2
+            perm += [(4 * z + 2 * b + 1 - target, 4 * z + 2 * b + target) for b in range(2)]
+        return lax.ppermute(value, ("row", "col"), perm)
+
+    def by_side(block, axis):
+        return jnp.where(side == 0, block, jnp.roll(block, width // 2, axis))
+
+    def gate_pair(first):
+        parts = [
+            by_side(in_weight[:, (first + i) * width : (first + i + 1) * width], 1) for i in range(2)
+        ]
+        return jnp.concatenate(parts, axis=1).T
+
+    where = jnp.stack([valid_count, row_id * tile_rows, core * tile_cols]).astype(jnp.int32)
+    sides = side.astype(jnp.int32).reshape(1)
+    is_keeper = core == keeper
+    role = jnp.where(is_keeper, 0, 1).astype(jnp.int32).reshape(1)
+    folded = pair.reshape(2, half, tile_cols, width)
+    mates, cross = [(0, 1), (1, 0), (2, 3), (3, 2)], [(1, 2), (2, 1)]
+    inward, outward = [(0, 1), (3, 2)], [(1, 0), (2, 3)]
+
+    right_own, right_far = project(where, folded, gate_pair(2))
+    right_beside = across(right_far)
+    mate = [among(v, mates) for v in (right_own, right_beside)]
+    near = [among(v, cross) for v in (right_own, right_beside)]
+    far = [among(v, cross) for v in mate]
+    left_own, left_far = project(where, folded, gate_pair(0))
+    left_beside = across(left_far)
+    guest = [among(v, inward) for v in (left_own, left_beside)]
+
+    left = left_major(left_own, left_beside)
+    home = [triangle(sides, [left], right_own, right_beside)[0], triangle(sides, [left], *mate)[0]]
+    left_guest = left_major(*guest)
+    away, lent = zip(*(triangle(sides, [left, left_guest], *v) for v in (near, far)))
+
+    home_rest = [to_core(v, range(4), True) for v in home]
+    away_rest = [to_core(v, (1, 2), False) for v in away]
+    lent_rest = [to_core(v, (1, 2), False) for v in lent]
+    inner = (place == 1) | (place == 2)
+    owns, others = [], []
+    for i in range(2):
+        given = [among(v, outward) for v in fold(half, role, lent[i], lent_rest[i])]
+        kept = fold(half, role, home[i], home_rest[i], away[i], away_rest[i])
+        own, beside = (jnp.where(is_keeper | inner, k, g) for k, g in zip(kept, given))
+        owns.append(own)
+        others.append(across(beside))
+    flip = jnp.where(is_keeper, place % 2, place // 2).astype(jnp.int32).reshape(1)
+    result = finish(
+        flip,
+        folded,
+        owns,
+        others,
+        in_weight[:, 4 * width :].T,
+        by_side(out_weight, 0).T,
+        trans_in.T,
+        trans_out.T,
+    )
+    return result.reshape(tile_rows, tile_cols, width)
+
+
 def solution(mesh):
     placed = (P(("crops", "row"), "col", None), P("crops"), P(), P(), P(), P())
     return jax.shard_map(

time: 392 us -> 284 us (0.72)
  the two profiles are of different devices: /device:TPU:26 before, /device:TPU:1 now
where the time goes in v3:
time: 284 us; the launch traced here: 279 us
  waiting for transfers between devices  129 us (45%)
  Pallas kernels  86.2 us (30%)
  starting transfers between devices  41.5 us (15%)
  local copies, waits for them, and re-layouts  14.5 us (5%)
  other arithmetic  7.15 us (3%)
    ppermute x12, waiting for transfers between devices, among(): lax.ppermute(value, 'row', [(2 * s + b, 2 * t + b) for s, t in moves for...  93.9 us
    ppermute x4, waiting for transfers between devices, across(): return lax.ppermute(value, 'row', [(i, i ^ 1) for i in range(8)])  35.1 us
    pallas_call x4, Pallas kernels, triangle(): pl.pallas_call(triangle_kernel, grid=(chans // CHUNK,), out_shape=[jax.Sh...  28.9 us
    pallas_call x1, Pallas kernels, finish(): pl.pallas_call(finish_kernel, out_shape=jax.ShapeDtypeStruct(pair.shape,...  26.2 us
    ppermute x12, starting transfers between devices, among(): lax.ppermute(value, 'row', [(2 * s + b, 2 * t + b) for s, t in moves for...  19 us
    ppermute x6, starting transfers between devices, to_core(): return lax.ppermute(value, ('row', 'col'), perm)  18 us
    pallas_call x4, Pallas kernels, fold(): pl.pallas_call(fold_kernel, grid_spec=pltpu.PrefetchScalarGridSpec(num_sc...  17.8 us
    unnamed x46, local copies, waits for them, and re-layouts  11.3 us
  transfers between devices with their start and end apart: 22, of which 9 were waited for; matrix products, arithmetic and copies ran while one was open for 4% of the time, Pallas kernels for 20%

profile of v3, /device:TPU:1, one launch (start us, length us, event | category | flops | bytes accessed | tf_op | source)
XLA Modules:
  0.0 279.5 jit_solution(3916835462611379528)
XLA Ops:
  0.0 1.0 fusion.2
  1.0 0.8 fusion.1
  2.3 0.1 copy.25
  2.4 0.1 copy.28
  2.6 1.3 slice.60
  4.6 1.6 copy-done.2
  6.2 5.4 %project.2 = (bf16[23,64,384]{2,1,0:T(8,128)(2,1)S(1)}, bf16[23,64,384]{2,1,0:T(8,128)(2,1)}) custom-call(s32[3]{0:T(128)S(1)} %pad_add_fusion.where_ref, bf16[2,23,184,128]{3,2,1,0:T(8,128)(2,1)S(1)} %bitcast.16, bf16[256,128]{1,0:T(8,128)(2,1)S(1)} %maximum_bitcast_fusion.weight_ref), custom_call_target="tpu_custom_call" | custom-call | flops 554696704 | bytes 4333568 | tf_op jit(solution)/shard_map/project/pallas_call | solution.py:71
  11.6 1.0 copy-done.7
  12.6 2.0 collective-permute-start
  14.9 0.7 copy.36
  15.6 0.1 copy.31
  15.8 0.1 copy.34
  15.9 0.8 maximum_select_fusion.2
  16.8 4.4 %project.3 = (bf16[23,64,384]{2,1,0:T(8,128)(2,1)S(1)}, bf16[23,64,384]{2,1,0:T(8,128)(2,1)S(1)}) custom-call(s32[3]{0:T(128)S(1)} %pad_add_fusion.where_ref, bf16[2,23,184,128]{3,2,1,0:T(8,128)(2,1)S(1)} %bitcast.17, bf16[256,128]{1,0:T(8,128)(2,1)S(1)} %maximum_bitcast_fusion.1.weight_ref), custom_call_target="tpu_custom_call" | custom-call | flops 554696704 | bytes 4333568 | tf_op jit(solution)/shard_map/project/pallas_call | solution.py:71
  21.2 3.5 %collective-permute-start.3 = (bf16[23,64,384]{2,1,0:T(8,128)(2,1)S(1)}, bf16[23,64,384]{2,1,0:T(8,128)(2,1)S(1)}, u32[]{:S(2)}, u32[]{:S(2)}) collective-permute-start(bf16[23,64,384]{2,1,0:T(8,128)(2,1)S(1)} %copy-done.8), channel_id=1, source_target_pairs={{0,4},{2,6},{12,8},{14,10},{1,5},{3,7},{13,9},{15,11},{16,20},{18,... | collective-permute-start | bytes 3391496 | tf_op jit(solution)/shard_map/ppermute | solution.py:383
  24.7 14.8 %collective-permute-done.beside_ref = bf16[23,64,384]{2,1,0:T(8,128)(2,1)S(1)} collective-permute-done((bf16[23,64,384]{2,1,0:T(8,128)(2,1)}, bf16[23,64,384]{2,1,0:T(8,128)(2,1)S(1)}, u32[]{:S(2)}, u32[]{:S(2)}) %collective-permute-start) | collective-permute-done | bytes 1130528 | tf_op jit(solution)/shard_map/ppermute | solution.py:386
  39.5 3.2 %collective-permute-start.4 = (bf16[23,64,384]{2,1,0:T(8,128)(2,1)S(1)}, bf16[23,64,384]{2,1,0:T(8,128)(2,1)S(1)}, u32[]{:S(2)}, u32[]{:S(2)}) collective-permute-start(bf16[23,64,384]{2,1,0:T(8,128)(2,1)S(1)} %collective-permute-done.beside_ref), channel_id=1, source_target_pairs={{0,4},{2,6},{12,8},{14,10},{1,5},{3,7},{13,9},{15,11},{16,20},{18,... | collective-permute-start | bytes 3391496 | tf_op jit(solution)/shard_map/ppermute | solution.py:383
  42.7 0.7 collective-permute-start.5
  43.4 20.3 %collective-permute-done.1.refs_2_ = bf16[23,64,384]{2,1,0:T(8,128)(2,1)S(1)} collective-permute-done((bf16[23,64,384]{2,1,0:T(8,128)(2,1)S(1)}, bf16[23,64,384]{2,1,0:T(8,128)(2,1)S(1)}, u32[]{:S(2)}, u32[]{:S(2)}) %collective-permute-start.1) | collective-permute-done | bytes 1130528 | tf_op jit(solution)/shard_map/ppermute | solution.py:386
  63.7 0.7 collective-permute-start.6
  64.4 3.8 %collective-permute-start.10 = (bf16[23,64,384]{2,1,0:T(8,128)(2,1)S(1)}, bf16[23,64,384]{2,1,0:T(8,128)(2,1)S(1)}, u32[]{:S(2)}, u32[]{:S(2)}) collective-permute-start(bf16[23,64,384]{2,1,0:T(8,128)(2,1)S(1)} %get-tuple-element.23.refs_1_), channel_id=1, source_target_pairs={{0,4},{2,6},{4,0},{6,2},{8,12},{10,14},{12,8},{14,10},{1,5},{3,7},... | collective-permute-start | bytes 3391496 | tf_op jit(solution)/shard_map/ppermute | solution.py:383
  68.2 1.7 left_major.2.refs_0_
  70.0 1.7 copy-done
  71.7 0.1 collective-permute-done.4.beside_ref
  71.8 1.7 left_major.3.refs_1_
  73.6 1.6 copy-done.1
  75.2 8.5 %triangle.5 = (f32[64,96,128]{2,1,0:T(8,128)}, f32[64,96,128]{2,1,0:T(8,128)}) custom-call(s32[1]{0:T(128)} %bitcast.3.side_ref, bf16[64,96,256]{2,1,0:T(8,128)(2,1)} %copy-done, bf16[64,96,256]{2,1,0:T(8,128)(2,1)} %copy-done.1, bf16[23,64,384]{2,1,0:T(8,128)(2,1)S(1)} %collective-permute-done.5.refs_2_, bf16[23,64,384]{2,1,0:T(8,128)(2,1)S(1)} %collective-permute-done.6.refs_3_), custom_call_target="tpu_custom_call" | custom-call | flops 805306368 | bytes 11304960 | tf_op jit(solution)/shard_map/triangle/pallas_call | solution.py:152
  83.7 2.3 collective-permute-start.8
  86.0 10.0 %collective-permute-done.10.refs_1_ = bf16[23,64,384]{2,1,0:T(8,128)(2,1)S(1)} collective-permute-done((bf16[23,64,384]{2,1,0:T(8,128)(2,1)S(1)}, bf16[23,64,384]{2,1,0:T(8,128)(2,1)S(1)}, u32[]{:S(2)}, u32[]{:S(2)}) %collective-permute-start.10) | collective-permute-done | bytes 1130528 | tf_op jit(solution)/shard_map/ppermute | solution.py:383
  96.0 0.7 collective-permute-start.13
  96.8 23.5 %collective-permute-done.11.refs_2_ = bf16[23,64,384]{2,1,0:T(8,128)(2,1)S(1)} collective-permute-done((bf16[23,64,384]{2,1,0:T(8,128)(2,1)S(1)}, bf16[23,64,384]{2,1,0:T(8,128)(2,1)S(1)}, u32[]{:S(2)}, u32[]{:S(2)}) %collective-permute-start.11) | collective-permute-done | bytes 1130528 | tf_op jit(solution)/shard_map/ppermute | solution.py:383
  120.3 0.7 collective-permute-start.14
  121.0 8.6 %triangle.7 = (f32[64,96,128]{2,1,0:T(8,128)}, f32[64,96,128]{2,1,0:T(8,128)}) custom-call(s32[1]{0:T(128)} %bitcast.3.side_ref, bf16[64,96,256]{2,1,0:T(8,128)(2,1)} %copy-done, bf16[64,96,256]{2,1,0:T(8,128)(2,1)} %copy-done.1, bf16[23,64,384]{2,1,0:T(8,128)(2,1)S(1)} %collective-permute-done.13.refs_2_, ...), custom_call_target="tpu_custom_call" | custom-call | flops 805306368 | bytes 11304960 | tf_op jit(solution)/shard_map/triangle/pallas_call | solution.py:152
  129.7 2.3 collective-permute-start.16
  131.9 6.5 %triangle.4.refs_0_ = f32[64,96,128]{2,1,0:T(8,128)} custom-call(s32[1]{0:T(128)} %bitcast.3.side_ref, bf16[64,96,256]{2,1,0:T(8,128)(2,1)} %copy-done, bf16[23,64,384]{2,1,0:T(8,128)(2,1)S(1)} %get-tuple-element.23.refs_1_, bf16[23,64,384]{2,1,0:T(8,128)(2,1)S(1)} %collective-permute-done.1.refs_2_), custom_call_target="tpu_custom_call" | custom-call | flops 402653184 | bytes 6782976 | tf_op jit(solution)/shard_map/triangle/pallas_call | solution.py:152
  138.4 5.7 %collective-permute-start.2 = (f32[64,96,128]{2,1,0:T(8,128)}, f32[64,96,128]{2,1,0:T(8,128)}, u32[]{:S(2)}, u32[]{:S(2)}) collective-permute-start(f32[64,96,128]{2,1,0:T(8,128)} %triangle.4.refs_0_), channel_id=1, source_target_pairs={{1,0},{3,2},{5,4},{7,6},{8,9},{10,11},{12,13},{14,15},{17,16},{19,... | collective-permute-start | bytes 9437192 | tf_op jit(solution)/shard_map/ppermute | solution.py:393
  144.1 2.4 collective-permute-start.7
  146.5 5.3 %triangle.6.refs_0_ = f32[64,96,128]{2,1,0:T(8,128)S(1)} custom-call(s32[1]{0:T(128)} %bitcast.3.side_ref, bf16[64,96,256]{2,1,0:T(8,128)(2,1)} %copy-done, bf16[23,64,384]{2,1,0:T(8,128)(2,1)S(1)} %collective-permute-done.10.refs_1_, bf16[23,64,384]{2,1,0:T(8,128)(2,1)S(1)} %collective-permute-done.11.refs_2_), custom_call_target="tpu_custom_call" | custom-call | flops 402653184 | bytes 6782976 | tf_op jit(solution)/shard_map/triangle/pallas_call | solution.py:152
  151.8 3.0 %collective-permute-start.12 = (f32[64,96,128]{2,1,0:T(8,128)S(1)}, f32[64,96,128]{2,1,0:T(8,128)}, u32[]{:S(2)}, u32[]{:S(2)}) collective-permute-start(f32[64,96,128]{2,1,0:T(8,128)S(1)} %triangle.6.refs_0_), channel_id=1, source_target_pairs={{1,0},{3,2},{5,4},{7,6},{8,9},{10,11},{12,13},{14,15},{17,16},{19,... | collective-permute-start | bytes 9437192 | tf_op jit(solution)/shard_map/ppermute | solution.py:393
  154.8 2.4 collective-permute-start.15
  157.2 1.9 copy-done.5
  159.1 4.4 %fold.5 = (bf16[23,96,128]{2,1,0:T(8,128)(2,1)S(1)}, bf16[23,96,128]{2,1,0:T(8,128)(2,1)}) custom-call(s32[1]{0:T(128)} %bitcast.2.role_ref, f32[64,96,128]{2,1,0:T(8,128)S(1)} %copy-done.5, f32[64,96,128]{2,1,0:T(8,128)} %collective-permute-done.8.refs_1_), custom_call_target="tpu_custom_call" | custom-call | bytes 7864320 | tf_op jit(solution)/shard_map/fold/pallas_call | solution.py:208
  163.4 1.4 collective-permute-start.18
  164.9 4.4 %fold.7 = (bf16[23,96,128]{2,1,0:T(8,128)(2,1)}, bf16[23,96,128]{2,1,0:T(8,128)(2,1)}) custom-call(s32[1]{0:T(128)} %bitcast.2.role_ref, f32[64,96,128]{2,1,0:T(8,128)S(1)} %copy-done.6, f32[64,96,128]{2,1,0:T(8,128)} %collective-permute-done.16.refs_1_), custom_call_target="tpu_custom_call" | custom-call | bytes 7864320 | tf_op jit(solution)/shard_map/fold/pallas_call | solution.py:208
  169.3 1.3 collective-permute-start.20
  170.6 0.1 copy.22
  170.8 1.5 collective-permute-start.9
  172.3 4.7 %fold.4 = (bf16[23,96,128]{2,1,0:T(8,128)(2,1)S(1)}, bf16[23,96,128]{2,1,0:T(8,128)(2,1)S(1)}) custom-call(s32[1]{0:T(128)} %bitcast.2.role_ref, f32[64,96,128]{2,1,0:T(8,128)} %triangle.4.refs_0_, f32[64,96,128]{2,1,0:T(8,128)} %collective-permute-done.2.refs_1_, f32[64,96,128]{2,1,0:T(8,128)} %get-tuple-element.25.refs_2_, ...), custom_call_target="tpu_custom_call" | custom-call | bytes 7864320 | tf_op jit(solution)/shard_map/fold/pallas_call | solution.py:208
  177.0 38.8 %collective-permute-done.18 = bf16[23,96,128]{2,1,0:T(8,128)(2,1)} collective-permute-done((bf16[23,96,128]{2,1,0:T(8,128)(2,1)}, bf16[23,96,128]{2,1,0:T(8,128)(2,1)}, u32[]{:S(2)}, u32[]{:S(2)}) %collective-permute-start.18) | collective-permute-done | bytes 565280 | tf_op jit(solution)/shard_map/ppermute | solution.py:383
  215.8 1.9 broadcast_select_fusion.1
  217.7 1.2 collective-permute-start.19
  218.9 1.4 collective-permute-start.17
  220.3 4.4 %fold.6 = (bf16[23,96,128]{2,1,0:T(8,128)(2,1)S(1)}, bf16[23,96,128]{2,1,0:T(8,128)(2,1)S(1)}) custom-call(s32[1]{0:T(128)} %bitcast.2.role_ref, f32[64,96,128]{2,1,0:T(8,128)S(1)} %triangle.6.refs_0_, f32[64,96,128]{2,1,0:T(8,128)} %collective-permute-done.12.refs_1_, f32[64,96,128]{2,1,0:T(8,128)} %get-tuple-element.29.refs_2_, ...), custom_call_target="tpu_custom_call" | custom-call | bytes 7864320 | tf_op jit(solution)/shard_map/fold/pallas_call | solution.py:208
  224.8 3.1 %collective-permute-done.20 = bf16[23,96,128]{2,1,0:T(8,128)(2,1)} collective-permute-done((bf16[23,96,128]{2,1,0:T(8,128)(2,1)}, bf16[23,96,128]{2,1,0:T(8,128)(2,1)}, u32[]{:S(2)}, u32[]{:S(2)}) %collective-permute-start.20) | collective-permute-done | bytes 565280 | tf_op jit(solution)/shard_map/ppermute | solution.py:383
  227.9 1.9 broadcast_select_fusion
  229.8 1.2 collective-permute-start.21
  231.1 0.1 copy.37
  231.3 0.2 copy.23
  231.4 1.2 copy.24
  232.6 7.4 %collective-permute-done.9 = bf16[23,96,128]{2,1,0:T(8,128)(2,1)} collective-permute-done((bf16[23,96,128]{2,1,0:T(8,128)(2,1)}, bf16[23,96,128]{2,1,0:T(8,128)(2,1)}, u32[]{:S(2)}, u32[]{:S(2)}) %collective-permute-start.9) | collective-permute-done | bytes 565280 | tf_op jit(solution)/shard_map/ppermute | solution.py:383
  240.0 1.1 broadcast_select_fusion.3.refs_0_
  241.1 11.0 %collective-permute-done.17 = bf16[23,96,128]{2,1,0:T(8,128)(2,1)} collective-permute-done((bf16[23,96,128]{2,1,0:T(8,128)(2,1)}, bf16[23,96,128]{2,1,0:T(8,128)(2,1)}, u32[]{:S(2)}, u32[]{:S(2)}) %collective-permute-start.17) | collective-permute-done | bytes 565280 | tf_op jit(solution)/shard_map/ppermute | solution.py:383
  252.1 1.1 broadcast_select_fusion.2.refs_1_
  253.2 26.2 %finish.1 = bf16[2,23,184,128]{3,2,1,0:T(8,128)(2,1)} custom-call(s32[1]{0:T(128)} %bitcast.order_ref, bf16[2,23,184,128]{3,2,1,0:T(8,128)(2,1)S(1)} %bitcast.18, bf16[23,96,128]{2,1,0:T(8,128)(2,1)S(1)} %broadcast_select_fusion.3.refs_0_, bf16[23,96,128]{2,1,0:T(8,128)(2,1)S(1)} %broadcast_select_fusion.2.refs_1_, ...), custom_call_target="tpu_custom_call" | custom-call | flops 3882876928 | bytes 6500352 | tf_op jit(solution)/shard_map/finish/pallas_call | solution.py:264
  (53 shorter events, 1.1 us)
Async XLA Ops:
  4.6 1.6 copy-start.2
  6.2 10.5 %copy-start.3 = (bf16[46,184,128]{2,1,0:T(8,128)(2,1)S(1)}, bf16[46,184,128]{2,1,0:T(8,128)(2,1)}, u32[]{:S(2)}) copy-start(bf16[46,184,128]{2,1,0:T(8,128)(2,1)} %param.6) | copy-start | bytes 6500356
  11.6 1.0 copy-start.7
  12.6 26.9 %collective-permute-start = (bf16[23,64,384]{2,1,0:T(8,128)(2,1)}, bf16[23,64,384]{2,1,0:T(8,128)(2,1)S(1)}, u32[]{:S(2)}, u32[]{:S(2)}) collective-permute-start(bf16[23,64,384]{2,1,0:T(8,128)(2,1)} %get-tuple-element.22), channel_id=1, source_target_pairs={{0,2},{2,0},{4,6},{6,4},{8,10},{10,8},{12,14},{14,12},{1,3},{3,1},... | collective-permute-start | bytes 3391496 | tf_op jit(solution)/shard_map/ppermute | solution.py:386
  15.9 5.3 %copy-start.8 = (bf16[23,64,384]{2,1,0:T(8,128)(2,1)S(1)}, bf16[23,64,384]{2,1,0:T(8,128)(2,1)}, u32[]{:S(2)}) copy-start(bf16[23,64,384]{2,1,0:T(8,128)(2,1)} %copy-done.7) | copy-start | bytes 3391492
  21.1 42.6 %collective-permute-start.1 = (bf16[23,64,384]{2,1,0:T(8,128)(2,1)S(1)}, bf16[23,64,384]{2,1,0:T(8,128)(2,1)S(1)}, u32[]{:S(2)}, u32[]{:S(2)}) collective-permute-start(bf16[23,64,384]{2,1,0:T(8,128)(2,1)S(1)} %get-tuple-element.24), channel_id=1, source_target_pairs={{0,2},{2,0},{4,6},{6,4},{8,10},{10,8},{12,14},{14,12},{1,3},{3,1},... | collective-permute-start | bytes 3391496 | tf_op jit(solution)/shard_map/ppermute | solution.py:386
  21.2 50.5 %collective-permute-start.3 = (bf16[23,64,384]{2,1,0:T(8,128)(2,1)S(1)}, bf16[23,64,384]{2,1,0:T(8,128)(2,1)S(1)}, u32[]{:S(2)}, u32[]{:S(2)}) collective-permute-start(bf16[23,64,384]{2,1,0:T(8,128)(2,1)S(1)} %copy-done.8), channel_id=1, source_target_pairs={{0,4},{2,6},{12,8},{14,10},{1,5},{3,7},{13,9},{15,11},{16,20},{18,... | collective-permute-start | bytes 3391496 | tf_op jit(solution)/shard_map/ppermute | solution.py:383
  39.5 32.3 %collective-permute-start.4 = (bf16[23,64,384]{2,1,0:T(8,128)(2,1)S(1)}, bf16[23,64,384]{2,1,0:T(8,128)(2,1)S(1)}, u32[]{:S(2)}, u32[]{:S(2)}) collective-permute-start(bf16[23,64,384]{2,1,0:T(8,128)(2,1)S(1)} %collective-permute-done.beside_ref), channel_id=1, source_target_pairs={{0,4},{2,6},{12,8},{14,10},{1,5},{3,7},{13,9},{15,11},{16,20},{18,... | collective-permute-start | bytes 3391496 | tf_op jit(solution)/shard_map/ppermute | solution.py:383
  42.7 32.5 %collective-permute-start.5 = (bf16[23,64,384]{2,1,0:T(8,128)(2,1)S(1)}, bf16[23,64,384]{2,1,0:T(8,128)(2,1)S(1)}, u32[]{:S(2)}, u32[]{:S(2)}) collective-permute-start(bf16[23,64,384]{2,1,0:T(8,128)(2,1)S(1)} %get-tuple-element.23.refs_1_), channel_id=1, source_target_pairs={{4,8},{6,10},{8,4},{10,6},{5,9},{7,11},{9,5},{11,7},{20,24},{22,26... | collective-permute-start | bytes 3391496 | tf_op jit(solution)/shard_map/ppermute | solution.py:383
  63.7 11.5 %collective-permute-start.6 = (bf16[23,64,384]{2,1,0:T(8,128)(2,1)S(1)}, bf16[23,64,384]{2,1,0:T(8,128)(2,1)S(1)}, u32[]{:S(2)}, u32[]{:S(2)}) collective-permute-start(bf16[23,64,384]{2,1,0:T(8,128)(2,1)S(1)} %collective-permute-done.1.refs_2_), channel_id=1, source_target_pairs={{4,8},{6,10},{8,4},{10,6},{5,9},{7,11},{9,5},{11,7},{20,24},{22,26... | collective-permute-start | bytes 3391496 | tf_op jit(solution)/shard_map/ppermute | solution.py:383
  64.4 31.6 %collective-permute-start.10 = (bf16[23,64,384]{2,1,0:T(8,128)(2,1)S(1)}, bf16[23,64,384]{2,1,0:T(8,128)(2,1)S(1)}, u32[]{:S(2)}, u32[]{:S(2)}) collective-permute-start(bf16[23,64,384]{2,1,0:T(8,128)(2,1)S(1)} %get-tuple-element.23.refs_1_), channel_id=1, source_target_pairs={{0,4},{2,6},{4,0},{6,2},{8,12},{10,14},{12,8},{14,10},{1,5},{3,7},... | collective-permute-start | bytes 3391496 | tf_op jit(solution)/shard_map/ppermute | solution.py:383
  70.0 1.7 copy-start
  71.7 48.6 %collective-permute-start.11 = (bf16[23,64,384]{2,1,0:T(8,128)(2,1)S(1)}, bf16[23,64,384]{2,1,0:T(8,128)(2,1)S(1)}, u32[]{:S(2)}, u32[]{:S(2)}) collective-permute-start(bf16[23,64,384]{2,1,0:T(8,128)(2,1)S(1)} %collective-permute-done.1.refs_2_), channel_id=1, source_target_pairs={{0,4},{2,6},{4,0},{6,2},{8,12},{10,14},{12,8},{14,10},{1,5},{3,7},... | collective-permute-start | bytes 3391496 | tf_op jit(solution)/shard_map/ppermute | solution.py:383
  73.6 1.6 copy-start.1
  83.7 71.0 %collective-permute-start.8 = (f32[64,96,128]{2,1,0:T(8,128)}, f32[64,96,128]{2,1,0:T(8,128)}, u32[]{:S(2)}, u32[]{:S(2)}) collective-permute-start(f32[64,96,128]{2,1,0:T(8,128)} %get-tuple-element.27.refs_0_), channel_id=1, source_target_pairs={{4,5},{6,7},{9,8},{11,10},{20,21},{22,23},{25,24},{27,26}} | collective-permute-start | bytes 9437192 | tf_op jit(solution)/shard_map/ppermute | solution.py:393
  96.0 25.0 %collective-permute-start.13 = (bf16[23,64,384]{2,1,0:T(8,128)(2,1)S(1)}, bf16[23,64,384]{2,1,0:T(8,128)(2,1)S(1)}, u32[]{:S(2)}, u32[]{:S(2)}) collective-permute-start(bf16[23,64,384]{2,1,0:T(8,128)(2,1)S(1)} %collective-permute-done.10.refs_1_), channel_id=1, source_target_pairs={{4,8},{6,10},{8,4},{10,6},{5,9},{7,11},{9,5},{11,7},{20,24},{22,26... | collective-permute-start | bytes 3391496 | tf_op jit(solution)/shard_map/ppermute | solution.py:383
  120.3 0.7 collective-permute-start.14
  129.7 33.8 %collective-permute-start.16 = (f32[64,96,128]{2,1,0:T(8,128)}, f32[64,96,128]{2,1,0:T(8,128)}, u32[]{:S(2)}, u32[]{:S(2)}) collective-permute-start(f32[64,96,128]{2,1,0:T(8,128)} %get-tuple-element.31.refs_0_), channel_id=1, source_target_pairs={{4,5},{6,7},{9,8},{11,10},{20,21},{22,23},{25,24},{27,26}} | collective-permute-start | bytes 9437192 | tf_op jit(solution)/shard_map/ppermute | solution.py:393
  138.4 30.8 %collective-permute-start.2 = (f32[64,96,128]{2,1,0:T(8,128)}, f32[64,96,128]{2,1,0:T(8,128)}, u32[]{:S(2)}, u32[]{:S(2)}) collective-permute-start(f32[64,96,128]{2,1,0:T(8,128)} %triangle.4.refs_0_), channel_id=1, source_target_pairs={{1,0},{3,2},{5,4},{7,6},{8,9},{10,11},{12,13},{14,15},{17,16},{19,... | collective-permute-start | bytes 9437192 | tf_op jit(solution)/shard_map/ppermute | solution.py:393
  144.1 26.6 %collective-permute-start.7 = (f32[64,96,128]{2,1,0:T(8,128)}, f32[64,96,128]{2,1,0:T(8,128)}, u32[]{:S(2)}, u32[]{:S(2)}) collective-permute-start(f32[64,96,128]{2,1,0:T(8,128)} %get-tuple-element.25.refs_2_), channel_id=1, source_target_pairs={{4,5},{6,7},{9,8},{11,10},{20,21},{22,23},{25,24},{27,26}} | collective-permute-start | bytes 9437192 | tf_op jit(solution)/shard_map/ppermute | solution.py:393
  151.8 67.1 %collective-permute-start.12 = (f32[64,96,128]{2,1,0:T(8,128)S(1)}, f32[64,96,128]{2,1,0:T(8,128)}, u32[]{:S(2)}, u32[]{:S(2)}) collective-permute-start(f32[64,96,128]{2,1,0:T(8,128)S(1)} %triangle.6.refs_0_), channel_id=1, source_target_pairs={{1,0},{3,2},{5,4},{7,6},{8,9},{10,11},{12,13},{14,15},{17,16},{19,... | collective-permute-start | bytes 9437192 | tf_op jit(solution)/shard_map/ppermute | solution.py:393
  154.8 65.6 %collective-permute-start.15 = (f32[64,96,128]{2,1,0:T(8,128)}, f32[64,96,128]{2,1,0:T(8,128)}, u32[]{:S(2)}, u32[]{:S(2)}) collective-permute-start(f32[64,96,128]{2,1,0:T(8,128)} %get-tuple-element.29.refs_2_), channel_id=1, source_target_pairs={{4,5},{6,7},{9,8},{11,10},{20,21},{22,23},{25,24},{27,26}} | collective-permute-start | bytes 9437192 | tf_op jit(solution)/shard_map/ppermute | solution.py:393
  157.2 1.9 copy-start.5
  159.1 5.8 %copy-start.6 = (f32[64,96,128]{2,1,0:T(8,128)S(1)}, f32[64,96,128]{2,1,0:T(8,128)}, u32[]{:S(2)}) copy-start(f32[64,96,128]{2,1,0:T(8,128)} %get-tuple-element.31.refs_0_) | copy-start | bytes 9437188
  163.4 5.8 %copy-start.12 = (bf16[23,96,128]{2,1,0:T(8,128)(2,1)}, bf16[23,96,128]{2,1,0:T(8,128)(2,1)S(1)}, u32[]{:S(2)}) copy-start(bf16[23,96,128]{2,1,0:T(8,128)(2,1)S(1)} %get-tuple-element.28) | copy-start | bytes 1695748
  163.4 7.1 %copy-start.14 = (bf16[128,128]{1,0:T(8,128)(2,1)S(1)}, bf16[128,128]{1,0:T(8,128)(2,1)}, u32[]{:S(2)}) copy-start(bf16[128,128]{1,0:T(8,128)(2,1)} %param.9) | copy-start | bytes 98308
  163.4 52.3 %collective-permute-start.18 = (bf16[23,96,128]{2,1,0:T(8,128)(2,1)}, bf16[23,96,128]{2,1,0:T(8,128)(2,1)}, u32[]{:S(2)}, u32[]{:S(2)}) collective-permute-start(bf16[23,96,128]{2,1,0:T(8,128)(2,1)} %get-tuple-element.34), channel_id=1, source_target_pairs={{4,0},{6,2},{8,12},{10,14},{5,1},{7,3},{9,13},{11,15},{20,16},{22,... | collective-permute-start | bytes 1695752 | tf_op jit(solution)/shard_map/ppermute | solution.py:383
  169.3 58.6 %collective-permute-start.20 = (bf16[23,96,128]{2,1,0:T(8,128)(2,1)}, bf16[23,96,128]{2,1,0:T(8,128)(2,1)}, u32[]{:S(2)}, u32[]{:S(2)}) collective-permute-start(bf16[23,96,128]{2,1,0:T(8,128)(2,1)} %get-tuple-element.36), channel_id=1, source_target_pairs={{4,0},{6,2},{8,12},{10,14},{5,1},{7,3},{9,13},{11,15},{20,16},{22,... | collective-permute-start | bytes 1695752 | tf_op jit(solution)/shard_map/ppermute | solution.py:383
  170.8 69.2 %collective-permute-start.9 = (bf16[23,96,128]{2,1,0:T(8,128)(2,1)}, bf16[23,96,128]{2,1,0:T(8,128)(2,1)}, u32[]{:S(2)}, u32[]{:S(2)}) collective-permute-start(bf16[23,96,128]{2,1,0:T(8,128)(2,1)} %copy-done.12), channel_id=1, source_target_pairs={{4,0},{6,2},{8,12},{10,14},{5,1},{7,3},{9,13},{11,15},{20,16},{22,... | collective-permute-start | bytes 1695752 | tf_op jit(solution)/shard_map/ppermute | solution.py:383
  176.9 41.9 %copy-start.9 = (bf16[23,96,128]{2,1,0:T(8,128)(2,1)}, bf16[23,96,128]{2,1,0:T(8,128)(2,1)S(1)}, u32[]{:S(2)}) copy-start(bf16[23,96,128]{2,1,0:T(8,128)(2,1)S(1)} %get-tuple-element.26) | copy-start | bytes 1695748
  217.7 35.5 %collective-permute-start.19 = (bf16[23,96,128]{2,1,0:T(8,128)(2,1)}, bf16[23,96,128]{2,1,0:T(8,128)(2,1)}, u32[]{:S(2)}, u32[]{:S(2)}) collective-permute-start(bf16[23,96,128]{2,1,0:T(8,128)(2,1)} %broadcast_select_fusion.1), channel_id=1, source_target_pairs={{0,2},{2,0},{4,6},{6,4},{8,10},{10,8},{12,14},{14,12},{1,3},{3,1},... | collective-permute-start | bytes 1695752 | tf_op jit(solution)/shard_map/ppermute | solution.py:386
  218.9 12.4 %copy-start.13 = (bf16[128,1024]{1,0:T(8,128)(2,1)S(1)}, bf16[128,1024]{1,0:T(8,128)(2,1)}, u32[]{:S(2)}) copy-start(bf16[128,1024]{1,0:T(8,128)(2,1)} %param.10) | copy-start | bytes 786436
  218.9 33.2 %collective-permute-start.17 = (bf16[23,96,128]{2,1,0:T(8,128)(2,1)}, bf16[23,96,128]{2,1,0:T(8,128)(2,1)}, u32[]{:S(2)}, u32[]{:S(2)}) collective-permute-start(bf16[23,96,128]{2,1,0:T(8,128)(2,1)} %get-tuple-element.32), channel_id=1, source_target_pairs={{4,0},{6,2},{8,12},{10,14},{5,1},{7,3},{9,13},{11,15},{20,16},{22,... | collective-permute-start | bytes 1695752 | tf_op jit(solution)/shard_map/ppermute | solution.py:383
  224.8 6.2 %copy-start.11 = (bf16[23,96,128]{2,1,0:T(8,128)(2,1)}, bf16[23,96,128]{2,1,0:T(8,128)(2,1)S(1)}, u32[]{:S(2)}) copy-start(bf16[23,96,128]{2,1,0:T(8,128)(2,1)S(1)} %get-tuple-element.30) | copy-start | bytes 1695748
  224.8 15.2 %copy-start.10 = (bf16[23,96,128]{2,1,0:T(8,128)(2,1)S(1)}, bf16[23,96,128]{2,1,0:T(8,128)(2,1)}, u32[]{:S(2)}) copy-start(bf16[23,96,128]{2,1,0:T(8,128)(2,1)} %copy-done.9) | copy-start | bytes 1695748
  229.8 23.4 %collective-permute-start.21 = (bf16[23,96,128]{2,1,0:T(8,128)(2,1)}, bf16[23,96,128]{2,1,0:T(8,128)(2,1)}, u32[]{:S(2)}, u32[]{:S(2)}) collective-permute-start(bf16[23,96,128]{2,1,0:T(8,128)(2,1)} %broadcast_select_fusion), channel_id=1, source_target_pairs={{0,2},{2,0},{4,6},{6,4},{8,10},{10,8},{12,14},{14,12},{1,3},{3,1},... | collective-permute-start | bytes 1695752 | tf_op jit(solution)/shard_map/ppermute | solution.py:386
  231.1 22.1 %copy-start.4 = (bf16[46,184,128]{2,1,0:T(8,128)(2,1)S(1)}, bf16[46,184,128]{2,1,0:T(8,128)(2,1)}, u32[]{:S(2)}) copy-start(bf16[46,184,128]{2,1,0:T(8,128)(2,1)} %param.6) | copy-start | bytes 6500356

commit v4 on v3

--- a/solution.py
+++ b/solution.py
@@ -140,7 +140,7 @@
         for left_ref, out_ref in zip(refs[:lefts], outs):
             out_ref[c] = lax.dot_general(
                 left_ref[c], right_ref[c], (((1,), (1,)), ((), ())), preferred_element_type=F32
-            )
+            ).astype(BF16)
 
 
 def triangle(side, lefts, own, beside):
@@ -152,12 +152,12 @@
     return pl.pallas_call(
         triangle_kernel,
         grid=(chans // CHUNK,),
-        out_shape=[jax.ShapeDtypeStruct((chans, rows, cols), F32) for _ in lefts],
+        out_shape=[jax.ShapeDtypeStruct((chans, rows, cols), BF16) for _ in lefts],
         in_specs=[pl.BlockSpec(memory_space=pltpu.SMEM)] + [left] * len(lefts) + [piece, piece],
         out_specs=[out] * len(lefts),
         scratch_shapes=[VMEM((CHUNK, cols, lanes // 3 * 2), BF16)],
         compiler_params=params(),
-        cost_estimate=cost(2 * len(lefts) * chans * rows * cols * lanes // 3 * 2, (4 + 8 * len(lefts)) * own.size),
+        cost_estimate=cost(2 * len(lefts) * chans * rows * cols * lanes // 3 * 2, (4 + 6 * len(lefts)) * own.size),
         name="triangle",
     )(side, *lefts, own, beside)
 
@@ -172,7 +172,7 @@
         mine_ref, rest_ref = refs[2 * option : 2 * option + 2]
 
         def gather():
-            total = (mine_ref[...] + rest_ref[...]).astype(BF16)
+            total = (mine_ref[...].astype(F32) + rest_ref[...].astype(F32)).astype(BF16)
             at = pl.ds(pl.multiple_of(c * CHUNK, CHUNK), CHUNK)
             work_ref[:, at, :] = jnp.swapaxes(total, 0, 1)
 
@@ -216,33 +216,35 @@
         ),
         out_shape=(out, out),
         compiler_params=params(),
-        cost_estimate=cost(0, 10 * parts[0].size),
+        cost_estimate=cost(0, 6 * parts[0].size),
         name="fold",
     )(role, *parts)
 
 
-def finish_kernel(order_ref, pair_ref, *refs):
-    owns, others = refs[0:2], refs[2:4]
-    gate_ref, out_w_ref, in_ref, back_ref, out_ref = refs[4:]
+def finish_kernel(flag_ref, pair_ref, own_ref, other_ref, *refs):
+    gate_ref, out_w_ref, in_ref, back_ref = refs[:4]
+    earlier_ref, out_ref = refs[4] if len(refs) == 6 else None, refs[-1]
     _, half, cols, width = pair_ref.shape
+    block, chans = cols // 2, width // 2
     hidden_units = back_ref.shape[1]
-    flip = order_ref[0] == 1
-
-    block = cols // 2
-    chans = width // 2
-
-    def step(r, carry):
-        rows = [[], []]
-        for own_ref, other_ref in zip(owns, others):
-            own, other = (ref[r].astype(F32).T[:, :block] for ref in (own_ref, other_ref))
-            for h in range(2):
-                at = slice(h * chans, (h + 1) * chans)
-                rows[h].append(jnp.concatenate([own[at], other[at]], axis=0))
-        lanes = []
-        for first, second in rows:
-            lanes += [jnp.where(flip, second, first), jnp.where(flip, first, second)]
-        tri_normed = norm_chans(jnp.concatenate(lanes, axis=1)).astype(BF16)
-        pair = jnp.concatenate([pair_ref[h, r].astype(F32) for h in range(2)], axis=0).T
+    front = flag_ref[0] == 0
+    steps = (half + 1) // 2
+
+    def step(i, carry):
+        first = jnp.minimum(2 * i, half - 2)
+        rows = [(h, first + e) for h in range(2) for e in range(2)]
+        turned = [[ref[first + e].T[:, :block] for ref in (own_ref, other_ref)] for e in range(2)]
+        tri = [
+            jnp.concatenate([t[h * chans : (h + 1) * chans] for t in turned[e]], axis=0)
+            for h in range(2)
+            for e in range(2)
+        ]
+        tri_normed = norm_chans(jnp.concatenate(tri, axis=1).astype(F32)).astype(BF16)
+        pair = []
+        for h, r in rows:
+            row = pair_ref[h, r].astype(F32)
+            pair.append(jnp.where(front, row[:block], row[block:]))
+        pair = jnp.concatenate(pair, axis=0).T
         normed = norm_chans(pair).astype(BF16)
         out_gate = sigmoid(jnp.dot(gate_ref[...], normed, preferred_element_type=F32))
         update = jnp.dot(out_w_ref[...], tri_normed, preferred_element_type=F32)
@@ -253,23 +255,32 @@
         hidden = (swish * sigmoid(swish) * linear).astype(BF16)
         result = updated + jnp.dot(back_ref[...], hidden, preferred_element_type=F32)
         result = result.T
-        for h in range(2):
-            out_ref[h, r] = result[h * cols : (h + 1) * cols].astype(BF16)
+        for s, (h, r) in enumerate(rows):
+            mine = result[s * block : (s + 1) * block]
+            if earlier_ref is None:
+                out_ref[h, r, :block] = mine.astype(BF16)
+            else:
+                past = earlier_ref[h, r].astype(F32)[:block]
+                parts = [jnp.where(front, mine, past), jnp.where(front, past, mine)]
+                out_ref[h, r] = jnp.concatenate(parts, axis=0).astype(BF16)
         return carry
 
-    lax.fori_loop(0, half, step, 0, unroll=2)
-
-
-def finish(order, pair, owns, others, gate_w, out_w, trans_in, trans_out):
+    lax.fori_loop(0, steps, step, 0, unroll=2)
+
+
+def finish(flag, pair, own, other, weights, earlier=None):
+    _, half, cols, width = pair.shape
+    shape = pair.shape if earlier is not None else (2, half, padded(cols // 2, 16), width)
+    extra = [] if earlier is None else [earlier]
     return pl.pallas_call(
         finish_kernel,
-        out_shape=jax.ShapeDtypeStruct(pair.shape, BF16),
-        in_specs=[pl.BlockSpec(memory_space=pltpu.SMEM)] + whole(9),
+        out_shape=jax.ShapeDtypeStruct(shape, BF16),
+        in_specs=[pl.BlockSpec(memory_space=pltpu.SMEM)] + whole(7 + len(extra)),
         out_specs=pl.BlockSpec(memory_space=VMEM),
         compiler_params=params(),
-        cost_estimate=cost(28 * pair.size * pair.shape[-1], 6 * pair.size, 6 * pair.size),
+        cost_estimate=cost(14 * pair.size * width, 4 * pair.size, 3 * pair.size),
         name="finish",
-    )(order, pair, *owns, *others, gate_w, out_w, trans_in, trans_out)
+    )(flag, pair, own, other, *weights, *extra)
 
 
 def layer_norm(values):
@@ -409,42 +420,39 @@
     mates, cross = [(0, 1), (1, 0), (2, 3), (3, 2)], [(1, 2), (2, 1)]
     inward, outward = [(0, 1), (3, 2)], [(1, 0), (2, 3)]
 
+    def after(value, *others):
+        return lax.optimization_barrier((value, *others))[0]
+
     right_own, right_far = project(where, folded, gate_pair(2))
+    mate_own, near_own = among(right_own, mates), among(right_own, cross)
     right_beside = across(right_far)
-    mate = [among(v, mates) for v in (right_own, right_beside)]
-    near = [among(v, cross) for v in (right_own, right_beside)]
-    far = [among(v, cross) for v in mate]
     left_own, left_far = project(where, folded, gate_pair(0))
-    left_beside = across(left_far)
-    guest = [among(v, inward) for v in (left_own, left_beside)]
+    left_beside = across(after(left_far, right_beside))
+    mate_beside, near_beside = among(right_beside, mates), among(right_beside, cross)
+    far_own = among(after(mate_own, near_own), cross)
+    guest_own = among(after(left_own, mate_own), inward)
+    far_beside = among(after(mate_beside, near_beside), cross)
+    guest_beside = among(after(left_beside, mate_beside), inward)
 
     left = left_major(left_own, left_beside)
-    home = [triangle(sides, [left], right_own, right_beside)[0], triangle(sides, [left], *mate)[0]]
-    left_guest = left_major(*guest)
-    away, lent = zip(*(triangle(sides, [left, left_guest], *v) for v in (near, far)))
-
-    home_rest = [to_core(v, range(4), True) for v in home]
-    away_rest = [to_core(v, (1, 2), False) for v in away]
-    lent_rest = [to_core(v, (1, 2), False) for v in lent]
+    (home_own,) = triangle(sides, [left], right_own, right_beside)
+    (home_mate,) = triangle(sides, [left], mate_own, mate_beside)
+    left_guest = left_major(guest_own, guest_beside)
+    away_near, lent_near = triangle(sides, [left, left_guest], near_own, near_beside)
+    away_far, lent_far = triangle(sides, [left, left_guest], far_own, far_beside)
+
     inner = (place == 1) | (place == 2)
-    owns, others = [], []
-    for i in range(2):
-        given = [among(v, outward) for v in fold(half, role, lent[i], lent_rest[i])]
-        kept = fold(half, role, home[i], home_rest[i], away[i], away_rest[i])
-        own, beside = (jnp.where(is_keeper | inner, k, g) for k, g in zip(kept, given))
-        owns.append(own)
-        others.append(across(beside))
-    flip = jnp.where(is_keeper, place % 2, place // 2).astype(jnp.int32).reshape(1)
-    result = finish(
-        flip,
-        folded,
-        owns,
-        others,
-        in_weight[:, 4 * width :].T,
-        by_side(out_weight, 0).T,
-        trans_in.T,
-        trans_out.T,
-    )
+    order = jnp.where(is_keeper, place % 2, place // 2).astype(jnp.int32).reshape(1)
+    weights = [w.T for w in (in_weight[:, 4 * width :], by_side(out_weight, 0), trans_in, trans_out)]
+    result = None
+    for i, (home, away, lent) in enumerate(
+        ((home_own, away_near, lent_near), (home_mate, away_far, lent_far))
+    ):
+        returned = [among(v, outward) for v in fold(half, role, lent, to_core(lent, (1, 2), False))]
+        kept = fold(half, role, home, to_core(home, range(4), True), away, to_core(away, (1, 2), False))
+        own, beside = (jnp.where(is_keeper | inner, k, g) for k, g in zip(kept, returned))
+        flag = order if i == 0 else 1 - order
+        result = finish(flag, folded, own, across(beside), weights, result)
     return result.reshape(tile_rows, tile_cols, width)
 
 

time: 284 us -> 262 us (0.923)
  waiting for transfers between devices: 129 us -> 114 us
  Pallas kernels: 86.2 us -> 82.3 us
    ppermute x12, waiting for transfers between devices: 93.9 us -> 82 us  [among(): lax.ppermute(value, 'row', [(2 * s + b, 2 * t + b) for s, t in moves for...]
    pallas_call x4, Pallas kernels: 17.8 us -> 14 us  [fold(): pl.pallas_call(fold_kernel, grid_spec=pltpu.PrefetchScalarGridSpec(num_sc...]
    ppermute x6, starting transfers between devices: 18 us -> 14.5 us  [to_core(): return lax.ppermute(value, ('row', 'col'), perm)]
    ppermute x4, waiting for transfers between devices: 35.1 us -> 31.5 us  [across(): return lax.ppermute(value, 'row', [(i, i ^ 1) for i in range(8)])]
    ppermute x12, starting transfers between devices: 19 us -> 22 us  [among(): lax.ppermute(value, 'row', [(2 * s + b, 2 * t + b) for s, t in moves for...]
    unnamed x46 -> x42, local copies, waits for them, and re-layouts: 11.3 us -> 13.5 us
    pallas_call x1 -> x2, Pallas kernels: 26.2 us -> 25.3 us  [finish(): pl.pallas_call(finish_kernel, out_shape=jax.ShapeDtypeStruct(shape, BF16)...]
  transfers between devices with their start and end apart: 22 -> 22, of which waited for: 9 -> 9; matrix products, arithmetic and copies ran while one was open for 4% -> 2% of each run, Pallas kernels for 20% -> 25%
where the time goes in v4:
time: 262 us; the launch traced here: 258 us
  waiting for transfers between devices  114 us (44%)
  Pallas kernels  82.3 us (31%)
  starting transfers between devices  40.3 us (15%)
  local copies, waits for them, and re-layouts  16.6 us (6%)
  other arithmetic  4.41 us (2%)
    ppermute x12, waiting for transfers between devices, among(): lax.ppermute(value, 'row', [(2 * s + b, 2 * t + b) for s, t in moves for...  82 us
    ppermute x4, waiting for transfers between devices, across(): return lax.ppermute(value, 'row', [(i, i ^ 1) for i in range(8)])  31.5 us
    pallas_call x4, Pallas kernels, triangle(): pl.pallas_call(triangle_kernel, grid=(chans // CHUNK,), out_shape=[jax.Sh...  28.3 us
    pallas_call x2, Pallas kernels, finish(): pl.pallas_call(finish_kernel, out_shape=jax.ShapeDtypeStruct(shape, BF16)...  25.3 us
    ppermute x12, starting transfers between devices, among(): lax.ppermute(value, 'row', [(2 * s + b, 2 * t + b) for s, t in moves for...  22 us
    ppermute x6, starting transfers between devices, to_core(): return lax.ppermute(value, ('row', 'col'), perm)  14.5 us
    pallas_call x4, Pallas kernels, fold(): pl.pallas_call(fold_kernel, grid_spec=pltpu.PrefetchScalarGridSpec(num_sc...  14 us
    unnamed x42, local copies, waits for them, and re-layouts  13.5 us
  transfers between devices with their start and end apart: 22, of which 9 were waited for; matrix products, arithmetic and copies ran while one was open for 2% of the time, Pallas kernels for 25%

profile of v4, /device:TPU:1, one launch (start us, length us, event | category | flops | bytes accessed | tf_op | source)
XLA Modules:
  0.0 258.1 jit_solution(590494337187052180)
XLA Ops:
  0.0 0.8 fusion.1
  0.8 1.0 fusion.2
  1.8 1.2 slice.60
  3.2 0.1 copy.31
  4.4 1.6 copy-done.2
  6.0 5.4 %project.3 = (bf16[23,64,384]{2,1,0:T(8,128)(2,1)S(1)}, bf16[23,64,384]{2,1,0:T(8,128)(2,1)}) custom-call(s32[3]{0:T(128)S(1)} %pad_add_fusion.where_ref, bf16[2,23,184,128]{3,2,1,0:T(8,128)(2,1)S(1)} %bitcast.16, bf16[256,128]{1,0:T(8,128)(2,1)S(1)} %maximum_bitcast_fusion.1.weight_ref), custom_call_target="tpu_custom_call" | custom-call | flops 554696704 | bytes 4333568 | tf_op jit(solution)/shard_map/project/pallas_call | solution.py:71
  11.4 2.0 collective-permute-start
  13.4 1.3 collective-permute-start.2
  14.7 0.7 copy.28
  15.9 0.8 maximum_select_fusion
  16.8 4.4 %project.2 = (bf16[23,64,384]{2,1,0:T(8,128)(2,1)S(1)}, bf16[23,64,384]{2,1,0:T(8,128)(2,1)S(1)}) custom-call(s32[3]{0:T(128)S(1)} %pad_add_fusion.where_ref, bf16[2,23,184,128]{3,2,1,0:T(8,128)(2,1)S(1)} %bitcast.17, bf16[256,128]{1,0:T(8,128)(2,1)S(1)} %maximum_bitcast_fusion.weight_ref), custom_call_target="tpu_custom_call" | custom-call | flops 554696704 | bytes 4333568 | tf_op jit(solution)/shard_map/project/pallas_call | solution.py:71
  21.2 17.2 %collective-permute-done.refs_2_ = bf16[23,64,384]{2,1,0:T(8,128)(2,1)} collective-permute-done((bf16[23,64,384]{2,1,0:T(8,128)(2,1)}, bf16[23,64,384]{2,1,0:T(8,128)(2,1)}, u32[]{:S(2)}, u32[]{:S(2)}) %collective-permute-start) | collective-permute-done | bytes 1130528 | tf_op jit(solution)/shard_map/ppermute | solution.py:397
  38.4 1.1 collective-permute-start.1
  39.5 1.3 collective-permute-start.3
  40.8 0.7 collective-permute-start.7
  41.5 0.7 collective-permute-start.9
  42.3 6.9 %collective-permute-start.5 = (bf16[23,64,384]{2,1,0:T(8,128)(2,1)S(1)}, bf16[23,64,384]{2,1,0:T(8,128)(2,1)S(1)}, u32[]{:S(2)}, u32[]{:S(2)}) collective-permute-start(bf16[23,64,384]{2,1,0:T(8,128)(2,1)S(1)} %get-tuple-element.31.own_ref), channel_id=1, source_target_pairs={{0,4},{2,6},{12,8},{14,10},{1,5},{3,7},{13,9},{15,11},{16,20},{18,... | collective-permute-start | bytes 3391496 | tf_op jit(solution)/shard_map/ppermute | solution.py:394
  49.2 14.3 %collective-permute-done.1.beside_ref = bf16[23,64,384]{2,1,0:T(8,128)(2,1)S(1)} collective-permute-done((bf16[23,64,384]{2,1,0:T(8,128)(2,1)S(1)}, bf16[23,64,384]{2,1,0:T(8,128)(2,1)S(1)}, u32[]{:S(2)}, u32[]{:S(2)}) %collective-permute-start.1) | collective-permute-done | bytes 1130528 | tf_op jit(solution)/shard_map/ppermute | solution.py:397
  63.5 0.8 collective-permute-done.3.refs_2_
  64.3 4.2 %collective-permute-start.6 = (bf16[23,64,384]{2,1,0:T(8,128)(2,1)S(1)}, bf16[23,64,384]{2,1,0:T(8,128)(2,1)}, u32[]{:S(2)}, u32[]{:S(2)}) collective-permute-start(bf16[23,64,384]{2,1,0:T(8,128)(2,1)S(1)} %collective-permute-done.1.beside_ref), channel_id=1, source_target_pairs={{0,4},{2,6},{12,8},{14,10},{1,5},{3,7},{13,9},{15,11},{16,20},{18,... | collective-permute-start | bytes 3391496 | tf_op jit(solution)/shard_map/ppermute | solution.py:394
  68.5 0.7 collective-permute-start.8
  69.2 0.7 collective-permute-start.10
  70.0 1.8 left_major.2.refs_0_
  71.7 1.6 copy-done
  73.4 14.2 %collective-permute-done.5.own_ref = bf16[23,64,384]{2,1,0:T(8,128)(2,1)S(1)} collective-permute-done((bf16[23,64,384]{2,1,0:T(8,128)(2,1)S(1)}, bf16[23,64,384]{2,1,0:T(8,128)(2,1)S(1)}, u32[]{:S(2)}, u32[]{:S(2)}) %collective-permute-start.5) | collective-permute-done | bytes 1130528 | tf_op jit(solution)/shard_map/ppermute | solution.py:394
  87.6 1.0 copy-done.8
  88.6 23.2 %collective-permute-done.6.beside_ref = bf16[23,64,384]{2,1,0:T(8,128)(2,1)} collective-permute-done((bf16[23,64,384]{2,1,0:T(8,128)(2,1)S(1)}, bf16[23,64,384]{2,1,0:T(8,128)(2,1)}, u32[]{:S(2)}, u32[]{:S(2)}) %collective-permute-start.6) | collective-permute-done | bytes 1130528 | tf_op jit(solution)/shard_map/ppermute | solution.py:394
  111.8 1.3 copy-done.9
  113.1 3.2 %left_major.3.refs_1_ = bf16[64,96,256]{2,1,0:T(8,128)(2,1)S(1)} custom-call(bf16[23,64,384]{2,1,0:T(8,128)(2,1)S(1)} %copy-done.9, bf16[23,64,384]{2,1,0:T(8,128)(2,1)} %collective-permute-done.6.beside_ref), custom_call_target="tpu_custom_call" | custom-call | bytes 4521984 | tf_op jit(solution)/shard_map/left_major/pallas_call | solution.py:110
  116.3 1.7 copy-done.1
  118.0 7.7 %triangle.7 = (bf16[64,96,128]{2,1,0:T(8,128)(2,1)}, bf16[64,96,128]{2,1,0:T(8,128)(2,1)S(1)}) custom-call(s32[1]{0:T(128)} %bitcast.3.side_ref, bf16[64,96,256]{2,1,0:T(8,128)(2,1)} %copy-done, bf16[64,96,256]{2,1,0:T(8,128)(2,1)} %copy-done.1, bf16[23,64,384]{2,1,0:T(8,128)(2,1)S(1)} %collective-permute-done.7.refs_2_, ...), custom_call_target="tpu_custom_call" | custom-call | flops 805306368 | bytes 9043968 | tf_op jit(solution)/shard_map/triangle/pallas_call | solution.py:152
  125.7 0.7 collective-permute-start.18
  126.4 8.0 %triangle.5 = (bf16[64,96,128]{2,1,0:T(8,128)(2,1)}, bf16[64,96,128]{2,1,0:T(8,128)(2,1)}) custom-call(s32[1]{0:T(128)} %bitcast.3.side_ref, bf16[64,96,256]{2,1,0:T(8,128)(2,1)} %copy-done, bf16[64,96,256]{2,1,0:T(8,128)(2,1)} %copy-done.1, bf16[23,64,384]{2,1,0:T(8,128)(2,1)S(1)} %collective-permute-done.8.refs_2_, ...), custom_call_target="tpu_custom_call" | custom-call | flops 805306368 | bytes 9043968 | tf_op jit(solution)/shard_map/triangle/pallas_call | solution.py:152
  134.5 1.8 collective-permute-start.12
  136.3 6.3 %triangle.4.refs_0_ = bf16[64,96,128]{2,1,0:T(8,128)(2,1)} custom-call(s32[1]{0:T(128)} %bitcast.3.side_ref, bf16[64,96,256]{2,1,0:T(8,128)(2,1)} %copy-done, bf16[23,64,384]{2,1,0:T(8,128)(2,1)} %collective-permute-done.2.refs_1_, bf16[23,64,384]{2,1,0:T(8,128)(2,1)S(1)} %collective-permute-done.3.refs_2_), custom_call_target="tpu_custom_call" | custom-call | flops 402653184 | bytes 5652480 | tf_op jit(solution)/shard_map/triangle/pallas_call | solution.py:152
  142.6 5.8 %collective-permute-start.4 = (bf16[64,96,128]{2,1,0:T(8,128)(2,1)}, bf16[64,96,128]{2,1,0:T(8,128)(2,1)}, u32[]{:S(2)}, u32[]{:S(2)}) collective-permute-start(bf16[64,96,128]{2,1,0:T(8,128)(2,1)} %triangle.4.refs_0_), channel_id=1, source_target_pairs={{1,0},{3,2},{5,4},{7,6},{8,9},{10,11},{12,13},{14,15},{17,16},{19,... | collective-permute-start | bytes 4718600 | tf_op jit(solution)/shard_map/ppermute | solution.py:404
  148.4 1.8 collective-permute-start.11
  150.2 6.3 %triangle.6.refs_0_ = bf16[64,96,128]{2,1,0:T(8,128)(2,1)} custom-call(s32[1]{0:T(128)} %bitcast.3.side_ref, bf16[64,96,256]{2,1,0:T(8,128)(2,1)} %copy-done, bf16[23,64,384]{2,1,0:T(8,128)(2,1)S(1)} %get-tuple-element.30.refs_1_, bf16[23,64,384]{2,1,0:T(8,128)(2,1)} %collective-permute-done.refs_2_), custom_call_target="tpu_custom_call" | custom-call | flops 402653184 | bytes 5652480 | tf_op jit(solution)/shard_map/triangle/pallas_call | solution.py:152
  156.5 2.5 collective-permute-start.16
  159.0 1.1 copy-done.6
  160.1 1.8 collective-permute-start.17
  162.0 1.4 copy-done.5
  163.4 1.4 copy-done.7
  164.8 2.1 fold.7
  166.9 1.3 collective-permute-start.20
  168.3 4.4 %fold.5 = (bf16[23,96,128]{2,1,0:T(8,128)(2,1)}, bf16[23,96,128]{2,1,0:T(8,128)(2,1)}) custom-call(s32[1]{0:T(128)} %bitcast.2.role_ref, bf16[64,96,128]{2,1,0:T(8,128)(2,1)} %get-tuple-element.37.refs_0_, bf16[64,96,128]{2,1,0:T(8,128)(2,1)} %collective-permute-done.12.refs_1_), custom_call_target="tpu_custom_call" | custom-call | bytes 4718592 | tf_op jit(solution)/shard_map/fold/pallas_call | solution.py:208
  172.8 1.3 collective-permute-start.14
  174.1 1.5 collective-permute-start.13
  175.7 0.1 copy.24
  176.0 0.2 copy.23
  176.2 3.7 %fold.4 = (bf16[23,96,128]{2,1,0:T(8,128)(2,1)S(1)}, bf16[23,96,128]{2,1,0:T(8,128)(2,1)S(1)}) custom-call(s32[1]{0:T(128)} %bitcast.2.role_ref, bf16[64,96,128]{2,1,0:T(8,128)(2,1)} %triangle.4.refs_0_, bf16[64,96,128]{2,1,0:T(8,128)(2,1)} %collective-permute-done.4.refs_1_, bf16[64,96,128]{2,1,0:T(8,128)(2,1)} %get-tuple-element.35.refs_2_, ...), custom_call_target="tpu_custom_call" | custom-call | bytes 4718592 | tf_op jit(solution)/shard_map/fold/pallas_call | solution.py:208
  179.9 1.3 collective-permute-start.19
  181.2 3.7 %fold.6 = (bf16[23,96,128]{2,1,0:T(8,128)(2,1)S(1)}, bf16[23,96,128]{2,1,0:T(8,128)(2,1)S(1)}) custom-call(s32[1]{0:T(128)} %bitcast.2.role_ref, bf16[64,96,128]{2,1,0:T(8,128)(2,1)} %triangle.6.refs_0_, bf16[64,96,128]{2,1,0:T(8,128)(2,1)} %collective-permute-done.16.refs_1_, bf16[64,96,128]{2,1,0:T(8,128)(2,1)} %get-tuple-element.41.refs_2_, ...), custom_call_target="tpu_custom_call" | custom-call | bytes 4718592 | tf_op jit(solution)/shard_map/fold/pallas_call | solution.py:208
  184.9 11.5 %collective-permute-done.20 = bf16[23,96,128]{2,1,0:T(8,128)(2,1)} collective-permute-done((bf16[23,96,128]{2,1,0:T(8,128)(2,1)}, bf16[23,96,128]{2,1,0:T(8,128)(2,1)}, u32[]{:S(2)}, u32[]{:S(2)}) %collective-permute-start.20) | collective-permute-done | bytes 565280 | tf_op jit(solution)/shard_map/ppermute | solution.py:394
  196.5 1.1 broadcast_select_fusion
  197.6 0.3 collective-permute-start.21
  197.9 10.7 %collective-permute-done.14 = bf16[23,96,128]{2,1,0:T(8,128)(2,1)} collective-permute-done((bf16[23,96,128]{2,1,0:T(8,128)(2,1)}, bf16[23,96,128]{2,1,0:T(8,128)(2,1)}, u32[]{:S(2)}, u32[]{:S(2)}) %collective-permute-start.14) | collective-permute-done | bytes 565280 | tf_op jit(solution)/shard_map/ppermute | solution.py:394
  208.6 1.1 broadcast_select_fusion.2
  209.7 0.3 collective-permute-start.15
  210.0 10.7 %collective-permute-done.13 = bf16[23,96,128]{2,1,0:T(8,128)(2,1)} collective-permute-done((bf16[23,96,128]{2,1,0:T(8,128)(2,1)}, bf16[23,96,128]{2,1,0:T(8,128)(2,1)}, u32[]{:S(2)}, u32[]{:S(2)}) %collective-permute-start.13) | collective-permute-done | bytes 565280 | tf_op jit(solution)/shard_map/ppermute | solution.py:394
  220.7 1.1 broadcast_select_fusion.3.own_ref
  221.8 10.9 %collective-permute-done.19 = bf16[23,96,128]{2,1,0:T(8,128)(2,1)S(1)} collective-permute-done((bf16[23,96,128]{2,1,0:T(8,128)(2,1)S(1)}, bf16[23,96,128]{2,1,0:T(8,128)(2,1)S(1)}, u32[]{:S(2)}, u32[]{:S(2)}) %collective-permute-start.19) | collective-permute-done | bytes 565280 | tf_op jit(solution)/shard_map/ppermute | solution.py:394
  232.8 12.0 %finish.2.refs_4_ = bf16[2,23,96,128]{3,2,1,0:T(8,128)(2,1)S(1)} custom-call(s32[1]{0:T(128)} %bitcast.flag_ref, bf16[2,23,184,128]{3,2,1,0:T(8,128)(2,1)S(1)} %bitcast.18, bf16[23,96,128]{2,1,0:T(8,128)(2,1)S(1)} %broadcast_select_fusion.1.own_ref, bf16[23,96,128]{2,1,0:T(8,128)(2,1)S(1)} %collective-permute-done.21.other_ref, ...), custom_call_target="tpu_custom_call" | custom-call | flops 1941438464 | bytes 4333568 | tf_op jit(solution)/shard_map/finish/pallas_call | solution.py:275
  244.8 13.3 %finish.3 = bf16[2,23,184,128]{3,2,1,0:T(8,128)(2,1)} custom-call(s32[1]{0:T(128)S(6)} %sub.17.flag_ref, bf16[2,23,184,128]{3,2,1,0:T(8,128)(2,1)S(1)} %bitcast.19, bf16[23,96,128]{2,1,0:T(8,128)(2,1)S(1)} %broadcast_select_fusion.3.own_ref, bf16[23,96,128]{2,1,0:T(8,128)(2,1)S(1)} %collective-permute-done.15.other_ref, bf16[128,128]{1,0:T(8,128)(2,1)S(1)} %bitcast.25, ...), custom_call_target="tpu_custom_call" | custom-call | flops 1941438464 | bytes 4333568 | tf_op jit(solution)/shard_map/finish/pallas_call | solution.py:275
  (50 shorter events, 1.6 us)
Async XLA Ops:
  4.4 1.6 copy-start.2
  6.0 10.7 %copy-start.3 = (bf16[46,184,128]{2,1,0:T(8,128)(2,1)S(1)}, bf16[46,184,128]{2,1,0:T(8,128)(2,1)}, u32[]{:S(2)}) copy-start(bf16[46,184,128]{2,1,0:T(8,128)(2,1)} %param.6) | copy-start | bytes 6500356
  11.4 27.0 %collective-permute-start = (bf16[23,64,384]{2,1,0:T(8,128)(2,1)}, bf16[23,64,384]{2,1,0:T(8,128)(2,1)}, u32[]{:S(2)}, u32[]{:S(2)}) collective-permute-start(bf16[23,64,384]{2,1,0:T(8,128)(2,1)} %get-tuple-element.28), channel_id=1, source_target_pairs={{0,2},{2,0},{4,6},{6,4},{8,10},{10,8},{12,14},{14,12},{1,3},{3,1},... | collective-permute-start | bytes 3391496 | tf_op jit(solution)/shard_map/ppermute | solution.py:397
  13.4 28.9 %collective-permute-start.2 = (bf16[23,64,384]{2,1,0:T(8,128)(2,1)S(1)}, bf16[23,64,384]{2,1,0:T(8,128)(2,1)}, u32[]{:S(2)}, u32[]{:S(2)}) collective-permute-start(bf16[23,64,384]{2,1,0:T(8,128)(2,1)S(1)} %get-tuple-element.30.refs_1_), channel_id=1, source_target_pairs={{0,4},{2,6},{4,0},{6,2},{8,12},{10,14},{12,8},{14,10},{1,5},{3,7},... | collective-permute-start | bytes 3391496 | tf_op jit(solution)/shard_map/ppermute | solution.py:394
  38.4 25.2 %collective-permute-start.1 = (bf16[23,64,384]{2,1,0:T(8,128)(2,1)S(1)}, bf16[23,64,384]{2,1,0:T(8,128)(2,1)S(1)}, u32[]{:S(2)}, u32[]{:S(2)}) collective-permute-start(bf16[23,64,384]{2,1,0:T(8,128)(2,1)S(1)} %get-tuple-element.29), channel_id=1, source_target_pairs={{0,2},{2,0},{4,6},{6,4},{8,10},{10,8},{12,14},{14,12},{1,3},{3,1},... | collective-permute-start | bytes 3391496 | tf_op jit(solution)/shard_map/ppermute | solution.py:397
  39.5 24.8 %collective-permute-start.3 = (bf16[23,64,384]{2,1,0:T(8,128)(2,1)}, bf16[23,64,384]{2,1,0:T(8,128)(2,1)S(1)}, u32[]{:S(2)}, u32[]{:S(2)}) collective-permute-start(bf16[23,64,384]{2,1,0:T(8,128)(2,1)} %collective-permute-done.refs_2_), channel_id=1, source_target_pairs={{0,4},{2,6},{4,0},{6,2},{8,12},{10,14},{12,8},{14,10},{1,5},{3,7},... | collective-permute-start | bytes 3391496 | tf_op jit(solution)/shard_map/ppermute | solution.py:394
  40.8 27.7 %collective-permute-start.7 = (bf16[23,64,384]{2,1,0:T(8,128)(2,1)S(1)}, bf16[23,64,384]{2,1,0:T(8,128)(2,1)S(1)}, u32[]{:S(2)}, u32[]{:S(2)}) collective-permute-start(bf16[23,64,384]{2,1,0:T(8,128)(2,1)S(1)} %get-tuple-element.30.refs_1_), channel_id=1, source_target_pairs={{4,8},{6,10},{8,4},{10,6},{5,9},{7,11},{9,5},{11,7},{20,24},{22,26... | collective-permute-start | bytes 3391496 | tf_op jit(solution)/shard_map/ppermute | solution.py:394
  41.5 27.7 %collective-permute-start.9 = (bf16[23,64,384]{2,1,0:T(8,128)(2,1)}, bf16[23,64,384]{2,1,0:T(8,128)(2,1)S(1)}, u32[]{:S(2)}, u32[]{:S(2)}) collective-permute-start(bf16[23,64,384]{2,1,0:T(8,128)(2,1)} %collective-permute-done.refs_2_), channel_id=1, source_target_pairs={{4,8},{6,10},{8,4},{10,6},{5,9},{7,11},{9,5},{11,7},{20,24},{22,26... | collective-permute-start | bytes 3391496 | tf_op jit(solution)/shard_map/ppermute | solution.py:394
  42.3 45.3 %collective-permute-start.5 = (bf16[23,64,384]{2,1,0:T(8,128)(2,1)S(1)}, bf16[23,64,384]{2,1,0:T(8,128)(2,1)S(1)}, u32[]{:S(2)}, u32[]{:S(2)}) collective-permute-start(bf16[23,64,384]{2,1,0:T(8,128)(2,1)S(1)} %get-tuple-element.31.own_ref), channel_id=1, source_target_pairs={{0,4},{2,6},{12,8},{14,10},{1,5},{3,7},{13,9},{15,11},{16,20},{18,... | collective-permute-start | bytes 3391496 | tf_op jit(solution)/shard_map/ppermute | solution.py:394
  64.3 47.5 %collective-permute-start.6 = (bf16[23,64,384]{2,1,0:T(8,128)(2,1)S(1)}, bf16[23,64,384]{2,1,0:T(8,128)(2,1)}, u32[]{:S(2)}, u32[]{:S(2)}) collective-permute-start(bf16[23,64,384]{2,1,0:T(8,128)(2,1)S(1)} %collective-permute-done.1.beside_ref), channel_id=1, source_target_pairs={{0,4},{2,6},{12,8},{14,10},{1,5},{3,7},{13,9},{15,11},{16,20},{18,... | collective-permute-start | bytes 3391496 | tf_op jit(solution)/shard_map/ppermute | solution.py:394
  68.5 57.9 %collective-permute-start.8 = (bf16[23,64,384]{2,1,0:T(8,128)(2,1)}, bf16[23,64,384]{2,1,0:T(8,128)(2,1)S(1)}, u32[]{:S(2)}, u32[]{:S(2)}) collective-permute-start(bf16[23,64,384]{2,1,0:T(8,128)(2,1)} %collective-permute-done.2.refs_1_), channel_id=1, source_target_pairs={{4,8},{6,10},{8,4},{10,6},{5,9},{7,11},{9,5},{11,7},{20,24},{22,26... | collective-permute-start | bytes 3391496 | tf_op jit(solution)/shard_map/ppermute | solution.py:394
  69.2 57.2 %collective-permute-start.10 = (bf16[23,64,384]{2,1,0:T(8,128)(2,1)S(1)}, bf16[23,64,384]{2,1,0:T(8,128)(2,1)S(1)}, u32[]{:S(2)}, u32[]{:S(2)}) collective-permute-start(bf16[23,64,384]{2,1,0:T(8,128)(2,1)S(1)} %collective-permute-done.3.refs_2_), channel_id=1, source_target_pairs={{4,8},{6,10},{8,4},{10,6},{5,9},{7,11},{9,5},{11,7},{20,24},{22,26... | collective-permute-start | bytes 3391496 | tf_op jit(solution)/shard_map/ppermute | solution.py:394
  71.7 1.6 copy-start
  87.6 1.0 copy-start.8
  111.8 1.3 copy-start.9
  116.3 1.7 copy-start.1
  125.7 8.8 %copy-start.4 = (bf16[64,96,128]{2,1,0:T(8,128)(2,1)}, bf16[64,96,128]{2,1,0:T(8,128)(2,1)S(1)}, u32[]{:S(2)}) copy-start(bf16[64,96,128]{2,1,0:T(8,128)(2,1)S(1)} %get-tuple-element.43.refs_0_) | copy-start | bytes 4718596
  125.7 33.3 %collective-permute-start.18 = (bf16[64,96,128]{2,1,0:T(8,128)(2,1)S(1)}, bf16[64,96,128]{2,1,0:T(8,128)(2,1)S(1)}, u32[]{:S(2)}, u32[]{:S(2)}) collective-permute-start(bf16[64,96,128]{2,1,0:T(8,128)(2,1)S(1)} %get-tuple-element.43.refs_0_), channel_id=1, source_target_pairs={{4,5},{6,7},{9,8},{11,10},{20,21},{22,23},{25,24},{27,26}} | collective-permute-start | bytes 4718600 | tf_op jit(solution)/shard_map/ppermute | solution.py:404
  134.5 32.4 %collective-permute-start.12 = (bf16[64,96,128]{2,1,0:T(8,128)(2,1)}, bf16[64,96,128]{2,1,0:T(8,128)(2,1)}, u32[]{:S(2)}, u32[]{:S(2)}) collective-permute-start(bf16[64,96,128]{2,1,0:T(8,128)(2,1)} %get-tuple-element.37.refs_0_), channel_id=1, source_target_pairs={{4,5},{6,7},{9,8},{11,10},{20,21},{22,23},{25,24},{27,26}} | collective-permute-start | bytes 4718600 | tf_op jit(solution)/shard_map/ppermute | solution.py:404
  142.6 30.2 %collective-permute-start.4 = (bf16[64,96,128]{2,1,0:T(8,128)(2,1)}, bf16[64,96,128]{2,1,0:T(8,128)(2,1)}, u32[]{:S(2)}, u32[]{:S(2)}) collective-permute-start(bf16[64,96,128]{2,1,0:T(8,128)(2,1)} %triangle.4.refs_0_), channel_id=1, source_target_pairs={{1,0},{3,2},{5,4},{7,6},{8,9},{10,11},{12,13},{14,15},{17,16},{19,... | collective-permute-start | bytes 4718600 | tf_op jit(solution)/shard_map/ppermute | solution.py:404
  148.4 25.7 %collective-permute-start.11 = (bf16[64,96,128]{2,1,0:T(8,128)(2,1)}, bf16[64,96,128]{2,1,0:T(8,128)(2,1)}, u32[]{:S(2)}, u32[]{:S(2)}) collective-permute-start(bf16[64,96,128]{2,1,0:T(8,128)(2,1)} %get-tuple-element.35.refs_2_), channel_id=1, source_target_pairs={{4,5},{6,7},{9,8},{11,10},{20,21},{22,23},{25,24},{27,26}} | collective-permute-start | bytes 4718600 | tf_op jit(solution)/shard_map/ppermute | solution.py:404
  156.5 23.4 %collective-permute-start.16 = (bf16[64,96,128]{2,1,0:T(8,128)(2,1)}, bf16[64,96,128]{2,1,0:T(8,128)(2,1)}, u32[]{:S(2)}, u32[]{:S(2)}) collective-permute-start(bf16[64,96,128]{2,1,0:T(8,128)(2,1)} %triangle.6.refs_0_), channel_id=1, source_target_pairs={{1,0},{3,2},{5,4},{7,6},{8,9},{10,11},{12,13},{14,15},{17,16},{19,... | collective-permute-start | bytes 4718600 | tf_op jit(solution)/shard_map/ppermute | solution.py:404
  159.0 1.1 copy-start.6
  160.1 21.1 %collective-permute-start.17 = (bf16[64,96,128]{2,1,0:T(8,128)(2,1)}, bf16[64,96,128]{2,1,0:T(8,128)(2,1)}, u32[]{:S(2)}, u32[]{:S(2)}) collective-permute-start(bf16[64,96,128]{2,1,0:T(8,128)(2,1)} %get-tuple-element.41.refs_2_), channel_id=1, source_target_pairs={{4,5},{6,7},{9,8},{11,10},{20,21},{22,23},{25,24},{27,26}} | collective-permute-start | bytes 4718600 | tf_op jit(solution)/shard_map/ppermute | solution.py:404
  162.0 1.4 copy-start.5
  163.4 1.4 copy-start.7
  164.8 3.4 %copy-start.12 = (bf16[128,128]{1,0:T(8,128)(2,1)S(1)}, bf16[128,128]{1,0:T(8,128)(2,1)}, u32[]{:S(2)}) copy-start(bf16[128,128]{1,0:T(8,128)(2,1)} %param.9) | copy-start | bytes 98308
  166.9 29.6 %collective-permute-start.20 = (bf16[23,96,128]{2,1,0:T(8,128)(2,1)}, bf16[23,96,128]{2,1,0:T(8,128)(2,1)}, u32[]{:S(2)}, u32[]{:S(2)}) collective-permute-start(bf16[23,96,128]{2,1,0:T(8,128)(2,1)} %get-tuple-element.46), channel_id=1, source_target_pairs={{4,0},{6,2},{8,12},{10,14},{5,1},{7,3},{9,13},{11,15},{20,16},{22,... | collective-permute-start | bytes 1695752 | tf_op jit(solution)/shard_map/ppermute | solution.py:394
  168.3 7.5 %copy-start.11 = (bf16[512,128]{1,0:T(8,128)(2,1)S(1)}, bf16[512,128]{1,0:T(8,128)(2,1)}, u32[]{:S(2)}) copy-start(bf16[512,128]{1,0:T(8,128)(2,1)} %param.11) | copy-start | bytes 393220
  168.3 7.7 %copy-start.10 = (bf16[128,1024]{1,0:T(8,128)(2,1)S(1)}, bf16[128,1024]{1,0:T(8,128)(2,1)}, u32[]{:S(2)}) copy-start(bf16[128,1024]{1,0:T(8,128)(2,1)} %param.10) | copy-start | bytes 786436
  172.8 35.8 %collective-permute-start.14 = (bf16[23,96,128]{2,1,0:T(8,128)(2,1)}, bf16[23,96,128]{2,1,0:T(8,128)(2,1)}, u32[]{:S(2)}, u32[]{:S(2)}) collective-permute-start(bf16[23,96,128]{2,1,0:T(8,128)(2,1)} %get-tuple-element.40), channel_id=1, source_target_pairs={{4,0},{6,2},{8,12},{10,14},{5,1},{7,3},{9,13},{11,15},{20,16},{22,... | collective-permute-start | bytes 1695752 | tf_op jit(solution)/shard_map/ppermute | solution.py:394
  174.1 46.6 %collective-permute-start.13 = (bf16[23,96,128]{2,1,0:T(8,128)(2,1)}, bf16[23,96,128]{2,1,0:T(8,128)(2,1)}, u32[]{:S(2)}, u32[]{:S(2)}) collective-permute-start(bf16[23,96,128]{2,1,0:T(8,128)(2,1)} %get-tuple-element.38), channel_id=1, source_target_pairs={{4,0},{6,2},{8,12},{10,14},{5,1},{7,3},{9,13},{11,15},{20,16},{22,... | collective-permute-start | bytes 1695752 | tf_op jit(solution)/shard_map/ppermute | solution.py:394
  179.9 52.8 %collective-permute-start.19 = (bf16[23,96,128]{2,1,0:T(8,128)(2,1)S(1)}, bf16[23,96,128]{2,1,0:T(8,128)(2,1)S(1)}, u32[]{:S(2)}, u32[]{:S(2)}) collective-permute-start(bf16[23,96,128]{2,1,0:T(8,128)(2,1)S(1)} %get-tuple-element.44), channel_id=1, source_target_pairs={{4,0},{6,2},{8,12},{10,14},{5,1},{7,3},{9,13},{11,15},{20,16},{22,... | collective-permute-start | bytes 1695752 | tf_op jit(solution)/shard_map/ppermute | solution.py:394
  197.6 35.2 %collective-permute-start.21 = (bf16[23,96,128]{2,1,0:T(8,128)(2,1)S(1)}, bf16[23,96,128]{2,1,0:T(8,128)(2,1)S(1)}, u32[]{:S(2)}, u32[]{:S(2)}) collective-permute-start(bf16[23,96,128]{2,1,0:T(8,128)(2,1)S(1)} %broadcast_select_fusion), channel_id=1, source_target_pairs={{0,2},{2,0},{4,6},{6,4},{8,10},{10,8},{12,14},{14,12},{1,3},{3,1},... | collective-permute-start | bytes 1695752 | tf_op jit(solution)/shard_map/ppermute | solution.py:397
  209.7 35.0 %collective-permute-start.15 = (bf16[23,96,128]{2,1,0:T(8,128)(2,1)S(1)}, bf16[23,96,128]{2,1,0:T(8,128)(2,1)S(1)}, u32[]{:S(2)}, u32[]{:S(2)}) collective-permute-start(bf16[23,96,128]{2,1,0:T(8,128)(2,1)S(1)} %broadcast_select_fusion.2), channel_id=1, source_target_pairs={{0,2},{2,0},{4,6},{6,4},{8,10},{10,8},{12,14},{14,12},{1,3},{3,1},... | collective-permute-start | bytes 1695752 | tf_op jit(solution)/shard_map/ppermute | solution.py:397

commit v5 on v4

--- a/solution.py
+++ b/solution.py
@@ -1,3 +1,5 @@
+import functools
+
 import jax
 import jax.numpy as jnp
 from jax import lax
@@ -79,16 +81,21 @@
     )(where, pair, weight)
 
 
-def channel_major(pieces, clear):
-    width = pieces[0].shape[2] // 3
+def channel_major(pieces, left):
+    half, chans, lanes = pieces[0].shape
+    width = lanes // 3
     main, rest = [], []
     for piece in pieces:
         tail = piece[:, :, 2 * width :]
         turned = jnp.concatenate([tail[:, :, width // 2 :], tail[:, :, : width // 2]], axis=2)
         main += [piece[:, :, :width], piece[:, :, width : 2 * width]]
         rest += [tail, turned]
+        if left:
+            gap = jnp.zeros((padded(2 * half, 16) - 2 * half, chans, width), BF16)
+            main.append(gap)
+            rest.append(gap)
     rest = jnp.concatenate(rest, axis=0)
-    if clear:
+    if left:
         low = lax.broadcasted_iota(jnp.int32, rest.shape, 2) < width // 2
         rest = jnp.where(low, rest, jnp.zeros_like(rest))
     main = jnp.swapaxes(jnp.concatenate(main, axis=0), 0, 1)
@@ -98,33 +105,37 @@
 def left_kernel(own_ref, beside_ref, out_ref):
     width = own_ref.shape[2] // 3
     main, rest = channel_major([own_ref[...], beside_ref[...]], True)
-    rows = main.shape[1]
-    out_ref[:, :rows, :width] = main
-    out_ref[:, :rows, width:] = rest
-    out_ref[:, rows:] = jnp.zeros_like(out_ref[:, rows:])
+    out_ref[:, :, :width] = main
+    out_ref[:, :, width:] = rest
 
 
 def left_major(own, beside):
     half, chans, lanes = own.shape
+    rows, deep = 2 * padded(2 * half, 16), lanes // 3 * 2
     piece = pl.BlockSpec((half, CHUNK, lanes), lambda c: (0, c, 0))
     return pl.pallas_call(
         left_kernel,
         grid=(chans // CHUNK,),
-        out_shape=jax.ShapeDtypeStruct((chans, padded(4 * half, 16), lanes // 3 * 2), BF16),
+        out_shape=jax.ShapeDtypeStruct((chans, rows, deep), BF16),
         in_specs=[piece, piece],
-        out_specs=pl.BlockSpec((CHUNK, padded(4 * half, 16), lanes // 3 * 2), lambda c: (c, 0, 0)),
+        out_specs=pl.BlockSpec((CHUNK, rows, deep), lambda c: (c, 0, 0)),
         compiler_params=params(),
         cost_estimate=cost(0, 8 * own.size),
         name="left_major",
     )(own, beside)
 
 
-def triangle_kernel(side_ref, *refs):
-    lefts = len(refs) // 2 - 1
-    own, beside = refs[lefts][...], refs[lefts + 1][...]
-    outs, right_ref = refs[lefts + 2 : -1], refs[-1]
+def triangle_kernel(flag_ref, *refs, guests, options):
+    lefts = refs[: 1 + guests]
+    rights = refs[1 + guests : 1 + guests + 2 * options]
+    outs, right_ref = refs[1 + guests + 2 * options : -1], refs[-1]
+    own, beside = rights[0][...], rights[1][...]
+    if options == 2:
+        plain = flag_ref[1] == 0
+        own = jnp.where(plain, own, rights[2][...])
+        beside = jnp.where(plain, beside, rights[3][...])
     width = own.shape[2] // 3
-    even = side_ref[0] == 0
+    even = flag_ref[0] == 0
     main, rest = channel_major(
         [jnp.where(even, own, beside), jnp.where(even, beside, own)], False
     )
@@ -137,56 +148,71 @@
     right_ref[:, :rows, :width] = main
     right_ref[:, :rows, width:] = rest
     for c in range(CHUNK):
-        for left_ref, out_ref in zip(refs[:lefts], outs):
-            out_ref[c] = lax.dot_general(
+        products = [
+            lax.dot_general(
                 left_ref[c], right_ref[c], (((1,), (1,)), ((), ())), preferred_element_type=F32
             ).astype(BF16)
-
-
-def triangle(side, lefts, own, beside):
-    half, chans, lanes = own.shape
-    rows, cols = padded(4 * half, 16), padded(4 * half, 128)
-    piece = pl.BlockSpec((half, CHUNK, lanes), lambda c: (0, c, 0))
-    left = pl.BlockSpec((CHUNK, rows, lanes // 3 * 2), lambda c: (c, 0, 0))
-    out = pl.BlockSpec((CHUNK, rows, cols), lambda c: (c, 0, 0))
+            for left_ref in lefts
+        ]
+        outs[0][c] = products[0]
+        if guests:
+            part = products[1].shape[0] // 2
+            outs[1][c] = products[1][:part]
+            outs[2][c] = products[1][part:]
+
+
+def triangle(flags, lefts, *pieces):
+    half, chans, lanes = pieces[0].shape
+    options, guests = len(pieces) // 2, len(lefts) - 1
+    rows, cols, deep = lefts[0].shape[1], padded(4 * half, 128), lanes // 3 * 2
+
+    def piece(option):
+        if options == 1:
+            return pl.BlockSpec((half, CHUNK, lanes), lambda c, flag_ref: (0, c, 0))
+        return pl.BlockSpec(
+            (half, CHUNK, lanes), lambda c, flag_ref: (0, jnp.where(flag_ref[1] == option, c, 0), 0)
+        )
+
+    def block(height, depth):
+        return pl.BlockSpec((CHUNK, height, depth), lambda c, flag_ref: (c, 0, 0))
+
+    heights = [rows] + [rows // 2] * (2 * guests)
     return pl.pallas_call(
-        triangle_kernel,
-        grid=(chans // CHUNK,),
-        out_shape=[jax.ShapeDtypeStruct((chans, rows, cols), BF16) for _ in lefts],
-        in_specs=[pl.BlockSpec(memory_space=pltpu.SMEM)] + [left] * len(lefts) + [piece, piece],
-        out_specs=[out] * len(lefts),
-        scratch_shapes=[VMEM((CHUNK, cols, lanes // 3 * 2), BF16)],
+        functools.partial(triangle_kernel, guests=guests, options=options),
+        grid_spec=pltpu.PrefetchScalarGridSpec(
+            num_scalar_prefetch=1,
+            grid=(chans // CHUNK,),
+            in_specs=[block(rows, deep)] * len(lefts) + [piece(i // 2) for i in range(len(pieces))],
+            out_specs=[block(h, cols) for h in heights],
+            scratch_shapes=[VMEM((CHUNK, cols, deep), BF16)],
+        ),
+        out_shape=[jax.ShapeDtypeStruct((chans, h, cols), BF16) for h in heights],
         compiler_params=params(),
-        cost_estimate=cost(2 * len(lefts) * chans * rows * cols * lanes // 3 * 2, (4 + 6 * len(lefts)) * own.size),
+        cost_estimate=cost(2 * len(lefts) * chans * rows * cols * deep, 10 * pieces[0].size),
         name="triangle",
-    )(side, *lefts, own, beside)
-
-
-def fold_kernel(role_ref, *refs):
-    own_ref, beside_ref, work_ref = refs[-3:]
-    half, cols, width = own_ref.shape
-    chans = width // 2
+    )(flags, *lefts, *pieces)
+
+
+def fold_kernel(role_ref, *refs, outputs, half):
+    outs, work_ref = refs[-1 - outputs : -1], refs[-1]
+    cols = outs[0].shape[1]
+    parts = refs[: -1 - outputs]
     c = pl.program_id(0)
-    options = len(refs[:-3]) // 2
-    for option in range(options):
-        mine_ref, rest_ref = refs[2 * option : 2 * option + 2]
-
-        def gather():
-            total = (mine_ref[...].astype(F32) + rest_ref[...].astype(F32)).astype(BF16)
+    for option in range(2):
+
+        @pl.when(role_ref[0] == option)
+        def _(option=option):
+            total = parts[2 * option][...].astype(F32) + parts[2 * option + 1][...].astype(F32)
             at = pl.ds(pl.multiple_of(c * CHUNK, CHUNK), CHUNK)
-            work_ref[:, at, :] = jnp.swapaxes(total, 0, 1)
-
-        if options == 1:
-            gather()
-        else:
-            pl.when(role_ref[0] == option)(gather)
+            work_ref[:, at, :] = jnp.swapaxes(total.astype(BF16), 0, 1)
 
     @pl.when(c == pl.num_programs(0) - 1)
     def _():
-        for o, out_ref in enumerate((own_ref, beside_ref)):
+        pitch = work_ref.shape[0] // outputs
+        for o, out_ref in enumerate(outs):
 
             def turn(r, carry, o=o, out_ref=out_ref):
-                at = o * 2 * half + r
+                at = o * pitch + r
                 stacked = jnp.concatenate([work_ref[at], work_ref[at + half]], axis=0)
                 out_ref[r] = stacked.T[:cols]
                 return carry
@@ -196,25 +222,24 @@
 
 def fold(half, role, *parts):
     chans, rows, cols = parts[0].shape
+    outputs = rows // padded(2 * half, 16)
     out = jax.ShapeDtypeStruct((half, padded(4 * half, 16), 2 * chans), BF16)
 
     def block(option):
-        if len(parts) == 2:
-            return pl.BlockSpec((CHUNK, rows, cols), lambda c, role_ref: (c, 0, 0))
         return pl.BlockSpec(
             (CHUNK, rows, cols), lambda c, role_ref: (jnp.where(role_ref[0] == option, c, 0), 0, 0)
         )
 
     return pl.pallas_call(
-        fold_kernel,
+        functools.partial(fold_kernel, outputs=outputs, half=half),
         grid_spec=pltpu.PrefetchScalarGridSpec(
             num_scalar_prefetch=1,
             grid=(chans // CHUNK,),
-            in_specs=[block(i // 2) for i in range(len(parts))],
-            out_specs=[pl.BlockSpec(out.shape, lambda c, role_ref: (0, 0, 0))] * 2,
+            in_specs=[block(i // 2) for i in range(4)],
+            out_specs=[pl.BlockSpec(out.shape, lambda c, role_ref: (0, 0, 0))] * outputs,
             scratch_shapes=[VMEM((rows, chans, cols), BF16)],
         ),
-        out_shape=(out, out),
+        out_shape=[out] * outputs,
         compiler_params=params(),
         cost_estimate=cost(0, 6 * parts[0].size),
         name="fold",
@@ -398,9 +423,17 @@
 
     def to_core(value, places, keep):
         perm = []
-        for z in places:
-            target = z // 2 if keep else 1 - z // 2
+        for z, towards in zip(places, keep):
+            target = z // 2 if towards else 1 - z // 2
             perm += [(4 * z + 2 * b + 1 - target, 4 * z + 2 * b + target) for b in range(2)]
+        return lax.ppermute(value, ("row", "col"), perm)
+
+    def give_back(value, swap):
+        perm = []
+        for s, t in ((1, 0), (2, 3)):
+            away = 1 - t // 2
+            source = 1 - away if swap else away
+            perm += [(4 * s + 2 * b + source, 4 * t + 2 * (b ^ swap) + away) for b in range(2)]
         return lax.ppermute(value, ("row", "col"), perm)
 
     def by_side(block, axis):
@@ -412,47 +445,62 @@
         ]
         return jnp.concatenate(parts, axis=1).T
 
-    where = jnp.stack([valid_count, row_id * tile_rows, core * tile_cols]).astype(jnp.int32)
-    sides = side.astype(jnp.int32).reshape(1)
-    is_keeper = core == keeper
-    role = jnp.where(is_keeper, 0, 1).astype(jnp.int32).reshape(1)
-    folded = pair.reshape(2, half, tile_cols, width)
-    mates, cross = [(0, 1), (1, 0), (2, 3), (3, 2)], [(1, 2), (2, 1)]
-    inward, outward = [(0, 1), (3, 2)], [(1, 0), (2, 3)]
-
     def after(value, *others):
         return lax.optimization_barrier((value, *others))[0]
 
+    def scalars(*values):
+        return jnp.stack([jnp.asarray(v).astype(jnp.int32) for v in values])
+
+    is_keeper = core == keeper
+    inner = (place == 1) | (place == 2)
+    where = scalars(valid_count, row_id * tile_rows, core * tile_cols)
+    folded = pair.reshape(2, half, tile_cols, width)
+    cross, inward, outward = [(1, 2), (2, 1)], [(0, 1), (3, 2)], [(1, 0), (2, 3)]
+    everyone, inners = range(4), (1, 2)
+
     right_own, right_far = project(where, folded, gate_pair(2))
-    mate_own, near_own = among(right_own, mates), among(right_own, cross)
+    from_end, near, from_inner = ([among(right_own, m)] for m in (inward, cross, outward))
     right_beside = across(right_far)
     left_own, left_far = project(where, folded, gate_pair(0))
     left_beside = across(after(left_far, right_beside))
-    mate_beside, near_beside = among(right_beside, mates), among(right_beside, cross)
-    far_own = among(after(mate_own, near_own), cross)
-    guest_own = among(after(left_own, mate_own), inward)
-    far_beside = among(after(mate_beside, near_beside), cross)
-    guest_beside = among(after(left_beside, mate_beside), inward)
+    from_end.append(among(right_beside, inward))
+    near.append(among(right_beside, cross))
+    relay = [among(after(near[0], from_inner[0]), outward)]
+    far = [among(after(from_end[0], near[0]), cross)]
+    relay.append(among(after(near[1], from_inner[0]), outward))
+    guest = [among(after(left_own, from_end[0]), inward)]
+    far.append(among(after(from_end[1], near[1]), cross))
+    from_inner.append(among(after(right_beside, relay[0]), outward))
+    guest.append(among(after(left_beside, from_end[1]), inward))
 
     left = left_major(left_own, left_beside)
-    (home_own,) = triangle(sides, [left], right_own, right_beside)
-    (home_mate,) = triangle(sides, [left], mate_own, mate_beside)
-    left_guest = left_major(guest_own, guest_beside)
-    away_near, lent_near = triangle(sides, [left, left_guest], near_own, near_beside)
-    away_far, lent_far = triangle(sides, [left, left_guest], far_own, far_beside)
-
-    inner = (place == 1) | (place == 2)
-    order = jnp.where(is_keeper, place % 2, place // 2).astype(jnp.int32).reshape(1)
+    (home,) = triangle(scalars(side, 0), [left], right_own, right_beside)
+    home_rest = to_core(home, everyone, [True] * 4)
+    (mate,) = triangle(scalars(side, 0), [left], *from_end)
+    mate_rest = to_core(mate, inners, [True] * 2)
+    (away,) = triangle(scalars(side, jnp.where(inner, 0, 1)), [left], *near, *relay)
+    away_rest = to_core(away, everyone, [False] * 4)
+    first = fold(half, scalars(jnp.where(is_keeper, 0, 1)), home, home_rest, away, away_rest)
+
+    left_guest = left_major(after(guest[0], *first), guest[1])
+    late, lent_own, lent_beside = triangle(
+        scalars(side, jnp.where(inner, 0, 1)), [left, left_guest], *far, *from_inner
+    )
+    lent_rest = to_core(lent_own, inners, [False] * 2), to_core(lent_beside, inners, [True] * 2)
+    late_rest = to_core(late, everyone, [True, False, False, True])
+    (lent,) = fold(
+        half, scalars(jnp.where(is_keeper, 0, 1)), lent_beside, lent_rest[1], lent_own, lent_rest[0]
+    )
+    given = give_back(lent, 0), give_back(lent, 1)
+    second = fold(half, scalars(jnp.where(is_keeper & inner, 0, 1)), mate, mate_rest, late, late_rest)
+
+    order = jnp.where(is_keeper, place % 2, place // 2)
     weights = [w.T for w in (in_weight[:, 4 * width :], by_side(out_weight, 0), trans_in, trans_out)]
-    result = None
-    for i, (home, away, lent) in enumerate(
-        ((home_own, away_near, lent_near), (home_mate, away_far, lent_far))
-    ):
-        returned = [among(v, outward) for v in fold(half, role, lent, to_core(lent, (1, 2), False))]
-        kept = fold(half, role, home, to_core(home, range(4), True), away, to_core(away, (1, 2), False))
-        own, beside = (jnp.where(is_keeper | inner, k, g) for k, g in zip(kept, returned))
-        flag = order if i == 0 else 1 - order
-        result = finish(flag, folded, own, across(beside), weights, result)
+    earlier = finish(scalars(order), folded, after(first[0], lent), across(first[1]), weights)
+    kept = is_keeper | inner
+    own = jnp.where(kept, second[0], given[0])
+    other = jnp.where(kept, across(second[1]), given[1])
+    result = finish(scalars(1 - order), folded, own, other, weights, earlier)
     return result.reshape(tile_rows, tile_cols, width)
 
 

time: 262 us -> 275 us (1.050)
  waiting for transfers between devices: 114 us -> 123 us
  starting transfers between devices: 40.3 us -> 49.2 us
  other arithmetic: 4.41 us -> 0.5 us
    ppermute x4, waiting for transfers between devices: 31.5 us -> 49.6 us  [across(): return lax.ppermute(value, 'row', [(i, i ^ 1) for i in range(8)])]
    ppermute x12, waiting for transfers between devices: 82 us -> 73.9 us  [among(): lax.ppermute(value, 'row', [(2 * s + b, 2 * t + b) for s, t in moves for...]
    select_n x4 -> x2, other arithmetic: 3.41 us -> 0.12 us  [the longest x1 0.06 us: two_by_four(): own = jnp.where(kept, second[0], given[0])]
    pallas_call x8 -> x7, Pallas kernels: 42.3 us -> 39 us  [the longest x4 28.7 us: triangle(): pl.pallas_call(functools.partial(triangle_kernel, guests=guests, options=...]
    ppermute x12, starting transfers between devices: 22 us -> 24.8 us  [among(): lax.ppermute(value, 'row', [(2 * s + b, 2 * t + b) for s, t in moves for...]
    ppermute x0 -> x2, starting transfers between devices: none -> 2.75 us  [give_back(): return lax.ppermute(value, ('row', 'col'), perm)]
    unnamed x42 -> x48, local copies, waits for them, and re-layouts: 13.5 us -> 12.1 us
  transfers between devices with their start and end apart: 22 -> 24, of which waited for: 9 -> 9; matrix products, arithmetic and copies ran while one was open for 2% -> 1% of each run, Pallas kernels for 25% -> 24%
where the time goes in v5:
time: 275 us; the launch traced here: 272 us
  waiting for transfers between devices  123 us (45%)
  Pallas kernels  82.9 us (30%)
  starting transfers between devices  49.2 us (18%)
  local copies, waits for them, and re-layouts  14.7 us (5%)
    ppermute x12, waiting for transfers between devices, among(): lax.ppermute(value, 'row', [(2 * s + b, 2 * t + b) for s, t in moves for...  73.9 us
    ppermute x4, waiting for transfers between devices, across(): return lax.ppermute(value, 'row', [(i, i ^ 1) for i in range(8)])  49.6 us
    pallas_call x4, Pallas kernels, triangle(): pl.pallas_call(functools.partial(triangle_kernel, guests=guests, options=...  28.7 us
    pallas_call x2, Pallas kernels, finish(): pl.pallas_call(finish_kernel, out_shape=jax.ShapeDtypeStruct(shape, BF16)...  26.2 us
    ppermute x12, starting transfers between devices, among(): lax.ppermute(value, 'row', [(2 * s + b, 2 * t + b) for s, t in moves for...  24.8 us
    ppermute x6, starting transfers between devices, to_core(): return lax.ppermute(value, ('row', 'col'), perm)  17 us
    unnamed x48, local copies, waits for them, and re-layouts  12.1 us
    pallas_call x2, Pallas kernels, project(): pl.pallas_call(project_kernel, out_shape=(piece, piece), in_specs=[pl.Blo...  11.1 us
  transfers between devices with their start and end apart: 24, of which 9 were waited for; matrix products, arithmetic and copies ran while one was open for 1% of the time, Pallas kernels for 24%

profile of v5, /device:TPU:1, one launch (start us, length us, event | category | flops | bytes accessed | tf_op | source)
XLA Modules:
  0.0 272.0 jit_solution(15713518790157669428)
XLA Ops:
  0.0 1.0 fusion.2
  1.0 0.8 fusion.1
  1.9 0.1 copy.33
  2.3 0.1 copy.31
  2.4 0.1 copy.34
  2.5 0.6 slice.60
  3.9 1.6 copy-done.2
  5.5 5.4 %project.3 = (bf16[23,64,384]{2,1,0:T(8,128)(2,1)}, bf16[23,64,384]{2,1,0:T(8,128)(2,1)S(1)}) custom-call(s32[3]{0:T(128)S(1)} %pad_add_fusion.1.where_ref, bf16[2,23,184,128]{3,2,1,0:T(8,128)(2,1)S(1)} %bitcast.19, bf16[256,128]{1,0:T(8,128)(2,1)S(1)} %maximum_bitcast_fusion.1.weight_ref), custom_call_target="tpu_custom_call" | custom-call | flops 554696704 | bytes 4333568 | tf_op jit(solution)/shard_map/project/pallas_call | solution.py:73
  10.9 2.0 collective-permute-start
  12.9 1.3 collective-permute-start.9
  14.2 0.7 collective-permute-start.7
  15.0 22.7 %collective-permute-done.refs_2_ = bf16[23,64,384]{2,1,0:T(8,128)(2,1)} collective-permute-done((bf16[23,64,384]{2,1,0:T(8,128)(2,1)S(1)}, bf16[23,64,384]{2,1,0:T(8,128)(2,1)}, u32[]{:S(2)}, u32[]{:S(2)}) %collective-permute-start) | collective-permute-done | bytes 1130528 | tf_op jit(solution)/shard_map/ppermute | solution.py:422
  37.7 1.7 collective-permute-start.8
  39.8 0.1 copy.25
  39.9 0.1 copy.28
  40.1 5.7 %project.2 = (bf16[23,64,384]{2,1,0:T(8,128)(2,1)}, bf16[23,64,384]{2,1,0:T(8,128)(2,1)}) custom-call(s32[3]{0:T(128)S(1)} %pad_add_fusion.1.where_ref, bf16[2,23,184,128]{3,2,1,0:T(8,128)(2,1)S(1)} %bitcast.20, bf16[256,128]{1,0:T(8,128)(2,1)S(1)} %maximum_bitcast_fusion.weight_ref), custom_call_target="tpu_custom_call" | custom-call | flops 554696704 | bytes 4333568 | tf_op jit(solution)/shard_map/project/pallas_call | solution.py:73
  45.8 1.1 collective-permute-start.1
  47.0 1.3 collective-permute-start.10
  48.3 1.3 collective-permute-start.11
  49.7 21.6 %collective-permute-done.1.beside_ref = bf16[23,64,384]{2,1,0:T(8,128)(2,1)} collective-permute-done((bf16[23,64,384]{2,1,0:T(8,128)(2,1)}, bf16[23,64,384]{2,1,0:T(8,128)(2,1)}, u32[]{:S(2)}, u32[]{:S(2)}) %collective-permute-start.1) | collective-permute-done | bytes 1130528 | tf_op jit(solution)/shard_map/ppermute | solution.py:422
  71.3 3.3 %left_major.2.refs_0_ = bf16[64,96,256]{2,1,0:T(8,128)(2,1)S(1)} custom-call(bf16[23,64,384]{2,1,0:T(8,128)(2,1)} %get-tuple-element.31.own_ref, bf16[23,64,384]{2,1,0:T(8,128)(2,1)} %collective-permute-done.1.beside_ref), custom_call_target="tpu_custom_call" | custom-call | bytes 4521984 | tf_op jit(solution)/shard_map/left_major/pallas_call | solution.py:116
  74.6 1.6 copy-done
  76.3 6.1 %triangle.5.refs_0_ = bf16[64,96,128]{2,1,0:T(8,128)(2,1)S(1)} custom-call(s32[2]{0:T(128)S(1)} %pad_add_fusion.flag_ref, bf16[64,96,256]{2,1,0:T(8,128)(2,1)} %copy-done, bf16[23,64,384]{2,1,0:T(8,128)(2,1)} %get-tuple-element.30.refs_1_, bf16[23,64,384]{2,1,0:T(8,128)(2,1)} %collective-permute-done.refs_2_), custom_call_target="tpu_custom_call" | custom-call | flops 402653184 | bytes 5652480 | tf_op jit(solution)/shard_map/triangle/pallas_call | solution.py:180
  82.4 4.2 %collective-permute-start.6 = (bf16[64,96,128]{2,1,0:T(8,128)(2,1)S(1)}, bf16[64,96,128]{2,1,0:T(8,128)(2,1)S(1)}, u32[]{:S(2)}, u32[]{:S(2)}) collective-permute-start(bf16[64,96,128]{2,1,0:T(8,128)(2,1)S(1)} %triangle.5.refs_0_), channel_id=1, source_target_pairs={{1,0},{3,2},{5,4},{7,6},{8,9},{10,11},{12,13},{14,15},{17,16},{19,... | collective-permute-start | bytes 4718600 | tf_op jit(solution)/shard_map/ppermute | solution.py:429
  86.6 11.9 %collective-permute-done.11.refs_4_ = bf16[23,64,384]{2,1,0:T(8,128)(2,1)} collective-permute-done((bf16[23,64,384]{2,1,0:T(8,128)(2,1)}, bf16[23,64,384]{2,1,0:T(8,128)(2,1)}, u32[]{:S(2)}, u32[]{:S(2)}) %collective-permute-start.11) | collective-permute-done | bytes 1130528 | tf_op jit(solution)/shard_map/ppermute | solution.py:419
  98.5 6.4 %triangle.6.refs_2_ = bf16[64,96,128]{2,1,0:T(8,128)(2,1)S(1)} custom-call(s32[2]{0:T(128)S(1)} %pad_add_fusion.2.flag_ref, bf16[64,96,256]{2,1,0:T(8,128)(2,1)} %copy-done, bf16[23,64,384]{2,1,0:T(8,128)(2,1)S(1)} %collective-permute-done.7.refs_1_, bf16[23,64,384]{2,1,0:T(8,128)(2,1)} %collective-permute-done.8.refs_2_, ...), custom_call_target="tpu_custom_call" | custom-call | flops 402653184 | bytes 5652480 | tf_op jit(solution)/shard_map/triangle/pallas_call | solution.py:180
  104.9 1.3 collective-permute-start.12
  106.2 1.2 copy-done.4
  107.4 2.3 collective-permute-start.2
  109.7 1.3 collective-permute-start.3
  111.1 19.5 %collective-permute-done.2.refs_1_ = bf16[23,64,384]{2,1,0:T(8,128)(2,1)} collective-permute-done((bf16[23,64,384]{2,1,0:T(8,128)(2,1)}, bf16[23,64,384]{2,1,0:T(8,128)(2,1)}, u32[]{:S(2)}, u32[]{:S(2)}) %collective-permute-start.2) | collective-permute-done | bytes 1130528 | tf_op jit(solution)/shard_map/ppermute | solution.py:419
  130.6 5.1 %collective-permute-start.5 = (bf16[23,64,384]{2,1,0:T(8,128)(2,1)}, bf16[23,64,384]{2,1,0:T(8,128)(2,1)}, u32[]{:S(2)}, u32[]{:S(2)}) collective-permute-start(bf16[23,64,384]{2,1,0:T(8,128)(2,1)} %get-tuple-element.31.own_ref), channel_id=1, source_target_pairs={{0,4},{2,6},{12,8},{14,10},{1,5},{3,7},{13,9},{15,11},{16,20},{18,... | collective-permute-start | bytes 3391496 | tf_op jit(solution)/shard_map/ppermute | solution.py:419
  135.7 1.7 collective-permute-start.14
  137.3 17.4 %collective-permute-done.3.refs_2_ = bf16[23,64,384]{2,1,0:T(8,128)(2,1)S(1)} collective-permute-done((bf16[23,64,384]{2,1,0:T(8,128)(2,1)}, bf16[23,64,384]{2,1,0:T(8,128)(2,1)S(1)}, u32[]{:S(2)}, u32[]{:S(2)}) %collective-permute-start.3) | collective-permute-done | bytes 1130528 | tf_op jit(solution)/shard_map/ppermute | solution.py:419
  154.8 5.1 %collective-permute-start.13 = (bf16[23,64,384]{2,1,0:T(8,128)(2,1)}, bf16[23,64,384]{2,1,0:T(8,128)(2,1)}, u32[]{:S(2)}, u32[]{:S(2)}) collective-permute-start(bf16[23,64,384]{2,1,0:T(8,128)(2,1)} %collective-permute-done.1.beside_ref), channel_id=1, source_target_pairs={{0,4},{2,6},{12,8},{14,10},{1,5},{3,7},{13,9},{15,11},{16,20},{18,... | collective-permute-start | bytes 3391496 | tf_op jit(solution)/shard_map/ppermute | solution.py:419
  159.9 1.2 copy-done.8
  161.1 1.3 collective-permute-start.16
  162.4 1.2 copy-done.13
  163.6 1.7 collective-permute-start.15
  165.3 7.1 %triangle.4.refs_0_ = bf16[64,96,128]{2,1,0:T(8,128)(2,1)} custom-call(s32[2]{0:T(128)S(1)} %pad_add_fusion.flag_ref, bf16[64,96,256]{2,1,0:T(8,128)(2,1)} %copy-done, bf16[23,64,384]{2,1,0:T(8,128)(2,1)} %collective-permute-done.2.refs_1_, bf16[23,64,384]{2,1,0:T(8,128)(2,1)S(1)} %collective-permute-done.3.refs_2_), custom_call_target="tpu_custom_call" | custom-call | flops 402653184 | bytes 5652480 | tf_op jit(solution)/shard_map/triangle/pallas_call | solution.py:180
  172.4 3.9 %fold.3 = (bf16[23,96,128]{2,1,0:T(8,128)(2,1)S(1)}, bf16[23,96,128]{2,1,0:T(8,128)(2,1)}) custom-call(s32[1]{0:T(128)} %bitcast.9.role_ref, bf16[64,96,128]{2,1,0:T(8,128)(2,1)S(1)} %copy-done.7, bf16[64,96,128]{2,1,0:T(8,128)(2,1)S(1)} %copy-done.9, bf16[64,96,128]{2,1,0:T(8,128)(2,1)S(1)} %copy-done.5, bf16[64,96,128]{2,1,0:T(8,128)(2,1)} %copy-done.13), custom_call_target="tpu_custom_call" | custom-call | bytes 4718592 | tf_op jit(solution)/shard_map/fold/pallas_call | solution.py:233
  176.3 2.7 collective-permute-done.5.own_ref
  179.0 1.9 collective-permute-start.4
  180.9 22.4 %collective-permute-done.13.beside_ref = bf16[23,64,384]{2,1,0:T(8,128)(2,1)} collective-permute-done((bf16[23,64,384]{2,1,0:T(8,128)(2,1)}, bf16[23,64,384]{2,1,0:T(8,128)(2,1)}, u32[]{:S(2)}, u32[]{:S(2)}) %collective-permute-start.13) | collective-permute-done | bytes 1130528 | tf_op jit(solution)/shard_map/ppermute | solution.py:419
  203.2 3.3 %left_major.3.refs_1_ = bf16[64,96,256]{2,1,0:T(8,128)(2,1)S(1)} custom-call(bf16[23,64,384]{2,1,0:T(8,128)(2,1)} %collective-permute-done.5.own_ref, bf16[23,64,384]{2,1,0:T(8,128)(2,1)} %collective-permute-done.13.beside_ref), custom_call_target="tpu_custom_call" | custom-call | bytes 4521984 | tf_op jit(solution)/shard_map/left_major/pallas_call | solution.py:116
  206.6 1.7 copy-done.1
  208.2 9.1 %triangle.7 = (bf16[64,96,128]{2,1,0:T(8,128)(2,1)}, bf16[64,48,128]{2,1,0:T(8,128)(2,1)S(1)}, bf16[64,48,128]{2,1,0:T(8,128)(2,1)}) custom-call(s32[2]{0:T(128)S(1)} %pad_add_fusion.2.flag_ref, bf16[64,96,256]{2,1,0:T(8,128)(2,1)} %copy-done, bf16[64,96,256]{2,1,0:T(8,128)(2,1)} %copy-done.1, bf16[23,64,384]{2,1,0:T(8,128)(2,1)} %collective-permute-done.14.refs_2_, ...), custom_call_target="tpu_custom_call" | custom-call | flops 805306368 | bytes 5652480 | tf_op jit(solution)/shard_map/triangle/pallas_call | solution.py:180
  217.3 6.7 %collective-permute-start.17 = (bf16[64,96,128]{2,1,0:T(8,128)(2,1)}, bf16[64,96,128]{2,1,0:T(8,128)(2,1)}, u32[]{:S(2)}, u32[]{:S(2)}) collective-permute-start(bf16[64,96,128]{2,1,0:T(8,128)(2,1)} %get-tuple-element.41.refs_2_), channel_id=1, source_target_pairs={{1,0},{3,2},{4,5},{6,7},{9,8},{11,10},{12,13},{14,15},{17,16},{19,... | collective-permute-start | bytes 4718600 | tf_op jit(solution)/shard_map/ppermute | solution.py:429
  224.0 1.5 collective-permute-start.18
  225.5 1.5 collective-permute-start.19
  227.0 0.2 collective-permute-start.23
  227.3 0.1 copy.22
  227.4 0.1 copy.37
  227.5 1.1 copy.23
  228.7 1.0 copy.24
  229.7 2.9 %fold.5 = bf16[23,96,128]{2,1,0:T(8,128)(2,1)S(1)} custom-call(s32[1]{0:T(128)} %bitcast.9.role_ref, bf16[64,48,128]{2,1,0:T(8,128)(2,1)} %get-tuple-element.43.refs_0_, bf16[64,48,128]{2,1,0:T(8,128)(2,1)} %collective-permute-done.18.refs_1_, bf16[64,48,128]{2,1,0:T(8,128)(2,1)S(1)} %get-tuple-element.44.refs_2_, ...), custom_call_target="tpu_custom_call" | custom-call | bytes 2359296 | tf_op jit(solution)/shard_map/fold/pallas_call | solution.py:233
  232.6 1.3 collective-permute-start.20
  234.0 1.5 collective-permute-start.22
  235.5 3.5 %fold.4 = (bf16[23,96,128]{2,1,0:T(8,128)(2,1)S(1)}, bf16[23,96,128]{2,1,0:T(8,128)(2,1)S(1)}) custom-call(s32[1]{0:T(128)} %bitcast.2.role_ref, bf16[64,96,128]{2,1,0:T(8,128)(2,1)} %triangle.4.refs_0_, bf16[64,96,128]{2,1,0:T(8,128)(2,1)} %collective-permute-done.4.refs_1_, bf16[64,96,128]{2,1,0:T(8,128)(2,1)S(1)} %copy-done.10, ...), custom_call_target="tpu_custom_call" | custom-call | bytes 4718592 | tf_op jit(solution)/shard_map/fold/pallas_call | solution.py:233
  239.0 1.3 collective-permute-start.21
  240.3 1.4 collective-permute-done.23.other_ref
  241.8 12.9 %finish.2.refs_4_ = bf16[2,23,96,128]{3,2,1,0:T(8,128)(2,1)S(1)} custom-call(s32[1]{0:T(128)} %bitcast.14.flag_ref, bf16[2,23,184,128]{3,2,1,0:T(8,128)(2,1)S(1)} %bitcast.21, bf16[23,96,128]{2,1,0:T(8,128)(2,1)S(1)} %copy-done.12, bf16[23,96,128]{2,1,0:T(8,128)(2,1)} %collective-permute-done.23.other_ref, bf16[128,128]{1,0:T(8,128)(2,1)S(1)} %bitcast.27, ...), custom_call_target="tpu_custom_call" | custom-call | flops 1941438464 | bytes 4333568 | tf_op jit(solution)/shard_map/finish/pallas_call | solution.py:300
  254.8 3.9 %collective-permute-done.21 = bf16[23,96,128]{2,1,0:T(8,128)(2,1)S(1)} collective-permute-done((bf16[23,96,128]{2,1,0:T(8,128)(2,1)S(1)}, bf16[23,96,128]{2,1,0:T(8,128)(2,1)S(1)}, u32[]{:S(2)}, u32[]{:S(2)}) %collective-permute-start.21) | collective-permute-done | bytes 565280 | tf_op jit(solution)/shard_map/ppermute | solution.py:422
  258.7 13.3 %finish.3 = bf16[2,23,184,128]{3,2,1,0:T(8,128)(2,1)} custom-call(s32[1]{0:T(128)} %bitcast.flag_ref, bf16[2,23,184,128]{3,2,1,0:T(8,128)(2,1)S(1)} %bitcast.22, bf16[23,96,128]{2,1,0:T(8,128)(2,1)S(1)} %broadcast_select_fusion.1.own_ref, bf16[23,96,128]{2,1,0:T(8,128)(2,1)S(1)} %broadcast_select_fusion.other_ref, bf16[128,128]{1,0:T(8,128)(2,1)S(1)} %bitcast.28, ...), custom_call_target="tpu_custom_call" | custom-call | flops 1941438464 | bytes 4333568 | tf_op jit(solution)/shard_map/finish/pallas_call | solution.py:300
  (59 shorter events, 1.3 us)
Async XLA Ops:
  0.0 2.5 copy-start.15
  3.9 1.6 copy-start.2
  5.5 34.5 %copy-start.3 = (bf16[46,184,128]{2,1,0:T(8,128)(2,1)S(1)}, bf16[46,184,128]{2,1,0:T(8,128)(2,1)}, u32[]{:S(2)}) copy-start(bf16[46,184,128]{2,1,0:T(8,128)(2,1)} %param.6) | copy-start | bytes 6500356
  10.9 26.8 %collective-permute-start = (bf16[23,64,384]{2,1,0:T(8,128)(2,1)S(1)}, bf16[23,64,384]{2,1,0:T(8,128)(2,1)}, u32[]{:S(2)}, u32[]{:S(2)}) collective-permute-start(bf16[23,64,384]{2,1,0:T(8,128)(2,1)S(1)} %get-tuple-element.28), channel_id=1, source_target_pairs={{0,2},{2,0},{4,6},{6,4},{8,10},{10,8},{12,14},{14,12},{1,3},{3,1},... | collective-permute-start | bytes 3391496 | tf_op jit(solution)/shard_map/ppermute | solution.py:422
  12.9 34.0 %collective-permute-start.9 = (bf16[23,64,384]{2,1,0:T(8,128)(2,1)}, bf16[23,64,384]{2,1,0:T(8,128)(2,1)}, u32[]{:S(2)}, u32[]{:S(2)}) collective-permute-start(bf16[23,64,384]{2,1,0:T(8,128)(2,1)} %get-tuple-element.30.refs_1_), channel_id=1, source_target_pairs={{4,0},{6,2},{8,12},{10,14},{5,1},{7,3},{9,13},{11,15},{20,16},{22,... | collective-permute-start | bytes 3391496 | tf_op jit(solution)/shard_map/ppermute | solution.py:419
  14.2 32.7 %collective-permute-start.7 = (bf16[23,64,384]{2,1,0:T(8,128)(2,1)}, bf16[23,64,384]{2,1,0:T(8,128)(2,1)S(1)}, u32[]{:S(2)}, u32[]{:S(2)}) collective-permute-start(bf16[23,64,384]{2,1,0:T(8,128)(2,1)} %get-tuple-element.30.refs_1_), channel_id=1, source_target_pairs={{4,8},{6,10},{8,4},{10,6},{5,9},{7,11},{9,5},{11,7},{20,24},{22,26... | collective-permute-start | bytes 3391496 | tf_op jit(solution)/shard_map/ppermute | solution.py:419
  37.7 10.6 %collective-permute-start.8 = (bf16[23,64,384]{2,1,0:T(8,128)(2,1)}, bf16[23,64,384]{2,1,0:T(8,128)(2,1)}, u32[]{:S(2)}, u32[]{:S(2)}) collective-permute-start(bf16[23,64,384]{2,1,0:T(8,128)(2,1)} %collective-permute-done.refs_2_), channel_id=1, source_target_pairs={{4,8},{6,10},{8,4},{10,6},{5,9},{7,11},{9,5},{11,7},{20,24},{22,26... | collective-permute-start | bytes 3391496 | tf_op jit(solution)/shard_map/ppermute | solution.py:419
  45.8 25.5 %collective-permute-start.1 = (bf16[23,64,384]{2,1,0:T(8,128)(2,1)}, bf16[23,64,384]{2,1,0:T(8,128)(2,1)}, u32[]{:S(2)}, u32[]{:S(2)}) collective-permute-start(bf16[23,64,384]{2,1,0:T(8,128)(2,1)} %get-tuple-element.29), channel_id=1, source_target_pairs={{0,2},{2,0},{4,6},{6,4},{8,10},{10,8},{12,14},{14,12},{1,3},{3,1},... | collective-permute-start | bytes 3391496 | tf_op jit(solution)/shard_map/ppermute | solution.py:422
  47.0 39.6 %collective-permute-start.10 = (bf16[23,64,384]{2,1,0:T(8,128)(2,1)S(1)}, bf16[23,64,384]{2,1,0:T(8,128)(2,1)}, u32[]{:S(2)}, u32[]{:S(2)}) collective-permute-start(bf16[23,64,384]{2,1,0:T(8,128)(2,1)S(1)} %collective-permute-done.7.refs_1_), channel_id=1, source_target_pairs={{4,0},{6,2},{8,12},{10,14},{5,1},{7,3},{9,13},{11,15},{20,16},{22,... | collective-permute-start | bytes 3391496 | tf_op jit(solution)/shard_map/ppermute | solution.py:419
  48.3 50.2 %collective-permute-start.11 = (bf16[23,64,384]{2,1,0:T(8,128)(2,1)}, bf16[23,64,384]{2,1,0:T(8,128)(2,1)}, u32[]{:S(2)}, u32[]{:S(2)}) collective-permute-start(bf16[23,64,384]{2,1,0:T(8,128)(2,1)} %collective-permute-done.8.refs_2_), channel_id=1, source_target_pairs={{4,0},{6,2},{8,12},{10,14},{5,1},{7,3},{9,13},{11,15},{20,16},{22,... | collective-permute-start | bytes 3391496 | tf_op jit(solution)/shard_map/ppermute | solution.py:419
  74.6 1.6 copy-start
  82.4 22.5 %copy-start.6 = (bf16[64,96,128]{2,1,0:T(8,128)(2,1)}, bf16[64,96,128]{2,1,0:T(8,128)(2,1)S(1)}, u32[]{:S(2)}) copy-start(bf16[64,96,128]{2,1,0:T(8,128)(2,1)S(1)} %triangle.5.refs_0_) | copy-start | bytes 4718596
  82.4 77.5 %collective-permute-start.6 = (bf16[64,96,128]{2,1,0:T(8,128)(2,1)S(1)}, bf16[64,96,128]{2,1,0:T(8,128)(2,1)S(1)}, u32[]{:S(2)}, u32[]{:S(2)}) collective-permute-start(bf16[64,96,128]{2,1,0:T(8,128)(2,1)S(1)} %triangle.5.refs_0_), channel_id=1, source_target_pairs={{1,0},{3,2},{5,4},{7,6},{8,9},{10,11},{12,13},{14,15},{17,16},{19,... | collective-permute-start | bytes 4718600 | tf_op jit(solution)/shard_map/ppermute | solution.py:429
  104.9 57.4 %collective-permute-start.12 = (bf16[64,96,128]{2,1,0:T(8,128)(2,1)S(1)}, bf16[64,96,128]{2,1,0:T(8,128)(2,1)S(1)}, u32[]{:S(2)}, u32[]{:S(2)}) collective-permute-start(bf16[64,96,128]{2,1,0:T(8,128)(2,1)S(1)} %triangle.6.refs_2_), channel_id=1, source_target_pairs={{0,1},{2,3},{4,5},{6,7},{9,8},{11,10},{13,12},{15,14},{16,17},{18,... | collective-permute-start | bytes 4718600 | tf_op jit(solution)/shard_map/ppermute | solution.py:429
  106.2 1.2 copy-start.4
  107.4 23.2 %collective-permute-start.2 = (bf16[23,64,384]{2,1,0:T(8,128)(2,1)}, bf16[23,64,384]{2,1,0:T(8,128)(2,1)}, u32[]{:S(2)}, u32[]{:S(2)}) collective-permute-start(bf16[23,64,384]{2,1,0:T(8,128)(2,1)} %get-tuple-element.30.refs_1_), channel_id=1, source_target_pairs={{0,4},{2,6},{12,8},{14,10},{1,5},{3,7},{13,9},{15,11},{16,20},{18,... | collective-permute-start | bytes 3391496 | tf_op jit(solution)/shard_map/ppermute | solution.py:419
  109.7 45.1 %collective-permute-start.3 = (bf16[23,64,384]{2,1,0:T(8,128)(2,1)}, bf16[23,64,384]{2,1,0:T(8,128)(2,1)S(1)}, u32[]{:S(2)}, u32[]{:S(2)}) collective-permute-start(bf16[23,64,384]{2,1,0:T(8,128)(2,1)} %collective-permute-done.refs_2_), channel_id=1, source_target_pairs={{0,4},{2,6},{12,8},{14,10},{1,5},{3,7},{13,9},{15,11},{16,20},{18,... | collective-permute-start | bytes 3391496 | tf_op jit(solution)/shard_map/ppermute | solution.py:419
  130.6 48.5 %collective-permute-start.5 = (bf16[23,64,384]{2,1,0:T(8,128)(2,1)}, bf16[23,64,384]{2,1,0:T(8,128)(2,1)}, u32[]{:S(2)}, u32[]{:S(2)}) collective-permute-start(bf16[23,64,384]{2,1,0:T(8,128)(2,1)} %get-tuple-element.31.own_ref), channel_id=1, source_target_pairs={{0,4},{2,6},{12,8},{14,10},{1,5},{3,7},{13,9},{15,11},{16,20},{18,... | collective-permute-start | bytes 3391496 | tf_op jit(solution)/shard_map/ppermute | solution.py:419
  135.7 72.6 %collective-permute-start.14 = (bf16[23,64,384]{2,1,0:T(8,128)(2,1)}, bf16[23,64,384]{2,1,0:T(8,128)(2,1)}, u32[]{:S(2)}, u32[]{:S(2)}) collective-permute-start(bf16[23,64,384]{2,1,0:T(8,128)(2,1)} %collective-permute-done.2.refs_1_), channel_id=1, source_target_pairs={{4,8},{6,10},{8,4},{10,6},{5,9},{7,11},{9,5},{11,7},{20,24},{22,26... | collective-permute-start | bytes 3391496 | tf_op jit(solution)/shard_map/ppermute | solution.py:419
  154.8 48.5 %collective-permute-start.13 = (bf16[23,64,384]{2,1,0:T(8,128)(2,1)}, bf16[23,64,384]{2,1,0:T(8,128)(2,1)}, u32[]{:S(2)}, u32[]{:S(2)}) collective-permute-start(bf16[23,64,384]{2,1,0:T(8,128)(2,1)} %collective-permute-done.1.beside_ref), channel_id=1, source_target_pairs={{0,4},{2,6},{12,8},{14,10},{1,5},{3,7},{13,9},{15,11},{16,20},{18,... | collective-permute-start | bytes 3391496 | tf_op jit(solution)/shard_map/ppermute | solution.py:419
  159.9 1.2 copy-start.8
  161.1 47.2 %collective-permute-start.16 = (bf16[23,64,384]{2,1,0:T(8,128)(2,1)}, bf16[23,64,384]{2,1,0:T(8,128)(2,1)}, u32[]{:S(2)}, u32[]{:S(2)}) collective-permute-start(bf16[23,64,384]{2,1,0:T(8,128)(2,1)} %collective-permute-done.refs_2_), channel_id=1, source_target_pairs={{4,0},{6,2},{8,12},{10,14},{5,1},{7,3},{9,13},{11,15},{20,16},{22,... | collective-permute-start | bytes 3391496 | tf_op jit(solution)/shard_map/ppermute | solution.py:419
  162.4 1.2 copy-start.13
  163.6 44.6 %collective-permute-start.15 = (bf16[23,64,384]{2,1,0:T(8,128)(2,1)S(1)}, bf16[23,64,384]{2,1,0:T(8,128)(2,1)}, u32[]{:S(2)}, u32[]{:S(2)}) collective-permute-start(bf16[23,64,384]{2,1,0:T(8,128)(2,1)S(1)} %collective-permute-done.3.refs_2_), channel_id=1, source_target_pairs={{4,8},{6,10},{8,4},{10,6},{5,9},{7,11},{9,5},{11,7},{20,24},{22,26... | collective-permute-start | bytes 3391496 | tf_op jit(solution)/shard_map/ppermute | solution.py:419
  165.3 7.1 %copy-start.5 = (bf16[64,96,128]{2,1,0:T(8,128)(2,1)S(1)}, bf16[64,96,128]{2,1,0:T(8,128)(2,1)}, u32[]{:S(2)}) copy-start(bf16[64,96,128]{2,1,0:T(8,128)(2,1)} %copy-done.4) | copy-start | bytes 4718596
  165.3 7.1 %copy-start.7 = (bf16[64,96,128]{2,1,0:T(8,128)(2,1)S(1)}, bf16[64,96,128]{2,1,0:T(8,128)(2,1)}, u32[]{:S(2)}) copy-start(bf16[64,96,128]{2,1,0:T(8,128)(2,1)} %copy-done.6) | copy-start | bytes 4718596
  165.3 7.1 %copy-start.9 = (bf16[64,96,128]{2,1,0:T(8,128)(2,1)S(1)}, bf16[64,96,128]{2,1,0:T(8,128)(2,1)}, u32[]{:S(2)}) copy-start(bf16[64,96,128]{2,1,0:T(8,128)(2,1)} %copy-done.8) | copy-start | bytes 4718596
  176.3 30.2 %copy-start.11 = (bf16[23,96,128]{2,1,0:T(8,128)(2,1)}, bf16[23,96,128]{2,1,0:T(8,128)(2,1)S(1)}, u32[]{:S(2)}) copy-start(bf16[23,96,128]{2,1,0:T(8,128)(2,1)S(1)} %get-tuple-element.46.own_ref) | copy-start | bytes 1695748
  179.0 56.4 %collective-permute-start.4 = (bf16[64,96,128]{2,1,0:T(8,128)(2,1)}, bf16[64,96,128]{2,1,0:T(8,128)(2,1)}, u32[]{:S(2)}, u32[]{:S(2)}) collective-permute-start(bf16[64,96,128]{2,1,0:T(8,128)(2,1)} %triangle.4.refs_0_), channel_id=1, source_target_pairs={{5,4},{7,6},{8,9},{10,11},{21,20},{23,22},{24,25},{26,27}} | collective-permute-start | bytes 4718600 | tf_op jit(solution)/shard_map/ppermute | solution.py:429
  206.5 1.7 copy-start.1
  208.2 19.1 %copy-start.14 = (bf16[128,128]{1,0:T(8,128)(2,1)S(1)}, bf16[128,128]{1,0:T(8,128)(2,1)}, u32[]{:S(2)}) copy-start(bf16[128,128]{1,0:T(8,128)(2,1)} %param.9) | copy-start | bytes 98308
  217.3 18.1 %collective-permute-start.17 = (bf16[64,96,128]{2,1,0:T(8,128)(2,1)}, bf16[64,96,128]{2,1,0:T(8,128)(2,1)}, u32[]{:S(2)}, u32[]{:S(2)}) collective-permute-start(bf16[64,96,128]{2,1,0:T(8,128)(2,1)} %get-tuple-element.41.refs_2_), channel_id=1, source_target_pairs={{1,0},{3,2},{4,5},{6,7},{9,8},{11,10},{12,13},{14,15},{17,16},{19,... | collective-permute-start | bytes 4718600 | tf_op jit(solution)/shard_map/ppermute | solution.py:429
  224.0 5.7 %collective-permute-start.18 = (bf16[64,48,128]{2,1,0:T(8,128)(2,1)}, bf16[64,48,128]{2,1,0:T(8,128)(2,1)}, u32[]{:S(2)}, u32[]{:S(2)}) collective-permute-start(bf16[64,48,128]{2,1,0:T(8,128)(2,1)} %get-tuple-element.43.refs_0_), channel_id=1, source_target_pairs={{5,4},{7,6},{8,9},{10,11},{21,20},{23,22},{24,25},{26,27}} | collective-permute-start | bytes 2359304 | tf_op jit(solution)/shard_map/ppermute | solution.py:429
  225.5 4.2 %collective-permute-start.19 = (bf16[64,48,128]{2,1,0:T(8,128)(2,1)S(1)}, bf16[64,48,128]{2,1,0:T(8,128)(2,1)}, u32[]{:S(2)}, u32[]{:S(2)}) collective-permute-start(bf16[64,48,128]{2,1,0:T(8,128)(2,1)S(1)} %get-tuple-element.44.refs_2_), channel_id=1, source_target_pairs={{4,5},{6,7},{9,8},{11,10},{20,21},{22,23},{25,24},{27,26}} | collective-permute-start | bytes 2359304 | tf_op jit(solution)/shard_map/ppermute | solution.py:429
  227.0 14.7 %collective-permute-start.23 = (bf16[23,96,128]{2,1,0:T(8,128)(2,1)}, bf16[23,96,128]{2,1,0:T(8,128)(2,1)}, u32[]{:S(2)}, u32[]{:S(2)}) collective-permute-start(bf16[23,96,128]{2,1,0:T(8,128)(2,1)} %get-tuple-element.35), channel_id=1, source_target_pairs={{0,2},{2,0},{4,6},{6,4},{8,10},{10,8},{12,14},{14,12},{1,3},{3,1},... | collective-permute-start | bytes 1695752 | tf_op jit(solution)/shard_map/ppermute | solution.py:422
  229.7 5.8 %copy-start.10 = (bf16[64,96,128]{2,1,0:T(8,128)(2,1)S(1)}, bf16[64,96,128]{2,1,0:T(8,128)(2,1)}, u32[]{:S(2)}) copy-start(bf16[64,96,128]{2,1,0:T(8,128)(2,1)} %get-tuple-element.41.refs_2_) | copy-start | bytes 4718596
  232.6 22.1 %collective-permute-start.20 = (bf16[23,96,128]{2,1,0:T(8,128)(2,1)S(1)}, bf16[23,96,128]{2,1,0:T(8,128)(2,1)S(1)}, u32[]{:S(2)}, u32[]{:S(2)}) collective-permute-start(bf16[23,96,128]{2,1,0:T(8,128)(2,1)S(1)} %fold.5), channel_id=1, source_target_pairs={{5,1},{7,3},{8,12},{10,14},{21,17},{23,19},{24,28},{26,30}} | collective-permute-start | bytes 1695752 | tf_op jit(solution)/shard_map/ppermute | solution.py:437
  234.0 20.8 %collective-permute-start.22 = (bf16[23,96,128]{2,1,0:T(8,128)(2,1)S(1)}, bf16[23,96,128]{2,1,0:T(8,128)(2,1)S(1)}, u32[]{:S(2)}, u32[]{:S(2)}) collective-permute-start(bf16[23,96,128]{2,1,0:T(8,128)(2,1)S(1)} %fold.5), channel_id=1, source_target_pairs={{4,3},{6,1},{9,14},{11,12},{20,19},{22,17},{25,30},{27,28}} | collective-permute-start | bytes 1695752 | tf_op jit(solution)/shard_map/ppermute | solution.py:437
  235.5 6.3 %copy-start.12 = (bf16[23,96,128]{2,1,0:T(8,128)(2,1)S(1)}, bf16[23,96,128]{2,1,0:T(8,128)(2,1)}, u32[]{:S(2)}) copy-start(bf16[23,96,128]{2,1,0:T(8,128)(2,1)} %copy-done.11) | copy-start | bytes 1695748
  239.0 19.7 %collective-permute-start.21 = (bf16[23,96,128]{2,1,0:T(8,128)(2,1)S(1)}, bf16[23,96,128]{2,1,0:T(8,128)(2,1)S(1)}, u32[]{:S(2)}, u32[]{:S(2)}) collective-permute-start(bf16[23,96,128]{2,1,0:T(8,128)(2,1)S(1)} %get-tuple-element.45), channel_id=1, source_target_pairs={{0,2},{2,0},{4,6},{6,4},{8,10},{10,8},{12,14},{14,12},{1,3},{3,1},... | collective-permute-start | bytes 1695752 | tf_op jit(solution)/shard_map/ppermute | solution.py:422

commit v6 on v5

--- a/solution.py
+++ b/solution.py
@@ -458,33 +458,46 @@
     cross, inward, outward = [(1, 2), (2, 1)], [(0, 1), (3, 2)], [(1, 0), (2, 3)]
     everyone, inners = range(4), (1, 2)
 
+    def phase(moves, finished):
+        values = lax.optimization_barrier(tuple(v for _, v in moves) + tuple(finished))
+        return [send(v) for (send, _), v in zip(moves, values)]
+
+    def hop(moves):
+        return lambda value: among(value, moves)
+
     right_own, right_far = project(where, folded, gate_pair(2))
-    from_end, near, from_inner = ([among(right_own, m)] for m in (inward, cross, outward))
-    right_beside = across(right_far)
+    one = phase(
+        [(hop(inward), right_own), (hop(cross), right_own), (hop(outward), right_own), (across, right_far)],
+        (),
+    )
+    end_own, near_own, inner_own, right_beside = one
     left_own, left_far = project(where, folded, gate_pair(0))
-    left_beside = across(after(left_far, right_beside))
-    from_end.append(among(right_beside, inward))
-    near.append(among(right_beside, cross))
-    relay = [among(after(near[0], from_inner[0]), outward)]
-    far = [among(after(from_end[0], near[0]), cross)]
-    relay.append(among(after(near[1], from_inner[0]), outward))
-    guest = [among(after(left_own, from_end[0]), inward)]
-    far.append(among(after(from_end[1], near[1]), cross))
-    from_inner.append(among(after(right_beside, relay[0]), outward))
-    guest.append(among(after(left_beside, from_end[1]), inward))
+    two = phase(
+        [(hop(inward), right_beside), (hop(cross), right_beside), (hop(outward), near_own), (across, left_far)],
+        one,
+    )
+    end_beside, near_beside, relay_own, left_beside = two
+    three = phase([(hop(cross), end_own), (hop(inward), left_own), (hop(outward), near_beside)], two)
+    far_own, guest_own, relay_beside = three
+    four = phase(
+        [(hop(cross), end_beside), (hop(inward), left_beside), (hop(outward), right_beside)], three
+    )
+    far_beside, guest_beside, inner_beside = four
 
     left = left_major(left_own, left_beside)
     (home,) = triangle(scalars(side, 0), [left], right_own, right_beside)
     home_rest = to_core(home, everyone, [True] * 4)
-    (mate,) = triangle(scalars(side, 0), [left], *from_end)
+    (mate,) = triangle(scalars(side, 0), [left], end_own, end_beside)
     mate_rest = to_core(mate, inners, [True] * 2)
-    (away,) = triangle(scalars(side, jnp.where(inner, 0, 1)), [left], *near, *relay)
+    outer = scalars(side, jnp.where(inner, 0, 1))
+    (away,) = triangle(outer, [left], near_own, near_beside, relay_own, relay_beside)
     away_rest = to_core(away, everyone, [False] * 4)
     first = fold(half, scalars(jnp.where(is_keeper, 0, 1)), home, home_rest, away, away_rest)
 
-    left_guest = left_major(after(guest[0], *first), guest[1])
+    first_other = across(first[1])
+    left_guest = left_major(after(guest_own, first_other, mate_rest), guest_beside)
     late, lent_own, lent_beside = triangle(
-        scalars(side, jnp.where(inner, 0, 1)), [left, left_guest], *far, *from_inner
+        outer, [left, left_guest], far_own, far_beside, inner_own, inner_beside
     )
     lent_rest = to_core(lent_own, inners, [False] * 2), to_core(lent_beside, inners, [True] * 2)
     late_rest = to_core(late, everyone, [True, False, False, True])
@@ -496,7 +509,7 @@
 
     order = jnp.where(is_keeper, place % 2, place // 2)
     weights = [w.T for w in (in_weight[:, 4 * width :], by_side(out_weight, 0), trans_in, trans_out)]
-    earlier = finish(scalars(order), folded, after(first[0], lent), across(first[1]), weights)
+    earlier = finish(scalars(order), folded, after(first[0], lent), first_other, weights)
     kept = is_keeper | inner
     own = jnp.where(kept, second[0], given[0])
     other = jnp.where(kept, across(second[1]), given[1])

time: 275 us -> 227 us (0.83)
  waiting for transfers between devices: 123 us -> 70 us
  starting transfers between devices: 49.2 us -> 56.3 us
    ppermute x12, waiting for transfers between devices: 73.9 us -> 23.4 us  [among(): lax.ppermute(value, 'row', [(2 * s + b, 2 * t + b) for s, t in moves for...]
    ppermute x12, starting transfers between devices: 24.8 us -> 30.4 us  [among(): lax.ppermute(value, 'row', [(2 * s + b, 2 * t + b) for s, t in moves for...]
    ppermute x4, waiting for transfers between devices: 49.6 us -> 46.6 us  [across(): return lax.ppermute(value, 'row', [(i, i ^ 1) for i in range(8)])]
    unnamed x48 -> x58, local copies, waits for them, and re-layouts: 12.1 us -> 14.8 us
  transfers between devices with their start and end apart: 24 -> 24, of which waited for: 9 -> 10; matrix products, arithmetic and copies ran while one was open for 1% -> 1% of each run, Pallas kernels for 24% -> 23%
where the time goes in v6:
time: 227 us; the launch traced here: 226 us
  Pallas kernels  80.7 us (36%)
  waiting for transfers between devices  70 us (31%)
  starting transfers between devices  56.3 us (25%)
  local copies, waits for them, and re-layouts  17.4 us (8%)
    ppermute x4, waiting for transfers between devices, across(): return lax.ppermute(value, 'row', [(i, i ^ 1) for i in range(8)])  46.6 us
    ppermute x12, starting transfers between devices, among(): lax.ppermute(value, 'row', [(2 * s + b, 2 * t + b) for s, t in moves for...  30.4 us
    pallas_call x4, Pallas kernels, triangle(): pl.pallas_call(functools.partial(triangle_kernel, guests=guests, options=...  30.2 us
    pallas_call x2, Pallas kernels, finish(): pl.pallas_call(finish_kernel, out_shape=jax.ShapeDtypeStruct(shape, BF16)...  25.3 us
    ppermute x12, waiting for transfers between devices, among(): lax.ppermute(value, 'row', [(2 * s + b, 2 * t + b) for s, t in moves for...  23.4 us
    ppermute x6, starting transfers between devices, to_core(): return lax.ppermute(value, ('row', 'col'), perm)  18.2 us
    unnamed x58, local copies, waits for them, and re-layouts  14.8 us
    pallas_call x3, Pallas kernels, fold(): pl.pallas_call(functools.partial(fold_kernel, outputs=outputs, half=half)...  10.2 us
  transfers between devices with their start and end apart: 24, of which 10 were waited for; matrix products, arithmetic and copies ran while one was open for 1% of the time, Pallas kernels for 23%

profile of v6, /device:TPU:1, one launch (start us, length us, event | category | flops | bytes accessed | tf_op | source)
XLA Modules:
  0.0 226.0 jit_solution(10540671503361692261)
XLA Ops:
  0.0 1.0 fusion.2
  1.0 0.8 fusion.1
  2.3 0.1 copy.31
  2.5 0.6 slice.60
  3.9 1.6 copy-done.2
  5.5 5.7 %project.3 = (bf16[23,64,384]{2,1,0:T(8,128)(2,1)}, bf16[23,64,384]{2,1,0:T(8,128)(2,1)}) custom-call(s32[3]{0:T(128)S(1)} %pad_add_fusion.1.where_ref, bf16[2,23,184,128]{3,2,1,0:T(8,128)(2,1)S(1)} %bitcast.19, bf16[256,128]{1,0:T(8,128)(2,1)S(1)} %maximum_bitcast_fusion.1.weight_ref), custom_call_target="tpu_custom_call" | custom-call | flops 554696704 | bytes 4333568 | tf_op jit(solution)/shard_map/project/pallas_call | solution.py:73
  11.2 2.0 collective-permute-start
  13.3 0.7 collective-permute-start.1
  14.0 6.7 %collective-permute-start.2 = (bf16[23,64,384]{2,1,0:T(8,128)(2,1)}, bf16[23,64,384]{2,1,0:T(8,128)(2,1)}, u32[]{:S(2)}, u32[]{:S(2)}) collective-permute-start(bf16[23,64,384]{2,1,0:T(8,128)(2,1)} %get-tuple-element.39.refs_1_), channel_id=1, source_target_pairs={{0,4},{2,6},{12,8},{14,10},{1,5},{3,7},{13,9},{15,11},{16,20},{18,... | collective-permute-start | bytes 3391496 | tf_op jit(solution)/shard_map/ppermute | solution.py:419
  20.7 1.3 collective-permute-start.3
  22.4 0.1 copy.25
  22.5 0.1 copy.28
  22.7 4.4 %project.2 = (bf16[23,64,384]{2,1,0:T(8,128)(2,1)S(1)}, bf16[23,64,384]{2,1,0:T(8,128)(2,1)S(1)}) custom-call(s32[3]{0:T(128)S(1)} %pad_add_fusion.1.where_ref, bf16[2,23,184,128]{3,2,1,0:T(8,128)(2,1)S(1)} %bitcast.20, bf16[256,128]{1,0:T(8,128)(2,1)S(1)} %maximum_bitcast_fusion.weight_ref), custom_call_target="tpu_custom_call" | custom-call | flops 554696704 | bytes 4333568 | tf_op jit(solution)/shard_map/project/pallas_call | solution.py:73
  27.1 11.2 %collective-permute-done.refs_2_ = bf16[23,64,384]{2,1,0:T(8,128)(2,1)} collective-permute-done((bf16[23,64,384]{2,1,0:T(8,128)(2,1)}, bf16[23,64,384]{2,1,0:T(8,128)(2,1)}, u32[]{:S(2)}, u32[]{:S(2)}) %collective-permute-start) | collective-permute-done | bytes 1130528 | tf_op jit(solution)/shard_map/ppermute | solution.py:422
  38.2 4.7 %collective-permute-done.2.refs_1_ = bf16[23,64,384]{2,1,0:T(8,128)(2,1)} collective-permute-done((bf16[23,64,384]{2,1,0:T(8,128)(2,1)}, bf16[23,64,384]{2,1,0:T(8,128)(2,1)}, u32[]{:S(2)}, u32[]{:S(2)}) %collective-permute-start.2) | collective-permute-done | bytes 1130528 | tf_op jit(solution)/shard_map/ppermute | solution.py:419
  42.9 4.8 %collective-permute-done.3.refs_4_ = bf16[23,64,384]{2,1,0:T(8,128)(2,1)} collective-permute-done((bf16[23,64,384]{2,1,0:T(8,128)(2,1)}, bf16[23,64,384]{2,1,0:T(8,128)(2,1)}, u32[]{:S(2)}, u32[]{:S(2)}) %collective-permute-start.3) | collective-permute-done | bytes 1130528 | tf_op jit(solution)/shard_map/ppermute | solution.py:419
  47.8 0.2 collective-permute-start.4
  48.0 2.3 %collective-permute-start.5 = (bf16[23,64,384]{2,1,0:T(8,128)(2,1)}, bf16[23,64,384]{2,1,0:T(8,128)(2,1)}, u32[]{:S(2)}, u32[]{:S(2)}) collective-permute-start(bf16[23,64,384]{2,1,0:T(8,128)(2,1)} %collective-permute-done.refs_2_), channel_id=1, source_target_pairs={{0,4},{2,6},{12,8},{14,10},{1,5},{3,7},{13,9},{15,11},{16,20},{18,... | collective-permute-start | bytes 3391496 | tf_op jit(solution)/shard_map/ppermute | solution.py:419
  50.3 1.7 collective-permute-start.7
  52.0 1.3 collective-permute-start.8
  53.3 18.5 %collective-permute-done.4.beside_ref = bf16[23,64,384]{2,1,0:T(8,128)(2,1)S(1)} collective-permute-done((bf16[23,64,384]{2,1,0:T(8,128)(2,1)S(1)}, bf16[23,64,384]{2,1,0:T(8,128)(2,1)S(1)}, u32[]{:S(2)}, u32[]{:S(2)}) %collective-permute-start.4) | collective-permute-done | bytes 1130528 | tf_op jit(solution)/shard_map/ppermute | solution.py:422
  71.8 5.6 %collective-permute-done.8.refs_3_ = bf16[23,64,384]{2,1,0:T(8,128)(2,1)S(1)} collective-permute-done((bf16[23,64,384]{2,1,0:T(8,128)(2,1)S(1)}, bf16[23,64,384]{2,1,0:T(8,128)(2,1)S(1)}, u32[]{:S(2)}, u32[]{:S(2)}) %collective-permute-start.8) | collective-permute-done | bytes 1130528 | tf_op jit(solution)/shard_map/ppermute | solution.py:419
  77.4 1.1 copy-done.5
  78.5 1.3 collective-permute-start.11
  79.9 1.8 left_major.2.refs_0_
  81.7 1.6 copy-done
  83.3 1.0 copy-done.7
  84.3 1.0 copy-done.9
  85.3 7.0 %triangle.5.refs_0_ = bf16[64,96,128]{2,1,0:T(8,128)(2,1)} custom-call(s32[2]{0:T(128)S(1)} %pad_add_fusion.flag_ref, bf16[64,96,256]{2,1,0:T(8,128)(2,1)} %copy-done, bf16[23,64,384]{2,1,0:T(8,128)(2,1)} %get-tuple-element.39.refs_1_, bf16[23,64,384]{2,1,0:T(8,128)(2,1)} %collective-permute-done.refs_2_), custom_call_target="tpu_custom_call" | custom-call | flops 402653184 | bytes 5652480 | tf_op jit(solution)/shard_map/triangle/pallas_call | solution.py:180
  92.3 6.9 %collective-permute-start.10 = (bf16[64,96,128]{2,1,0:T(8,128)(2,1)}, bf16[64,96,128]{2,1,0:T(8,128)(2,1)}, u32[]{:S(2)}, u32[]{:S(2)}) collective-permute-start(bf16[64,96,128]{2,1,0:T(8,128)(2,1)} %triangle.5.refs_0_), channel_id=1, source_target_pairs={{1,0},{3,2},{5,4},{7,6},{8,9},{10,11},{12,13},{14,15},{17,16},{19,... | collective-permute-start | bytes 4718600 | tf_op jit(solution)/shard_map/ppermute | solution.py:429
  99.2 0.7 collective-permute-start.14
  99.9 6.5 %collective-permute-start.9 = (bf16[23,64,384]{2,1,0:T(8,128)(2,1)}, bf16[23,64,384]{2,1,0:T(8,128)(2,1)S(1)}, u32[]{:S(2)}, u32[]{:S(2)}) collective-permute-start(bf16[23,64,384]{2,1,0:T(8,128)(2,1)} %copy-done.9), channel_id=1, source_target_pairs={{0,4},{2,6},{12,8},{14,10},{1,5},{3,7},{13,9},{15,11},{16,20},{18,... | collective-permute-start | bytes 3391496 | tf_op jit(solution)/shard_map/ppermute | solution.py:419
  106.5 1.3 copy-done.6
  107.8 7.2 %triangle.6.refs_2_ = bf16[64,96,128]{2,1,0:T(8,128)(2,1)} custom-call(s32[2]{0:T(128)S(1)} %pad_add_fusion.2.flag_ref, bf16[64,96,256]{2,1,0:T(8,128)(2,1)} %copy-done, bf16[23,64,384]{2,1,0:T(8,128)(2,1)S(1)} %collective-permute-done.1.refs_1_, bf16[23,64,384]{2,1,0:T(8,128)(2,1)} %collective-permute-done.7.refs_2_, bf16[23,64,384]{2,1,0:T(8,128)(2,1)S(1)} %copy-done.6, ...), custom_call_target="tpu_custom_call" | custom-call | flops 402653184 | bytes 5652480 | tf_op jit(solution)/shard_map/triangle/pallas_call | solution.py:180
  115.0 1.4 collective-permute-start.12
  116.4 7.0 %triangle.4.refs_0_ = bf16[64,96,128]{2,1,0:T(8,128)(2,1)} custom-call(s32[2]{0:T(128)S(1)} %pad_add_fusion.flag_ref, bf16[64,96,256]{2,1,0:T(8,128)(2,1)} %copy-done, bf16[23,64,384]{2,1,0:T(8,128)(2,1)} %collective-permute-done.2.refs_1_, bf16[23,64,384]{2,1,0:T(8,128)(2,1)} %collective-permute-done.5.refs_2_), custom_call_target="tpu_custom_call" | custom-call | flops 402653184 | bytes 5652480 | tf_op jit(solution)/shard_map/triangle/pallas_call | solution.py:180
  123.4 1.9 collective-permute-start.6
  125.3 1.0 copy-done.12
  126.3 4.8 %collective-permute-done.9.own_ref = bf16[23,64,384]{2,1,0:T(8,128)(2,1)S(1)} collective-permute-done((bf16[23,64,384]{2,1,0:T(8,128)(2,1)}, bf16[23,64,384]{2,1,0:T(8,128)(2,1)S(1)}, u32[]{:S(2)}, u32[]{:S(2)}) %collective-permute-start.9) | collective-permute-done | bytes 1130528 | tf_op jit(solution)/shard_map/ppermute | solution.py:419
  131.1 1.0 copy-done.10
  132.1 5.0 %collective-permute-start.15 = (bf16[23,64,384]{2,1,0:T(8,128)(2,1)S(1)}, bf16[23,64,384]{2,1,0:T(8,128)(2,1)}, u32[]{:S(2)}, u32[]{:S(2)}) collective-permute-start(bf16[23,64,384]{2,1,0:T(8,128)(2,1)S(1)} %copy-done.8), channel_id=1, source_target_pairs={{0,4},{2,6},{12,8},{14,10},{1,5},{3,7},{13,9},{15,11},{16,20},{18,... | collective-permute-start | bytes 3391496 | tf_op jit(solution)/shard_map/ppermute | solution.py:419
  137.1 1.7 collective-permute-start.16
  138.8 1.3 collective-permute-start.17
  140.1 3.8 %fold.3 = (bf16[23,96,128]{2,1,0:T(8,128)(2,1)S(1)}, bf16[23,96,128]{2,1,0:T(8,128)(2,1)S(1)}) custom-call(s32[1]{0:T(128)} %bitcast.9.role_ref, bf16[64,96,128]{2,1,0:T(8,128)(2,1)} %triangle.5.refs_0_, bf16[64,96,128]{2,1,0:T(8,128)(2,1)} %collective-permute-done.10.refs_1_, bf16[64,96,128]{2,1,0:T(8,128)(2,1)} %triangle.6.refs_2_, ...), custom_call_target="tpu_custom_call" | custom-call | bytes 4718592 | tf_op jit(solution)/shard_map/fold/pallas_call | solution.py:233
  143.9 0.8 copy-done.14
  144.7 1.3 collective-permute-start.13
  146.0 12.1 %collective-permute-done.13.other_ref = bf16[23,96,128]{2,1,0:T(8,128)(2,1)S(1)} collective-permute-done((bf16[23,96,128]{2,1,0:T(8,128)(2,1)S(1)}, bf16[23,96,128]{2,1,0:T(8,128)(2,1)S(1)}, u32[]{:S(2)}, u32[]{:S(2)}) %collective-permute-start.13) | collective-permute-done | bytes 565280 | tf_op jit(solution)/shard_map/ppermute | solution.py:422
  158.2 1.5 collective-permute-done.15.beside_ref
  159.6 3.2 %left_major.3.refs_1_ = bf16[64,96,256]{2,1,0:T(8,128)(2,1)S(1)} custom-call(bf16[23,64,384]{2,1,0:T(8,128)(2,1)S(1)} %copy-done.11, bf16[23,64,384]{2,1,0:T(8,128)(2,1)} %collective-permute-done.15.beside_ref), custom_call_target="tpu_custom_call" | custom-call | bytes 4521984 | tf_op jit(solution)/shard_map/left_major/pallas_call | solution.py:116
  162.9 1.7 copy-done.1
  164.5 1.9 collective-permute-done.17.refs_5_
  166.4 8.9 %triangle.7 = (bf16[64,96,128]{2,1,0:T(8,128)(2,1)}, bf16[64,48,128]{2,1,0:T(8,128)(2,1)S(1)}, bf16[64,48,128]{2,1,0:T(8,128)(2,1)}) custom-call(s32[2]{0:T(128)S(1)} %pad_add_fusion.2.flag_ref, bf16[64,96,256]{2,1,0:T(8,128)(2,1)} %copy-done, bf16[64,96,256]{2,1,0:T(8,128)(2,1)} %copy-done.1, bf16[23,64,384]{2,1,0:T(8,128)(2,1)S(1)} %copy-done.13, ...), custom_call_target="tpu_custom_call" | custom-call | flops 805306368 | bytes 5652480 | tf_op jit(solution)/shard_map/triangle/pallas_call | solution.py:180
  175.4 5.0 %collective-permute-start.18 = (bf16[64,96,128]{2,1,0:T(8,128)(2,1)}, bf16[64,96,128]{2,1,0:T(8,128)(2,1)}, u32[]{:S(2)}, u32[]{:S(2)}) collective-permute-start(bf16[64,96,128]{2,1,0:T(8,128)(2,1)} %get-tuple-element.52.refs_2_), channel_id=1, source_target_pairs={{1,0},{3,2},{4,5},{6,7},{9,8},{11,10},{12,13},{14,15},{17,16},{19,... | collective-permute-start | bytes 4718600 | tf_op jit(solution)/shard_map/ppermute | solution.py:429
  180.3 1.5 collective-permute-start.19
  181.9 1.5 collective-permute-start.20
  183.7 1.1 copy.23
  185.0 2.9 %fold.5 = bf16[23,96,128]{2,1,0:T(8,128)(2,1)S(1)} custom-call(s32[1]{0:T(128)} %bitcast.9.role_ref, bf16[64,48,128]{2,1,0:T(8,128)(2,1)} %get-tuple-element.54.refs_0_, bf16[64,48,128]{2,1,0:T(8,128)(2,1)} %collective-permute-done.19.refs_1_, bf16[64,48,128]{2,1,0:T(8,128)(2,1)S(1)} %get-tuple-element.55.refs_2_, ...), custom_call_target="tpu_custom_call" | custom-call | bytes 2359296 | tf_op jit(solution)/shard_map/fold/pallas_call | solution.py:233
  187.8 1.3 collective-permute-start.21
  189.2 1.5 collective-permute-start.23
  190.7 3.5 %fold.4 = (bf16[23,96,128]{2,1,0:T(8,128)(2,1)S(1)}, bf16[23,96,128]{2,1,0:T(8,128)(2,1)S(1)}) custom-call(s32[1]{0:T(128)} %bitcast.2.role_ref, bf16[64,96,128]{2,1,0:T(8,128)(2,1)} %triangle.4.refs_0_, bf16[64,96,128]{2,1,0:T(8,128)(2,1)} %collective-permute-done.6.refs_1_, bf16[64,96,128]{2,1,0:T(8,128)(2,1)S(1)} %copy-done.4, ...), custom_call_target="tpu_custom_call" | custom-call | bytes 4718592 | tf_op jit(solution)/shard_map/fold/pallas_call | solution.py:233
  194.2 1.3 collective-permute-start.22
  195.7 11.9 %finish.2.refs_4_ = bf16[2,23,96,128]{3,2,1,0:T(8,128)(2,1)S(1)} custom-call(s32[1]{0:T(128)} %bitcast.14.flag_ref, bf16[2,23,184,128]{3,2,1,0:T(8,128)(2,1)S(1)} %bitcast.21, bf16[23,96,128]{2,1,0:T(8,128)(2,1)S(1)} %copy-done.15, bf16[23,96,128]{2,1,0:T(8,128)(2,1)S(1)} %copy-done.17, bf16[128,128]{1,0:T(8,128)(2,1)S(1)} %bitcast.27, ...), custom_call_target="tpu_custom_call" | custom-call | flops 1941438464 | bytes 4333568 | tf_op jit(solution)/shard_map/finish/pallas_call | solution.py:300
  207.7 4.9 %collective-permute-done.22 = bf16[23,96,128]{2,1,0:T(8,128)(2,1)S(1)} collective-permute-done((bf16[23,96,128]{2,1,0:T(8,128)(2,1)S(1)}, bf16[23,96,128]{2,1,0:T(8,128)(2,1)S(1)}, u32[]{:S(2)}, u32[]{:S(2)}) %collective-permute-start.22) | collective-permute-done | bytes 565280 | tf_op jit(solution)/shard_map/ppermute | solution.py:422
  212.6 13.4 %finish.3 = bf16[2,23,184,128]{3,2,1,0:T(8,128)(2,1)} custom-call(s32[1]{0:T(128)} %bitcast.flag_ref, bf16[2,23,184,128]{3,2,1,0:T(8,128)(2,1)S(1)} %bitcast.22, bf16[23,96,128]{2,1,0:T(8,128)(2,1)S(1)} %broadcast_select_fusion.1.own_ref, bf16[23,96,128]{2,1,0:T(8,128)(2,1)S(1)} %broadcast_select_fusion.other_ref, bf16[128,128]{1,0:T(8,128)(2,1)S(1)} %bitcast.28, ...), custom_call_target="tpu_custom_call" | custom-call | flops 1941438464 | bytes 4333568 | tf_op jit(solution)/shard_map/finish/pallas_call | solution.py:300
  (69 shorter events, 1.9 us)
Async XLA Ops:
  0.0 2.5 %copy-start.20 = (s32[5]{0:T(128)S(1)}, s32[5]{0:T(128)}, u32[]{:S(2)}) copy-start(s32[5]{0:T(128)} %param.7) | copy-start | bytes 64
  3.9 1.6 copy-start.2
  5.5 17.2 %copy-start.3 = (bf16[46,184,128]{2,1,0:T(8,128)(2,1)S(1)}, bf16[46,184,128]{2,1,0:T(8,128)(2,1)}, u32[]{:S(2)}) copy-start(bf16[46,184,128]{2,1,0:T(8,128)(2,1)} %param.6) | copy-start | bytes 6500356
  11.2 27.0 %collective-permute-start = (bf16[23,64,384]{2,1,0:T(8,128)(2,1)}, bf16[23,64,384]{2,1,0:T(8,128)(2,1)}, u32[]{:S(2)}, u32[]{:S(2)}) collective-permute-start(bf16[23,64,384]{2,1,0:T(8,128)(2,1)} %get-tuple-element.35), channel_id=1, source_target_pairs={{0,2},{2,0},{4,6},{6,4},{8,10},{10,8},{12,14},{14,12},{1,3},{3,1},... | collective-permute-start | bytes 3391496 | tf_op jit(solution)/shard_map/ppermute | solution.py:422
  13.3 25.0 %collective-permute-start.1 = (bf16[23,64,384]{2,1,0:T(8,128)(2,1)}, bf16[23,64,384]{2,1,0:T(8,128)(2,1)S(1)}, u32[]{:S(2)}, u32[]{:S(2)}) collective-permute-start(bf16[23,64,384]{2,1,0:T(8,128)(2,1)} %get-tuple-element.39.refs_1_), channel_id=1, source_target_pairs={{4,8},{6,10},{8,4},{10,6},{5,9},{7,11},{9,5},{11,7},{20,24},{22,26... | collective-permute-start | bytes 3391496 | tf_op jit(solution)/shard_map/ppermute | solution.py:419
  14.0 29.0 %collective-permute-start.2 = (bf16[23,64,384]{2,1,0:T(8,128)(2,1)}, bf16[23,64,384]{2,1,0:T(8,128)(2,1)}, u32[]{:S(2)}, u32[]{:S(2)}) collective-permute-start(bf16[23,64,384]{2,1,0:T(8,128)(2,1)} %get-tuple-element.39.refs_1_), channel_id=1, source_target_pairs={{0,4},{2,6},{12,8},{14,10},{1,5},{3,7},{13,9},{15,11},{16,20},{18,... | collective-permute-start | bytes 3391496 | tf_op jit(solution)/shard_map/ppermute | solution.py:419
  20.7 27.1 %collective-permute-start.3 = (bf16[23,64,384]{2,1,0:T(8,128)(2,1)}, bf16[23,64,384]{2,1,0:T(8,128)(2,1)}, u32[]{:S(2)}, u32[]{:S(2)}) collective-permute-start(bf16[23,64,384]{2,1,0:T(8,128)(2,1)} %get-tuple-element.39.refs_1_), channel_id=1, source_target_pairs={{4,0},{6,2},{8,12},{10,14},{5,1},{7,3},{9,13},{11,15},{20,16},{22,... | collective-permute-start | bytes 3391496 | tf_op jit(solution)/shard_map/ppermute | solution.py:419
  47.8 24.0 %collective-permute-start.4 = (bf16[23,64,384]{2,1,0:T(8,128)(2,1)S(1)}, bf16[23,64,384]{2,1,0:T(8,128)(2,1)S(1)}, u32[]{:S(2)}, u32[]{:S(2)}) collective-permute-start(bf16[23,64,384]{2,1,0:T(8,128)(2,1)S(1)} %get-tuple-element.40), channel_id=1, source_target_pairs={{0,2},{2,0},{4,6},{6,4},{8,10},{10,8},{12,14},{14,12},{1,3},{3,1},... | collective-permute-start | bytes 3391496 | tf_op jit(solution)/shard_map/ppermute | solution.py:422
  48.0 23.7 %collective-permute-start.5 = (bf16[23,64,384]{2,1,0:T(8,128)(2,1)}, bf16[23,64,384]{2,1,0:T(8,128)(2,1)}, u32[]{:S(2)}, u32[]{:S(2)}) collective-permute-start(bf16[23,64,384]{2,1,0:T(8,128)(2,1)} %collective-permute-done.refs_2_), channel_id=1, source_target_pairs={{0,4},{2,6},{12,8},{14,10},{1,5},{3,7},{13,9},{15,11},{16,20},{18,... | collective-permute-start | bytes 3391496 | tf_op jit(solution)/shard_map/ppermute | solution.py:419
  50.3 21.4 %collective-permute-start.7 = (bf16[23,64,384]{2,1,0:T(8,128)(2,1)}, bf16[23,64,384]{2,1,0:T(8,128)(2,1)}, u32[]{:S(2)}, u32[]{:S(2)}) collective-permute-start(bf16[23,64,384]{2,1,0:T(8,128)(2,1)} %collective-permute-done.refs_2_), channel_id=1, source_target_pairs={{4,8},{6,10},{8,4},{10,6},{5,9},{7,11},{9,5},{11,7},{20,24},{22,26... | collective-permute-start | bytes 3391496 | tf_op jit(solution)/shard_map/ppermute | solution.py:419
  52.0 25.4 %collective-permute-start.8 = (bf16[23,64,384]{2,1,0:T(8,128)(2,1)S(1)}, bf16[23,64,384]{2,1,0:T(8,128)(2,1)S(1)}, u32[]{:S(2)}, u32[]{:S(2)}) collective-permute-start(bf16[23,64,384]{2,1,0:T(8,128)(2,1)S(1)} %collective-permute-done.1.refs_1_), channel_id=1, source_target_pairs={{4,0},{6,2},{8,12},{10,14},{5,1},{7,3},{9,13},{11,15},{20,16},{22,... | collective-permute-start | bytes 3391496 | tf_op jit(solution)/shard_map/ppermute | solution.py:419
  77.4 1.1 copy-start.5
  78.5 28.0 %collective-permute-start.11 = (bf16[23,64,384]{2,1,0:T(8,128)(2,1)}, bf16[23,64,384]{2,1,0:T(8,128)(2,1)}, u32[]{:S(2)}, u32[]{:S(2)}) collective-permute-start(bf16[23,64,384]{2,1,0:T(8,128)(2,1)} %collective-permute-done.7.refs_2_), channel_id=1, source_target_pairs={{4,0},{6,2},{8,12},{10,14},{5,1},{7,3},{9,13},{11,15},{20,16},{22,... | collective-permute-start | bytes 3391496 | tf_op jit(solution)/shard_map/ppermute | solution.py:419
  81.6 1.6 copy-start
  83.3 1.0 copy-start.7
  84.3 1.0 copy-start.9
  92.3 46.4 %collective-permute-start.10 = (bf16[64,96,128]{2,1,0:T(8,128)(2,1)}, bf16[64,96,128]{2,1,0:T(8,128)(2,1)}, u32[]{:S(2)}, u32[]{:S(2)}) collective-permute-start(bf16[64,96,128]{2,1,0:T(8,128)(2,1)} %triangle.5.refs_0_), channel_id=1, source_target_pairs={{1,0},{3,2},{5,4},{7,6},{8,9},{10,11},{12,13},{14,15},{17,16},{19,... | collective-permute-start | bytes 4718600 | tf_op jit(solution)/shard_map/ppermute | solution.py:429
  99.2 26.1 %collective-permute-start.14 = (bf16[23,64,384]{2,1,0:T(8,128)(2,1)}, bf16[23,64,384]{2,1,0:T(8,128)(2,1)S(1)}, u32[]{:S(2)}, u32[]{:S(2)}) collective-permute-start(bf16[23,64,384]{2,1,0:T(8,128)(2,1)} %collective-permute-done.2.refs_1_), channel_id=1, source_target_pairs={{4,8},{6,10},{8,4},{10,6},{5,9},{7,11},{9,5},{11,7},{20,24},{22,26... | collective-permute-start | bytes 3391496 | tf_op jit(solution)/shard_map/ppermute | solution.py:419
  99.9 31.2 %collective-permute-start.9 = (bf16[23,64,384]{2,1,0:T(8,128)(2,1)}, bf16[23,64,384]{2,1,0:T(8,128)(2,1)S(1)}, u32[]{:S(2)}, u32[]{:S(2)}) collective-permute-start(bf16[23,64,384]{2,1,0:T(8,128)(2,1)} %copy-done.9), channel_id=1, source_target_pairs={{0,4},{2,6},{12,8},{14,10},{1,5},{3,7},{13,9},{15,11},{16,20},{18,... | collective-permute-start | bytes 3391496 | tf_op jit(solution)/shard_map/ppermute | solution.py:419
  106.5 1.3 copy-start.6
  115.0 17.2 %copy-start.8 = (bf16[23,64,384]{2,1,0:T(8,128)(2,1)S(1)}, bf16[23,64,384]{2,1,0:T(8,128)(2,1)}, u32[]{:S(2)}) copy-start(bf16[23,64,384]{2,1,0:T(8,128)(2,1)} %copy-done.7) | copy-start | bytes 3391492
  115.0 25.1 %collective-permute-start.12 = (bf16[64,96,128]{2,1,0:T(8,128)(2,1)}, bf16[64,96,128]{2,1,0:T(8,128)(2,1)}, u32[]{:S(2)}, u32[]{:S(2)}) collective-permute-start(bf16[64,96,128]{2,1,0:T(8,128)(2,1)} %triangle.6.refs_2_), channel_id=1, source_target_pairs={{0,1},{2,3},{4,5},{6,7},{9,8},{11,10},{13,12},{15,14},{16,17},{18,... | collective-permute-start | bytes 4718600 | tf_op jit(solution)/shard_map/ppermute | solution.py:429
  123.4 22.6 %collective-permute-start.6 = (bf16[64,96,128]{2,1,0:T(8,128)(2,1)}, bf16[64,96,128]{2,1,0:T(8,128)(2,1)}, u32[]{:S(2)}, u32[]{:S(2)}) collective-permute-start(bf16[64,96,128]{2,1,0:T(8,128)(2,1)} %triangle.4.refs_0_), channel_id=1, source_target_pairs={{5,4},{7,6},{8,9},{10,11},{21,20},{23,22},{24,25},{26,27}} | collective-permute-start | bytes 4718600 | tf_op jit(solution)/shard_map/ppermute | solution.py:429
  125.3 1.0 copy-start.12
  131.1 1.0 copy-start.10
  132.1 27.5 %collective-permute-start.15 = (bf16[23,64,384]{2,1,0:T(8,128)(2,1)S(1)}, bf16[23,64,384]{2,1,0:T(8,128)(2,1)}, u32[]{:S(2)}, u32[]{:S(2)}) collective-permute-start(bf16[23,64,384]{2,1,0:T(8,128)(2,1)S(1)} %copy-done.8), channel_id=1, source_target_pairs={{0,4},{2,6},{12,8},{14,10},{1,5},{3,7},{13,9},{15,11},{16,20},{18,... | collective-permute-start | bytes 3391496 | tf_op jit(solution)/shard_map/ppermute | solution.py:419
  137.1 27.4 %collective-permute-start.16 = (bf16[23,64,384]{2,1,0:T(8,128)(2,1)}, bf16[23,64,384]{2,1,0:T(8,128)(2,1)}, u32[]{:S(2)}, u32[]{:S(2)}) collective-permute-start(bf16[23,64,384]{2,1,0:T(8,128)(2,1)} %collective-permute-done.5.refs_2_), channel_id=1, source_target_pairs={{4,8},{6,10},{8,4},{10,6},{5,9},{7,11},{9,5},{11,7},{20,24},{22,26... | collective-permute-start | bytes 3391496 | tf_op jit(solution)/shard_map/ppermute | solution.py:419
  138.8 27.6 %collective-permute-start.17 = (bf16[23,64,384]{2,1,0:T(8,128)(2,1)}, bf16[23,64,384]{2,1,0:T(8,128)(2,1)}, u32[]{:S(2)}, u32[]{:S(2)}) collective-permute-start(bf16[23,64,384]{2,1,0:T(8,128)(2,1)} %collective-permute-done.refs_2_), channel_id=1, source_target_pairs={{4,0},{6,2},{8,12},{10,14},{5,1},{7,3},{9,13},{11,15},{20,16},{22,... | collective-permute-start | bytes 3391496 | tf_op jit(solution)/shard_map/ppermute | solution.py:419
  140.1 19.5 %copy-start.11 = (bf16[23,64,384]{2,1,0:T(8,128)(2,1)S(1)}, bf16[23,64,384]{2,1,0:T(8,128)(2,1)}, u32[]{:S(2)}) copy-start(bf16[23,64,384]{2,1,0:T(8,128)(2,1)} %copy-done.10) | copy-start | bytes 3391492
  143.9 0.8 copy-start.14
  144.7 21.7 %copy-start.13 = (bf16[23,64,384]{2,1,0:T(8,128)(2,1)S(1)}, bf16[23,64,384]{2,1,0:T(8,128)(2,1)}, u32[]{:S(2)}) copy-start(bf16[23,64,384]{2,1,0:T(8,128)(2,1)} %copy-done.12) | copy-start | bytes 3391492
  144.7 13.4 %collective-permute-start.13 = (bf16[23,96,128]{2,1,0:T(8,128)(2,1)S(1)}, bf16[23,96,128]{2,1,0:T(8,128)(2,1)S(1)}, u32[]{:S(2)}, u32[]{:S(2)}) collective-permute-start(bf16[23,96,128]{2,1,0:T(8,128)(2,1)S(1)} %get-tuple-element.46), channel_id=1, source_target_pairs={{0,2},{2,0},{4,6},{6,4},{8,10},{10,8},{12,14},{14,12},{1,3},{3,1},... | collective-permute-start | bytes 1695752 | tf_op jit(solution)/shard_map/ppermute | solution.py:422
  158.2 4.7 %copy-start.16 = (bf16[23,96,128]{2,1,0:T(8,128)(2,1)}, bf16[23,96,128]{2,1,0:T(8,128)(2,1)S(1)}, u32[]{:S(2)}) copy-start(bf16[23,96,128]{2,1,0:T(8,128)(2,1)S(1)} %collective-permute-done.13.other_ref) | copy-start | bytes 1695748
  162.8 1.7 copy-start.1
  164.5 18.9 %copy-start.19 = (bf16[128,128]{1,0:T(8,128)(2,1)S(1)}, bf16[128,128]{1,0:T(8,128)(2,1)}, u32[]{:S(2)}) copy-start(bf16[128,128]{1,0:T(8,128)(2,1)} %param.9) | copy-start | bytes 98308
  164.5 20.3 %copy-start.18 = (bf16[512,128]{1,0:T(8,128)(2,1)S(1)}, bf16[512,128]{1,0:T(8,128)(2,1)}, u32[]{:S(2)}) copy-start(bf16[512,128]{1,0:T(8,128)(2,1)} %param.11) | copy-start | bytes 393220
  175.4 15.3 %collective-permute-start.18 = (bf16[64,96,128]{2,1,0:T(8,128)(2,1)}, bf16[64,96,128]{2,1,0:T(8,128)(2,1)}, u32[]{:S(2)}, u32[]{:S(2)}) collective-permute-start(bf16[64,96,128]{2,1,0:T(8,128)(2,1)} %get-tuple-element.52.refs_2_), channel_id=1, source_target_pairs={{1,0},{3,2},{4,5},{6,7},{9,8},{11,10},{12,13},{14,15},{17,16},{19,... | collective-permute-start | bytes 4718600 | tf_op jit(solution)/shard_map/ppermute | solution.py:429
  180.3 4.6 %collective-permute-start.19 = (bf16[64,48,128]{2,1,0:T(8,128)(2,1)}, bf16[64,48,128]{2,1,0:T(8,128)(2,1)}, u32[]{:S(2)}, u32[]{:S(2)}) collective-permute-start(bf16[64,48,128]{2,1,0:T(8,128)(2,1)} %get-tuple-element.54.refs_0_), channel_id=1, source_target_pairs={{5,4},{7,6},{8,9},{10,11},{21,20},{23,22},{24,25},{26,27}} | collective-permute-start | bytes 2359304 | tf_op jit(solution)/shard_map/ppermute | solution.py:429
  181.9 3.1 %collective-permute-start.20 = (bf16[64,48,128]{2,1,0:T(8,128)(2,1)S(1)}, bf16[64,48,128]{2,1,0:T(8,128)(2,1)}, u32[]{:S(2)}, u32[]{:S(2)}) collective-permute-start(bf16[64,48,128]{2,1,0:T(8,128)(2,1)S(1)} %get-tuple-element.55.refs_2_), channel_id=1, source_target_pairs={{4,5},{6,7},{9,8},{11,10},{20,21},{22,23},{25,24},{27,26}} | collective-permute-start | bytes 2359304 | tf_op jit(solution)/shard_map/ppermute | solution.py:429
  184.9 5.8 %copy-start.4 = (bf16[64,96,128]{2,1,0:T(8,128)(2,1)S(1)}, bf16[64,96,128]{2,1,0:T(8,128)(2,1)}, u32[]{:S(2)}) copy-start(bf16[64,96,128]{2,1,0:T(8,128)(2,1)} %get-tuple-element.52.refs_2_) | copy-start | bytes 4718596
  187.8 19.8 %collective-permute-start.21 = (bf16[23,96,128]{2,1,0:T(8,128)(2,1)S(1)}, bf16[23,96,128]{2,1,0:T(8,128)(2,1)S(1)}, u32[]{:S(2)}, u32[]{:S(2)}) collective-permute-start(bf16[23,96,128]{2,1,0:T(8,128)(2,1)S(1)} %fold.5), channel_id=1, source_target_pairs={{5,1},{7,3},{8,12},{10,14},{21,17},{23,19},{24,28},{26,30}} | collective-permute-start | bytes 1695752 | tf_op jit(solution)/shard_map/ppermute | solution.py:437
  189.2 18.5 %collective-permute-start.23 = (bf16[23,96,128]{2,1,0:T(8,128)(2,1)S(1)}, bf16[23,96,128]{2,1,0:T(8,128)(2,1)S(1)}, u32[]{:S(2)}, u32[]{:S(2)}) collective-permute-start(bf16[23,96,128]{2,1,0:T(8,128)(2,1)S(1)} %fold.5), channel_id=1, source_target_pairs={{4,3},{6,1},{9,14},{11,12},{20,19},{22,17},{25,30},{27,28}} | collective-permute-start | bytes 1695752 | tf_op jit(solution)/shard_map/ppermute | solution.py:437
  190.7 5.0 %copy-start.15 = (bf16[23,96,128]{2,1,0:T(8,128)(2,1)S(1)}, bf16[23,96,128]{2,1,0:T(8,128)(2,1)}, u32[]{:S(2)}) copy-start(bf16[23,96,128]{2,1,0:T(8,128)(2,1)} %copy-done.14) | copy-start | bytes 1695748
  190.7 5.0 %copy-start.17 = (bf16[23,96,128]{2,1,0:T(8,128)(2,1)S(1)}, bf16[23,96,128]{2,1,0:T(8,128)(2,1)}, u32[]{:S(2)}) copy-start(bf16[23,96,128]{2,1,0:T(8,128)(2,1)} %copy-done.16) | copy-start | bytes 1695748
  194.2 18.3 %collective-permute-start.22 = (bf16[23,96,128]{2,1,0:T(8,128)(2,1)S(1)}, bf16[23,96,128]{2,1,0:T(8,128)(2,1)S(1)}, u32[]{:S(2)}, u32[]{:S(2)}) collective-permute-start(bf16[23,96,128]{2,1,0:T(8,128)(2,1)S(1)} %get-tuple-element.56), channel_id=1, source_target_pairs={{0,2},{2,0},{4,6},{6,4},{8,10},{10,8},{12,14},{14,12},{1,3},{3,1},... | collective-permute-start | bytes 1695752 | tf_op jit(solution)/shard_map/ppermute | solution.py:422

commit v7 on v6

--- a/solution.py
+++ b/solution.py
@@ -455,7 +455,7 @@
     inner = (place == 1) | (place == 2)
     where = scalars(valid_count, row_id * tile_rows, core * tile_cols)
     folded = pair.reshape(2, half, tile_cols, width)
-    cross, inward, outward = [(1, 2), (2, 1)], [(0, 1), (3, 2)], [(1, 0), (2, 3)]
+    cross = [(1, 2), (2, 1)]
     everyone, inners = range(4), (1, 2)
 
     def phase(moves, finished):
@@ -465,39 +465,39 @@
     def hop(moves):
         return lambda value: among(value, moves)
 
+    def either(at_inner, at_end):
+        return jnp.where(inner, at_inner, at_end)
+
+    swap = hop([(0, 1), (1, 0), (2, 3), (3, 2)])
     right_own, right_far = project(where, folded, gate_pair(2))
-    one = phase(
-        [(hop(inward), right_own), (hop(cross), right_own), (hop(outward), right_own), (across, right_far)],
-        (),
-    )
-    end_own, near_own, inner_own, right_beside = one
+    one = phase([(swap, right_own), (hop(cross), right_own), (across, right_far)], ())
+    mate_own, near_own, right_beside = one
     left_own, left_far = project(where, folded, gate_pair(0))
     two = phase(
-        [(hop(inward), right_beside), (hop(cross), right_beside), (hop(outward), near_own), (across, left_far)],
-        one,
-    )
-    end_beside, near_beside, relay_own, left_beside = two
-    three = phase([(hop(cross), end_own), (hop(inward), left_own), (hop(outward), near_beside)], two)
-    far_own, guest_own, relay_beside = three
-    four = phase(
-        [(hop(cross), end_beside), (hop(inward), left_beside), (hop(outward), right_beside)], three
-    )
-    far_beside, guest_beside, inner_beside = four
-
+        [(swap, either(near_own, right_beside)), (hop(cross), right_beside), (across, left_far)], one
+    )
+    mate_beside, near_beside, left_beside = two
+    three = phase([(swap, either(near_beside, left_own)), (hop(cross), mate_own)], two)
+    guest_own, far_own = three
     left = left_major(left_own, left_beside)
     (home,) = triangle(scalars(side, 0), [left], right_own, right_beside)
     home_rest = to_core(home, everyone, [True] * 4)
-    (mate,) = triangle(scalars(side, 0), [left], end_own, end_beside)
+    (mate,) = triangle(scalars(side, 0), [left], mate_own, mate_beside)
     mate_rest = to_core(mate, inners, [True] * 2)
+    four = phase([(swap, either(right_beside, left_beside)), (hop(cross), mate_beside)], three + [home, mate])
+    guest_beside, far_beside = four
+
     outer = scalars(side, jnp.where(inner, 0, 1))
-    (away,) = triangle(outer, [left], near_own, near_beside, relay_own, relay_beside)
+    (away,) = triangle(
+        outer, [left], after(near_own, far_own, mate), near_beside, mate_beside, guest_own
+    )
     away_rest = to_core(away, everyone, [False] * 4)
     first = fold(half, scalars(jnp.where(is_keeper, 0, 1)), home, home_rest, away, away_rest)
 
     first_other = across(first[1])
     left_guest = left_major(after(guest_own, first_other, mate_rest), guest_beside)
     late, lent_own, lent_beside = triangle(
-        outer, [left, left_guest], far_own, far_beside, inner_own, inner_beside
+        outer, [left, left_guest], far_own, far_beside, mate_own, guest_beside
     )
     lent_rest = to_core(lent_own, inners, [False] * 2), to_core(lent_beside, inners, [True] * 2)
     late_rest = to_core(late, everyone, [True, False, False, True])

time: 227 us -> 207 us (0.912)
  starting transfers between devices: 56.3 us -> 42.9 us
  waiting for transfers between devices: 70 us -> 61.1 us
  other arithmetic: 0.53 us -> 3.18 us
    ppermute x12 -> x8, waiting for transfers between devices: 23.4 us -> 7.82 us  [among(): lax.ppermute(value, 'row', [(2 * s + b, 2 * t + b) for s, t in moves for...]
    ppermute x12 -> x8, starting transfers between devices: 30.4 us -> 19.5 us  [among(): lax.ppermute(value, 'row', [(2 * s + b, 2 * t + b) for s, t in moves for...]
    ppermute x4, waiting for transfers between devices: 46.6 us -> 53.3 us  [across(): return lax.ppermute(value, 'row', [(i, i ^ 1) for i in range(8)])]
    select_n x0 -> x3, other arithmetic: none -> 2.65 us  [either(): return jnp.where(inner, at_inner, at_end)]
    ppermute x6, starting transfers between devices: 18.2 us -> 15.9 us  [to_core(): return lax.ppermute(value, ('row', 'col'), perm)]
    unnamed x58 -> x52, local copies, waits for them, and re-layouts: 14.8 us -> 13.8 us
  transfers between devices with their start and end apart: 24 -> 20, of which waited for: 10 -> 7; matrix products, arithmetic and copies ran while one was open for 1% -> 3% of each run, Pallas kernels for 23% -> 26%
where the time goes in v7:
time: 207 us; the launch traced here: 205 us
  Pallas kernels  80.8 us (39%)
  waiting for transfers between devices  61.1 us (30%)
  starting transfers between devices  42.9 us (21%)
  local copies, waits for them, and re-layouts  16.3 us (8%)
  other arithmetic  3.18 us (2%)
    ppermute x4, waiting for transfers between devices, across(): return lax.ppermute(value, 'row', [(i, i ^ 1) for i in range(8)])  53.3 us
    pallas_call x4, Pallas kernels, triangle(): pl.pallas_call(functools.partial(triangle_kernel, guests=guests, options=...  30.2 us
    pallas_call x2, Pallas kernels, finish(): pl.pallas_call(finish_kernel, out_shape=jax.ShapeDtypeStruct(shape, BF16)...  25.3 us
    ppermute x8, starting transfers between devices, among(): lax.ppermute(value, 'row', [(2 * s + b, 2 * t + b) for s, t in moves for...  19.5 us
    ppermute x6, starting transfers between devices, to_core(): return lax.ppermute(value, ('row', 'col'), perm)  15.9 us
    unnamed x52, local copies, waits for them, and re-layouts  13.8 us
    pallas_call x3, Pallas kernels, fold(): pl.pallas_call(functools.partial(fold_kernel, outputs=outputs, half=half)...  10.2 us
    pallas_call x2, Pallas kernels, project(): pl.pallas_call(project_kernel, out_shape=(piece, piece), in_specs=[pl.Blo...  10.2 us
  transfers between devices with their start and end apart: 20, of which 7 were waited for; matrix products, arithmetic and copies ran while one was open for 3% of the time, Pallas kernels for 26%

profile of v7, /device:TPU:1, one launch (start us, length us, event | category | flops | bytes accessed | tf_op | source)
XLA Modules:
  0.0 205.4 jit_solution(6158727449606758390)
XLA Ops:
  0.0 1.0 fusion.2
  1.0 0.8 fusion.1
  1.9 0.1 copy.33
  2.3 0.1 copy.31
  2.4 0.1 copy.34
  2.5 0.6 slice.60
  3.7 1.6 copy-done.2
  5.4 5.8 %project.3 = (bf16[23,64,384]{2,1,0:T(8,128)(2,1)}, bf16[23,64,384]{2,1,0:T(8,128)(2,1)}) custom-call(s32[3]{0:T(128)S(1)} %pad_add_fusion.1.where_ref, bf16[2,23,184,128]{3,2,1,0:T(8,128)(2,1)S(1)} %bitcast.19, bf16[256,128]{1,0:T(8,128)(2,1)S(1)} %maximum_bitcast_fusion.1.weight_ref), custom_call_target="tpu_custom_call" | custom-call | flops 554696704 | bytes 4333568 | tf_op jit(solution)/shard_map/project/pallas_call | solution.py:73
  11.2 1.7 collective-permute-start
  12.8 2.0 collective-permute-start.1
  14.9 2.9 %collective-permute-start.2 = (bf16[23,64,384]{2,1,0:T(8,128)(2,1)}, bf16[23,64,384]{2,1,0:T(8,128)(2,1)}, u32[]{:S(2)}, u32[]{:S(2)}) collective-permute-start(bf16[23,64,384]{2,1,0:T(8,128)(2,1)} %get-tuple-element.35.refs_1_), channel_id=1, source_target_pairs={{0,4},{2,6},{4,0},{6,2},{8,12},{10,14},{12,8},{14,10},{1,5},{3,7},... | collective-permute-start | bytes 3391496 | tf_op jit(solution)/shard_map/ppermute | solution.py:419
  18.2 0.1 copy.25
  18.3 0.1 copy.28
  18.5 4.4 %project.2 = (bf16[23,64,384]{2,1,0:T(8,128)(2,1)S(1)}, bf16[23,64,384]{2,1,0:T(8,128)(2,1)S(1)}) custom-call(s32[3]{0:T(128)S(1)} %pad_add_fusion.1.where_ref, bf16[2,23,184,128]{3,2,1,0:T(8,128)(2,1)S(1)} %bitcast.20, bf16[256,128]{1,0:T(8,128)(2,1)S(1)} %maximum_bitcast_fusion.weight_ref), custom_call_target="tpu_custom_call" | custom-call | flops 554696704 | bytes 4333568 | tf_op jit(solution)/shard_map/project/pallas_call | solution.py:73
  22.9 16.9 %collective-permute-done.1.refs_2_ = bf16[23,64,384]{2,1,0:T(8,128)(2,1)S(1)} collective-permute-done((bf16[23,64,384]{2,1,0:T(8,128)(2,1)}, bf16[23,64,384]{2,1,0:T(8,128)(2,1)S(1)}, u32[]{:S(2)}, u32[]{:S(2)}) %collective-permute-start.1) | collective-permute-done | bytes 1130528 | tf_op jit(solution)/shard_map/ppermute | solution.py:422
  39.8 0.2 broadcast_select_fusion.2
  40.0 2.0 collective-permute-done.2.refs_1_.refs_4_
  42.1 0.7 collective-permute-start.6
  42.8 0.3 collective-permute-start.3
  43.2 4.1 %collective-permute-start.4 = (bf16[23,64,384]{2,1,0:T(8,128)(2,1)S(1)}, bf16[23,64,384]{2,1,0:T(8,128)(2,1)}, u32[]{:S(2)}, u32[]{:S(2)}) collective-permute-start(bf16[23,64,384]{2,1,0:T(8,128)(2,1)S(1)} %broadcast_select_fusion.2), channel_id=1, source_target_pairs={{0,4},{2,6},{4,0},{6,2},{8,12},{10,14},{12,8},{14,10},{1,5},{3,7},... | collective-permute-start | bytes 3391496 | tf_op jit(solution)/shard_map/ppermute | solution.py:419
  47.2 1.3 broadcast_select_fusion.1
  48.5 0.2 copy-done.4
  48.7 18.8 %collective-permute-done.3.beside_ref = bf16[23,64,384]{2,1,0:T(8,128)(2,1)S(1)} collective-permute-done((bf16[23,64,384]{2,1,0:T(8,128)(2,1)S(1)}, bf16[23,64,384]{2,1,0:T(8,128)(2,1)S(1)}, u32[]{:S(2)}, u32[]{:S(2)}) %collective-permute-start.3) | collective-permute-done | bytes 1130528 | tf_op jit(solution)/shard_map/ppermute | solution.py:422
  67.5 1.0 copy-done.6
  68.5 1.8 collective-permute-done.4.refs_2_.refs_3_
  70.3 1.7 collective-permute-start.9
  72.0 3.2 %collective-permute-start.7 = (bf16[23,64,384]{2,1,0:T(8,128)(2,1)}, bf16[23,64,384]{2,1,0:T(8,128)(2,1)}, u32[]{:S(2)}, u32[]{:S(2)}) collective-permute-start(bf16[23,64,384]{2,1,0:T(8,128)(2,1)} %broadcast_select_fusion.1), channel_id=1, source_target_pairs={{0,4},{2,6},{4,0},{6,2},{8,12},{10,14},{12,8},{14,10},{1,5},{3,7},... | collective-permute-start | bytes 3391496 | tf_op jit(solution)/shard_map/ppermute | solution.py:419
  75.4 1.3 copy-done.7
  76.6 1.3 copy-done.10
  77.9 1.8 left_major.2.refs_0_
  79.7 1.6 copy-done
  81.3 6.9 %triangle.5.refs_0_ = bf16[64,96,128]{2,1,0:T(8,128)(2,1)} custom-call(s32[2]{0:T(128)S(1)} %pad_add_fusion.flag_ref, bf16[64,96,256]{2,1,0:T(8,128)(2,1)} %copy-done, bf16[23,64,384]{2,1,0:T(8,128)(2,1)} %get-tuple-element.35.refs_1_, bf16[23,64,384]{2,1,0:T(8,128)(2,1)S(1)} %collective-permute-done.1.refs_2_), custom_call_target="tpu_custom_call" | custom-call | flops 402653184 | bytes 5652480 | tf_op jit(solution)/shard_map/triangle/pallas_call | solution.py:180
  88.2 6.4 %collective-permute-start.8 = (bf16[64,96,128]{2,1,0:T(8,128)(2,1)}, bf16[64,96,128]{2,1,0:T(8,128)(2,1)}, u32[]{:S(2)}, u32[]{:S(2)}) collective-permute-start(bf16[64,96,128]{2,1,0:T(8,128)(2,1)} %triangle.5.refs_0_), channel_id=1, source_target_pairs={{1,0},{3,2},{5,4},{7,6},{8,9},{10,11},{12,13},{14,15},{17,16},{19,... | collective-permute-start | bytes 4718600 | tf_op jit(solution)/shard_map/ppermute | solution.py:429
  94.6 7.0 %triangle.4.refs_0_ = bf16[64,96,128]{2,1,0:T(8,128)(2,1)} custom-call(s32[2]{0:T(128)S(1)} %pad_add_fusion.flag_ref, bf16[64,96,256]{2,1,0:T(8,128)(2,1)} %copy-done, bf16[23,64,384]{2,1,0:T(8,128)(2,1)} %collective-permute-done.2.refs_1_.refs_4_, bf16[23,64,384]{2,1,0:T(8,128)(2,1)} %collective-permute-done.4.refs_2_.refs_3_), custom_call_target="tpu_custom_call" | custom-call | flops 402653184 | bytes 5652480 | tf_op jit(solution)/shard_map/triangle/pallas_call | solution.py:180
  101.6 7.4 %triangle.6.refs_2_ = bf16[64,96,128]{2,1,0:T(8,128)(2,1)} custom-call(s32[2]{0:T(128)S(1)} %pad_add_fusion.2.flag_ref, bf16[64,96,256]{2,1,0:T(8,128)(2,1)} %copy-done, bf16[23,64,384]{2,1,0:T(8,128)(2,1)} %collective-permute-done.refs_1_, bf16[23,64,384]{2,1,0:T(8,128)(2,1)S(1)} %copy-done.5, bf16[23,64,384]{2,1,0:T(8,128)(2,1)} %collective-permute-done.4.refs_2_.refs_3_, ...), custom_call_target="tpu_custom_call" | custom-call | flops 402653184 | bytes 5652480 | tf_op jit(solution)/shard_map/triangle/pallas_call | solution.py:180
  109.0 1.3 collective-permute-start.10
  110.3 1.9 collective-permute-start.5
  112.1 1.2 broadcast_select_fusion
  113.3 3.5 %collective-permute-start.12 = (bf16[23,64,384]{2,1,0:T(8,128)(2,1)}, bf16[23,64,384]{2,1,0:T(8,128)(2,1)S(1)}, u32[]{:S(2)}, u32[]{:S(2)}) collective-permute-start(bf16[23,64,384]{2,1,0:T(8,128)(2,1)} %broadcast_select_fusion), channel_id=1, source_target_pairs={{0,4},{2,6},{4,0},{6,2},{8,12},{10,14},{12,8},{14,10},{1,5},{3,7},... | collective-permute-start | bytes 3391496 | tf_op jit(solution)/shard_map/ppermute | solution.py:419
  116.8 1.7 collective-permute-start.13
  118.5 3.7 %fold.3 = (bf16[23,96,128]{2,1,0:T(8,128)(2,1)S(1)}, bf16[23,96,128]{2,1,0:T(8,128)(2,1)S(1)}) custom-call(s32[1]{0:T(128)} %bitcast.9.role_ref, bf16[64,96,128]{2,1,0:T(8,128)(2,1)} %triangle.5.refs_0_, bf16[64,96,128]{2,1,0:T(8,128)(2,1)} %collective-permute-done.8.refs_1_, bf16[64,96,128]{2,1,0:T(8,128)(2,1)} %triangle.6.refs_2_, ...), custom_call_target="tpu_custom_call" | custom-call | bytes 4718592 | tf_op jit(solution)/shard_map/fold/pallas_call | solution.py:233
  122.2 0.8 copy-done.12
  123.0 1.2 collective-permute-start.11
  124.2 12.9 %collective-permute-done.11.other_ref = bf16[23,96,128]{2,1,0:T(8,128)(2,1)S(1)} collective-permute-done((bf16[23,96,128]{2,1,0:T(8,128)(2,1)S(1)}, bf16[23,96,128]{2,1,0:T(8,128)(2,1)S(1)}, u32[]{:S(2)}, u32[]{:S(2)}) %collective-permute-start.11) | collective-permute-done | bytes 565280 | tf_op jit(solution)/shard_map/ppermute | solution.py:422
  137.1 0.8 copy-done.14
  137.9 4.0 %collective-permute-done.12.beside_ref.refs_5_ = bf16[23,64,384]{2,1,0:T(8,128)(2,1)S(1)} collective-permute-done((bf16[23,64,384]{2,1,0:T(8,128)(2,1)}, bf16[23,64,384]{2,1,0:T(8,128)(2,1)S(1)}, u32[]{:S(2)}, u32[]{:S(2)}) %collective-permute-start.12) | collective-permute-done | bytes 1130528 | tf_op jit(solution)/shard_map/ppermute | solution.py:419
  141.9 3.1 %left_major.3.refs_1_ = bf16[64,96,256]{2,1,0:T(8,128)(2,1)S(1)} custom-call(bf16[23,64,384]{2,1,0:T(8,128)(2,1)} %collective-permute-done.7.refs_4_.own_ref, bf16[23,64,384]{2,1,0:T(8,128)(2,1)S(1)} %collective-permute-done.12.beside_ref.refs_5_), custom_call_target="tpu_custom_call" | custom-call | bytes 4521984 | tf_op jit(solution)/shard_map/left_major/pallas_call | solution.py:116
  145.0 1.7 copy-done.1
  146.7 9.0 %triangle.7 = (bf16[64,96,128]{2,1,0:T(8,128)(2,1)}, bf16[64,48,128]{2,1,0:T(8,128)(2,1)}, bf16[64,48,128]{2,1,0:T(8,128)(2,1)}) custom-call(s32[2]{0:T(128)S(1)} %pad_add_fusion.2.flag_ref, bf16[64,96,256]{2,1,0:T(8,128)(2,1)} %copy-done, bf16[64,96,256]{2,1,0:T(8,128)(2,1)} %copy-done.1, bf16[23,64,384]{2,1,0:T(8,128)(2,1)} %collective-permute-done.9.refs_2_, ...), custom_call_target="tpu_custom_call" | custom-call | flops 805306368 | bytes 5652480 | tf_op jit(solution)/shard_map/triangle/pallas_call | solution.py:180
  155.7 4.1 %collective-permute-start.14 = (bf16[64,96,128]{2,1,0:T(8,128)(2,1)}, bf16[64,96,128]{2,1,0:T(8,128)(2,1)}, u32[]{:S(2)}, u32[]{:S(2)}) collective-permute-start(bf16[64,96,128]{2,1,0:T(8,128)(2,1)} %get-tuple-element.46.refs_2_), channel_id=1, source_target_pairs={{1,0},{3,2},{4,5},{6,7},{9,8},{11,10},{12,13},{14,15},{17,16},{19,... | collective-permute-start | bytes 4718600 | tf_op jit(solution)/shard_map/ppermute | solution.py:429
  159.8 0.7 collective-permute-start.15
  160.5 1.6 collective-permute-start.16
  162.1 0.1 copy.22
  162.2 0.1 copy.37
  162.3 1.1 copy.23
  163.4 1.0 copy.24
  164.5 3.0 %fold.5 = bf16[23,96,128]{2,1,0:T(8,128)(2,1)S(1)} custom-call(s32[1]{0:T(128)} %bitcast.9.role_ref, bf16[64,48,128]{2,1,0:T(8,128)(2,1)} %get-tuple-element.48.refs_0_, bf16[64,48,128]{2,1,0:T(8,128)(2,1)S(1)} %collective-permute-done.15.refs_1_, bf16[64,48,128]{2,1,0:T(8,128)(2,1)} %get-tuple-element.49.refs_2_, ...), custom_call_target="tpu_custom_call" | custom-call | bytes 2359296 | tf_op jit(solution)/shard_map/fold/pallas_call | solution.py:233
  167.5 1.3 collective-permute-start.17
  168.9 1.5 collective-permute-start.19
  170.4 3.5 %fold.4 = (bf16[23,96,128]{2,1,0:T(8,128)(2,1)S(1)}, bf16[23,96,128]{2,1,0:T(8,128)(2,1)S(1)}) custom-call(s32[1]{0:T(128)} %bitcast.2.role_ref, bf16[64,96,128]{2,1,0:T(8,128)(2,1)} %triangle.4.refs_0_, bf16[64,96,128]{2,1,0:T(8,128)(2,1)} %collective-permute-done.5.refs_1_, bf16[64,96,128]{2,1,0:T(8,128)(2,1)S(1)} %copy-done.11, ...), custom_call_target="tpu_custom_call" | custom-call | bytes 4718592 | tf_op jit(solution)/shard_map/fold/pallas_call | solution.py:233
  173.9 1.3 collective-permute-start.18
  175.3 11.9 %finish.2.refs_4_ = bf16[2,23,96,128]{3,2,1,0:T(8,128)(2,1)S(1)} custom-call(s32[1]{0:T(128)} %bitcast.14.flag_ref, bf16[2,23,184,128]{3,2,1,0:T(8,128)(2,1)S(1)} %bitcast.21, bf16[23,96,128]{2,1,0:T(8,128)(2,1)S(1)} %copy-done.13, bf16[23,96,128]{2,1,0:T(8,128)(2,1)S(1)} %copy-done.15, bf16[128,128]{1,0:T(8,128)(2,1)S(1)} %bitcast.27, ...), custom_call_target="tpu_custom_call" | custom-call | flops 1941438464 | bytes 4333568 | tf_op jit(solution)/shard_map/finish/pallas_call | solution.py:300
  187.3 4.7 %collective-permute-done.18 = bf16[23,96,128]{2,1,0:T(8,128)(2,1)S(1)} collective-permute-done((bf16[23,96,128]{2,1,0:T(8,128)(2,1)S(1)}, bf16[23,96,128]{2,1,0:T(8,128)(2,1)S(1)}, u32[]{:S(2)}, u32[]{:S(2)}) %collective-permute-start.18) | collective-permute-done | bytes 565280 | tf_op jit(solution)/shard_map/ppermute | solution.py:422
  192.0 13.4 %finish.3 = bf16[2,23,184,128]{3,2,1,0:T(8,128)(2,1)} custom-call(s32[1]{0:T(128)} %bitcast.flag_ref, bf16[2,23,184,128]{3,2,1,0:T(8,128)(2,1)S(1)} %bitcast.22, bf16[23,96,128]{2,1,0:T(8,128)(2,1)S(1)} %broadcast_select_fusion.4.own_ref, bf16[23,96,128]{2,1,0:T(8,128)(2,1)S(1)} %broadcast_select_fusion.3.other_ref, bf16[128,128]{1,0:T(8,128)(2,1)S(1)} %bitcast.28, ...), custom_call_target="tpu_custom_call" | custom-call | flops 1941438464 | bytes 4333568 | tf_op jit(solution)/shard_map/finish/pallas_call | solution.py:300
  (58 shorter events, 1.3 us)
Async XLA Ops:
  0.0 2.5 %copy-start.17 = (s32[5]{0:T(128)S(1)}, s32[5]{0:T(128)}, u32[]{:S(2)}) copy-start(s32[5]{0:T(128)} %param.7) | copy-start | bytes 64
  3.7 1.6 copy-start.2
  5.4 13.1 %copy-start.3 = (bf16[46,184,128]{2,1,0:T(8,128)(2,1)S(1)}, bf16[46,184,128]{2,1,0:T(8,128)(2,1)}, u32[]{:S(2)}) copy-start(bf16[46,184,128]{2,1,0:T(8,128)(2,1)} %param.6) | copy-start | bytes 6500356
  11.2 11.7 %collective-permute-start = (bf16[23,64,384]{2,1,0:T(8,128)(2,1)}, bf16[23,64,384]{2,1,0:T(8,128)(2,1)}, u32[]{:S(2)}, u32[]{:S(2)}) collective-permute-start(bf16[23,64,384]{2,1,0:T(8,128)(2,1)} %get-tuple-element.35.refs_1_), channel_id=1, source_target_pairs={{4,8},{6,10},{8,4},{10,6},{5,9},{7,11},{9,5},{11,7},{20,24},{22,26... | collective-permute-start | bytes 3391496 | tf_op jit(solution)/shard_map/ppermute | solution.py:419
  12.8 27.0 %collective-permute-start.1 = (bf16[23,64,384]{2,1,0:T(8,128)(2,1)}, bf16[23,64,384]{2,1,0:T(8,128)(2,1)S(1)}, u32[]{:S(2)}, u32[]{:S(2)}) collective-permute-start(bf16[23,64,384]{2,1,0:T(8,128)(2,1)} %get-tuple-element.33), channel_id=1, source_target_pairs={{0,2},{2,0},{4,6},{6,4},{8,10},{10,8},{12,14},{14,12},{1,3},{3,1},... | collective-permute-start | bytes 3391496 | tf_op jit(solution)/shard_map/ppermute | solution.py:422
  14.9 27.2 %collective-permute-start.2 = (bf16[23,64,384]{2,1,0:T(8,128)(2,1)}, bf16[23,64,384]{2,1,0:T(8,128)(2,1)}, u32[]{:S(2)}, u32[]{:S(2)}) collective-permute-start(bf16[23,64,384]{2,1,0:T(8,128)(2,1)} %get-tuple-element.35.refs_1_), channel_id=1, source_target_pairs={{0,4},{2,6},{4,0},{6,2},{8,12},{10,14},{12,8},{14,10},{1,5},{3,7},... | collective-permute-start | bytes 3391496 | tf_op jit(solution)/shard_map/ppermute | solution.py:419
  22.9 24.4 %copy-start.9 = (bf16[23,64,384]{2,1,0:T(8,128)(2,1)}, bf16[23,64,384]{2,1,0:T(8,128)(2,1)S(1)}, u32[]{:S(2)}) copy-start(bf16[23,64,384]{2,1,0:T(8,128)(2,1)S(1)} %get-tuple-element.29.own_ref) | copy-start | bytes 3391492
  42.1 5.1 %collective-permute-start.6 = (bf16[23,64,384]{2,1,0:T(8,128)(2,1)S(1)}, bf16[23,64,384]{2,1,0:T(8,128)(2,1)S(1)}, u32[]{:S(2)}, u32[]{:S(2)}) collective-permute-start(bf16[23,64,384]{2,1,0:T(8,128)(2,1)S(1)} %collective-permute-done.1.refs_2_), channel_id=1, source_target_pairs={{4,8},{6,10},{8,4},{10,6},{5,9},{7,11},{9,5},{11,7},{20,24},{22,26... | collective-permute-start | bytes 3391496 | tf_op jit(solution)/shard_map/ppermute | solution.py:419
  42.8 24.7 %collective-permute-start.3 = (bf16[23,64,384]{2,1,0:T(8,128)(2,1)S(1)}, bf16[23,64,384]{2,1,0:T(8,128)(2,1)S(1)}, u32[]{:S(2)}, u32[]{:S(2)}) collective-permute-start(bf16[23,64,384]{2,1,0:T(8,128)(2,1)S(1)} %get-tuple-element.36), channel_id=1, source_target_pairs={{0,2},{2,0},{4,6},{6,4},{8,10},{10,8},{12,14},{14,12},{1,3},{3,1},... | collective-permute-start | bytes 3391496 | tf_op jit(solution)/shard_map/ppermute | solution.py:422
  43.2 27.1 %collective-permute-start.4 = (bf16[23,64,384]{2,1,0:T(8,128)(2,1)S(1)}, bf16[23,64,384]{2,1,0:T(8,128)(2,1)}, u32[]{:S(2)}, u32[]{:S(2)}) collective-permute-start(bf16[23,64,384]{2,1,0:T(8,128)(2,1)S(1)} %broadcast_select_fusion.2), channel_id=1, source_target_pairs={{0,4},{2,6},{4,0},{6,2},{8,12},{10,14},{12,8},{14,10},{1,5},{3,7},... | collective-permute-start | bytes 3391496 | tf_op jit(solution)/shard_map/ppermute | solution.py:419
  47.2 1.5 copy-start.4
  67.5 1.0 copy-start.6
  70.3 31.3 %collective-permute-start.9 = (bf16[23,64,384]{2,1,0:T(8,128)(2,1)}, bf16[23,64,384]{2,1,0:T(8,128)(2,1)}, u32[]{:S(2)}, u32[]{:S(2)}) collective-permute-start(bf16[23,64,384]{2,1,0:T(8,128)(2,1)} %collective-permute-done.2.refs_1_.refs_4_), channel_id=1, source_target_pairs={{4,8},{6,10},{8,4},{10,6},{5,9},{7,11},{9,5},{11,7},{20,24},{22,26... | collective-permute-start | bytes 3391496 | tf_op jit(solution)/shard_map/ppermute | solution.py:419
  72.0 29.6 %collective-permute-start.7 = (bf16[23,64,384]{2,1,0:T(8,128)(2,1)}, bf16[23,64,384]{2,1,0:T(8,128)(2,1)}, u32[]{:S(2)}, u32[]{:S(2)}) collective-permute-start(bf16[23,64,384]{2,1,0:T(8,128)(2,1)} %broadcast_select_fusion.1), channel_id=1, source_target_pairs={{0,4},{2,6},{4,0},{6,2},{8,12},{10,14},{12,8},{14,10},{1,5},{3,7},... | collective-permute-start | bytes 3391496 | tf_op jit(solution)/shard_map/ppermute | solution.py:419
  75.4 1.3 copy-start.7
  76.6 1.3 copy-start.10
  79.7 1.6 copy-start
  88.2 13.5 %copy-start.5 = (bf16[23,64,384]{2,1,0:T(8,128)(2,1)S(1)}, bf16[23,64,384]{2,1,0:T(8,128)(2,1)}, u32[]{:S(2)}) copy-start(bf16[23,64,384]{2,1,0:T(8,128)(2,1)} %copy-done.4) | copy-start | bytes 3391492
  88.2 30.3 %collective-permute-start.8 = (bf16[64,96,128]{2,1,0:T(8,128)(2,1)}, bf16[64,96,128]{2,1,0:T(8,128)(2,1)}, u32[]{:S(2)}, u32[]{:S(2)}) collective-permute-start(bf16[64,96,128]{2,1,0:T(8,128)(2,1)} %triangle.5.refs_0_), channel_id=1, source_target_pairs={{1,0},{3,2},{5,4},{7,6},{8,9},{10,11},{12,13},{14,15},{17,16},{19,... | collective-permute-start | bytes 4718600 | tf_op jit(solution)/shard_map/ppermute | solution.py:429
  101.6 10.5 %copy-start.8 = (bf16[23,64,384]{2,1,0:T(8,128)(2,1)S(1)}, bf16[23,64,384]{2,1,0:T(8,128)(2,1)}, u32[]{:S(2)}) copy-start(bf16[23,64,384]{2,1,0:T(8,128)(2,1)} %copy-done.6) | copy-start | bytes 3391492
  109.0 9.5 %collective-permute-start.10 = (bf16[64,96,128]{2,1,0:T(8,128)(2,1)}, bf16[64,96,128]{2,1,0:T(8,128)(2,1)}, u32[]{:S(2)}, u32[]{:S(2)}) collective-permute-start(bf16[64,96,128]{2,1,0:T(8,128)(2,1)} %triangle.6.refs_2_), channel_id=1, source_target_pairs={{0,1},{2,3},{4,5},{6,7},{9,8},{11,10},{13,12},{15,14},{16,17},{18,... | collective-permute-start | bytes 4718600 | tf_op jit(solution)/shard_map/ppermute | solution.py:429
  110.3 13.9 %collective-permute-start.5 = (bf16[64,96,128]{2,1,0:T(8,128)(2,1)}, bf16[64,96,128]{2,1,0:T(8,128)(2,1)}, u32[]{:S(2)}, u32[]{:S(2)}) collective-permute-start(bf16[64,96,128]{2,1,0:T(8,128)(2,1)} %triangle.4.refs_0_), channel_id=1, source_target_pairs={{5,4},{7,6},{8,9},{10,11},{21,20},{23,22},{24,25},{26,27}} | collective-permute-start | bytes 4718600 | tf_op jit(solution)/shard_map/ppermute | solution.py:429
  113.3 28.6 %collective-permute-start.12 = (bf16[23,64,384]{2,1,0:T(8,128)(2,1)}, bf16[23,64,384]{2,1,0:T(8,128)(2,1)S(1)}, u32[]{:S(2)}, u32[]{:S(2)}) collective-permute-start(bf16[23,64,384]{2,1,0:T(8,128)(2,1)} %broadcast_select_fusion), channel_id=1, source_target_pairs={{0,4},{2,6},{4,0},{6,2},{8,12},{10,14},{12,8},{14,10},{1,5},{3,7},... | collective-permute-start | bytes 3391496 | tf_op jit(solution)/shard_map/ppermute | solution.py:419
  116.8 29.9 %collective-permute-start.13 = (bf16[23,64,384]{2,1,0:T(8,128)(2,1)}, bf16[23,64,384]{2,1,0:T(8,128)(2,1)}, u32[]{:S(2)}, u32[]{:S(2)}) collective-permute-start(bf16[23,64,384]{2,1,0:T(8,128)(2,1)} %collective-permute-done.4.refs_2_.refs_3_), channel_id=1, source_target_pairs={{4,8},{6,10},{8,4},{10,6},{5,9},{7,11},{9,5},{11,7},{20,24},{22,26... | collective-permute-start | bytes 3391496 | tf_op jit(solution)/shard_map/ppermute | solution.py:419
  122.2 0.8 copy-start.12
  123.0 14.0 %collective-permute-start.11 = (bf16[23,96,128]{2,1,0:T(8,128)(2,1)S(1)}, bf16[23,96,128]{2,1,0:T(8,128)(2,1)S(1)}, u32[]{:S(2)}, u32[]{:S(2)}) collective-permute-start(bf16[23,96,128]{2,1,0:T(8,128)(2,1)S(1)} %get-tuple-element.42), channel_id=1, source_target_pairs={{0,2},{2,0},{4,6},{6,4},{8,10},{10,8},{12,14},{14,12},{1,3},{3,1},... | collective-permute-start | bytes 1695752 | tf_op jit(solution)/shard_map/ppermute | solution.py:422
  137.1 0.8 copy-start.14
  145.0 1.7 copy-start.1
  146.7 15.4 %copy-start.16 = (bf16[128,128]{1,0:T(8,128)(2,1)S(1)}, bf16[128,128]{1,0:T(8,128)(2,1)}, u32[]{:S(2)}) copy-start(bf16[128,128]{1,0:T(8,128)(2,1)} %param.9) | copy-start | bytes 98308
  155.7 14.7 %collective-permute-start.14 = (bf16[64,96,128]{2,1,0:T(8,128)(2,1)}, bf16[64,96,128]{2,1,0:T(8,128)(2,1)}, u32[]{:S(2)}, u32[]{:S(2)}) collective-permute-start(bf16[64,96,128]{2,1,0:T(8,128)(2,1)} %get-tuple-element.46.refs_2_), channel_id=1, source_target_pairs={{1,0},{3,2},{4,5},{6,7},{9,8},{11,10},{12,13},{14,15},{17,16},{19,... | collective-permute-start | bytes 4718600 | tf_op jit(solution)/shard_map/ppermute | solution.py:429
  159.8 4.7 %collective-permute-start.15 = (bf16[64,48,128]{2,1,0:T(8,128)(2,1)}, bf16[64,48,128]{2,1,0:T(8,128)(2,1)S(1)}, u32[]{:S(2)}, u32[]{:S(2)}) collective-permute-start(bf16[64,48,128]{2,1,0:T(8,128)(2,1)} %get-tuple-element.48.refs_0_), channel_id=1, source_target_pairs={{5,4},{7,6},{8,9},{10,11},{21,20},{23,22},{24,25},{26,27}} | collective-permute-start | bytes 2359304 | tf_op jit(solution)/shard_map/ppermute | solution.py:429
  160.5 4.0 %collective-permute-start.16 = (bf16[64,48,128]{2,1,0:T(8,128)(2,1)}, bf16[64,48,128]{2,1,0:T(8,128)(2,1)}, u32[]{:S(2)}, u32[]{:S(2)}) collective-permute-start(bf16[64,48,128]{2,1,0:T(8,128)(2,1)} %get-tuple-element.49.refs_2_), channel_id=1, source_target_pairs={{4,5},{6,7},{9,8},{11,10},{20,21},{22,23},{25,24},{27,26}} | collective-permute-start | bytes 2359304 | tf_op jit(solution)/shard_map/ppermute | solution.py:429
  164.5 5.9 %copy-start.11 = (bf16[64,96,128]{2,1,0:T(8,128)(2,1)S(1)}, bf16[64,96,128]{2,1,0:T(8,128)(2,1)}, u32[]{:S(2)}) copy-start(bf16[64,96,128]{2,1,0:T(8,128)(2,1)} %get-tuple-element.46.refs_2_) | copy-start | bytes 4718596
  167.5 19.7 %collective-permute-start.17 = (bf16[23,96,128]{2,1,0:T(8,128)(2,1)S(1)}, bf16[23,96,128]{2,1,0:T(8,128)(2,1)S(1)}, u32[]{:S(2)}, u32[]{:S(2)}) collective-permute-start(bf16[23,96,128]{2,1,0:T(8,128)(2,1)S(1)} %fold.5), channel_id=1, source_target_pairs={{5,1},{7,3},{8,12},{10,14},{21,17},{23,19},{24,28},{26,30}} | collective-permute-start | bytes 1695752 | tf_op jit(solution)/shard_map/ppermute | solution.py:437
  168.9 18.4 %collective-permute-start.19 = (bf16[23,96,128]{2,1,0:T(8,128)(2,1)S(1)}, bf16[23,96,128]{2,1,0:T(8,128)(2,1)S(1)}, u32[]{:S(2)}, u32[]{:S(2)}) collective-permute-start(bf16[23,96,128]{2,1,0:T(8,128)(2,1)S(1)} %fold.5), channel_id=1, source_target_pairs={{4,3},{6,1},{9,14},{11,12},{20,19},{22,17},{25,30},{27,28}} | collective-permute-start | bytes 1695752 | tf_op jit(solution)/shard_map/ppermute | solution.py:437
  170.4 4.9 %copy-start.13 = (bf16[23,96,128]{2,1,0:T(8,128)(2,1)S(1)}, bf16[23,96,128]{2,1,0:T(8,128)(2,1)}, u32[]{:S(2)}) copy-start(bf16[23,96,128]{2,1,0:T(8,128)(2,1)} %copy-done.12) | copy-start | bytes 1695748
  170.4 4.9 %copy-start.15 = (bf16[23,96,128]{2,1,0:T(8,128)(2,1)S(1)}, bf16[23,96,128]{2,1,0:T(8,128)(2,1)}, u32[]{:S(2)}) copy-start(bf16[23,96,128]{2,1,0:T(8,128)(2,1)} %copy-done.14) | copy-start | bytes 1695748
  173.9 18.0 %collective-permute-start.18 = (bf16[23,96,128]{2,1,0:T(8,128)(2,1)S(1)}, bf16[23,96,128]{2,1,0:T(8,128)(2,1)S(1)}, u32[]{:S(2)}, u32[]{:S(2)}) collective-permute-start(bf16[23,96,128]{2,1,0:T(8,128)(2,1)S(1)} %get-tuple-element.50), channel_id=1, source_target_pairs={{0,2},{2,0},{4,6},{6,4},{8,10},{10,8},{12,14},{14,12},{1,3},{3,1},... | collective-permute-start | bytes 1695752 | tf_op jit(solution)/shard_map/ppermute | solution.py:422

commit v8 on v7

--- a/solution.py
+++ b/solution.py
@@ -24,8 +24,8 @@
     return pl.CostEstimate(flops=flops, bytes_accessed=moved, transcendentals=transcendentals)
 
 
-def sigmoid(values):
-    return 0.5 * jnp.tanh(0.5 * values) + 0.5
+def twice_sigmoid(halved):
+    return jnp.tanh(halved) + 1.0
 
 
 def norm_chans(values):
@@ -59,7 +59,7 @@
         both = jnp.dot(weight_ref[...], normed, preferred_element_type=F32)
         limits = [jnp.where(row0 + h * half + r < valid, valid, 0) for h in range(2)]
         keep = jnp.where(token < limits[1] + is_first * (limits[0] - limits[1]), 1.0, 0.0)
-        out = (sigmoid(both[:width]) * both[width:] * keep).astype(BF16)
+        out = (twice_sigmoid(both[:width]) * both[width:] * keep).astype(BF16)
         own_ref[r] = out[:chans]
         far_ref[r] = out[chans:]
         return carry
@@ -125,10 +125,11 @@
     )(own, beside)
 
 
-def triangle_kernel(flag_ref, *refs, guests, options):
-    lefts = refs[: 1 + guests]
-    rights = refs[1 + guests : 1 + guests + 2 * options]
-    outs, right_ref = refs[1 + guests + 2 * options : -1], refs[-1]
+def triangle_kernel(flag_ref, left_ref, *refs, guests, options):
+    guest_refs = refs[:guests]
+    rights = refs[guests : guests + 2 * options]
+    outs = refs[guests + 2 * options : -1 - bool(guests)]
+    right_ref = refs[-1]
     own, beside = rights[0][...], rights[1][...]
     if options == 2:
         plain = flag_ref[1] == 0
@@ -147,24 +148,29 @@
 
     right_ref[:, :rows, :width] = main
     right_ref[:, :rows, width:] = rest
+    if guests:
+        guest_ref = refs[-2]
+        main, rest = channel_major([ref[...] for ref in guest_refs], True)
+        guest_ref[:, :, :width] = main
+        guest_ref[:, :, width:] = rest
+
+    def product(rows):
+        dims = (((1,), (1,)), ((), ()))
+        return lax.dot_general(rows, right_ref[c], dims, preferred_element_type=F32).astype(BF16)
+
     for c in range(CHUNK):
-        products = [
-            lax.dot_general(
-                left_ref[c], right_ref[c], (((1,), (1,)), ((), ())), preferred_element_type=F32
-            ).astype(BF16)
-            for left_ref in lefts
-        ]
-        outs[0][c] = products[0]
+        outs[0][c] = product(left_ref[c])
         if guests:
-            part = products[1].shape[0] // 2
-            outs[1][c] = products[1][:part]
-            outs[2][c] = products[1][part:]
-
-
-def triangle(flags, lefts, *pieces):
+            lent = product(guest_ref[c])
+            part = lent.shape[0] // guests
+            for g in range(guests):
+                outs[1 + g][c] = lent[g * part : (g + 1) * part]
+
+
+def triangle(flags, left, pieces, guests=()):
     half, chans, lanes = pieces[0].shape
-    options, guests = len(pieces) // 2, len(lefts) - 1
-    rows, cols, deep = lefts[0].shape[1], padded(4 * half, 128), lanes // 3 * 2
+    options = len(pieces) // 2
+    rows, cols, deep = left.shape[1], padded(4 * half, 128), lanes // 3 * 2
 
     def piece(option):
         if options == 1:
@@ -176,21 +182,25 @@
     def block(height, depth):
         return pl.BlockSpec((CHUNK, height, depth), lambda c, flag_ref: (c, 0, 0))
 
-    heights = [rows] + [rows // 2] * (2 * guests)
+    every = pl.BlockSpec((half, CHUNK, lanes), lambda c, flag_ref: (0, c, 0))
+    heights = [rows] + [rows // 2] * len(guests)
+    work = [VMEM((CHUNK, rows, deep), BF16)] if guests else []
     return pl.pallas_call(
-        functools.partial(triangle_kernel, guests=guests, options=options),
+        functools.partial(triangle_kernel, guests=len(guests), options=options),
         grid_spec=pltpu.PrefetchScalarGridSpec(
             num_scalar_prefetch=1,
             grid=(chans // CHUNK,),
-            in_specs=[block(rows, deep)] * len(lefts) + [piece(i // 2) for i in range(len(pieces))],
+            in_specs=[block(rows, deep)]
+            + [every] * len(guests)
+            + [piece(i // 2) for i in range(len(pieces))],
             out_specs=[block(h, cols) for h in heights],
-            scratch_shapes=[VMEM((CHUNK, cols, deep), BF16)],
+            scratch_shapes=work + [VMEM((CHUNK, cols, deep), BF16)],
         ),
         out_shape=[jax.ShapeDtypeStruct((chans, h, cols), BF16) for h in heights],
         compiler_params=params(),
-        cost_estimate=cost(2 * len(lefts) * chans * rows * cols * deep, 10 * pieces[0].size),
+        cost_estimate=cost(2 * chans * sum(heights) * cols * deep, 10 * pieces[0].size),
         name="triangle",
-    )(flags, *lefts, *pieces)
+    )(flags, left, *guests, *pieces)
 
 
 def fold_kernel(role_ref, *refs, outputs, half):
@@ -198,9 +208,10 @@
     cols = outs[0].shape[1]
     parts = refs[: -1 - outputs]
     c = pl.program_id(0)
-    for option in range(2):
-
-        @pl.when(role_ref[0] == option)
+    options = len(parts) // 2
+    for option in range(options):
+
+        @pl.when((options == 1) | (role_ref[0] == option))
         def _(option=option):
             total = parts[2 * option][...].astype(F32) + parts[2 * option + 1][...].astype(F32)
             at = pl.ds(pl.multiple_of(c * CHUNK, CHUNK), CHUNK)
@@ -227,7 +238,10 @@
 
     def block(option):
         return pl.BlockSpec(
-            (CHUNK, rows, cols), lambda c, role_ref: (jnp.where(role_ref[0] == option, c, 0), 0, 0)
+            (CHUNK, rows, cols),
+            lambda c, role_ref: (
+                c if len(parts) == 2 else jnp.where(role_ref[0] == option, c, 0), 0, 0
+            ),
         )
 
     return pl.pallas_call(
@@ -235,7 +249,7 @@
         grid_spec=pltpu.PrefetchScalarGridSpec(
             num_scalar_prefetch=1,
             grid=(chans // CHUNK,),
-            in_specs=[block(i // 2) for i in range(4)],
+            in_specs=[block(i // 2) for i in range(len(parts))],
             out_specs=[pl.BlockSpec(out.shape, lambda c, role_ref: (0, 0, 0))] * outputs,
             scratch_shapes=[VMEM((rows, chans, cols), BF16)],
         ),
@@ -271,13 +285,13 @@
             pair.append(jnp.where(front, row[:block], row[block:]))
         pair = jnp.concatenate(pair, axis=0).T
         normed = norm_chans(pair).astype(BF16)
-        out_gate = sigmoid(jnp.dot(gate_ref[...], normed, preferred_element_type=F32))
+        out_gate = twice_sigmoid(jnp.dot(gate_ref[...], normed, preferred_element_type=F32))
         update = jnp.dot(out_w_ref[...], tri_normed, preferred_element_type=F32)
         updated = pair + out_gate * update
         trans_normed = norm_chans(updated).astype(BF16)
         expanded = jnp.dot(in_ref[...], trans_normed, preferred_element_type=F32)
         swish, linear = expanded[:hidden_units], expanded[hidden_units:]
-        hidden = (swish * sigmoid(swish) * linear).astype(BF16)
+        hidden = (swish * twice_sigmoid(swish) * linear).astype(BF16)
         result = updated + jnp.dot(back_ref[...], hidden, preferred_element_type=F32)
         result = result.T
         for s, (h, r) in enumerate(rows):
@@ -290,7 +304,7 @@
                 out_ref[h, r] = jnp.concatenate(parts, axis=0).astype(BF16)
         return carry
 
-    lax.fori_loop(0, steps, step, 0, unroll=2)
+    lax.fori_loop(0, steps, step, 0, unroll=4)
 
 
 def finish(flag, pair, own, other, weights, earlier=None):
@@ -436,6 +450,13 @@
             perm += [(4 * s + 2 * b + source, 4 * t + 2 * (b ^ swap) + away) for b in range(2)]
         return lax.ppermute(value, ("row", "col"), perm)
 
+    def late_across(value):
+        perm = []
+        for z in range(4):
+            holder = 1 - z // 2 if z in (1, 2) else z // 2
+            perm += [(4 * z + 2 * b + holder, 4 * z + 2 * (1 - b) + holder) for b in range(2)]
+        return lax.ppermute(value, ("row", "col"), perm)
+
     def by_side(block, axis):
         return jnp.where(side == 0, block, jnp.roll(block, width // 2, axis))
 
@@ -443,7 +464,7 @@
         parts = [
             by_side(in_weight[:, (first + i) * width : (first + i + 1) * width], 1) for i in range(2)
         ]
-        return jnp.concatenate(parts, axis=1).T
+        return jnp.concatenate(parts, axis=1).T * BF16(0.5)
 
     def after(value, *others):
         return lax.optimization_barrier((value, *others))[0]
@@ -479,40 +500,53 @@
     mate_beside, near_beside, left_beside = two
     three = phase([(swap, either(near_beside, left_own)), (hop(cross), mate_own)], two)
     guest_own, far_own = three
+
     left = left_major(left_own, left_beside)
-    (home,) = triangle(scalars(side, 0), [left], right_own, right_beside)
+    plain, outer = scalars(side, 0), scalars(side, jnp.where(inner, 0, 1))
+    (home,) = triangle(plain, left, [right_own, right_beside])
     home_rest = to_core(home, everyone, [True] * 4)
-    (mate,) = triangle(scalars(side, 0), [left], mate_own, mate_beside)
+    (mate,) = triangle(plain, left, [mate_own, mate_beside])
     mate_rest = to_core(mate, inners, [True] * 2)
-    four = phase([(swap, either(right_beside, left_beside)), (hop(cross), mate_beside)], three + [home, mate])
+    four = phase(
+        [(swap, either(right_beside, left_beside)), (hop(cross), mate_beside)], three + [home, mate]
+    )
+    (away,) = triangle(
+        outer, left, [after(near_own, far_own, mate), near_beside, mate_beside, guest_own]
+    )
     guest_beside, far_beside = four
-
-    outer = scalars(side, jnp.where(inner, 0, 1))
-    (away,) = triangle(
-        outer, [left], after(near_own, far_own, mate), near_beside, mate_beside, guest_own
-    )
     away_rest = to_core(away, everyone, [False] * 4)
-    first = fold(half, scalars(jnp.where(is_keeper, 0, 1)), home, home_rest, away, away_rest)
-
+    role = scalars(jnp.where(is_keeper, 0, 1))
+    first = fold(half, role, home, home_rest, away, away_rest)
     first_other = across(first[1])
-    left_guest = left_major(after(guest_own, first_other, mate_rest), guest_beside)
+    mate_block = fold(half, role, mate, mate_rest)
+    mate_other = across(mate_block[1])
+
     late, lent_own, lent_beside = triangle(
-        outer, [left, left_guest], far_own, far_beside, mate_own, guest_beside
+        outer,
+        left,
+        [after(far_own, first_other, mate_other), far_beside, mate_own, guest_beside],
+        [guest_own, guest_beside],
     )
     lent_rest = to_core(lent_own, inners, [False] * 2), to_core(lent_beside, inners, [True] * 2)
     late_rest = to_core(late, everyone, [True, False, False, True])
-    (lent,) = fold(
-        half, scalars(jnp.where(is_keeper, 0, 1)), lent_beside, lent_rest[1], lent_own, lent_rest[0]
-    )
+    (lent,) = fold(half, role, lent_beside, lent_rest[1], lent_own, lent_rest[0])
     given = give_back(lent, 0), give_back(lent, 1)
-    second = fold(half, scalars(jnp.where(is_keeper & inner, 0, 1)), mate, mate_rest, late, late_rest)
+    late_block = fold(half, role, late, late_rest)
+    late_other = late_across(late_block[1])
 
     order = jnp.where(is_keeper, place % 2, place // 2)
-    weights = [w.T for w in (in_weight[:, 4 * width :], by_side(out_weight, 0), trans_in, trans_out)]
+    weights = [
+        in_weight[:, 4 * width :].T * BF16(0.5),
+        by_side(out_weight, 0).T * BF16(0.5),
+        jnp.where(jnp.arange(trans_in.shape[1])[:, None] < trans_out.shape[0], BF16(0.5), BF16(1.0))
+        * trans_in.T,
+        trans_out.T,
+    ]
     earlier = finish(scalars(order), folded, after(first[0], lent), first_other, weights)
-    kept = is_keeper | inner
-    own = jnp.where(kept, second[0], given[0])
-    other = jnp.where(kept, across(second[1]), given[1])
+    own, other = (
+        jnp.where(inner & is_keeper, early, jnp.where(inner | is_keeper, end, back))
+        for early, end, back in zip((mate_block[0], mate_other), (late_block[0], late_other), given)
+    )
     result = finish(scalars(1 - order), folded, own, other, weights, earlier)
     return result.reshape(tile_rows, tile_cols, width)
 

time: 207 us -> 211 us (1.019)
  the two profiles are of different devices: /device:TPU:1 before, /device:TPU:9 now
where the time goes in v8:
time: 211 us; the launch traced here: 210 us
  Pallas kernels  79.5 us (38%)
  waiting for transfers between devices  62.8 us (30%)
  starting transfers between devices  41 us (19%)
  local copies, waits for them, and re-layouts  18.8 us (9%)
  other arithmetic  6.54 us (3%)
    ppermute x8, waiting for transfers between devices, among(): lax.ppermute(value, 'row', [(2 * s + b, 2 * t + b) for s, t in moves for...  40.3 us
    pallas_call x4, Pallas kernels, triangle(): pl.pallas_call(functools.partial(triangle_kernel, guests=len(guests), opt...  30.2 us
    pallas_call x2, Pallas kernels, finish(): pl.pallas_call(finish_kernel, out_shape=jax.ShapeDtypeStruct(shape, BF16)...  22.8 us
    ppermute x4, waiting for transfers between devices, across(): return lax.ppermute(value, 'row', [(i, i ^ 1) for i in range(8)])  21.1 us
    ppermute x6, starting transfers between devices, to_core(): return lax.ppermute(value, ('row', 'col'), perm)  17.3 us
    unnamed x58, local copies, waits for them, and re-layouts  15.6 us
    pallas_call x4, Pallas kernels, fold(): pl.pallas_call(functools.partial(fold_kernel, outputs=outputs, half=half)...  14.6 us
    ppermute x8, starting transfers between devices, among(): lax.ppermute(value, 'row', [(2 * s + b, 2 * t + b) for s, t in moves for...  12.8 us
  transfers between devices with their start and end apart: 21, of which 6 were waited for; matrix products, arithmetic and copies ran while one was open for 4% of the time, Pallas kernels for 25%

profile of v8, /device:TPU:9, one launch (start us, length us, event | category | flops | bytes accessed | tf_op | source)
XLA Modules:
  0.0 209.8 jit_solution(16210856536907587569)
XLA Ops:
  0.0 0.8 fusion.5
  0.8 1.0 fusion.6
  1.8 1.2 slice.60
  3.4 0.1 copy.34
  4.4 1.6 copy-done.1
  6.0 5.8 %project.3 = (bf16[23,64,384]{2,1,0:T(8,128)(2,1)}, bf16[23,64,384]{2,1,0:T(8,128)(2,1)}) custom-call(s32[3]{0:T(128)S(1)} %pad_add_fusion.1.where_ref, bf16[2,23,184,128]{3,2,1,0:T(8,128)(2,1)S(1)} %bitcast.20, bf16[256,128]{1,0:T(8,128)(2,1)S(1)} %fusion.1.weight_ref), custom_call_target="tpu_custom_call" | custom-call | flops 554696704 | bytes 4333568 | tf_op jit(solution)/shard_map/project/pallas_call | solution.py:73
  11.8 3.2 %collective-permute-start = (bf16[23,64,384]{2,1,0:T(8,128)(2,1)}, bf16[23,64,384]{2,1,0:T(8,128)(2,1)}, u32[]{:S(2)}, u32[]{:S(2)}) collective-permute-start(bf16[23,64,384]{2,1,0:T(8,128)(2,1)} %get-tuple-element.37.refs_0_), channel_id=1, source_target_pairs={{4,8},{6,10},{8,4},{10,6},{5,9},{7,11},{9,5},{11,7},{20,24},{22,26... | collective-permute-start | bytes 3391496 | tf_op jit(solution)/shard_map/ppermute | solution.py:433
  15.0 1.3 collective-permute-start.1
  16.3 0.7 copy.25
  17.2 0.1 copy.28
  17.6 0.8 maximum_select_fusion
  18.4 4.3 %project.2 = (bf16[23,64,384]{2,1,0:T(8,128)(2,1)S(1)}, bf16[23,64,384]{2,1,0:T(8,128)(2,1)S(1)}) custom-call(s32[3]{0:T(128)S(1)} %pad_add_fusion.1.where_ref, bf16[2,23,184,128]{3,2,1,0:T(8,128)(2,1)S(1)} %bitcast.21, bf16[256,128]{1,0:T(8,128)(2,1)S(1)} %fusion.weight_ref), custom_call_target="tpu_custom_call" | custom-call | flops 554696704 | bytes 4333568 | tf_op jit(solution)/shard_map/project/pallas_call | solution.py:73
  22.8 17.1 %collective-permute-done.refs_0_ = bf16[23,64,384]{2,1,0:T(8,128)(2,1)} collective-permute-done((bf16[23,64,384]{2,1,0:T(8,128)(2,1)}, bf16[23,64,384]{2,1,0:T(8,128)(2,1)}, u32[]{:S(2)}, u32[]{:S(2)}) %collective-permute-start) | collective-permute-done | bytes 1130528 | tf_op jit(solution)/shard_map/ppermute | solution.py:433
  39.8 1.1 collective-permute-done.1.refs_1_
  40.9 1.5 broadcast_select_fusion.2
  42.4 2.1 %collective-permute-start.6 = (bf16[23,64,384]{2,1,0:T(8,128)(2,1)S(1)}, bf16[23,64,384]{2,1,0:T(8,128)(2,1)S(1)}, u32[]{:S(2)}, u32[]{:S(2)}) collective-permute-start(bf16[23,64,384]{2,1,0:T(8,128)(2,1)S(1)} %collective-permute-done.1.refs_1_), channel_id=1, source_target_pairs={{4,8},{6,10},{8,4},{10,6},{5,9},{7,11},{9,5},{11,7},{20,24},{22,26... | collective-permute-start | bytes 3391496 | tf_op jit(solution)/shard_map/ppermute | solution.py:433
  44.5 1.3 collective-permute-start.3
  45.8 23.2 %collective-permute-done.6.refs_1_ = bf16[23,64,384]{2,1,0:T(8,128)(2,1)S(1)} collective-permute-done((bf16[23,64,384]{2,1,0:T(8,128)(2,1)S(1)}, bf16[23,64,384]{2,1,0:T(8,128)(2,1)S(1)}, u32[]{:S(2)}, u32[]{:S(2)}) %collective-permute-start.6) | collective-permute-done | bytes 1130528 | tf_op jit(solution)/shard_map/ppermute | solution.py:433
  69.0 1.3 broadcast_select_fusion.1
  70.4 1.0 copy-done.5
  71.4 2.2 %collective-permute-start.8 = (bf16[23,64,384]{2,1,0:T(8,128)(2,1)}, bf16[23,64,384]{2,1,0:T(8,128)(2,1)}, u32[]{:S(2)}, u32[]{:S(2)}) collective-permute-start(bf16[23,64,384]{2,1,0:T(8,128)(2,1)} %collective-permute-done.2.refs_0_.refs_4_), channel_id=1, source_target_pairs={{4,8},{6,10},{8,4},{10,6},{5,9},{7,11},{9,5},{11,7},{20,24},{22,26... | collective-permute-start | bytes 3391496 | tf_op jit(solution)/shard_map/ppermute | solution.py:433
  73.9 1.3 copy-done.6
  75.1 1.3 copy-done.9
  76.4 1.8 left_major.1.left_ref
  78.2 1.6 copy-done
  79.8 7.0 %triangle.4.refs_0_ = bf16[64,96,128]{2,1,0:T(8,128)(2,1)} custom-call(s32[2]{0:T(128)S(1)} %pad_add_fusion.flag_ref, bf16[64,96,256]{2,1,0:T(8,128)(2,1)} %copy-done, bf16[23,64,384]{2,1,0:T(8,128)(2,1)} %collective-permute-done.2.refs_0_.refs_4_, bf16[23,64,384]{2,1,0:T(8,128)(2,1)} %collective-permute-done.4.refs_1_.refs_2_), custom_call_target="tpu_custom_call" | custom-call | flops 402653184 | bytes 5652480 | tf_op jit(solution)/shard_map/triangle/pallas_call | solution.py:188
  86.8 6.2 %collective-permute-start.5 = (bf16[64,96,128]{2,1,0:T(8,128)(2,1)}, bf16[64,96,128]{2,1,0:T(8,128)(2,1)}, u32[]{:S(2)}, u32[]{:S(2)}) collective-permute-start(bf16[64,96,128]{2,1,0:T(8,128)(2,1)} %triangle.4.refs_0_), channel_id=1, source_target_pairs={{5,4},{7,6},{8,9},{10,11},{21,20},{23,22},{24,25},{26,27}} | collective-permute-start | bytes 4718600 | tf_op jit(solution)/shard_map/ppermute | solution.py:443
  93.0 6.9 %triangle.5.refs_0_ = bf16[64,96,128]{2,1,0:T(8,128)(2,1)} custom-call(s32[2]{0:T(128)S(1)} %pad_add_fusion.flag_ref, bf16[64,96,256]{2,1,0:T(8,128)(2,1)} %copy-done, bf16[23,64,384]{2,1,0:T(8,128)(2,1)} %get-tuple-element.37.refs_0_, bf16[23,64,384]{2,1,0:T(8,128)(2,1)S(1)} %collective-permute-done.1.refs_1_), custom_call_target="tpu_custom_call" | custom-call | flops 402653184 | bytes 5652480 | tf_op jit(solution)/shard_map/triangle/pallas_call | solution.py:188
  99.9 2.6 %collective-permute-start.10 = (bf16[64,96,128]{2,1,0:T(8,128)(2,1)}, bf16[64,96,128]{2,1,0:T(8,128)(2,1)}, u32[]{:S(2)}, u32[]{:S(2)}) collective-permute-start(bf16[64,96,128]{2,1,0:T(8,128)(2,1)} %triangle.5.refs_0_), channel_id=1, source_target_pairs={{1,0},{3,2},{5,4},{7,6},{8,9},{10,11},{12,13},{14,15},{17,16},{19,... | collective-permute-start | bytes 4718600 | tf_op jit(solution)/shard_map/ppermute | solution.py:443
  102.5 7.3 %triangle.6.refs_2_ = bf16[64,96,128]{2,1,0:T(8,128)(2,1)} custom-call(s32[2]{0:T(128)S(1)} %pad_add_fusion.2.flag_ref, bf16[64,96,256]{2,1,0:T(8,128)(2,1)} %copy-done, bf16[23,64,384]{2,1,0:T(8,128)(2,1)} %collective-permute-done.refs_0_, bf16[23,64,384]{2,1,0:T(8,128)(2,1)S(1)} %copy-done.4, bf16[23,64,384]{2,1,0:T(8,128)(2,1)} %collective-permute-done.4.refs_1_.refs_2_, ...), custom_call_target="tpu_custom_call" | custom-call | flops 402653184 | bytes 5652480 | tf_op jit(solution)/shard_map/triangle/pallas_call | solution.py:188
  109.8 1.3 collective-permute-start.11
  111.1 1.2 broadcast_select_fusion
  112.2 1.2 collective-permute-start.9
  113.4 4.0 %collective-permute-start.14 = (bf16[23,64,384]{2,1,0:T(8,128)(2,1)}, bf16[23,64,384]{2,1,0:T(8,128)(2,1)}, u32[]{:S(2)}, u32[]{:S(2)}) collective-permute-start(bf16[23,64,384]{2,1,0:T(8,128)(2,1)} %collective-permute-done.4.refs_1_.refs_2_), channel_id=1, source_target_pairs={{4,8},{6,10},{8,4},{10,6},{5,9},{7,11},{9,5},{11,7},{20,24},{22,26... | collective-permute-start | bytes 3391496 | tf_op jit(solution)/shard_map/ppermute | solution.py:433
  117.5 3.4 %fold.4 = (bf16[23,96,128]{2,1,0:T(8,128)(2,1)S(1)}, bf16[23,96,128]{2,1,0:T(8,128)(2,1)S(1)}) custom-call(s32[1]{0:T(128)} %bitcast.2.role_ref, bf16[64,96,128]{2,1,0:T(8,128)(2,1)} %triangle.4.refs_0_, bf16[64,96,128]{2,1,0:T(8,128)(2,1)} %collective-permute-done.5.refs_1_), custom_call_target="tpu_custom_call" | custom-call | bytes 4718592 | tf_op jit(solution)/shard_map/fold/pallas_call | solution.py:247
  120.9 0.8 copy-done.11
  121.7 1.2 collective-permute-start.13
  123.0 3.7 %fold.5 = (bf16[23,96,128]{2,1,0:T(8,128)(2,1)S(1)}, bf16[23,96,128]{2,1,0:T(8,128)(2,1)S(1)}) custom-call(s32[1]{0:T(128)} %bitcast.2.role_ref, bf16[64,96,128]{2,1,0:T(8,128)(2,1)} %triangle.5.refs_0_, bf16[64,96,128]{2,1,0:T(8,128)(2,1)} %collective-permute-done.10.refs_1_, bf16[64,96,128]{2,1,0:T(8,128)(2,1)} %triangle.6.refs_2_, ...), custom_call_target="tpu_custom_call" | custom-call | bytes 4718592 | tf_op jit(solution)/shard_map/fold/pallas_call | solution.py:247
  126.7 0.8 copy-done.13
  127.5 0.2 collective-permute-start.12
  127.7 8.1 %collective-permute-done.13 = bf16[23,96,128]{2,1,0:T(8,128)(2,1)S(1)} collective-permute-done((bf16[23,96,128]{2,1,0:T(8,128)(2,1)S(1)}, bf16[23,96,128]{2,1,0:T(8,128)(2,1)S(1)}, u32[]{:S(2)}, u32[]{:S(2)}) %collective-permute-start.13) | collective-permute-done | bytes 565280 | tf_op jit(solution)/shard_map/ppermute | solution.py:436
  135.8 12.0 %collective-permute-done.12.other_ref = bf16[23,96,128]{2,1,0:T(8,128)(2,1)S(1)} collective-permute-done((bf16[23,96,128]{2,1,0:T(8,128)(2,1)S(1)}, bf16[23,96,128]{2,1,0:T(8,128)(2,1)S(1)}, u32[]{:S(2)}, u32[]{:S(2)}) %collective-permute-start.12) | collective-permute-done | bytes 565280 | tf_op jit(solution)/shard_map/ppermute | solution.py:436
  147.8 0.8 copy-done.15
  148.7 9.0 %triangle.7 = (bf16[64,96,128]{2,1,0:T(8,128)(2,1)}, bf16[64,48,128]{2,1,0:T(8,128)(2,1)}, bf16[64,48,128]{2,1,0:T(8,128)(2,1)}) custom-call(s32[2]{0:T(128)S(1)} %pad_add_fusion.2.flag_ref, bf16[64,96,256]{2,1,0:T(8,128)(2,1)} %copy-done, bf16[23,64,384]{2,1,0:T(8,128)(2,1)} %collective-permute-done.7.refs_3_.refs_0_, ...), custom_call_target="tpu_custom_call" | custom-call | flops 805306368 | bytes 5652480 | tf_op jit(solution)/shard_map/triangle/pallas_call | solution.py:188
  157.7 1.3 collective-permute-start.15
  159.0 4.4 %collective-permute-start.16 = (bf16[64,48,128]{2,1,0:T(8,128)(2,1)}, bf16[64,48,128]{2,1,0:T(8,128)(2,1)S(1)}, u32[]{:S(2)}, u32[]{:S(2)}) collective-permute-start(bf16[64,48,128]{2,1,0:T(8,128)(2,1)} %get-tuple-element.52.refs_0_), channel_id=1, source_target_pairs={{5,4},{7,6},{8,9},{10,11},{21,20},{23,22},{24,25},{26,27}} | collective-permute-start | bytes 2359304 | tf_op jit(solution)/shard_map/ppermute | solution.py:443
  163.3 1.5 collective-permute-start.17
  164.8 0.1 copy.37
  165.0 0.1 copy.22
  165.1 1.1 copy.23
  166.3 0.2 multiply_bitcast_fusion.refs_2_
  166.5 1.3 collective-permute-done.17.refs_3_
  167.9 3.6 %fold.7 = bf16[23,96,128]{2,1,0:T(8,128)(2,1)} custom-call(s32[1]{0:T(128)} %bitcast.2.role_ref, bf16[64,48,128]{2,1,0:T(8,128)(2,1)} %get-tuple-element.52.refs_0_, bf16[64,48,128]{2,1,0:T(8,128)(2,1)S(1)} %collective-permute-done.16.refs_1_, bf16[64,48,128]{2,1,0:T(8,128)(2,1)} %get-tuple-element.53.refs_2_, ...), custom_call_target="tpu_custom_call" | custom-call | bytes 2359296 | tf_op jit(solution)/shard_map/fold/pallas_call | solution.py:247
  171.5 2.1 collective-permute-start.18
  173.6 1.6 collective-permute-start.20
  175.2 3.9 %fold.6 = (bf16[23,96,128]{2,1,0:T(8,128)(2,1)S(1)}, bf16[23,96,128]{2,1,0:T(8,128)(2,1)}) custom-call(s32[1]{0:T(128)} %bitcast.2.role_ref, bf16[64,96,128]{2,1,0:T(8,128)(2,1)S(1)} %copy-done.10, bf16[64,96,128]{2,1,0:T(8,128)(2,1)} %collective-permute-done.15.refs_1_), custom_call_target="tpu_custom_call" | custom-call | bytes 4718592 | tf_op jit(solution)/shard_map/fold/pallas_call | solution.py:247
  179.1 3.2 %collective-permute-start.19 = (bf16[23,96,128]{2,1,0:T(8,128)(2,1)}, bf16[23,96,128]{2,1,0:T(8,128)(2,1)}, u32[]{:S(2)}, u32[]{:S(2)}) collective-permute-start(bf16[23,96,128]{2,1,0:T(8,128)(2,1)} %get-tuple-element.54), channel_id=1, source_target_pairs={{0,2},{2,0},{5,7},{7,5},{8,10},{10,8},{13,15},{15,13},{16,18},{18,... | collective-permute-start | bytes 1695752 | tf_op jit(solution)/shard_map/ppermute | solution.py:458
  182.5 0.1 copy.24
  182.6 1.0 copy-done.14
  183.7 1.1 copy-done.16
  184.7 10.6 %finish.2.refs_4_ = bf16[2,23,96,128]{3,2,1,0:T(8,128)(2,1)S(1)} custom-call(s32[1]{0:T(128)} %bitcast.13.flag_ref, bf16[2,23,184,128]{3,2,1,0:T(8,128)(2,1)S(1)} %bitcast.22, bf16[23,96,128]{2,1,0:T(8,128)(2,1)S(1)} %copy-done.14, bf16[23,96,128]{2,1,0:T(8,128)(2,1)S(1)} %copy-done.16, bf16[128,128]{1,0:T(8,128)(2,1)S(1)} %multiply_bitcast_fusion.1.refs_0_, ...), custom_call_target="tpu_custom_call" | custom-call | flops 1941438464 | bytes 4333568 | tf_op jit(solution)/shard_map/finish/pallas_call | solution.py:314
  195.4 0.9 copy-done.18
  196.4 1.1 select_select_fusion.other_ref
  197.5 12.3 %finish.3 = bf16[2,23,184,128]{3,2,1,0:T(8,128)(2,1)} custom-call(s32[1]{0:T(128)} %bitcast.flag_ref, bf16[2,23,184,128]{3,2,1,0:T(8,128)(2,1)S(1)} %bitcast.23, bf16[23,96,128]{2,1,0:T(8,128)(2,1)S(1)} %select_select_fusion.1.own_ref, bf16[23,96,128]{2,1,0:T(8,128)(2,1)S(1)} %select_select_fusion.other_ref, ...), custom_call_target="tpu_custom_call" | custom-call | flops 1941438464 | bytes 4333568 | tf_op jit(solution)/shard_map/finish/pallas_call | solution.py:314
  (69 shorter events, 1.7 us)
Async XLA Ops:
  4.4 1.6 copy-start.1
  6.0 12.4 %copy-start.2 = (bf16[46,184,128]{2,1,0:T(8,128)(2,1)S(1)}, bf16[46,184,128]{2,1,0:T(8,128)(2,1)}, u32[]{:S(2)}) copy-start(bf16[46,184,128]{2,1,0:T(8,128)(2,1)} %param.6) | copy-start | bytes 6500356
  11.8 28.0 %collective-permute-start = (bf16[23,64,384]{2,1,0:T(8,128)(2,1)}, bf16[23,64,384]{2,1,0:T(8,128)(2,1)}, u32[]{:S(2)}, u32[]{:S(2)}) collective-permute-start(bf16[23,64,384]{2,1,0:T(8,128)(2,1)} %get-tuple-element.37.refs_0_), channel_id=1, source_target_pairs={{4,8},{6,10},{8,4},{10,6},{5,9},{7,11},{9,5},{11,7},{20,24},{22,26... | collective-permute-start | bytes 3391496 | tf_op jit(solution)/shard_map/ppermute | solution.py:433
  15.0 25.8 %collective-permute-start.1 = (bf16[23,64,384]{2,1,0:T(8,128)(2,1)}, bf16[23,64,384]{2,1,0:T(8,128)(2,1)S(1)}, u32[]{:S(2)}, u32[]{:S(2)}) collective-permute-start(bf16[23,64,384]{2,1,0:T(8,128)(2,1)} %get-tuple-element.35), channel_id=1, source_target_pairs={{0,2},{2,0},{4,6},{6,4},{8,10},{10,8},{12,14},{14,12},{1,3},{3,1},... | collective-permute-start | bytes 3391496 | tf_op jit(solution)/shard_map/ppermute | solution.py:436
  16.3 26.0 %collective-permute-start.2 = (bf16[23,64,384]{2,1,0:T(8,128)(2,1)}, bf16[23,64,384]{2,1,0:T(8,128)(2,1)}, u32[]{:S(2)}, u32[]{:S(2)}) collective-permute-start(bf16[23,64,384]{2,1,0:T(8,128)(2,1)} %get-tuple-element.37.refs_0_), channel_id=1, source_target_pairs={{0,4},{2,6},{4,0},{6,2},{8,12},{10,14},{12,8},{14,10},{1,5},{3,7},... | collective-permute-start | bytes 3391496 | tf_op jit(solution)/shard_map/ppermute | solution.py:433
  22.8 46.2 %copy-start.8 = (bf16[23,64,384]{2,1,0:T(8,128)(2,1)}, bf16[23,64,384]{2,1,0:T(8,128)(2,1)S(1)}, u32[]{:S(2)}) copy-start(bf16[23,64,384]{2,1,0:T(8,128)(2,1)S(1)} %get-tuple-element.31.own_ref) | copy-start | bytes 3391492
  42.4 26.6 %collective-permute-start.6 = (bf16[23,64,384]{2,1,0:T(8,128)(2,1)S(1)}, bf16[23,64,384]{2,1,0:T(8,128)(2,1)S(1)}, u32[]{:S(2)}, u32[]{:S(2)}) collective-permute-start(bf16[23,64,384]{2,1,0:T(8,128)(2,1)S(1)} %collective-permute-done.1.refs_1_), channel_id=1, source_target_pairs={{4,8},{6,10},{8,4},{10,6},{5,9},{7,11},{9,5},{11,7},{20,24},{22,26... | collective-permute-start | bytes 3391496 | tf_op jit(solution)/shard_map/ppermute | solution.py:433
  44.5 25.9 %collective-permute-start.3 = (bf16[23,64,384]{2,1,0:T(8,128)(2,1)S(1)}, bf16[23,64,384]{2,1,0:T(8,128)(2,1)S(1)}, u32[]{:S(2)}, u32[]{:S(2)}) collective-permute-start(bf16[23,64,384]{2,1,0:T(8,128)(2,1)S(1)} %get-tuple-element.38), channel_id=1, source_target_pairs={{0,2},{2,0},{4,6},{6,4},{8,10},{10,8},{12,14},{14,12},{1,3},{3,1},... | collective-permute-start | bytes 3391496 | tf_op jit(solution)/shard_map/ppermute | solution.py:436
  45.8 25.6 %collective-permute-start.4 = (bf16[23,64,384]{2,1,0:T(8,128)(2,1)S(1)}, bf16[23,64,384]{2,1,0:T(8,128)(2,1)}, u32[]{:S(2)}, u32[]{:S(2)}) collective-permute-start(bf16[23,64,384]{2,1,0:T(8,128)(2,1)S(1)} %broadcast_select_fusion.2), channel_id=1, source_target_pairs={{0,4},{2,6},{4,0},{6,2},{8,12},{10,14},{12,8},{14,10},{1,5},{3,7},... | collective-permute-start | bytes 3391496 | tf_op jit(solution)/shard_map/ppermute | solution.py:433
  69.0 1.4 copy-start.3
  70.4 1.0 copy-start.5
  71.4 31.1 %collective-permute-start.8 = (bf16[23,64,384]{2,1,0:T(8,128)(2,1)}, bf16[23,64,384]{2,1,0:T(8,128)(2,1)}, u32[]{:S(2)}, u32[]{:S(2)}) collective-permute-start(bf16[23,64,384]{2,1,0:T(8,128)(2,1)} %collective-permute-done.2.refs_0_.refs_4_), channel_id=1, source_target_pairs={{4,8},{6,10},{8,4},{10,6},{5,9},{7,11},{9,5},{11,7},{20,24},{22,26... | collective-permute-start | bytes 3391496 | tf_op jit(solution)/shard_map/ppermute | solution.py:433
  73.6 28.9 %collective-permute-start.7 = (bf16[23,64,384]{2,1,0:T(8,128)(2,1)}, bf16[23,64,384]{2,1,0:T(8,128)(2,1)}, u32[]{:S(2)}, u32[]{:S(2)}) collective-permute-start(bf16[23,64,384]{2,1,0:T(8,128)(2,1)} %broadcast_select_fusion.1), channel_id=1, source_target_pairs={{0,4},{2,6},{4,0},{6,2},{8,12},{10,14},{12,8},{14,10},{1,5},{3,7},... | collective-permute-start | bytes 3391496 | tf_op jit(solution)/shard_map/ppermute | solution.py:433
  73.9 1.3 copy-start.6
  75.1 1.3 copy-start.9
  78.1 1.6 copy-start
  86.8 15.7 %copy-start.4 = (bf16[23,64,384]{2,1,0:T(8,128)(2,1)S(1)}, bf16[23,64,384]{2,1,0:T(8,128)(2,1)}, u32[]{:S(2)}) copy-start(bf16[23,64,384]{2,1,0:T(8,128)(2,1)} %copy-done.3) | copy-start | bytes 3391492
  86.8 30.7 %collective-permute-start.5 = (bf16[64,96,128]{2,1,0:T(8,128)(2,1)}, bf16[64,96,128]{2,1,0:T(8,128)(2,1)}, u32[]{:S(2)}, u32[]{:S(2)}) collective-permute-start(bf16[64,96,128]{2,1,0:T(8,128)(2,1)} %triangle.4.refs_0_), channel_id=1, source_target_pairs={{5,4},{7,6},{8,9},{10,11},{21,20},{23,22},{24,25},{26,27}} | collective-permute-start | bytes 4718600 | tf_op jit(solution)/shard_map/ppermute | solution.py:443
  99.9 11.2 %copy-start.7 = (bf16[23,64,384]{2,1,0:T(8,128)(2,1)S(1)}, bf16[23,64,384]{2,1,0:T(8,128)(2,1)}, u32[]{:S(2)}) copy-start(bf16[23,64,384]{2,1,0:T(8,128)(2,1)} %copy-done.5) | copy-start | bytes 3391492
  99.9 23.1 %collective-permute-start.10 = (bf16[64,96,128]{2,1,0:T(8,128)(2,1)}, bf16[64,96,128]{2,1,0:T(8,128)(2,1)}, u32[]{:S(2)}, u32[]{:S(2)}) collective-permute-start(bf16[64,96,128]{2,1,0:T(8,128)(2,1)} %triangle.5.refs_0_), channel_id=1, source_target_pairs={{1,0},{3,2},{5,4},{7,6},{8,9},{10,11},{12,13},{14,15},{17,16},{19,... | collective-permute-start | bytes 4718600 | tf_op jit(solution)/shard_map/ppermute | solution.py:443
  109.8 13.2 %collective-permute-start.11 = (bf16[64,96,128]{2,1,0:T(8,128)(2,1)}, bf16[64,96,128]{2,1,0:T(8,128)(2,1)}, u32[]{:S(2)}, u32[]{:S(2)}) collective-permute-start(bf16[64,96,128]{2,1,0:T(8,128)(2,1)} %triangle.6.refs_2_), channel_id=1, source_target_pairs={{0,1},{2,3},{4,5},{6,7},{9,8},{11,10},{13,12},{15,14},{16,17},{18,... | collective-permute-start | bytes 4718600 | tf_op jit(solution)/shard_map/ppermute | solution.py:443
  112.2 36.4 %collective-permute-start.9 = (bf16[23,64,384]{2,1,0:T(8,128)(2,1)}, bf16[23,64,384]{2,1,0:T(8,128)(2,1)S(1)}, u32[]{:S(2)}, u32[]{:S(2)}) collective-permute-start(bf16[23,64,384]{2,1,0:T(8,128)(2,1)} %broadcast_select_fusion), channel_id=1, source_target_pairs={{0,4},{2,6},{4,0},{6,2},{8,12},{10,14},{12,8},{14,10},{1,5},{3,7},... | collective-permute-start | bytes 3391496 | tf_op jit(solution)/shard_map/ppermute | solution.py:433
  113.4 35.2 %collective-permute-start.14 = (bf16[23,64,384]{2,1,0:T(8,128)(2,1)}, bf16[23,64,384]{2,1,0:T(8,128)(2,1)}, u32[]{:S(2)}, u32[]{:S(2)}) collective-permute-start(bf16[23,64,384]{2,1,0:T(8,128)(2,1)} %collective-permute-done.4.refs_1_.refs_2_), channel_id=1, source_target_pairs={{4,8},{6,10},{8,4},{10,6},{5,9},{7,11},{9,5},{11,7},{20,24},{22,26... | collective-permute-start | bytes 3391496 | tf_op jit(solution)/shard_map/ppermute | solution.py:433
  120.9 0.8 copy-start.11
  121.7 14.1 %collective-permute-start.13 = (bf16[23,96,128]{2,1,0:T(8,128)(2,1)S(1)}, bf16[23,96,128]{2,1,0:T(8,128)(2,1)S(1)}, u32[]{:S(2)}, u32[]{:S(2)}) collective-permute-start(bf16[23,96,128]{2,1,0:T(8,128)(2,1)S(1)} %get-tuple-element.47), channel_id=1, source_target_pairs={{0,2},{2,0},{4,6},{6,4},{8,10},{10,8},{12,14},{14,12},{1,3},{3,1},... | collective-permute-start | bytes 1695752 | tf_op jit(solution)/shard_map/ppermute | solution.py:436
  126.7 0.8 copy-start.13
  127.5 37.5 %copy-start.20 = (bf16[128,128]{1,0:T(8,128)(2,1)S(1)}, bf16[128,128]{1,0:T(8,128)(2,1)}, u32[]{:S(2)}) copy-start(bf16[128,128]{1,0:T(8,128)(2,1)} %param.9) | copy-start | bytes 98308
  127.5 20.3 %collective-permute-start.12 = (bf16[23,96,128]{2,1,0:T(8,128)(2,1)S(1)}, bf16[23,96,128]{2,1,0:T(8,128)(2,1)S(1)}, u32[]{:S(2)}, u32[]{:S(2)}) collective-permute-start(bf16[23,96,128]{2,1,0:T(8,128)(2,1)S(1)} %get-tuple-element.46), channel_id=1, source_target_pairs={{0,2},{2,0},{4,6},{6,4},{8,10},{10,8},{12,14},{14,12},{1,3},{3,1},... | collective-permute-start | bytes 1695752 | tf_op jit(solution)/shard_map/ppermute | solution.py:436
  135.8 21.9 %copy-start.17 = (bf16[23,96,128]{2,1,0:T(8,128)(2,1)}, bf16[23,96,128]{2,1,0:T(8,128)(2,1)S(1)}, u32[]{:S(2)}) copy-start(bf16[23,96,128]{2,1,0:T(8,128)(2,1)S(1)} %collective-permute-done.13) | copy-start | bytes 1695748
  147.8 0.8 copy-start.15
  157.7 17.5 %collective-permute-start.15 = (bf16[64,96,128]{2,1,0:T(8,128)(2,1)}, bf16[64,96,128]{2,1,0:T(8,128)(2,1)}, u32[]{:S(2)}, u32[]{:S(2)}) collective-permute-start(bf16[64,96,128]{2,1,0:T(8,128)(2,1)} %get-tuple-element.50.refs_0_), channel_id=1, source_target_pairs={{1,0},{3,2},{4,5},{6,7},{9,8},{11,10},{12,13},{14,15},{17,16},{19,... | collective-permute-start | bytes 4718600 | tf_op jit(solution)/shard_map/ppermute | solution.py:443
  159.0 7.6 %collective-permute-start.16 = (bf16[64,48,128]{2,1,0:T(8,128)(2,1)}, bf16[64,48,128]{2,1,0:T(8,128)(2,1)S(1)}, u32[]{:S(2)}, u32[]{:S(2)}) collective-permute-start(bf16[64,48,128]{2,1,0:T(8,128)(2,1)} %get-tuple-element.52.refs_0_), channel_id=1, source_target_pairs={{5,4},{7,6},{8,9},{10,11},{21,20},{23,22},{24,25},{26,27}} | collective-permute-start | bytes 2359304 | tf_op jit(solution)/shard_map/ppermute | solution.py:443
  163.3 4.5 %collective-permute-start.17 = (bf16[64,48,128]{2,1,0:T(8,128)(2,1)}, bf16[64,48,128]{2,1,0:T(8,128)(2,1)}, u32[]{:S(2)}, u32[]{:S(2)}) collective-permute-start(bf16[64,48,128]{2,1,0:T(8,128)(2,1)} %get-tuple-element.53.refs_2_), channel_id=1, source_target_pairs={{4,5},{6,7},{9,8},{11,10},{20,21},{22,23},{25,24},{27,26}} | collective-permute-start | bytes 2359304 | tf_op jit(solution)/shard_map/ppermute | solution.py:443
  166.5 8.7 %copy-start.10 = (bf16[64,96,128]{2,1,0:T(8,128)(2,1)S(1)}, bf16[64,96,128]{2,1,0:T(8,128)(2,1)}, u32[]{:S(2)}) copy-start(bf16[64,96,128]{2,1,0:T(8,128)(2,1)} %get-tuple-element.50.refs_0_) | copy-start | bytes 4718596
  171.5 23.8 %collective-permute-start.18 = (bf16[23,96,128]{2,1,0:T(8,128)(2,1)}, bf16[23,96,128]{2,1,0:T(8,128)(2,1)}, u32[]{:S(2)}, u32[]{:S(2)}) collective-permute-start(bf16[23,96,128]{2,1,0:T(8,128)(2,1)} %fold.7), channel_id=1, source_target_pairs={{5,1},{7,3},{8,12},{10,14},{21,17},{23,19},{24,28},{26,30}} | collective-permute-start | bytes 1695752 | tf_op jit(solution)/shard_map/ppermute | solution.py:451
  173.6 8.9 %copy-start.19 = (bf16[512,128]{1,0:T(8,128)(2,1)S(1)}, bf16[512,128]{1,0:T(8,128)(2,1)}, u32[]{:S(2)}) copy-start(bf16[512,128]{1,0:T(8,128)(2,1)} %param.11) | copy-start | bytes 393220
  173.6 21.8 %collective-permute-start.20 = (bf16[23,96,128]{2,1,0:T(8,128)(2,1)}, bf16[23,96,128]{2,1,0:T(8,128)(2,1)}, u32[]{:S(2)}, u32[]{:S(2)}) collective-permute-start(bf16[23,96,128]{2,1,0:T(8,128)(2,1)} %fold.7), channel_id=1, source_target_pairs={{4,3},{6,1},{9,14},{11,12},{20,19},{22,17},{25,30},{27,28}} | collective-permute-start | bytes 1695752 | tf_op jit(solution)/shard_map/ppermute | solution.py:451
  179.1 16.3 %collective-permute-start.19 = (bf16[23,96,128]{2,1,0:T(8,128)(2,1)}, bf16[23,96,128]{2,1,0:T(8,128)(2,1)}, u32[]{:S(2)}, u32[]{:S(2)}) collective-permute-start(bf16[23,96,128]{2,1,0:T(8,128)(2,1)} %get-tuple-element.54), channel_id=1, source_target_pairs={{0,2},{2,0},{5,7},{7,5},{8,10},{10,8},{13,15},{15,13},{16,18},{18,... | collective-permute-start | bytes 1695752 | tf_op jit(solution)/shard_map/ppermute | solution.py:458
  182.6 1.1 copy-start.14
  183.7 1.1 copy-start.16
  184.7 10.6 %copy-start.12 = (bf16[23,96,128]{2,1,0:T(8,128)(2,1)S(1)}, bf16[23,96,128]{2,1,0:T(8,128)(2,1)}, u32[]{:S(2)}) copy-start(bf16[23,96,128]{2,1,0:T(8,128)(2,1)} %copy-done.11) | copy-start | bytes 1695748
  195.3 1.1 copy-start.18

commit v9 on v8

--- a/solution.py
+++ b/solution.py
@@ -450,10 +450,9 @@
             perm += [(4 * s + 2 * b + source, 4 * t + 2 * (b ^ swap) + away) for b in range(2)]
         return lax.ppermute(value, ("row", "col"), perm)
 
-    def late_across(value):
+    def side_to_side(value, places, holders):
         perm = []
-        for z in range(4):
-            holder = 1 - z // 2 if z in (1, 2) else z // 2
+        for z, holder in zip(places, holders):
             perm += [(4 * z + 2 * b + holder, 4 * z + 2 * (1 - b) + holder) for b in range(2)]
         return lax.ppermute(value, ("row", "col"), perm)
 
@@ -495,10 +494,13 @@
     mate_own, near_own, right_beside = one
     left_own, left_far = project(where, folded, gate_pair(0))
     two = phase(
-        [(swap, either(near_own, right_beside)), (hop(cross), right_beside), (across, left_far)], one
+        [(swap, either(near_own, right_beside)), (hop(cross), right_beside), (across, left_far)],
+        one,
     )
     mate_beside, near_beside, left_beside = two
-    three = phase([(swap, either(near_beside, left_own)), (hop(cross), mate_own)], two)
+    three = phase(
+        [(swap, either(near_beside, left_own)), (hop(cross), mate_own)], (near_beside, left_beside)
+    )
     guest_own, far_own = three
 
     left = left_major(left_own, left_beside)
@@ -519,20 +521,7 @@
     first = fold(half, role, home, home_rest, away, away_rest)
     first_other = across(first[1])
     mate_block = fold(half, role, mate, mate_rest)
-    mate_other = across(mate_block[1])
-
-    late, lent_own, lent_beside = triangle(
-        outer,
-        left,
-        [after(far_own, first_other, mate_other), far_beside, mate_own, guest_beside],
-        [guest_own, guest_beside],
-    )
-    lent_rest = to_core(lent_own, inners, [False] * 2), to_core(lent_beside, inners, [True] * 2)
-    late_rest = to_core(late, everyone, [True, False, False, True])
-    (lent,) = fold(half, role, lent_beside, lent_rest[1], lent_own, lent_rest[0])
-    given = give_back(lent, 0), give_back(lent, 1)
-    late_block = fold(half, role, late, late_rest)
-    late_other = late_across(late_block[1])
+    mate_other = side_to_side(mate_block[1], inners, (0, 1))
 
     order = jnp.where(is_keeper, place % 2, place // 2)
     weights = [
@@ -542,7 +531,20 @@
         * trans_in.T,
         trans_out.T,
     ]
-    earlier = finish(scalars(order), folded, after(first[0], lent), first_other, weights)
+    earlier = finish(scalars(order), folded, first[0], first_other, weights)
+    late, lent_own, lent_beside = triangle(
+        outer,
+        left,
+        [after(far_own, earlier, mate_other), far_beside, mate_own, guest_beside],
+        [guest_own, guest_beside],
+    )
+    lent_rest = to_core(lent_own, inners, [False] * 2), to_core(lent_beside, inners, [True] * 2)
+    late_rest = to_core(late, everyone, [True, False, False, True])
+    (lent,) = fold(half, role, lent_beside, lent_rest[1], lent_own, lent_rest[0])
+    given = give_back(lent, 0), give_back(lent, 1)
+    late_block = fold(half, role, late, late_rest)
+    late_other = side_to_side(late_block[1], everyone, (0, 1, 0, 1))
+
     own, other = (
         jnp.where(inner & is_keeper, early, jnp.where(inner | is_keeper, end, back))
         for early, end, back in zip((mate_block[0], mate_other), (late_block[0], late_other), given)

time: 211 us -> 212 us (level)
  the two profiles are of different devices: /device:TPU:9 before, /device:TPU:1 now
where the time goes in v9:
time: 212 us; the launch traced here: 210 us
  Pallas kernels  77.4 us (37%)
  waiting for transfers between devices  58 us (27%)
  starting transfers between devices  45.9 us (22%)
  local copies, waits for them, and re-layouts  19.4 us (9%)
  other arithmetic  8.36 us (4%)
    ppermute x3, waiting for transfers between devices, across(): return lax.ppermute(value, 'row', [(i, i ^ 1) for i in range(8)])  40.2 us
    pallas_call x4, Pallas kernels, triangle(): pl.pallas_call(functools.partial(triangle_kernel, guests=len(guests), opt...  30.1 us
    pallas_call x2, Pallas kernels, finish(): pl.pallas_call(finish_kernel, out_shape=jax.ShapeDtypeStruct(shape, BF16)...  23.9 us
    ppermute x8, starting transfers between devices, among(): lax.ppermute(value, 'row', [(2 * s + b, 2 * t + b) for s, t in moves for...  20 us
    ppermute x2, waiting for transfers between devices, give_back(): return lax.ppermute(value, ('row', 'col'), perm)  16.8 us
    ppermute x6, starting transfers between devices, to_core(): return lax.ppermute(value, ('row', 'col'), perm)  16.7 us
    unnamed x58, local copies, waits for them, and re-layouts  16.2 us
    pallas_call x4, Pallas kernels, fold(): pl.pallas_call(functools.partial(fold_kernel, outputs=outputs, half=half)...  11.6 us
  transfers between devices with their start and end apart: 21, of which 6 were waited for; matrix products, arithmetic and copies ran while one was open for 5% of the time, Pallas kernels for 24%

profile of v9, /device:TPU:1, one launch (start us, length us, event | category | flops | bytes accessed | tf_op | source)
XLA Modules:
  0.0 210.2 jit_solution(4840458510721677921)
XLA Ops:
  0.0 0.8 fusion.5
  0.8 1.0 fusion.6
  1.8 1.3 slice.60
  3.5 0.1 copy.34
  4.6 1.6 copy-done.1
  6.2 5.7 %project.3 = (bf16[23,64,384]{2,1,0:T(8,128)(2,1)}, bf16[23,64,384]{2,1,0:T(8,128)(2,1)}) custom-call(s32[3]{0:T(128)S(1)} %pad_add_fusion.1.where_ref, bf16[2,23,184,128]{3,2,1,0:T(8,128)(2,1)S(1)} %bitcast.20, bf16[256,128]{1,0:T(8,128)(2,1)S(1)} %fusion.1.weight_ref), custom_call_target="tpu_custom_call" | custom-call | flops 554696704 | bytes 4333568 | tf_op jit(solution)/shard_map/project/pallas_call | solution.py:73
  12.0 1.7 collective-permute-start
  13.6 2.0 collective-permute-start.1
  15.7 2.9 %collective-permute-start.2 = (bf16[23,64,384]{2,1,0:T(8,128)(2,1)}, bf16[23,64,384]{2,1,0:T(8,128)(2,1)}, u32[]{:S(2)}, u32[]{:S(2)}) collective-permute-start(bf16[23,64,384]{2,1,0:T(8,128)(2,1)} %get-tuple-element.36.refs_0_), channel_id=1, source_target_pairs={{0,4},{2,6},{4,0},{6,2},{8,12},{10,14},{12,8},{14,10},{1,5},{3,7},... | collective-permute-start | bytes 3391496 | tf_op jit(solution)/shard_map/ppermute | solution.py:433
  18.6 0.7 copy.25
  19.8 0.8 maximum_select_fusion
  20.6 4.4 %project.2 = (bf16[23,64,384]{2,1,0:T(8,128)(2,1)S(1)}, bf16[23,64,384]{2,1,0:T(8,128)(2,1)S(1)}) custom-call(s32[3]{0:T(128)S(1)} %pad_add_fusion.1.where_ref, bf16[2,23,184,128]{3,2,1,0:T(8,128)(2,1)S(1)} %bitcast.21, bf16[256,128]{1,0:T(8,128)(2,1)S(1)} %fusion.weight_ref), custom_call_target="tpu_custom_call" | custom-call | flops 554696704 | bytes 4333568 | tf_op jit(solution)/shard_map/project/pallas_call | solution.py:73
  25.0 15.6 %collective-permute-done.1.refs_1_ = bf16[23,64,384]{2,1,0:T(8,128)(2,1)S(1)} collective-permute-done((bf16[23,64,384]{2,1,0:T(8,128)(2,1)}, bf16[23,64,384]{2,1,0:T(8,128)(2,1)S(1)}, u32[]{:S(2)}, u32[]{:S(2)}) %collective-permute-start.1) | collective-permute-done | bytes 1130528 | tf_op jit(solution)/shard_map/ppermute | solution.py:436
  40.6 1.2 broadcast_select_fusion.2
  41.9 1.0 collective-permute-done.2.refs_0_.refs_4_
  42.9 0.7 collective-permute-start.6
  43.6 0.3 collective-permute-start.3
  43.9 5.1 %collective-permute-start.4 = (bf16[23,64,384]{2,1,0:T(8,128)(2,1)}, bf16[23,64,384]{2,1,0:T(8,128)(2,1)}, u32[]{:S(2)}, u32[]{:S(2)}) collective-permute-start(bf16[23,64,384]{2,1,0:T(8,128)(2,1)} %broadcast_select_fusion.2), channel_id=1, source_target_pairs={{0,4},{2,6},{4,0},{6,2},{8,12},{10,14},{12,8},{14,10},{1,5},{3,7},... | collective-permute-start | bytes 3391496 | tf_op jit(solution)/shard_map/ppermute | solution.py:433
  49.0 1.3 broadcast_select_fusion.1
  50.4 17.9 %collective-permute-done.3.beside_ref = bf16[23,64,384]{2,1,0:T(8,128)(2,1)S(1)} collective-permute-done((bf16[23,64,384]{2,1,0:T(8,128)(2,1)S(1)}, bf16[23,64,384]{2,1,0:T(8,128)(2,1)S(1)}, u32[]{:S(2)}, u32[]{:S(2)}) %collective-permute-start.3) | collective-permute-done | bytes 1130528 | tf_op jit(solution)/shard_map/ppermute | solution.py:436
  68.3 1.0 copy-done.5
  69.3 1.7 collective-permute-start.8
  71.0 6.0 %collective-permute-start.7 = (bf16[23,64,384]{2,1,0:T(8,128)(2,1)}, bf16[23,64,384]{2,1,0:T(8,128)(2,1)}, u32[]{:S(2)}, u32[]{:S(2)}) collective-permute-start(bf16[23,64,384]{2,1,0:T(8,128)(2,1)} %broadcast_select_fusion.1), channel_id=1, source_target_pairs={{0,4},{2,6},{4,0},{6,2},{8,12},{10,14},{12,8},{14,10},{1,5},{3,7},... | collective-permute-start | bytes 3391496 | tf_op jit(solution)/shard_map/ppermute | solution.py:433
  77.1 1.3 copy-done.6
  78.3 1.3 copy-done.9
  79.6 1.8 left_major.1.left_ref
  81.4 1.6 copy-done
  83.0 7.0 %triangle.4.refs_0_ = bf16[64,96,128]{2,1,0:T(8,128)(2,1)} custom-call(s32[2]{0:T(128)S(1)} %pad_add_fusion.flag_ref, bf16[64,96,256]{2,1,0:T(8,128)(2,1)} %copy-done, bf16[23,64,384]{2,1,0:T(8,128)(2,1)} %collective-permute-done.2.refs_0_.refs_4_, bf16[23,64,384]{2,1,0:T(8,128)(2,1)} %collective-permute-done.4.refs_1_.refs_2_), custom_call_target="tpu_custom_call" | custom-call | flops 402653184 | bytes 5652480 | tf_op jit(solution)/shard_map/triangle/pallas_call | solution.py:188
  90.0 2.0 collective-permute-start.5
  92.0 6.8 %triangle.5.refs_0_ = bf16[64,96,128]{2,1,0:T(8,128)(2,1)} custom-call(s32[2]{0:T(128)S(1)} %pad_add_fusion.flag_ref, bf16[64,96,256]{2,1,0:T(8,128)(2,1)} %copy-done, bf16[23,64,384]{2,1,0:T(8,128)(2,1)} %get-tuple-element.36.refs_0_, bf16[23,64,384]{2,1,0:T(8,128)(2,1)S(1)} %collective-permute-done.1.refs_1_), custom_call_target="tpu_custom_call" | custom-call | flops 402653184 | bytes 5652480 | tf_op jit(solution)/shard_map/triangle/pallas_call | solution.py:188
  98.9 6.3 %collective-permute-start.10 = (bf16[64,96,128]{2,1,0:T(8,128)(2,1)}, bf16[64,96,128]{2,1,0:T(8,128)(2,1)}, u32[]{:S(2)}, u32[]{:S(2)}) collective-permute-start(bf16[64,96,128]{2,1,0:T(8,128)(2,1)} %triangle.5.refs_0_), channel_id=1, source_target_pairs={{1,0},{3,2},{5,4},{7,6},{8,9},{10,11},{12,13},{14,15},{17,16},{19,... | collective-permute-start | bytes 4718600 | tf_op jit(solution)/shard_map/ppermute | solution.py:443
  105.2 7.3 %triangle.6.refs_2_ = bf16[64,96,128]{2,1,0:T(8,128)(2,1)} custom-call(s32[2]{0:T(128)S(1)} %pad_add_fusion.2.flag_ref, bf16[64,96,256]{2,1,0:T(8,128)(2,1)} %copy-done, bf16[23,64,384]{2,1,0:T(8,128)(2,1)} %collective-permute-done.refs_0_, bf16[23,64,384]{2,1,0:T(8,128)(2,1)S(1)} %copy-done.4, bf16[23,64,384]{2,1,0:T(8,128)(2,1)} %collective-permute-done.4.refs_1_.refs_2_, ...), custom_call_target="tpu_custom_call" | custom-call | flops 402653184 | bytes 5652480 | tf_op jit(solution)/shard_map/triangle/pallas_call | solution.py:188
  112.5 1.4 collective-permute-start.11
  113.9 1.2 broadcast_select_fusion
  115.1 0.3 collective-permute-start.9
  115.4 1.7 collective-permute-start.14
  117.4 4.2 %fold.4 = (bf16[23,96,128]{2,1,0:T(8,128)(2,1)S(1)}, bf16[23,96,128]{2,1,0:T(8,128)(2,1)}) custom-call(s32[1]{0:T(128)} %bitcast.2.role_ref, bf16[64,96,128]{2,1,0:T(8,128)(2,1)} %triangle.4.refs_0_, bf16[64,96,128]{2,1,0:T(8,128)(2,1)} %collective-permute-done.5.refs_1_), custom_call_target="tpu_custom_call" | custom-call | bytes 4718592 | tf_op jit(solution)/shard_map/fold/pallas_call | solution.py:247
  121.6 0.8 copy-done.11
  122.4 1.5 collective-permute-start.13
  123.8 4.5 %fold.5 = (bf16[23,96,128]{2,1,0:T(8,128)(2,1)S(1)}, bf16[23,96,128]{2,1,0:T(8,128)(2,1)}) custom-call(s32[1]{0:T(128)} %bitcast.2.role_ref, bf16[64,96,128]{2,1,0:T(8,128)(2,1)} %triangle.5.refs_0_, bf16[64,96,128]{2,1,0:T(8,128)(2,1)} %collective-permute-done.10.refs_1_, bf16[64,96,128]{2,1,0:T(8,128)(2,1)} %triangle.6.refs_2_, ...), custom_call_target="tpu_custom_call" | custom-call | bytes 4718592 | tf_op jit(solution)/shard_map/fold/pallas_call | solution.py:247
  128.3 0.8 copy-done.16
  129.1 1.2 collective-permute-start.12
  130.4 1.8 copy.23
  132.2 1.0 copy.24
  133.2 1.1 multiply_bitcast_fusion.refs_2_
  134.4 6.8 %collective-permute-done.12.other_ref = bf16[23,96,128]{2,1,0:T(8,128)(2,1)} collective-permute-done((bf16[23,96,128]{2,1,0:T(8,128)(2,1)}, bf16[23,96,128]{2,1,0:T(8,128)(2,1)}, u32[]{:S(2)}, u32[]{:S(2)}) %collective-permute-start.12) | collective-permute-done | bytes 565280 | tf_op jit(solution)/shard_map/ppermute | solution.py:436
  141.2 1.1 copy-done.17
  142.2 11.6 %finish.2.refs_4_ = bf16[2,23,96,128]{3,2,1,0:T(8,128)(2,1)S(1)} custom-call(s32[1]{0:T(128)} %bitcast.9.flag_ref, bf16[2,23,184,128]{3,2,1,0:T(8,128)(2,1)S(1)} %bitcast.22, bf16[23,96,128]{2,1,0:T(8,128)(2,1)S(1)} %copy-done.17, bf16[23,96,128]{2,1,0:T(8,128)(2,1)} %collective-permute-done.12.other_ref, bf16[128,128]{1,0:T(8,128)(2,1)S(1)} %get-tuple-element.75.refs_0_, ...), custom_call_target="tpu_custom_call" | custom-call | flops 1941438464 | bytes 4333568 | tf_op jit(solution)/shard_map/finish/pallas_call | solution.py:314
  153.9 1.0 copy-done.18
  154.9 8.9 %triangle.7 = (bf16[64,96,128]{2,1,0:T(8,128)(2,1)}, bf16[64,48,128]{2,1,0:T(8,128)(2,1)S(1)}, bf16[64,48,128]{2,1,0:T(8,128)(2,1)S(1)}) custom-call(s32[2]{0:T(128)S(1)} %pad_add_fusion.2.flag_ref, bf16[64,96,256]{2,1,0:T(8,128)(2,1)} %copy-done, bf16[23,64,384]{2,1,0:T(8,128)(2,1)} %collective-permute-done.7.refs_3_.refs_0_, ...), custom_call_target="tpu_custom_call" | custom-call | flops 805306368 | bytes 5652480 | tf_op jit(solution)/shard_map/triangle/pallas_call | solution.py:188
  163.8 5.5 %collective-permute-start.15 = (bf16[64,96,128]{2,1,0:T(8,128)(2,1)}, bf16[64,96,128]{2,1,0:T(8,128)(2,1)S(1)}, u32[]{:S(2)}, u32[]{:S(2)}) collective-permute-start(bf16[64,96,128]{2,1,0:T(8,128)(2,1)} %get-tuple-element.50.refs_0_), channel_id=1, source_target_pairs={{1,0},{3,2},{4,5},{6,7},{9,8},{11,10},{12,13},{14,15},{17,16},{19,... | collective-permute-start | bytes 4718600 | tf_op jit(solution)/shard_map/ppermute | solution.py:443
  169.2 0.7 collective-permute-start.16
  170.0 0.8 collective-permute-start.17
  170.9 0.8 fold.7
  171.6 1.4 collective-permute-start.18
  173.1 1.3 collective-permute-start.20
  174.4 2.1 %fold.6 = (bf16[23,96,128]{2,1,0:T(8,128)(2,1)S(1)}, bf16[23,96,128]{2,1,0:T(8,128)(2,1)}) custom-call(s32[1]{0:T(128)} %bitcast.2.role_ref, bf16[64,96,128]{2,1,0:T(8,128)(2,1)S(1)} %copy-done.10, bf16[64,96,128]{2,1,0:T(8,128)(2,1)S(1)} %collective-permute-done.15.refs_1_), custom_call_target="tpu_custom_call" | custom-call | bytes 4718592 | tf_op jit(solution)/shard_map/fold/pallas_call | solution.py:247
  176.5 0.8 copy-done.13
  177.3 1.5 collective-permute-start.19
  178.8 15.2 %collective-permute-done.18 = bf16[23,96,128]{2,1,0:T(8,128)(2,1)} collective-permute-done((bf16[23,96,128]{2,1,0:T(8,128)(2,1)S(1)}, bf16[23,96,128]{2,1,0:T(8,128)(2,1)}, u32[]{:S(2)}, u32[]{:S(2)}) %collective-permute-start.18) | collective-permute-done | bytes 565280 | tf_op jit(solution)/shard_map/ppermute | solution.py:451
  194.0 1.2 select_select_fusion.1.own_ref
  195.2 1.6 collective-permute-done.20
  196.8 1.1 select_select_fusion.other_ref
  197.9 12.2 %finish.3 = bf16[2,23,184,128]{3,2,1,0:T(8,128)(2,1)} custom-call(s32[1]{0:T(128)} %bitcast.flag_ref, bf16[2,23,184,128]{3,2,1,0:T(8,128)(2,1)S(1)} %bitcast.23, bf16[23,96,128]{2,1,0:T(8,128)(2,1)S(1)} %select_select_fusion.1.own_ref, bf16[23,96,128]{2,1,0:T(8,128)(2,1)S(1)} %select_select_fusion.other_ref, bf16[128,128]{1,0:T(8,128)(2,1)S(1)} %get-tuple-element.75.refs_0_, ...), custom_call_target="tpu_custom_call" | custom-call | flops 1941438464 | bytes 4333568 | tf_op jit(solution)/shard_map/finish/pallas_call | solution.py:314
  (68 shorter events, 1.9 us)
Async XLA Ops:
  4.6 1.6 copy-start.1
  6.2 14.4 %copy-start.2 = (bf16[46,184,128]{2,1,0:T(8,128)(2,1)S(1)}, bf16[46,184,128]{2,1,0:T(8,128)(2,1)}, u32[]{:S(2)}) copy-start(bf16[46,184,128]{2,1,0:T(8,128)(2,1)} %param.6) | copy-start | bytes 6500356
  12.0 13.1 %collective-permute-start = (bf16[23,64,384]{2,1,0:T(8,128)(2,1)}, bf16[23,64,384]{2,1,0:T(8,128)(2,1)}, u32[]{:S(2)}, u32[]{:S(2)}) collective-permute-start(bf16[23,64,384]{2,1,0:T(8,128)(2,1)} %get-tuple-element.36.refs_0_), channel_id=1, source_target_pairs={{4,8},{6,10},{8,4},{10,6},{5,9},{7,11},{9,5},{11,7},{20,24},{22,26... | collective-permute-start | bytes 3391496 | tf_op jit(solution)/shard_map/ppermute | solution.py:433
  13.6 27.0 %collective-permute-start.1 = (bf16[23,64,384]{2,1,0:T(8,128)(2,1)}, bf16[23,64,384]{2,1,0:T(8,128)(2,1)S(1)}, u32[]{:S(2)}, u32[]{:S(2)}) collective-permute-start(bf16[23,64,384]{2,1,0:T(8,128)(2,1)} %get-tuple-element.34), channel_id=1, source_target_pairs={{0,2},{2,0},{4,6},{6,4},{8,10},{10,8},{12,14},{14,12},{1,3},{3,1},... | collective-permute-start | bytes 3391496 | tf_op jit(solution)/shard_map/ppermute | solution.py:436
  15.7 27.2 %collective-permute-start.2 = (bf16[23,64,384]{2,1,0:T(8,128)(2,1)}, bf16[23,64,384]{2,1,0:T(8,128)(2,1)}, u32[]{:S(2)}, u32[]{:S(2)}) collective-permute-start(bf16[23,64,384]{2,1,0:T(8,128)(2,1)} %get-tuple-element.36.refs_0_), channel_id=1, source_target_pairs={{0,4},{2,6},{4,0},{6,2},{8,12},{10,14},{12,8},{14,10},{1,5},{3,7},... | collective-permute-start | bytes 3391496 | tf_op jit(solution)/shard_map/ppermute | solution.py:433
  25.0 24.0 %copy-start.8 = (bf16[23,64,384]{2,1,0:T(8,128)(2,1)}, bf16[23,64,384]{2,1,0:T(8,128)(2,1)S(1)}, u32[]{:S(2)}) copy-start(bf16[23,64,384]{2,1,0:T(8,128)(2,1)S(1)} %get-tuple-element.30.own_ref) | copy-start | bytes 3391492
  42.9 6.2 %collective-permute-start.6 = (bf16[23,64,384]{2,1,0:T(8,128)(2,1)S(1)}, bf16[23,64,384]{2,1,0:T(8,128)(2,1)S(1)}, u32[]{:S(2)}, u32[]{:S(2)}) collective-permute-start(bf16[23,64,384]{2,1,0:T(8,128)(2,1)S(1)} %collective-permute-done.1.refs_1_), channel_id=1, source_target_pairs={{4,8},{6,10},{8,4},{10,6},{5,9},{7,11},{9,5},{11,7},{20,24},{22,26... | collective-permute-start | bytes 3391496 | tf_op jit(solution)/shard_map/ppermute | solution.py:433
  43.6 24.7 %collective-permute-start.3 = (bf16[23,64,384]{2,1,0:T(8,128)(2,1)S(1)}, bf16[23,64,384]{2,1,0:T(8,128)(2,1)S(1)}, u32[]{:S(2)}, u32[]{:S(2)}) collective-permute-start(bf16[23,64,384]{2,1,0:T(8,128)(2,1)S(1)} %get-tuple-element.37), channel_id=1, source_target_pairs={{0,2},{2,0},{4,6},{6,4},{8,10},{10,8},{12,14},{14,12},{1,3},{3,1},... | collective-permute-start | bytes 3391496 | tf_op jit(solution)/shard_map/ppermute | solution.py:436
  43.9 39.1 %collective-permute-start.4 = (bf16[23,64,384]{2,1,0:T(8,128)(2,1)}, bf16[23,64,384]{2,1,0:T(8,128)(2,1)}, u32[]{:S(2)}, u32[]{:S(2)}) collective-permute-start(bf16[23,64,384]{2,1,0:T(8,128)(2,1)} %broadcast_select_fusion.2), channel_id=1, source_target_pairs={{0,4},{2,6},{4,0},{6,2},{8,12},{10,14},{12,8},{14,10},{1,5},{3,7},... | collective-permute-start | bytes 3391496 | tf_op jit(solution)/shard_map/ppermute | solution.py:433
  49.0 1.4 copy-start.3
  68.3 1.0 copy-start.5
  69.3 35.9 %collective-permute-start.8 = (bf16[23,64,384]{2,1,0:T(8,128)(2,1)}, bf16[23,64,384]{2,1,0:T(8,128)(2,1)}, u32[]{:S(2)}, u32[]{:S(2)}) collective-permute-start(bf16[23,64,384]{2,1,0:T(8,128)(2,1)} %collective-permute-done.2.refs_0_.refs_4_), channel_id=1, source_target_pairs={{4,8},{6,10},{8,4},{10,6},{5,9},{7,11},{9,5},{11,7},{20,24},{22,26... | collective-permute-start | bytes 3391496 | tf_op jit(solution)/shard_map/ppermute | solution.py:433
  71.0 34.2 %collective-permute-start.7 = (bf16[23,64,384]{2,1,0:T(8,128)(2,1)}, bf16[23,64,384]{2,1,0:T(8,128)(2,1)}, u32[]{:S(2)}, u32[]{:S(2)}) collective-permute-start(bf16[23,64,384]{2,1,0:T(8,128)(2,1)} %broadcast_select_fusion.1), channel_id=1, source_target_pairs={{0,4},{2,6},{4,0},{6,2},{8,12},{10,14},{12,8},{14,10},{1,5},{3,7},... | collective-permute-start | bytes 3391496 | tf_op jit(solution)/shard_map/ppermute | solution.py:433
  77.1 1.3 copy-start.6
  78.3 1.3 copy-start.9
  81.4 1.6 copy-start
  90.0 15.1 %copy-start.4 = (bf16[23,64,384]{2,1,0:T(8,128)(2,1)S(1)}, bf16[23,64,384]{2,1,0:T(8,128)(2,1)}, u32[]{:S(2)}) copy-start(bf16[23,64,384]{2,1,0:T(8,128)(2,1)} %copy-done.3) | copy-start | bytes 3391492
  90.0 27.3 %collective-permute-start.5 = (bf16[64,96,128]{2,1,0:T(8,128)(2,1)}, bf16[64,96,128]{2,1,0:T(8,128)(2,1)}, u32[]{:S(2)}, u32[]{:S(2)}) collective-permute-start(bf16[64,96,128]{2,1,0:T(8,128)(2,1)} %triangle.4.refs_0_), channel_id=1, source_target_pairs={{5,4},{7,6},{8,9},{10,11},{21,20},{23,22},{24,25},{26,27}} | collective-permute-start | bytes 4718600 | tf_op jit(solution)/shard_map/ppermute | solution.py:443
  98.9 15.0 %copy-start.7 = (bf16[23,64,384]{2,1,0:T(8,128)(2,1)S(1)}, bf16[23,64,384]{2,1,0:T(8,128)(2,1)}, u32[]{:S(2)}) copy-start(bf16[23,64,384]{2,1,0:T(8,128)(2,1)} %copy-done.5) | copy-start | bytes 3391492
  98.9 24.9 %collective-permute-start.10 = (bf16[64,96,128]{2,1,0:T(8,128)(2,1)}, bf16[64,96,128]{2,1,0:T(8,128)(2,1)}, u32[]{:S(2)}, u32[]{:S(2)}) collective-permute-start(bf16[64,96,128]{2,1,0:T(8,128)(2,1)} %triangle.5.refs_0_), channel_id=1, source_target_pairs={{1,0},{3,2},{5,4},{7,6},{8,9},{10,11},{12,13},{14,15},{17,16},{19,... | collective-permute-start | bytes 4718600 | tf_op jit(solution)/shard_map/ppermute | solution.py:443
  112.5 4.5 %copy-start.20 = (bf16[128,128]{1,0:T(8,128)(2,1)S(1)}, bf16[128,128]{1,0:T(8,128)(2,1)}, u32[]{:S(2)}) copy-start(bf16[128,128]{1,0:T(8,128)(2,1)} %param.9) | copy-start | bytes 98308
  112.5 11.3 %collective-permute-start.11 = (bf16[64,96,128]{2,1,0:T(8,128)(2,1)}, bf16[64,96,128]{2,1,0:T(8,128)(2,1)}, u32[]{:S(2)}, u32[]{:S(2)}) collective-permute-start(bf16[64,96,128]{2,1,0:T(8,128)(2,1)} %triangle.6.refs_2_), channel_id=1, source_target_pairs={{0,1},{2,3},{4,5},{6,7},{9,8},{11,10},{13,12},{15,14},{16,17},{18,... | collective-permute-start | bytes 4718600 | tf_op jit(solution)/shard_map/ppermute | solution.py:443
  115.1 39.8 %collective-permute-start.9 = (bf16[23,64,384]{2,1,0:T(8,128)(2,1)}, bf16[23,64,384]{2,1,0:T(8,128)(2,1)S(1)}, u32[]{:S(2)}, u32[]{:S(2)}) collective-permute-start(bf16[23,64,384]{2,1,0:T(8,128)(2,1)} %broadcast_select_fusion), channel_id=1, source_target_pairs={{0,4},{2,6},{4,0},{6,2},{8,12},{10,14},{12,8},{14,10},{1,5},{3,7},... | collective-permute-start | bytes 3391496 | tf_op jit(solution)/shard_map/ppermute | solution.py:433
  115.4 39.5 %collective-permute-start.14 = (bf16[23,64,384]{2,1,0:T(8,128)(2,1)}, bf16[23,64,384]{2,1,0:T(8,128)(2,1)}, u32[]{:S(2)}, u32[]{:S(2)}) collective-permute-start(bf16[23,64,384]{2,1,0:T(8,128)(2,1)} %collective-permute-done.4.refs_1_.refs_2_), channel_id=1, source_target_pairs={{4,8},{6,10},{8,4},{10,6},{5,9},{7,11},{9,5},{11,7},{20,24},{22,26... | collective-permute-start | bytes 3391496 | tf_op jit(solution)/shard_map/ppermute | solution.py:433
  121.6 0.8 copy-start.11
  122.4 32.5 %collective-permute-start.13 = (bf16[23,96,128]{2,1,0:T(8,128)(2,1)}, bf16[23,96,128]{2,1,0:T(8,128)(2,1)}, u32[]{:S(2)}, u32[]{:S(2)}) collective-permute-start(bf16[23,96,128]{2,1,0:T(8,128)(2,1)} %get-tuple-element.47), channel_id=1, source_target_pairs={{4,6},{6,4},{9,11},{11,9},{20,22},{22,20},{25,27},{27,25}} | collective-permute-start | bytes 1695752 | tf_op jit(solution)/shard_map/ppermute | solution.py:457
  128.3 0.8 copy-start.16
  129.1 12.1 %collective-permute-start.12 = (bf16[23,96,128]{2,1,0:T(8,128)(2,1)}, bf16[23,96,128]{2,1,0:T(8,128)(2,1)}, u32[]{:S(2)}, u32[]{:S(2)}) collective-permute-start(bf16[23,96,128]{2,1,0:T(8,128)(2,1)} %get-tuple-element.46), channel_id=1, source_target_pairs={{0,2},{2,0},{4,6},{6,4},{8,10},{10,8},{12,14},{14,12},{1,3},{3,1},... | collective-permute-start | bytes 1695752 | tf_op jit(solution)/shard_map/ppermute | solution.py:436
  134.4 19.5 %copy-start.14 = (bf16[1024,128]{1,0:T(8,128)(2,1)}, bf16[1024,128]{1,0:T(8,128)(2,1)S(1)}, u32[]{:S(2)}) copy-start(bf16[1024,128]{1,0:T(8,128)(2,1)S(1)} %multiply_bitcast_fusion.refs_2_) | copy-start | bytes 786436
  141.2 1.1 copy-start.17
  153.9 1.0 copy-start.18
  163.8 10.6 %collective-permute-start.15 = (bf16[64,96,128]{2,1,0:T(8,128)(2,1)}, bf16[64,96,128]{2,1,0:T(8,128)(2,1)S(1)}, u32[]{:S(2)}, u32[]{:S(2)}) collective-permute-start(bf16[64,96,128]{2,1,0:T(8,128)(2,1)} %get-tuple-element.50.refs_0_), channel_id=1, source_target_pairs={{1,0},{3,2},{4,5},{6,7},{9,8},{11,10},{12,13},{14,15},{17,16},{19,... | collective-permute-start | bytes 4718600 | tf_op jit(solution)/shard_map/ppermute | solution.py:443
  169.2 1.6 collective-permute-start.16
  170.0 4.4 %copy-start.10 = (bf16[64,96,128]{2,1,0:T(8,128)(2,1)S(1)}, bf16[64,96,128]{2,1,0:T(8,128)(2,1)}, u32[]{:S(2)}) copy-start(bf16[64,96,128]{2,1,0:T(8,128)(2,1)} %get-tuple-element.50.refs_0_) | copy-start | bytes 4718596
  170.0 0.9 collective-permute-start.17
  171.6 22.3 %copy-start.12 = (bf16[23,96,128]{2,1,0:T(8,128)(2,1)S(1)}, bf16[23,96,128]{2,1,0:T(8,128)(2,1)}, u32[]{:S(2)}) copy-start(bf16[23,96,128]{2,1,0:T(8,128)(2,1)} %copy-done.11) | copy-start | bytes 1695748
  171.6 22.3 %collective-permute-start.18 = (bf16[23,96,128]{2,1,0:T(8,128)(2,1)S(1)}, bf16[23,96,128]{2,1,0:T(8,128)(2,1)}, u32[]{:S(2)}, u32[]{:S(2)}) collective-permute-start(bf16[23,96,128]{2,1,0:T(8,128)(2,1)S(1)} %fold.7), channel_id=1, source_target_pairs={{5,1},{7,3},{8,12},{10,14},{21,17},{23,19},{24,28},{26,30}} | collective-permute-start | bytes 1695752 | tf_op jit(solution)/shard_map/ppermute | solution.py:451
  173.1 23.7 %collective-permute-start.20 = (bf16[23,96,128]{2,1,0:T(8,128)(2,1)S(1)}, bf16[23,96,128]{2,1,0:T(8,128)(2,1)}, u32[]{:S(2)}, u32[]{:S(2)}) collective-permute-start(bf16[23,96,128]{2,1,0:T(8,128)(2,1)S(1)} %fold.7), channel_id=1, source_target_pairs={{4,3},{6,1},{9,14},{11,12},{20,19},{22,17},{25,30},{27,28}} | collective-permute-start | bytes 1695752 | tf_op jit(solution)/shard_map/ppermute | solution.py:451
  176.5 0.8 copy-start.13
  177.3 19.5 %collective-permute-start.19 = (bf16[23,96,128]{2,1,0:T(8,128)(2,1)}, bf16[23,96,128]{2,1,0:T(8,128)(2,1)}, u32[]{:S(2)}, u32[]{:S(2)}) collective-permute-start(bf16[23,96,128]{2,1,0:T(8,128)(2,1)} %get-tuple-element.54), channel_id=1, source_target_pairs={{0,2},{2,0},{5,7},{7,5},{8,10},{10,8},{13,15},{15,13},{16,18},{18,... | collective-permute-start | bytes 1695752 | tf_op jit(solution)/shard_map/ppermute | solution.py:457
  195.2 2.7 %copy-start.15 = (bf16[1024,128]{1,0:T(8,128)(2,1)S(1)}, bf16[1024,128]{1,0:T(8,128)(2,1)}, u32[]{:S(2)}) copy-start(bf16[1024,128]{1,0:T(8,128)(2,1)} %copy-done.14) | copy-start | bytes 786436
  195.2 2.7 %copy-start.19 = (bf16[2,23,96,128]{3,2,1,0:T(8,128)(2,1)S(1)}, bf16[2,23,96,128]{3,2,1,0:T(8,128)(2,1)}, u32[]{:S(2)}) copy-start(bf16[2,23,96,128]{3,2,1,0:T(8,128)(2,1)} %copy-done.18) | copy-start | bytes 3391492

commit v10 on v9

--- a/solution.py
+++ b/solution.py
@@ -125,18 +125,21 @@
     )(own, beside)
 
 
-def triangle_kernel(flag_ref, left_ref, *refs, guests, options):
-    guest_refs = refs[:guests]
-    rights = refs[guests : guests + 2 * options]
-    outs = refs[guests + 2 * options : -1 - bool(guests)]
-    right_ref = refs[-1]
-    own, beside = rights[0][...], rights[1][...]
+def triangle_kernel(flag_ref, left_ref, *refs, counts, guests, options):
+    pieces, refs = [], list(refs)
+    for count in counts:
+        parts = [refs.pop(0)[...] for _ in range(count)]
+        pieces.append(parts[0] if count == 1 else jnp.concatenate(parts, axis=0))
+    outs, work = refs[: 1 + guests], refs[1 + guests :]
+    visitors, rights = pieces[:guests], pieces[guests:]
+    own, beside = rights[:2]
     if options == 2:
         plain = flag_ref[1] == 0
-        own = jnp.where(plain, own, rights[2][...])
-        beside = jnp.where(plain, beside, rights[3][...])
+        own = jnp.where(plain, own, rights[2])
+        beside = jnp.where(plain, beside, rights[3])
     width = own.shape[2] // 3
     even = flag_ref[0] == 0
+    right_ref = work[0]
     main, rest = channel_major(
         [jnp.where(even, own, beside), jnp.where(even, beside, own)], False
     )
@@ -149,8 +152,8 @@
     right_ref[:, :rows, :width] = main
     right_ref[:, :rows, width:] = rest
     if guests:
-        guest_ref = refs[-2]
-        main, rest = channel_major([ref[...] for ref in guest_refs], True)
+        guest_ref = work[1]
+        main, rest = channel_major(visitors, True)
         guest_ref[:, :, :width] = main
         guest_ref[:, :, width:] = rest
 
@@ -168,39 +171,46 @@
 
 
 def triangle(flags, left, pieces, guests=()):
-    half, chans, lanes = pieces[0].shape
-    options = len(pieces) // 2
-    rows, cols, deep = left.shape[1], padded(4 * half, 128), lanes // 3 * 2
-
-    def piece(option):
-        if options == 1:
-            return pl.BlockSpec((half, CHUNK, lanes), lambda c, flag_ref: (0, c, 0))
-        return pl.BlockSpec(
-            (half, CHUNK, lanes), lambda c, flag_ref: (0, jnp.where(flag_ref[1] == option, c, 0), 0)
-        )
+    chans, rows, deep = left.shape
+    lanes, half = deep // 2 * 3, sum(part.shape[0] for part in pieces[0])
+    options, cols = len(pieces) // 2, padded(4 * half, 128)
+
+    def spec(part, option):
+        def at(c, flag_ref):
+            return (0, c if option is None else jnp.where(flag_ref[1] == option, c, 0), 0)
+
+        return pl.BlockSpec((part.shape[0], CHUNK, lanes), at)
 
     def block(height, depth):
         return pl.BlockSpec((CHUNK, height, depth), lambda c, flag_ref: (c, 0, 0))
 
-    every = pl.BlockSpec((half, CHUNK, lanes), lambda c, flag_ref: (0, c, 0))
+    specs = [spec(part, None) for piece in guests for part in piece]
+    for i, piece in enumerate(pieces):
+        specs += [spec(part, i // 2 if options == 2 else None) for part in piece]
     heights = [rows] + [rows // 2] * len(guests)
-    work = [VMEM((CHUNK, rows, deep), BF16)] if guests else []
+    work = [VMEM((CHUNK, cols, deep), BF16)]
+    if guests:
+        work.append(VMEM((CHUNK, rows, deep), BF16))
+    everything = list(guests) + list(pieces)
     return pl.pallas_call(
-        functools.partial(triangle_kernel, guests=len(guests), options=options),
+        functools.partial(
+            triangle_kernel,
+            counts=[len(piece) for piece in everything],
+            guests=len(guests),
+            options=options,
+        ),
         grid_spec=pltpu.PrefetchScalarGridSpec(
             num_scalar_prefetch=1,
             grid=(chans // CHUNK,),
-            in_specs=[block(rows, deep)]
-            + [every] * len(guests)
-            + [piece(i // 2) for i in range(len(pieces))],
+            in_specs=[block(rows, deep)] + specs,
             out_specs=[block(h, cols) for h in heights],
-            scratch_shapes=work + [VMEM((CHUNK, cols, deep), BF16)],
+            scratch_shapes=work,
         ),
         out_shape=[jax.ShapeDtypeStruct((chans, h, cols), BF16) for h in heights],
         compiler_params=params(),
-        cost_estimate=cost(2 * chans * sum(heights) * cols * deep, 10 * pieces[0].size),
+        cost_estimate=cost(2 * chans * sum(heights) * cols * deep, 10 * half * chans * lanes),
         name="triangle",
-    )(flags, left, *guests, *pieces)
+    )(flags, left, *[part for piece in everything for part in piece])
 
 
 def fold_kernel(role_ref, *refs, outputs, half):
@@ -492,37 +502,6 @@
     right_own, right_far = project(where, folded, gate_pair(2))
     one = phase([(swap, right_own), (hop(cross), right_own), (across, right_far)], ())
     mate_own, near_own, right_beside = one
-    left_own, left_far = project(where, folded, gate_pair(0))
-    two = phase(
-        [(swap, either(near_own, right_beside)), (hop(cross), right_beside), (across, left_far)],
-        one,
-    )
-    mate_beside, near_beside, left_beside = two
-    three = phase(
-        [(swap, either(near_beside, left_own)), (hop(cross), mate_own)], (near_beside, left_beside)
-    )
-    guest_own, far_own = three
-
-    left = left_major(left_own, left_beside)
-    plain, outer = scalars(side, 0), scalars(side, jnp.where(inner, 0, 1))
-    (home,) = triangle(plain, left, [right_own, right_beside])
-    home_rest = to_core(home, everyone, [True] * 4)
-    (mate,) = triangle(plain, left, [mate_own, mate_beside])
-    mate_rest = to_core(mate, inners, [True] * 2)
-    four = phase(
-        [(swap, either(right_beside, left_beside)), (hop(cross), mate_beside)], three + [home, mate]
-    )
-    (away,) = triangle(
-        outer, left, [after(near_own, far_own, mate), near_beside, mate_beside, guest_own]
-    )
-    guest_beside, far_beside = four
-    away_rest = to_core(away, everyone, [False] * 4)
-    role = scalars(jnp.where(is_keeper, 0, 1))
-    first = fold(half, role, home, home_rest, away, away_rest)
-    first_other = across(first[1])
-    mate_block = fold(half, role, mate, mate_rest)
-    mate_other = side_to_side(mate_block[1], inners, (0, 1))
-
     order = jnp.where(is_keeper, place % 2, place // 2)
     weights = [
         in_weight[:, 4 * width :].T * BF16(0.5),
@@ -531,12 +510,45 @@
         * trans_in.T,
         trans_out.T,
     ]
-    earlier = finish(scalars(order), folded, first[0], first_other, weights)
+    left_own, left_far = project(where, folded, gate_pair(0))
+    two = phase(
+        [(swap, either(near_own, right_beside)), (hop(cross), right_beside), (across, left_far)],
+        one + weights,
+    )
+    mate_beside, near_beside, left_beside = two
+    three = phase(
+        [(swap, either(near_beside, left_own)), (hop(cross), mate_own)], (near_beside, left_beside)
+    )
+    guest_own, far_own = three
+
+    left = left_major(left_own, left_beside)
+    plain, outer = scalars(side, 0), scalars(side, jnp.where(inner, 0, 1))
+    (home,) = triangle(plain, left, [[right_own], [right_beside]])
+    home_rest = to_core(home, everyone, [True] * 4)
+    (mate,) = triangle(plain, left, [[mate_own], [mate_beside]])
+    mate_rest = to_core(mate, inners, [True] * 2)
+    four = phase(
+        [(swap, either(right_beside, left_beside)), (hop(cross), mate_beside)], three + [home, mate]
+    )
+    guest_beside, far_beside = four
+
+    (away,) = triangle(
+        outer,
+        left,
+        [[after(near_own, far_own, mate)], [near_beside], [mate_beside], [guest_own]],
+    )
+    away_rest = to_core(away, everyone, [False] * 4)
+    role = scalars(jnp.where(is_keeper, 0, 1))
+    first = fold(half, role, home, home_rest, away, away_rest)
+    first_other = across(first[1])
+    mate_block = fold(half, role, mate, mate_rest)
+    mate_other = side_to_side(mate_block[1], inners, (0, 1))
+
     late, lent_own, lent_beside = triangle(
         outer,
         left,
-        [after(far_own, earlier, mate_other), far_beside, mate_own, guest_beside],
-        [guest_own, guest_beside],
+        [[after(far_own, mate_other)], [far_beside], [mate_own], [guest_beside]],
+        [[guest_own], [guest_beside]],
     )
     lent_rest = to_core(lent_own, inners, [False] * 2), to_core(lent_beside, inners, [True] * 2)
     late_rest = to_core(late, everyone, [True, False, False, True])
@@ -545,6 +557,7 @@
     late_block = fold(half, role, late, late_rest)
     late_other = side_to_side(late_block[1], everyone, (0, 1, 0, 1))
 
+    earlier = finish(scalars(order), folded, after(first[0], lent), first_other, weights)
     own, other = (
         jnp.where(inner & is_keeper, early, jnp.where(inner | is_keeper, end, back))
         for early, end, back in zip((mate_block[0], mate_other), (late_block[0], late_other), given)

time: 212 us -> 191 us (0.901)
  waiting for transfers between devices: 58 us -> 38.5 us
  local copies, waits for them, and re-layouts: 19.4 us -> 24.3 us
  starting transfers between devices: 45.9 us -> 42.6 us
  Pallas kernels: 77.4 us -> 75.2 us
    ppermute x2, waiting for transfers between devices: 16.8 us -> 0.01 us  [give_back(): return lax.ppermute(value, ('row', 'col'), perm)]
    ppermute x3, waiting for transfers between devices: 40.2 us -> 32.7 us  [across(): return lax.ppermute(value, 'row', [(i, i ^ 1) for i in range(8)])]
    ppermute x8, waiting for transfers between devices: 1.02 us -> 5.83 us  [among(): lax.ppermute(value, 'row', [(2 * s + b, 2 * t + b) for s, t in moves for...]
    unnamed x58 -> x68, local copies, waits for them, and re-layouts: 16.2 us -> 20.7 us
    ppermute x6, starting transfers between devices: 16.7 us -> 13.9 us  [to_core(): return lax.ppermute(value, ('row', 'col'), perm)]
  transfers between devices with their start and end apart: 21 -> 21, of which waited for: 6 -> 6; matrix products, arithmetic and copies ran while one was open for 5% -> 6% of each run, Pallas kernels for 24% -> 30%
where the time goes in v10:
time: 191 us; the launch traced here: 189 us
  Pallas kernels  75.2 us (39%)
  starting transfers between devices  42.6 us (22%)
  waiting for transfers between devices  38.5 us (20%)
  local copies, waits for them, and re-layouts  24.3 us (13%)
  other arithmetic  7.81 us (4%)
    ppermute x3, waiting for transfers between devices, across(): return lax.ppermute(value, 'row', [(i, i ^ 1) for i in range(8)])  32.7 us
    pallas_call x4, Pallas kernels, triangle(): pl.pallas_call(functools.partial(triangle_kernel, counts=[len(piece) for...  28.2 us
    pallas_call x2, Pallas kernels, finish(): pl.pallas_call(finish_kernel, out_shape=jax.ShapeDtypeStruct(shape, BF16)...  24.1 us
    unnamed x68, local copies, waits for them, and re-layouts  20.7 us
    ppermute x8, starting transfers between devices, among(): lax.ppermute(value, 'row', [(2 * s + b, 2 * t + b) for s, t in moves for...  19.5 us
    ppermute x6, starting transfers between devices, to_core(): return lax.ppermute(value, ('row', 'col'), perm)  13.9 us
    pallas_call x4, Pallas kernels, fold(): pl.pallas_call(functools.partial(fold_kernel, outputs=outputs, half=half)...  11.1 us
    pallas_call x2, Pallas kernels, project(): pl.pallas_call(project_kernel, out_shape=(piece, piece), in_specs=[pl.Blo...  10.1 us
  transfers between devices with their start and end apart: 21, of which 6 were waited for; matrix products, arithmetic and copies ran while one was open for 6% of the time, Pallas kernels for 30%

profile of v10, /device:TPU:1, one launch (start us, length us, event | category | flops | bytes accessed | tf_op | source)
XLA Modules:
  0.0 189.5 jit_solution(14852664960112104278)
XLA Ops:
  0.0 0.8 fusion.5
  0.8 1.5 fusion.6
  2.4 1.2 slice.60
  4.9 1.6 copy-done.1
  6.5 5.7 %project.3 = (bf16[23,64,384]{2,1,0:T(8,128)(2,1)}, bf16[23,64,384]{2,1,0:T(8,128)(2,1)}) custom-call(s32[3]{0:T(128)S(1)} %pad_add_fusion.1.where_ref, bf16[2,23,184,128]{3,2,1,0:T(8,128)(2,1)S(1)} %bitcast.20, bf16[256,128]{1,0:T(8,128)(2,1)S(1)} %fusion.1.weight_ref), custom_call_target="tpu_custom_call" | custom-call | flops 554696704 | bytes 4333568 | tf_op jit(solution)/shard_map/project/pallas_call | solution.py:73
  12.3 1.7 collective-permute-start
  14.0 2.0 %collective-permute-start.1 = (bf16[23,64,384]{2,1,0:T(8,128)(2,1)}, bf16[23,64,384]{2,1,0:T(8,128)(2,1)S(1)}, u32[]{:S(2)}, u32[]{:S(2)}) collective-permute-start(bf16[23,64,384]{2,1,0:T(8,128)(2,1)} %get-tuple-element.35), channel_id=1, source_target_pairs={{0,2},{2,0},{4,6},{6,4},{8,10},{10,8},{12,14},{14,12},{1,3},{3,1},... | collective-permute-start | bytes 3391496 | tf_op jit(solution)/shard_map/ppermute | solution.py:446
  16.1 2.8 %collective-permute-start.2 = (bf16[23,64,384]{2,1,0:T(8,128)(2,1)}, bf16[23,64,384]{2,1,0:T(8,128)(2,1)}, u32[]{:S(2)}, u32[]{:S(2)}) collective-permute-start(bf16[23,64,384]{2,1,0:T(8,128)(2,1)} %get-tuple-element.37.refs_0_), channel_id=1, source_target_pairs={{0,4},{2,6},{4,0},{6,2},{8,12},{10,14},{12,8},{14,10},{1,5},{3,7},... | collective-permute-start | bytes 3391496 | tf_op jit(solution)/shard_map/ppermute | solution.py:443
  19.7 0.8 copy.30
  20.9 0.8 maximum_select_fusion
  21.7 4.4 %project.2 = (bf16[23,64,384]{2,1,0:T(8,128)(2,1)S(1)}, bf16[23,64,384]{2,1,0:T(8,128)(2,1)S(1)}) custom-call(s32[3]{0:T(128)S(1)} %pad_add_fusion.1.where_ref, bf16[2,23,184,128]{3,2,1,0:T(8,128)(2,1)S(1)} %bitcast.21, bf16[256,128]{1,0:T(8,128)(2,1)S(1)} %fusion.weight_ref), custom_call_target="tpu_custom_call" | custom-call | flops 554696704 | bytes 4333568 | tf_op jit(solution)/shard_map/project/pallas_call | solution.py:73
  26.1 1.0 copy-done.9
  27.1 1.1 copy-done.21
  28.3 1.0 copy.24
  29.3 0.7 copy.37
  30.0 1.8 copy.23
  31.9 0.8 fusion.3
  32.8 1.9 multiply_bitcast_fusion.refs_2_
  34.6 6.4 %collective-permute-done.1.refs_1_ = bf16[23,64,384]{2,1,0:T(8,128)(2,1)S(1)} collective-permute-done((bf16[23,64,384]{2,1,0:T(8,128)(2,1)}, bf16[23,64,384]{2,1,0:T(8,128)(2,1)S(1)}, u32[]{:S(2)}, u32[]{:S(2)}) %collective-permute-start.1) | collective-permute-done | bytes 1130528 | tf_op jit(solution)/shard_map/ppermute | solution.py:446
  41.2 2.0 %collective-permute-done.2.refs_0_.refs_4_ = bf16[23,64,384]{2,1,0:T(8,128)(2,1)} collective-permute-done((bf16[23,64,384]{2,1,0:T(8,128)(2,1)}, bf16[23,64,384]{2,1,0:T(8,128)(2,1)}, u32[]{:S(2)}, u32[]{:S(2)}) %collective-permute-start.2) | collective-permute-done | bytes 1130528 | tf_op jit(solution)/shard_map/ppermute | solution.py:443
  43.2 0.7 collective-permute-start.6
  44.2 4.1 %collective-permute-start.4 = (bf16[23,64,384]{2,1,0:T(8,128)(2,1)S(1)}, bf16[23,64,384]{2,1,0:T(8,128)(2,1)}, u32[]{:S(2)}, u32[]{:S(2)}) collective-permute-start(bf16[23,64,384]{2,1,0:T(8,128)(2,1)S(1)} %broadcast_select_fusion.2), channel_id=1, source_target_pairs={{0,4},{2,6},{4,0},{6,2},{8,12},{10,14},{12,8},{14,10},{1,5},{3,7},... | collective-permute-start | bytes 3391496 | tf_op jit(solution)/shard_map/ppermute | solution.py:443
  48.5 0.9 copy-done.7
  49.4 19.2 %collective-permute-done.3.beside_ref = bf16[23,64,384]{2,1,0:T(8,128)(2,1)S(1)} collective-permute-done((bf16[23,64,384]{2,1,0:T(8,128)(2,1)S(1)}, bf16[23,64,384]{2,1,0:T(8,128)(2,1)S(1)}, u32[]{:S(2)}, u32[]{:S(2)}) %collective-permute-start.3) | collective-permute-done | bytes 1130528 | tf_op jit(solution)/shard_map/ppermute | solution.py:446
  68.7 4.0 %collective-permute-start.7 = (bf16[23,64,384]{2,1,0:T(8,128)(2,1)S(1)}, bf16[23,64,384]{2,1,0:T(8,128)(2,1)S(1)}, u32[]{:S(2)}, u32[]{:S(2)}) collective-permute-start(bf16[23,64,384]{2,1,0:T(8,128)(2,1)S(1)} %broadcast_select_fusion.1), channel_id=1, source_target_pairs={{0,4},{2,6},{4,0},{6,2},{8,12},{10,14},{12,8},{14,10},{1,5},{3,7},... | collective-permute-start | bytes 3391496 | tf_op jit(solution)/shard_map/ppermute | solution.py:443
  72.6 0.7 collective-permute-start.8
  73.4 1.8 left_major.1.left_ref
  75.2 1.6 copy-done
  76.9 7.0 %triangle.4.refs_0_ = bf16[64,96,128]{2,1,0:T(8,128)(2,1)} custom-call(s32[2]{0:T(128)S(1)} %pad_add_fusion.flag_ref, bf16[64,96,256]{2,1,0:T(8,128)(2,1)} %copy-done, bf16[23,64,384]{2,1,0:T(8,128)(2,1)} %collective-permute-done.2.refs_0_.refs_4_, bf16[23,64,384]{2,1,0:T(8,128)(2,1)} %collective-permute-done.4.refs_1_.refs_2_), custom_call_target="tpu_custom_call" | custom-call | flops 402653184 | bytes 5652480 | tf_op jit(solution)/shard_map/triangle/pallas_call | solution.py:195
  83.9 1.8 collective-permute-start.5
  85.7 5.9 %triangle.5.refs_0_ = bf16[64,96,128]{2,1,0:T(8,128)(2,1)S(1)} custom-call(s32[2]{0:T(128)S(1)} %pad_add_fusion.flag_ref, bf16[64,96,256]{2,1,0:T(8,128)(2,1)} %copy-done, bf16[23,64,384]{2,1,0:T(8,128)(2,1)} %get-tuple-element.37.refs_0_, bf16[23,64,384]{2,1,0:T(8,128)(2,1)S(1)} %collective-permute-done.1.refs_1_), custom_call_target="tpu_custom_call" | custom-call | flops 402653184 | bytes 5652480 | tf_op jit(solution)/shard_map/triangle/pallas_call | solution.py:195
  91.7 1.3 broadcast_select_fusion
  93.2 2.1 %collective-permute-done.7.refs_0_.refs_3_ = bf16[23,64,384]{2,1,0:T(8,128)(2,1)S(1)} collective-permute-done((bf16[23,64,384]{2,1,0:T(8,128)(2,1)S(1)}, bf16[23,64,384]{2,1,0:T(8,128)(2,1)S(1)}, u32[]{:S(2)}, u32[]{:S(2)}) %collective-permute-start.7) | collective-permute-done | bytes 1130528 | tf_op jit(solution)/shard_map/ppermute | solution.py:443
  95.3 1.0 copy-done.5
  96.3 1.0 copy-done.12
  97.3 3.7 %collective-permute-start.9 = (bf16[23,64,384]{2,1,0:T(8,128)(2,1)}, bf16[23,64,384]{2,1,0:T(8,128)(2,1)}, u32[]{:S(2)}, u32[]{:S(2)}) collective-permute-start(bf16[23,64,384]{2,1,0:T(8,128)(2,1)} %broadcast_select_fusion), channel_id=1, source_target_pairs={{0,4},{2,6},{4,0},{6,2},{8,12},{10,14},{12,8},{14,10},{1,5},{3,7},... | collective-permute-start | bytes 3391496 | tf_op jit(solution)/shard_map/ppermute | solution.py:443
  101.0 1.7 collective-permute-start.11
  102.7 4.3 %fold.4 = (bf16[23,96,128]{2,1,0:T(8,128)(2,1)S(1)}, bf16[23,96,128]{2,1,0:T(8,128)(2,1)}) custom-call(s32[1]{0:T(128)} %bitcast.2.role_ref, bf16[64,96,128]{2,1,0:T(8,128)(2,1)} %triangle.4.refs_0_, bf16[64,96,128]{2,1,0:T(8,128)(2,1)} %collective-permute-done.5.refs_1_), custom_call_target="tpu_custom_call" | custom-call | bytes 4718592 | tf_op jit(solution)/shard_map/fold/pallas_call | solution.py:257
  107.0 0.9 copy-done.16
  107.8 1.5 collective-permute-start.10
  109.3 4.4 %collective-permute-start.18 = (bf16[64,96,128]{2,1,0:T(8,128)(2,1)}, bf16[64,96,128]{2,1,0:T(8,128)(2,1)S(1)}, u32[]{:S(2)}, u32[]{:S(2)}) collective-permute-start(bf16[64,96,128]{2,1,0:T(8,128)(2,1)} %copy-done.3), channel_id=1, source_target_pairs={{1,0},{3,2},{5,4},{7,6},{8,9},{10,11},{12,13},{14,15},{17,16},{19,... | collective-permute-start | bytes 4718600 | tf_op jit(solution)/shard_map/ppermute | solution.py:453
  113.7 1.2 copy-done.8
  115.0 6.2 %triangle.7.refs_2_ = bf16[64,96,128]{2,1,0:T(8,128)(2,1)S(1)} custom-call(s32[2]{0:T(128)S(1)} %pad_add_fusion.2.flag_ref, bf16[64,96,256]{2,1,0:T(8,128)(2,1)} %copy-done, bf16[23,64,384]{2,1,0:T(8,128)(2,1)} %collective-permute-done.refs_0_, bf16[23,64,384]{2,1,0:T(8,128)(2,1)S(1)} %copy-done.8, ...), custom_call_target="tpu_custom_call" | custom-call | flops 402653184 | bytes 5652480 | tf_op jit(solution)/shard_map/triangle/pallas_call | solution.py:195
  121.2 1.4 collective-permute-start.19
  122.7 1.8 collective-permute-done.9.refs_1_.refs_5_
  124.5 9.0 %triangle.6 = (bf16[64,96,128]{2,1,0:T(8,128)(2,1)}, bf16[64,48,128]{2,1,0:T(8,128)(2,1)S(1)}, bf16[64,48,128]{2,1,0:T(8,128)(2,1)S(1)}) custom-call(s32[2]{0:T(128)S(1)} %pad_add_fusion.2.flag_ref, bf16[64,96,256]{2,1,0:T(8,128)(2,1)} %copy-done, bf16[23,64,384]{2,1,0:T(8,128)(2,1)S(1)} %copy-done.6, ...), custom_call_target="tpu_custom_call" | custom-call | flops 805306368 | bytes 5652480 | tf_op jit(solution)/shard_map/triangle/pallas_call | solution.py:195
  133.4 4.7 %collective-permute-start.12 = (bf16[64,96,128]{2,1,0:T(8,128)(2,1)}, bf16[64,96,128]{2,1,0:T(8,128)(2,1)S(1)}, u32[]{:S(2)}, u32[]{:S(2)}) collective-permute-start(bf16[64,96,128]{2,1,0:T(8,128)(2,1)} %get-tuple-element.48.refs_0_), channel_id=1, source_target_pairs={{1,0},{3,2},{4,5},{6,7},{9,8},{11,10},{12,13},{14,15},{17,16},{19,... | collective-permute-start | bytes 4718600 | tf_op jit(solution)/shard_map/ppermute | solution.py:453
  138.9 0.9 collective-permute-start.14
  139.8 4.0 %fold.7 = (bf16[23,96,128]{2,1,0:T(8,128)(2,1)S(1)}, bf16[23,96,128]{2,1,0:T(8,128)(2,1)}) custom-call(s32[1]{0:T(128)} %bitcast.2.role_ref, bf16[64,96,128]{2,1,0:T(8,128)(2,1)S(1)} %copy-done.4, bf16[64,96,128]{2,1,0:T(8,128)(2,1)S(1)} %collective-permute-done.18.refs_1_, bf16[64,96,128]{2,1,0:T(8,128)(2,1)S(1)} %triangle.7.refs_2_, ...), custom_call_target="tpu_custom_call" | custom-call | bytes 4718592 | tf_op jit(solution)/shard_map/fold/pallas_call | solution.py:257
  143.8 0.8 copy-done.23
  144.6 1.2 collective-permute-start.20
  145.8 1.1 copy-done.15
  146.9 0.7 fold.6
  147.7 1.4 collective-permute-start.15
  149.1 1.3 collective-permute-start.17
  150.4 2.1 %fold.5 = (bf16[23,96,128]{2,1,0:T(8,128)(2,1)S(1)}, bf16[23,96,128]{2,1,0:T(8,128)(2,1)}) custom-call(s32[1]{0:T(128)} %bitcast.2.role_ref, bf16[64,96,128]{2,1,0:T(8,128)(2,1)S(1)} %copy-done.11, bf16[64,96,128]{2,1,0:T(8,128)(2,1)S(1)} %collective-permute-done.12.refs_1_), custom_call_target="tpu_custom_call" | custom-call | bytes 4718592 | tf_op jit(solution)/shard_map/fold/pallas_call | solution.py:257
  152.6 0.8 copy-done.18
  153.4 1.5 collective-permute-start.16
  154.8 7.1 %collective-permute-done.20.other_ref = bf16[23,96,128]{2,1,0:T(8,128)(2,1)} collective-permute-done((bf16[23,96,128]{2,1,0:T(8,128)(2,1)}, bf16[23,96,128]{2,1,0:T(8,128)(2,1)}, u32[]{:S(2)}, u32[]{:S(2)}) %collective-permute-start.20) | collective-permute-done | bytes 565280 | tf_op jit(solution)/shard_map/ppermute | solution.py:446
  161.9 1.1 copy-done.24
  163.0 11.8 %finish.2.refs_4_ = bf16[2,23,96,128]{3,2,1,0:T(8,128)(2,1)S(1)} custom-call(s32[1]{0:T(128)} %bitcast.13.flag_ref, bf16[2,23,184,128]{3,2,1,0:T(8,128)(2,1)S(1)} %bitcast.22, bf16[23,96,128]{2,1,0:T(8,128)(2,1)S(1)} %copy-done.24, bf16[23,96,128]{2,1,0:T(8,128)(2,1)} %collective-permute-done.20.other_ref, bf16[128,128]{1,0:T(8,128)(2,1)S(1)} %get-tuple-element.77.refs_0_, ...), custom_call_target="tpu_custom_call" | custom-call | flops 1941438464 | bytes 4333568 | tf_op jit(solution)/shard_map/finish/pallas_call | solution.py:324
  174.8 1.2 select_select_fusion.1.own_ref
  176.0 1.2 select_select_fusion.other_ref
  177.2 12.3 %finish.3 = bf16[2,23,184,128]{3,2,1,0:T(8,128)(2,1)} custom-call(s32[1]{0:T(128)} %bitcast.flag_ref, bf16[2,23,184,128]{3,2,1,0:T(8,128)(2,1)S(1)} %bitcast.23, bf16[23,96,128]{2,1,0:T(8,128)(2,1)S(1)} %select_select_fusion.1.own_ref, bf16[23,96,128]{2,1,0:T(8,128)(2,1)S(1)} %select_select_fusion.other_ref, bf16[128,128]{1,0:T(8,128)(2,1)S(1)} %get-tuple-element.77.refs_0_, ...), custom_call_target="tpu_custom_call" | custom-call | flops 1941438464 | bytes 4333568 | tf_op jit(solution)/shard_map/finish/pallas_call | solution.py:324
  (78 shorter events, 3.9 us)
Async XLA Ops:
  4.9 1.6 copy-start.1
  6.5 15.2 %copy-start.2 = (bf16[46,184,128]{2,1,0:T(8,128)(2,1)S(1)}, bf16[46,184,128]{2,1,0:T(8,128)(2,1)}, u32[]{:S(2)}) copy-start(bf16[46,184,128]{2,1,0:T(8,128)(2,1)} %param.6) | copy-start | bytes 6500356
  12.3 22.4 %collective-permute-start = (bf16[23,64,384]{2,1,0:T(8,128)(2,1)}, bf16[23,64,384]{2,1,0:T(8,128)(2,1)}, u32[]{:S(2)}, u32[]{:S(2)}) collective-permute-start(bf16[23,64,384]{2,1,0:T(8,128)(2,1)} %get-tuple-element.37.refs_0_), channel_id=1, source_target_pairs={{4,8},{6,10},{8,4},{10,6},{5,9},{7,11},{9,5},{11,7},{20,24},{22,26... | collective-permute-start | bytes 3391496 | tf_op jit(solution)/shard_map/ppermute | solution.py:443
  14.0 27.0 %collective-permute-start.1 = (bf16[23,64,384]{2,1,0:T(8,128)(2,1)}, bf16[23,64,384]{2,1,0:T(8,128)(2,1)S(1)}, u32[]{:S(2)}, u32[]{:S(2)}) collective-permute-start(bf16[23,64,384]{2,1,0:T(8,128)(2,1)} %get-tuple-element.35), channel_id=1, source_target_pairs={{0,2},{2,0},{4,6},{6,4},{8,10},{10,8},{12,14},{14,12},{1,3},{3,1},... | collective-permute-start | bytes 3391496 | tf_op jit(solution)/shard_map/ppermute | solution.py:446
  16.1 27.1 %collective-permute-start.2 = (bf16[23,64,384]{2,1,0:T(8,128)(2,1)}, bf16[23,64,384]{2,1,0:T(8,128)(2,1)}, u32[]{:S(2)}, u32[]{:S(2)}) collective-permute-start(bf16[23,64,384]{2,1,0:T(8,128)(2,1)} %get-tuple-element.37.refs_0_), channel_id=1, source_target_pairs={{0,4},{2,6},{4,0},{6,2},{8,12},{10,14},{12,8},{14,10},{1,5},{3,7},... | collective-permute-start | bytes 3391496 | tf_op jit(solution)/shard_map/ppermute | solution.py:443
  21.7 6.4 %copy-start.25 = (bf16[128,128]{1,0:T(8,128)(2,1)S(1)}, bf16[128,128]{1,0:T(8,128)(2,1)}, u32[]{:S(2)}) copy-start(bf16[128,128]{1,0:T(8,128)(2,1)} %param.9) | copy-start | bytes 98308
  26.1 1.0 copy-start.9
  27.1 1.1 copy-start.21
  34.6 9.3 %copy-start.22 = (bf16[23,64,384]{2,1,0:T(8,128)(2,1)S(1)}, bf16[23,64,384]{2,1,0:T(8,128)(2,1)}, u32[]{:S(2)}) copy-start(bf16[23,64,384]{2,1,0:T(8,128)(2,1)} %copy-done.21) | copy-start | bytes 3391492
  34.6 13.7 %copy-start.10 = (bf16[23,64,384]{2,1,0:T(8,128)(2,1)S(1)}, bf16[23,64,384]{2,1,0:T(8,128)(2,1)}, u32[]{:S(2)}) copy-start(bf16[23,64,384]{2,1,0:T(8,128)(2,1)} %copy-done.9) | copy-start | bytes 3391492
  43.2 5.2 %collective-permute-start.6 = (bf16[23,64,384]{2,1,0:T(8,128)(2,1)S(1)}, bf16[23,64,384]{2,1,0:T(8,128)(2,1)S(1)}, u32[]{:S(2)}, u32[]{:S(2)}) collective-permute-start(bf16[23,64,384]{2,1,0:T(8,128)(2,1)S(1)} %collective-permute-done.1.refs_1_), channel_id=1, source_target_pairs={{4,8},{6,10},{8,4},{10,6},{5,9},{7,11},{9,5},{11,7},{20,24},{22,26... | collective-permute-start | bytes 3391496 | tf_op jit(solution)/shard_map/ppermute | solution.py:443
  43.9 24.7 %collective-permute-start.3 = (bf16[23,64,384]{2,1,0:T(8,128)(2,1)S(1)}, bf16[23,64,384]{2,1,0:T(8,128)(2,1)S(1)}, u32[]{:S(2)}, u32[]{:S(2)}) collective-permute-start(bf16[23,64,384]{2,1,0:T(8,128)(2,1)S(1)} %copy-done.22), channel_id=1, source_target_pairs={{0,2},{2,0},{4,6},{6,4},{8,10},{10,8},{12,14},{14,12},{1,3},{3,1},... | collective-permute-start | bytes 3391496 | tf_op jit(solution)/shard_map/ppermute | solution.py:446
  44.2 32.6 %collective-permute-start.4 = (bf16[23,64,384]{2,1,0:T(8,128)(2,1)S(1)}, bf16[23,64,384]{2,1,0:T(8,128)(2,1)}, u32[]{:S(2)}, u32[]{:S(2)}) collective-permute-start(bf16[23,64,384]{2,1,0:T(8,128)(2,1)S(1)} %broadcast_select_fusion.2), channel_id=1, source_target_pairs={{0,4},{2,6},{4,0},{6,2},{8,12},{10,14},{12,8},{14,10},{1,5},{3,7},... | collective-permute-start | bytes 3391496 | tf_op jit(solution)/shard_map/ppermute | solution.py:443
  48.4 1.1 copy-start.7
  68.7 26.6 %collective-permute-start.7 = (bf16[23,64,384]{2,1,0:T(8,128)(2,1)S(1)}, bf16[23,64,384]{2,1,0:T(8,128)(2,1)S(1)}, u32[]{:S(2)}, u32[]{:S(2)}) collective-permute-start(bf16[23,64,384]{2,1,0:T(8,128)(2,1)S(1)} %broadcast_select_fusion.1), channel_id=1, source_target_pairs={{0,4},{2,6},{4,0},{6,2},{8,12},{10,14},{12,8},{14,10},{1,5},{3,7},... | collective-permute-start | bytes 3391496 | tf_op jit(solution)/shard_map/ppermute | solution.py:443
  72.6 23.6 %collective-permute-start.8 = (bf16[23,64,384]{2,1,0:T(8,128)(2,1)}, bf16[23,64,384]{2,1,0:T(8,128)(2,1)S(1)}, u32[]{:S(2)}, u32[]{:S(2)}) collective-permute-start(bf16[23,64,384]{2,1,0:T(8,128)(2,1)} %collective-permute-done.2.refs_0_.refs_4_), channel_id=1, source_target_pairs={{4,8},{6,10},{8,4},{10,6},{5,9},{7,11},{9,5},{11,7},{20,24},{22,26... | collective-permute-start | bytes 3391496 | tf_op jit(solution)/shard_map/ppermute | solution.py:443
  75.2 1.6 copy-start
  83.9 18.8 %collective-permute-start.5 = (bf16[64,96,128]{2,1,0:T(8,128)(2,1)}, bf16[64,96,128]{2,1,0:T(8,128)(2,1)}, u32[]{:S(2)}, u32[]{:S(2)}) collective-permute-start(bf16[64,96,128]{2,1,0:T(8,128)(2,1)} %triangle.4.refs_0_), channel_id=1, source_target_pairs={{5,4},{7,6},{8,9},{10,11},{21,20},{23,22},{24,25},{26,27}} | collective-permute-start | bytes 4718600 | tf_op jit(solution)/shard_map/ppermute | solution.py:453
  91.7 1.5 copy-start.3
  95.3 1.0 copy-start.5
  96.3 1.0 copy-start.12
  97.3 27.1 %collective-permute-start.9 = (bf16[23,64,384]{2,1,0:T(8,128)(2,1)}, bf16[23,64,384]{2,1,0:T(8,128)(2,1)}, u32[]{:S(2)}, u32[]{:S(2)}) collective-permute-start(bf16[23,64,384]{2,1,0:T(8,128)(2,1)} %broadcast_select_fusion), channel_id=1, source_target_pairs={{0,4},{2,6},{4,0},{6,2},{8,12},{10,14},{12,8},{14,10},{1,5},{3,7},... | collective-permute-start | bytes 3391496 | tf_op jit(solution)/shard_map/ppermute | solution.py:443
  101.0 23.5 %collective-permute-start.11 = (bf16[23,64,384]{2,1,0:T(8,128)(2,1)}, bf16[23,64,384]{2,1,0:T(8,128)(2,1)}, u32[]{:S(2)}, u32[]{:S(2)}) collective-permute-start(bf16[23,64,384]{2,1,0:T(8,128)(2,1)} %collective-permute-done.4.refs_1_.refs_2_), channel_id=1, source_target_pairs={{4,8},{6,10},{8,4},{10,6},{5,9},{7,11},{9,5},{11,7},{20,24},{22,26... | collective-permute-start | bytes 3391496 | tf_op jit(solution)/shard_map/ppermute | solution.py:443
  102.7 11.0 %copy-start.6 = (bf16[23,64,384]{2,1,0:T(8,128)(2,1)S(1)}, bf16[23,64,384]{2,1,0:T(8,128)(2,1)}, u32[]{:S(2)}) copy-start(bf16[23,64,384]{2,1,0:T(8,128)(2,1)} %copy-done.5) | copy-start | bytes 3391492
  107.0 0.9 copy-start.16
  107.8 14.9 %collective-permute-start.10 = (bf16[23,96,128]{2,1,0:T(8,128)(2,1)}, bf16[23,96,128]{2,1,0:T(8,128)(2,1)}, u32[]{:S(2)}, u32[]{:S(2)}) collective-permute-start(bf16[23,96,128]{2,1,0:T(8,128)(2,1)} %get-tuple-element.45), channel_id=1, source_target_pairs={{4,6},{6,4},{9,11},{11,9},{20,22},{22,20},{25,27},{27,25}} | collective-permute-start | bytes 1695752 | tf_op jit(solution)/shard_map/ppermute | solution.py:467
  109.3 30.4 %collective-permute-start.18 = (bf16[64,96,128]{2,1,0:T(8,128)(2,1)}, bf16[64,96,128]{2,1,0:T(8,128)(2,1)S(1)}, u32[]{:S(2)}, u32[]{:S(2)}) collective-permute-start(bf16[64,96,128]{2,1,0:T(8,128)(2,1)} %copy-done.3), channel_id=1, source_target_pairs={{1,0},{3,2},{5,4},{7,6},{8,9},{10,11},{12,13},{14,15},{17,16},{19,... | collective-permute-start | bytes 4718600 | tf_op jit(solution)/shard_map/ppermute | solution.py:453
  113.7 1.3 copy-start.8
  115.0 9.5 %copy-start.13 = (bf16[23,64,384]{2,1,0:T(8,128)(2,1)S(1)}, bf16[23,64,384]{2,1,0:T(8,128)(2,1)}, u32[]{:S(2)}) copy-start(bf16[23,64,384]{2,1,0:T(8,128)(2,1)} %copy-done.12) | copy-start | bytes 3391492
  121.2 18.6 %copy-start.4 = (bf16[64,96,128]{2,1,0:T(8,128)(2,1)S(1)}, bf16[64,96,128]{2,1,0:T(8,128)(2,1)}, u32[]{:S(2)}) copy-start(bf16[64,96,128]{2,1,0:T(8,128)(2,1)} %copy-done.3) | copy-start | bytes 4718596
  121.2 18.5 %collective-permute-start.19 = (bf16[64,96,128]{2,1,0:T(8,128)(2,1)S(1)}, bf16[64,96,128]{2,1,0:T(8,128)(2,1)}, u32[]{:S(2)}, u32[]{:S(2)}) collective-permute-start(bf16[64,96,128]{2,1,0:T(8,128)(2,1)S(1)} %triangle.7.refs_2_), channel_id=1, source_target_pairs={{0,1},{2,3},{4,5},{6,7},{9,8},{11,10},{13,12},{15,14},{16,17},{18,... | collective-permute-start | bytes 4718600 | tf_op jit(solution)/shard_map/ppermute | solution.py:453
  133.4 10.3 %copy-start.14 = (bf16[64,48,128]{2,1,0:T(8,128)(2,1)}, bf16[64,48,128]{2,1,0:T(8,128)(2,1)S(1)}, u32[]{:S(2)}) copy-start(bf16[64,48,128]{2,1,0:T(8,128)(2,1)S(1)} %get-tuple-element.50.refs_0_) | copy-start | bytes 2359300
  133.4 17.0 %collective-permute-start.12 = (bf16[64,96,128]{2,1,0:T(8,128)(2,1)}, bf16[64,96,128]{2,1,0:T(8,128)(2,1)S(1)}, u32[]{:S(2)}, u32[]{:S(2)}) collective-permute-start(bf16[64,96,128]{2,1,0:T(8,128)(2,1)} %get-tuple-element.48.refs_0_), channel_id=1, source_target_pairs={{1,0},{3,2},{4,5},{6,7},{9,8},{11,10},{12,13},{14,15},{17,16},{19,... | collective-permute-start | bytes 4718600 | tf_op jit(solution)/shard_map/ppermute | solution.py:453
  138.2 7.6 %collective-permute-start.13 = (bf16[64,48,128]{2,1,0:T(8,128)(2,1)S(1)}, bf16[64,48,128]{2,1,0:T(8,128)(2,1)S(1)}, u32[]{:S(2)}, u32[]{:S(2)}) collective-permute-start(bf16[64,48,128]{2,1,0:T(8,128)(2,1)S(1)} %get-tuple-element.50.refs_0_), channel_id=1, source_target_pairs={{5,4},{7,6},{8,9},{10,11},{21,20},{23,22},{24,25},{26,27}} | collective-permute-start | bytes 2359304 | tf_op jit(solution)/shard_map/ppermute | solution.py:453
  138.9 6.9 %collective-permute-start.14 = (bf16[64,48,128]{2,1,0:T(8,128)(2,1)S(1)}, bf16[64,48,128]{2,1,0:T(8,128)(2,1)S(1)}, u32[]{:S(2)}, u32[]{:S(2)}) collective-permute-start(bf16[64,48,128]{2,1,0:T(8,128)(2,1)S(1)} %get-tuple-element.51.refs_2_), channel_id=1, source_target_pairs={{4,5},{6,7},{9,8},{11,10},{20,21},{22,23},{25,24},{27,26}} | collective-permute-start | bytes 2359304 | tf_op jit(solution)/shard_map/ppermute | solution.py:453
  143.8 0.8 copy-start.23
  144.6 5.9 %copy-start.11 = (bf16[64,96,128]{2,1,0:T(8,128)(2,1)S(1)}, bf16[64,96,128]{2,1,0:T(8,128)(2,1)}, u32[]{:S(2)}) copy-start(bf16[64,96,128]{2,1,0:T(8,128)(2,1)} %get-tuple-element.48.refs_0_) | copy-start | bytes 4718596
  144.6 17.4 %collective-permute-start.20 = (bf16[23,96,128]{2,1,0:T(8,128)(2,1)}, bf16[23,96,128]{2,1,0:T(8,128)(2,1)}, u32[]{:S(2)}, u32[]{:S(2)}) collective-permute-start(bf16[23,96,128]{2,1,0:T(8,128)(2,1)} %get-tuple-element.56), channel_id=1, source_target_pairs={{0,2},{2,0},{4,6},{6,4},{8,10},{10,8},{12,14},{14,12},{1,3},{3,1},... | collective-permute-start | bytes 1695752 | tf_op jit(solution)/shard_map/ppermute | solution.py:446
  145.8 1.1 copy-start.15
  147.7 14.3 %copy-start.20 = (bf16[1024,128]{1,0:T(8,128)(2,1)S(1)}, bf16[1024,128]{1,0:T(8,128)(2,1)}, u32[]{:S(2)}) copy-start(bf16[1024,128]{1,0:T(8,128)(2,1)} %multiply_bitcast_fusion.refs_2_) | copy-start | bytes 786436
  147.7 27.1 %collective-permute-start.15 = (bf16[23,96,128]{2,1,0:T(8,128)(2,1)S(1)}, bf16[23,96,128]{2,1,0:T(8,128)(2,1)}, u32[]{:S(2)}, u32[]{:S(2)}) collective-permute-start(bf16[23,96,128]{2,1,0:T(8,128)(2,1)S(1)} %fold.6), channel_id=1, source_target_pairs={{5,1},{7,3},{8,12},{10,14},{21,17},{23,19},{24,28},{26,30}} | collective-permute-start | bytes 1695752 | tf_op jit(solution)/shard_map/ppermute | solution.py:461
  149.1 26.9 %collective-permute-start.17 = (bf16[23,96,128]{2,1,0:T(8,128)(2,1)S(1)}, bf16[23,96,128]{2,1,0:T(8,128)(2,1)}, u32[]{:S(2)}, u32[]{:S(2)}) collective-permute-start(bf16[23,96,128]{2,1,0:T(8,128)(2,1)S(1)} %fold.6), channel_id=1, source_target_pairs={{4,3},{6,1},{9,14},{11,12},{20,19},{22,17},{25,30},{27,28}} | collective-permute-start | bytes 1695752 | tf_op jit(solution)/shard_map/ppermute | solution.py:461
  152.6 0.8 copy-start.18
  153.4 22.7 %collective-permute-start.16 = (bf16[23,96,128]{2,1,0:T(8,128)(2,1)}, bf16[23,96,128]{2,1,0:T(8,128)(2,1)}, u32[]{:S(2)}, u32[]{:S(2)}) collective-permute-start(bf16[23,96,128]{2,1,0:T(8,128)(2,1)} %get-tuple-element.52), channel_id=1, source_target_pairs={{0,2},{2,0},{5,7},{7,5},{8,10},{10,8},{13,15},{15,13},{16,18},{18,... | collective-permute-start | bytes 1695752 | tf_op jit(solution)/shard_map/ppermute | solution.py:467
  161.9 1.1 copy-start.24
  163.0 11.8 %copy-start.17 = (bf16[23,96,128]{2,1,0:T(8,128)(2,1)S(1)}, bf16[23,96,128]{2,1,0:T(8,128)(2,1)}, u32[]{:S(2)}) copy-start(bf16[23,96,128]{2,1,0:T(8,128)(2,1)} %copy-done.16) | copy-start | bytes 1695748
  163.0 11.8 %copy-start.19 = (bf16[23,96,128]{2,1,0:T(8,128)(2,1)S(1)}, bf16[23,96,128]{2,1,0:T(8,128)(2,1)}, u32[]{:S(2)}) copy-start(bf16[23,96,128]{2,1,0:T(8,128)(2,1)} %copy-done.18) | copy-start | bytes 1695748

commit v11 on v10

--- a/solution.py
+++ b/solution.py
@@ -270,14 +270,49 @@
     )(role, *parts)
 
 
-def finish_kernel(flag_ref, pair_ref, own_ref, other_ref, *refs):
-    gate_ref, out_w_ref, in_ref, back_ref = refs[:4]
-    earlier_ref, out_ref = refs[4] if len(refs) == 6 else None, refs[-1]
+def prepare_kernel(flag_ref, pair_ref, gate_w_ref, pair_out_ref, gate_ref):
     _, half, cols, width = pair_ref.shape
+    block = cols // 2
+    front = flag_ref[0] == 0
+
+    def step(i, carry):
+        first = jnp.minimum(2 * i, half - 2)
+        pair = []
+        for h, r in [(h, first + e) for h in range(2) for e in range(2)]:
+            row = pair_ref[h, r].astype(F32)
+            pair.append(jnp.where(front, row[:block], row[block:]))
+        pair = jnp.concatenate(pair, axis=0).T
+        normed = norm_chans(pair).astype(BF16)
+        pair_out_ref[i, :, : 4 * block] = pair.astype(BF16)
+        gate = jnp.dot(gate_w_ref[...], normed, preferred_element_type=F32)
+        gate_ref[i, :, : 4 * block] = twice_sigmoid(gate)
+        return carry
+
+    lax.fori_loop(0, pair_out_ref.shape[0], step, 0, unroll=4)
+
+
+def prepare(flag, pair, gate_w):
+    _, half, cols, width = pair.shape
+    shape = ((half + 1) // 2, width, padded(2 * cols, 128))
+    return pl.pallas_call(
+        prepare_kernel,
+        out_shape=(jax.ShapeDtypeStruct(shape, BF16), jax.ShapeDtypeStruct(shape, F32)),
+        in_specs=[pl.BlockSpec(memory_space=pltpu.SMEM)] + whole(2),
+        out_specs=whole(2),
+        compiler_params=params(),
+        cost_estimate=cost(pair.size * width, 6 * pair.size, pair.size // 2),
+        name="prepare",
+    )(flag, pair, gate_w)
+
+
+def finish_kernel(flag_ref, pair_ref, gate_ref, own_ref, other_ref, *refs, cols):
+    out_w_ref, in_ref, back_ref = refs[:3]
+    earlier_ref, out_ref = refs[3] if len(refs) == 5 else None, refs[-1]
+    steps, width, _ = pair_ref.shape
+    half = own_ref.shape[0]
     block, chans = cols // 2, width // 2
     hidden_units = back_ref.shape[1]
     front = flag_ref[0] == 0
-    steps = (half + 1) // 2
 
     def step(i, carry):
         first = jnp.minimum(2 * i, half - 2)
@@ -289,15 +324,9 @@
             for e in range(2)
         ]
         tri_normed = norm_chans(jnp.concatenate(tri, axis=1).astype(F32)).astype(BF16)
-        pair = []
-        for h, r in rows:
-            row = pair_ref[h, r].astype(F32)
-            pair.append(jnp.where(front, row[:block], row[block:]))
-        pair = jnp.concatenate(pair, axis=0).T
-        normed = norm_chans(pair).astype(BF16)
-        out_gate = twice_sigmoid(jnp.dot(gate_ref[...], normed, preferred_element_type=F32))
+        pair = pair_ref[i, :, : 4 * block].astype(F32)
         update = jnp.dot(out_w_ref[...], tri_normed, preferred_element_type=F32)
-        updated = pair + out_gate * update
+        updated = pair + gate_ref[i, :, : 4 * block] * update
         trans_normed = norm_chans(updated).astype(BF16)
         expanded = jnp.dot(in_ref[...], trans_normed, preferred_element_type=F32)
         swish, linear = expanded[:hidden_units], expanded[hidden_units:]
@@ -317,19 +346,20 @@
     lax.fori_loop(0, steps, step, 0, unroll=4)
 
 
-def finish(flag, pair, own, other, weights, earlier=None):
-    _, half, cols, width = pair.shape
-    shape = pair.shape if earlier is not None else (2, half, padded(cols // 2, 16), width)
+def finish(flag, cols, prepared, own, other, weights, earlier=None):
+    half, _, width = own.shape
+    shape = (2, half, padded(cols // 2, 16) if earlier is None else cols, width)
     extra = [] if earlier is None else [earlier]
+    size = own.size * 2
     return pl.pallas_call(
-        finish_kernel,
+        functools.partial(finish_kernel, cols=cols),
         out_shape=jax.ShapeDtypeStruct(shape, BF16),
         in_specs=[pl.BlockSpec(memory_space=pltpu.SMEM)] + whole(7 + len(extra)),
         out_specs=pl.BlockSpec(memory_space=VMEM),
         compiler_params=params(),
-        cost_estimate=cost(14 * pair.size * width, 4 * pair.size, 3 * pair.size),
+        cost_estimate=cost(26 * size * width, 10 * size, 5 * size),
         name="finish",
-    )(flag, pair, own, other, *weights, *extra)
+    )(flag, *prepared, own, other, *weights, *extra)
 
 
 def layer_norm(values):
@@ -504,20 +534,21 @@
     mate_own, near_own, right_beside = one
     order = jnp.where(is_keeper, place % 2, place // 2)
     weights = [
-        in_weight[:, 4 * width :].T * BF16(0.5),
         by_side(out_weight, 0).T * BF16(0.5),
         jnp.where(jnp.arange(trans_in.shape[1])[:, None] < trans_out.shape[0], BF16(0.5), BF16(1.0))
         * trans_in.T,
         trans_out.T,
     ]
+    gate_weight = in_weight[:, 4 * width :].T * BF16(0.5)
     left_own, left_far = project(where, folded, gate_pair(0))
     two = phase(
         [(swap, either(near_own, right_beside)), (hop(cross), right_beside), (across, left_far)],
-        one + weights,
-    )
+        one + weights + [gate_weight],
+    )
+    prepared = [prepare(scalars(f), after(folded, *one), gate_weight) for f in (order, 1 - order)]
     mate_beside, near_beside, left_beside = two
     three = phase(
-        [(swap, either(near_beside, left_own)), (hop(cross), mate_own)], (near_beside, left_beside)
+        [(swap, either(near_beside, left_own)), (hop(cross), mate_own)], (near_beside, left_beside, *prepared[0], *prepared[1]),
     )
     guest_own, far_own = three
 
@@ -557,12 +588,14 @@
     late_block = fold(half, role, late, late_rest)
     late_other = side_to_side(late_block[1], everyone, (0, 1, 0, 1))
 
-    earlier = finish(scalars(order), folded, after(first[0], lent), first_other, weights)
+    earlier = finish(
+        scalars(order), tile_cols, prepared[0], after(first[0], lent), first_other, weights
+    )
     own, other = (
         jnp.where(inner & is_keeper, early, jnp.where(inner | is_keeper, end, back))
         for early, end, back in zip((mate_block[0], mate_other), (late_block[0], late_other), given)
     )
-    result = finish(scalars(1 - order), folded, own, other, weights, earlier)
+    result = finish(scalars(1 - order), tile_cols, prepared[1], own, other, weights, earlier)
     return result.reshape(tile_rows, tile_cols, width)
 
 

time: 191 us -> 193 us (1.010)
  Pallas kernels: 75.2 us -> 78.5 us
  waiting for transfers between devices: 38.5 us -> 36.1 us
  other arithmetic: 7.81 us -> 10.1 us
    ppermute x3, waiting for transfers between devices: 32.7 us -> 29.4 us  [across(): return lax.ppermute(value, 'row', [(i, i ^ 1) for i in range(8)])]
    ppermute x8, starting transfers between devices: 19.5 us -> 22.4 us  [among(): lax.ppermute(value, 'row', [(2 * s + b, 2 * t + b) for s, t in moves for...]
    ppermute x6, starting transfers between devices: 13.9 us -> 11.1 us  [to_core(): return lax.ppermute(value, ('row', 'col'), perm)]
    select_n x3, other arithmetic: 1.63 us -> 3.81 us  [either(): return jnp.where(inner, at_inner, at_end)]
    unnamed x68 -> x56, local copies, waits for them, and re-layouts: 20.7 us -> 19.4 us
    pallas_call x2 -> x4, Pallas kernels: 24.1 us -> 24.9 us  [the longest x2 21.4 us: finish(): pl.pallas_call(functools.partial(finish_kernel, cols=cols), out_shape=jax...]
  transfers between devices with their start and end apart: 21 -> 21, of which waited for: 6 -> 4; matrix products, arithmetic and copies ran while one was open for 6% -> 8% of each run, Pallas kernels for 30% -> 32%
where the time goes in v11:
time: 193 us; the launch traced here: 192 us
  Pallas kernels  78.5 us (41%)
  starting transfers between devices  42.9 us (22%)
  waiting for transfers between devices  36.1 us (19%)
  local copies, waits for them, and re-layouts  23.2 us (12%)
  other arithmetic  10.1 us (5%)
    ppermute x3, waiting for transfers between devices, across(): return lax.ppermute(value, 'row', [(i, i ^ 1) for i in range(8)])  29.4 us
    pallas_call x4, Pallas kernels, triangle(): pl.pallas_call(functools.partial(triangle_kernel, counts=[len(piece) for...  28.3 us
    ppermute x8, starting transfers between devices, among(): lax.ppermute(value, 'row', [(2 * s + b, 2 * t + b) for s, t in moves for...  22.4 us
    pallas_call x2, Pallas kernels, finish(): pl.pallas_call(functools.partial(finish_kernel, cols=cols), out_shape=jax...  21.4 us
    unnamed x56, local copies, waits for them, and re-layouts  19.4 us
    ppermute x6, starting transfers between devices, to_core(): return lax.ppermute(value, ('row', 'col'), perm)  11.1 us
    pallas_call x2, Pallas kernels, project(): pl.pallas_call(project_kernel, out_shape=(piece, piece), in_specs=[pl.Blo...  11.1 us
    pallas_call x4, Pallas kernels, fold(): pl.pallas_call(functools.partial(fold_kernel, outputs=outputs, half=half)...  11.1 us
  transfers between devices with their start and end apart: 21, of which 4 were waited for; matrix products, arithmetic and copies ran while one was open for 8% of the time, Pallas kernels for 32%

profile of v11, /device:TPU:1, one launch (start us, length us, event | category | flops | bytes accessed | tf_op | source)
XLA Modules:
  0.0 191.8 jit_solution(6956864892881602355)
XLA Ops:
  0.0 0.8 fusion.6
  0.8 1.6 fusion.5
  2.5 1.2 slice.60
  5.1 1.6 copy-done.1
  6.7 5.7 %project.2 = (bf16[23,64,384]{2,1,0:T(8,128)(2,1)}, bf16[23,64,384]{2,1,0:T(8,128)(2,1)}) custom-call(s32[3]{0:T(128)S(1)} %pad_add_fusion.where_ref, bf16[2,23,184,128]{3,2,1,0:T(8,128)(2,1)S(1)} %bitcast.20, bf16[256,128]{1,0:T(8,128)(2,1)S(1)} %fusion.weight_ref), custom_call_target="tpu_custom_call" | custom-call | flops 554696704 | bytes 4333568 | tf_op jit(solution)/shard_map/project/pallas_call | solution.py:73
  12.4 2.1 %collective-permute-start = (bf16[23,64,384]{2,1,0:T(8,128)(2,1)}, bf16[23,64,384]{2,1,0:T(8,128)(2,1)}, u32[]{:S(2)}, u32[]{:S(2)}) collective-permute-start(bf16[23,64,384]{2,1,0:T(8,128)(2,1)} %get-tuple-element.39.refs_0_), channel_id=1, source_target_pairs={{0,4},{2,6},{4,0},{6,2},{8,12},{10,14},{12,8},{14,10},{1,5},{3,7},... | collective-permute-start | bytes 3391496 | tf_op jit(solution)/shard_map/ppermute | solution.py:473
  14.5 1.7 collective-permute-start.1
  16.2 1.2 collective-permute-start.2
  17.4 0.7 copy.32
  18.2 0.8 copy.33
  19.4 0.8 maximum_select_fusion.2
  20.3 5.4 %project.3 = (bf16[23,64,384]{2,1,0:T(8,128)(2,1)S(1)}, bf16[23,64,384]{2,1,0:T(8,128)(2,1)}) custom-call(s32[3]{0:T(128)S(1)} %pad_add_fusion.where_ref, bf16[2,23,184,128]{3,2,1,0:T(8,128)(2,1)S(1)} %bitcast.21, bf16[256,128]{1,0:T(8,128)(2,1)S(1)} %fusion.1.weight_ref), custom_call_target="tpu_custom_call" | custom-call | flops 554696704 | bytes 4333568 | tf_op jit(solution)/shard_map/project/pallas_call | solution.py:73
  25.6 1.1 copy-done.5
  26.8 1.0 copy.24
  28.6 1.8 copy.23
  30.5 0.8 fusion.3
  31.3 1.9 multiply_bitcast_fusion.refs_1_
  33.2 8.7 %collective-permute-done.2.refs_1_ = bf16[23,64,384]{2,1,0:T(8,128)(2,1)S(1)} collective-permute-done((bf16[23,64,384]{2,1,0:T(8,128)(2,1)}, bf16[23,64,384]{2,1,0:T(8,128)(2,1)S(1)}, u32[]{:S(2)}, u32[]{:S(2)}) %collective-permute-start.2) | collective-permute-done | bytes 1130528 | tf_op jit(solution)/shard_map/ppermute | solution.py:476
  41.9 1.2 broadcast_select_fusion.2
  43.1 1.7 collective-permute-start.6
  44.8 1.2 collective-permute-start.3
  46.0 4.6 %collective-permute-start.4 = (bf16[23,64,384]{2,1,0:T(8,128)(2,1)}, bf16[23,64,384]{2,1,0:T(8,128)(2,1)}, u32[]{:S(2)}, u32[]{:S(2)}) collective-permute-start(bf16[23,64,384]{2,1,0:T(8,128)(2,1)} %broadcast_select_fusion.2), channel_id=1, source_target_pairs={{0,4},{2,6},{4,0},{6,2},{8,12},{10,14},{12,8},{14,10},{1,5},{3,7},... | collective-permute-start | bytes 3391496 | tf_op jit(solution)/shard_map/ppermute | solution.py:473
  50.6 1.8 prepare.3
  52.4 1.4 copy-done.14
  53.8 1.0 copy-done.15
  54.9 1.8 prepare.2
  56.7 1.0 copy-done.9
  57.8 1.3 copy-done.7
  59.1 10.6 %collective-permute-done.3.beside_ref = bf16[23,64,384]{2,1,0:T(8,128)(2,1)} collective-permute-done((bf16[23,64,384]{2,1,0:T(8,128)(2,1)}, bf16[23,64,384]{2,1,0:T(8,128)(2,1)}, u32[]{:S(2)}, u32[]{:S(2)}) %collective-permute-start.3) | collective-permute-done | bytes 1130528 | tf_op jit(solution)/shard_map/ppermute | solution.py:476
  69.6 5.3 %collective-permute-start.7 = (bf16[23,64,384]{2,1,0:T(8,128)(2,1)S(1)}, bf16[23,64,384]{2,1,0:T(8,128)(2,1)S(1)}, u32[]{:S(2)}, u32[]{:S(2)}) collective-permute-start(bf16[23,64,384]{2,1,0:T(8,128)(2,1)S(1)} %broadcast_select_fusion.1), channel_id=1, source_target_pairs={{0,4},{2,6},{4,0},{6,2},{8,12},{10,14},{12,8},{14,10},{1,5},{3,7},... | collective-permute-start | bytes 3391496 | tf_op jit(solution)/shard_map/ppermute | solution.py:473
  74.9 0.7 collective-permute-start.8
  75.7 3.2 %left_major.1.left_ref = bf16[64,96,256]{2,1,0:T(8,128)(2,1)S(1)} custom-call(bf16[23,64,384]{2,1,0:T(8,128)(2,1)S(1)} %copy-done.6, bf16[23,64,384]{2,1,0:T(8,128)(2,1)} %collective-permute-done.3.beside_ref), custom_call_target="tpu_custom_call" | custom-call | bytes 4521984 | tf_op jit(solution)/shard_map/left_major/pallas_call | solution.py:116
  78.9 1.6 copy-done
  80.6 7.0 %triangle.4.refs_0_ = bf16[64,96,128]{2,1,0:T(8,128)(2,1)} custom-call(s32[2]{0:T(128)S(1)} %pad_add_fusion.1.flag_ref, bf16[64,96,256]{2,1,0:T(8,128)(2,1)} %copy-done, bf16[23,64,384]{2,1,0:T(8,128)(2,1)} %collective-permute-done.refs_0_.refs_4_, bf16[23,64,384]{2,1,0:T(8,128)(2,1)} %collective-permute-done.4.refs_1_.refs_2_), custom_call_target="tpu_custom_call" | custom-call | flops 402653184 | bytes 5652480 | tf_op jit(solution)/shard_map/triangle/pallas_call | solution.py:195
  87.6 1.9 collective-permute-start.5
  89.5 5.9 %triangle.5.refs_0_ = bf16[64,96,128]{2,1,0:T(8,128)(2,1)S(1)} custom-call(s32[2]{0:T(128)S(1)} %pad_add_fusion.1.flag_ref, bf16[64,96,256]{2,1,0:T(8,128)(2,1)} %copy-done, bf16[23,64,384]{2,1,0:T(8,128)(2,1)} %get-tuple-element.39.refs_0_, bf16[23,64,384]{2,1,0:T(8,128)(2,1)S(1)} %collective-permute-done.2.refs_1_), custom_call_target="tpu_custom_call" | custom-call | flops 402653184 | bytes 5652480 | tf_op jit(solution)/shard_map/triangle/pallas_call | solution.py:195
  95.4 2.4 %broadcast_select_fusion = bf16[23,64,384]{2,1,0:T(8,128)(2,1)} fusion(bf16[23,64,384]{2,1,0:T(8,128)(2,1)S(1)} %collective-permute-done.2.refs_1_, bf16[23,64,384]{2,1,0:T(8,128)(2,1)} %collective-permute-done.3.beside_ref, pred[]{:T(512)S(6)} %or.7), kind=kLoop, calls=%fused_computation | loop fusion | flops 565248 | bytes 3391489 | tf_op jit(solution)/shard_map/jit(_where)/select_n | solution.py:529
  97.8 1.1 copy-done.3
  98.9 1.0 copy-done.11
  99.9 4.7 %collective-permute-start.9 = (bf16[23,64,384]{2,1,0:T(8,128)(2,1)}, bf16[23,64,384]{2,1,0:T(8,128)(2,1)}, u32[]{:S(2)}, u32[]{:S(2)}) collective-permute-start(bf16[23,64,384]{2,1,0:T(8,128)(2,1)} %broadcast_select_fusion), channel_id=1, source_target_pairs={{0,4},{2,6},{4,0},{6,2},{8,12},{10,14},{12,8},{14,10},{1,5},{3,7},... | collective-permute-start | bytes 3391496 | tf_op jit(solution)/shard_map/ppermute | solution.py:473
  104.7 1.6 collective-permute-start.11
  106.3 4.3 %fold.4 = (bf16[23,96,128]{2,1,0:T(8,128)(2,1)S(1)}, bf16[23,96,128]{2,1,0:T(8,128)(2,1)}) custom-call(s32[1]{0:T(128)} %bitcast.6.role_ref, bf16[64,96,128]{2,1,0:T(8,128)(2,1)} %triangle.4.refs_0_, bf16[64,96,128]{2,1,0:T(8,128)(2,1)} %collective-permute-done.5.refs_1_), custom_call_target="tpu_custom_call" | custom-call | bytes 4718592 | tf_op jit(solution)/shard_map/fold/pallas_call | solution.py:257
  110.6 1.5 collective-permute-start.10
  112.2 3.1 %collective-permute-start.18 = (bf16[64,96,128]{2,1,0:T(8,128)(2,1)S(1)}, bf16[64,96,128]{2,1,0:T(8,128)(2,1)S(1)}, u32[]{:S(2)}, u32[]{:S(2)}) collective-permute-start(bf16[64,96,128]{2,1,0:T(8,128)(2,1)S(1)} %triangle.5.refs_0_), channel_id=1, source_target_pairs={{1,0},{3,2},{5,4},{7,6},{8,9},{10,11},{12,13},{14,15},{17,16},{19,... | collective-permute-start | bytes 4718600 | tf_op jit(solution)/shard_map/ppermute | solution.py:483
  115.3 6.3 %triangle.7.refs_2_ = bf16[64,96,128]{2,1,0:T(8,128)(2,1)S(1)} custom-call(s32[2]{0:T(128)S(1)} %pad_add_fusion.2.flag_ref, bf16[64,96,256]{2,1,0:T(8,128)(2,1)} %copy-done, bf16[23,64,384]{2,1,0:T(8,128)(2,1)} %collective-permute-done.1.refs_0_, bf16[23,64,384]{2,1,0:T(8,128)(2,1)} %collective-permute-done.6.refs_1_, ...), custom_call_target="tpu_custom_call" | custom-call | flops 402653184 | bytes 5652480 | tf_op jit(solution)/shard_map/triangle/pallas_call | solution.py:195
  121.6 1.3 collective-permute-start.19
  122.9 6.6 %collective-permute-done.9.refs_1_.refs_5_ = bf16[23,64,384]{2,1,0:T(8,128)(2,1)} collective-permute-done((bf16[23,64,384]{2,1,0:T(8,128)(2,1)}, bf16[23,64,384]{2,1,0:T(8,128)(2,1)}, u32[]{:S(2)}, u32[]{:S(2)}) %collective-permute-start.9) | collective-permute-done | bytes 1130528 | tf_op jit(solution)/shard_map/ppermute | solution.py:473
  129.6 8.9 %triangle.6 = (bf16[64,96,128]{2,1,0:T(8,128)(2,1)}, bf16[64,48,128]{2,1,0:T(8,128)(2,1)S(1)}, bf16[64,48,128]{2,1,0:T(8,128)(2,1)S(1)}) custom-call(s32[2]{0:T(128)S(1)} %pad_add_fusion.2.flag_ref, bf16[64,96,256]{2,1,0:T(8,128)(2,1)} %copy-done, bf16[23,64,384]{2,1,0:T(8,128)(2,1)S(1)} %copy-done.4, ...), custom_call_target="tpu_custom_call" | custom-call | flops 805306368 | bytes 5652480 | tf_op jit(solution)/shard_map/triangle/pallas_call | solution.py:195
  138.5 3.3 %collective-permute-start.12 = (bf16[64,96,128]{2,1,0:T(8,128)(2,1)}, bf16[64,96,128]{2,1,0:T(8,128)(2,1)S(1)}, u32[]{:S(2)}, u32[]{:S(2)}) collective-permute-start(bf16[64,96,128]{2,1,0:T(8,128)(2,1)} %get-tuple-element.58.refs_0_), channel_id=1, source_target_pairs={{1,0},{3,2},{4,5},{6,7},{9,8},{11,10},{12,13},{14,15},{17,16},{19,... | collective-permute-start | bytes 4718600 | tf_op jit(solution)/shard_map/ppermute | solution.py:483
  141.8 0.9 collective-permute-start.13
  143.4 3.9 %fold.7 = (bf16[23,96,128]{2,1,0:T(8,128)(2,1)S(1)}, bf16[23,96,128]{2,1,0:T(8,128)(2,1)}) custom-call(s32[1]{0:T(128)} %bitcast.6.role_ref, bf16[64,96,128]{2,1,0:T(8,128)(2,1)S(1)} %triangle.5.refs_0_, bf16[64,96,128]{2,1,0:T(8,128)(2,1)S(1)} %collective-permute-done.18.refs_1_, bf16[64,96,128]{2,1,0:T(8,128)(2,1)S(1)} %triangle.7.refs_2_, ...), custom_call_target="tpu_custom_call" | custom-call | bytes 4718592 | tf_op jit(solution)/shard_map/fold/pallas_call | solution.py:257
  147.4 0.8 copy-done.17
  148.2 1.2 collective-permute-start.20
  149.4 0.7 fold.6
  150.2 1.4 collective-permute-start.15
  151.6 1.3 collective-permute-start.17
  152.9 2.1 %fold.5 = (bf16[23,96,128]{2,1,0:T(8,128)(2,1)S(1)}, bf16[23,96,128]{2,1,0:T(8,128)(2,1)}) custom-call(s32[1]{0:T(128)} %bitcast.6.role_ref, bf16[64,96,128]{2,1,0:T(8,128)(2,1)S(1)} %copy-done.8, bf16[64,96,128]{2,1,0:T(8,128)(2,1)S(1)} %collective-permute-done.12.refs_1_), custom_call_target="tpu_custom_call" | custom-call | bytes 4718592 | tf_op jit(solution)/shard_map/fold/pallas_call | solution.py:257
  155.0 1.5 collective-permute-start.16
  156.5 10.2 %collective-permute-done.20.other_ref = bf16[23,96,128]{2,1,0:T(8,128)(2,1)} collective-permute-done((bf16[23,96,128]{2,1,0:T(8,128)(2,1)}, bf16[23,96,128]{2,1,0:T(8,128)(2,1)}, u32[]{:S(2)}, u32[]{:S(2)}) %collective-permute-start.20) | collective-permute-done | bytes 565280 | tf_op jit(solution)/shard_map/ppermute | solution.py:476
  166.7 1.1 copy-done.18
  167.7 9.9 %finish.2.refs_3_ = bf16[2,23,96,128]{3,2,1,0:T(8,128)(2,1)S(1)} custom-call(s32[1]{0:T(128)} %bitcast.13.flag_ref, bf16[12,128,384]{2,1,0:T(8,128)(2,1)S(1)} %copy-done.16, f32[12,128,384]{2,1,0:T(8,128)} %copy-done.14, bf16[23,96,128]{2,1,0:T(8,128)(2,1)S(1)} %copy-done.18, bf16[23,96,128]{2,1,0:T(8,128)(2,1)} %collective-permute-done.20.other_ref, ...), custom_call_target="tpu_custom_call" | custom-call | flops 1881145344 | bytes 5652480 | tf_op jit(solution)/shard_map/finish/pallas_call | solution.py:354
  177.7 1.2 select_select_fusion.1.own_ref
  178.9 1.2 select_select_fusion.other_ref
  180.3 11.5 %finish.3 = bf16[2,23,184,128]{3,2,1,0:T(8,128)(2,1)} custom-call(s32[1]{0:T(128)} %bitcast.flag_ref, bf16[12,128,384]{2,1,0:T(8,128)(2,1)S(1)} %copy-done.10, f32[12,128,384]{2,1,0:T(8,128)} %copy-done.7, bf16[23,96,128]{2,1,0:T(8,128)(2,1)S(1)} %select_select_fusion.1.own_ref, bf16[23,96,128]{2,1,0:T(8,128)(2,1)S(1)} %select_select_fusion.other_ref, ...), custom_call_target="tpu_custom_call" | custom-call | flops 1881145344 | bytes 5652480 | tf_op jit(solution)/shard_map/finish/pallas_call | solution.py:354
  (68 shorter events, 3.3 us)
Async XLA Ops:
  5.1 1.6 copy-start.1
  6.7 13.6 %copy-start.2 = (bf16[46,184,128]{2,1,0:T(8,128)(2,1)S(1)}, bf16[46,184,128]{2,1,0:T(8,128)(2,1)}, u32[]{:S(2)}) copy-start(bf16[46,184,128]{2,1,0:T(8,128)(2,1)} %param.6) | copy-start | bytes 6500356
  12.4 30.7 %collective-permute-start = (bf16[23,64,384]{2,1,0:T(8,128)(2,1)}, bf16[23,64,384]{2,1,0:T(8,128)(2,1)}, u32[]{:S(2)}, u32[]{:S(2)}) collective-permute-start(bf16[23,64,384]{2,1,0:T(8,128)(2,1)} %get-tuple-element.39.refs_0_), channel_id=1, source_target_pairs={{0,4},{2,6},{4,0},{6,2},{8,12},{10,14},{12,8},{14,10},{1,5},{3,7},... | collective-permute-start | bytes 3391496 | tf_op jit(solution)/shard_map/ppermute | solution.py:473
  14.5 18.6 %collective-permute-start.1 = (bf16[23,64,384]{2,1,0:T(8,128)(2,1)}, bf16[23,64,384]{2,1,0:T(8,128)(2,1)}, u32[]{:S(2)}, u32[]{:S(2)}) collective-permute-start(bf16[23,64,384]{2,1,0:T(8,128)(2,1)} %get-tuple-element.39.refs_0_), channel_id=1, source_target_pairs={{4,8},{6,10},{8,4},{10,6},{5,9},{7,11},{9,5},{11,7},{20,24},{22,26... | collective-permute-start | bytes 3391496 | tf_op jit(solution)/shard_map/ppermute | solution.py:473
  16.2 25.7 %collective-permute-start.2 = (bf16[23,64,384]{2,1,0:T(8,128)(2,1)}, bf16[23,64,384]{2,1,0:T(8,128)(2,1)S(1)}, u32[]{:S(2)}, u32[]{:S(2)}) collective-permute-start(bf16[23,64,384]{2,1,0:T(8,128)(2,1)} %get-tuple-element.40), channel_id=1, source_target_pairs={{0,2},{2,0},{4,6},{6,4},{8,10},{10,8},{12,14},{14,12},{1,3},{3,1},... | collective-permute-start | bytes 3391496 | tf_op jit(solution)/shard_map/ppermute | solution.py:476
  20.2 6.5 %copy-start.19 = (bf16[128,128]{1,0:T(8,128)(2,1)S(1)}, bf16[128,128]{1,0:T(8,128)(2,1)}, u32[]{:S(2)}) copy-start(bf16[128,128]{1,0:T(8,128)(2,1)} %param.9) | copy-start | bytes 98308
  25.6 1.1 copy-start.5
  43.1 14.6 %collective-permute-start.6 = (bf16[23,64,384]{2,1,0:T(8,128)(2,1)S(1)}, bf16[23,64,384]{2,1,0:T(8,128)(2,1)}, u32[]{:S(2)}, u32[]{:S(2)}) collective-permute-start(bf16[23,64,384]{2,1,0:T(8,128)(2,1)S(1)} %collective-permute-done.2.refs_1_), channel_id=1, source_target_pairs={{4,8},{6,10},{8,4},{10,6},{5,9},{7,11},{9,5},{11,7},{20,24},{22,26... | collective-permute-start | bytes 3391496 | tf_op jit(solution)/shard_map/ppermute | solution.py:473
  44.8 24.9 %collective-permute-start.3 = (bf16[23,64,384]{2,1,0:T(8,128)(2,1)}, bf16[23,64,384]{2,1,0:T(8,128)(2,1)}, u32[]{:S(2)}, u32[]{:S(2)}) collective-permute-start(bf16[23,64,384]{2,1,0:T(8,128)(2,1)} %get-tuple-element.46), channel_id=1, source_target_pairs={{0,2},{2,0},{4,6},{6,4},{8,10},{10,8},{12,14},{14,12},{1,3},{3,1},... | collective-permute-start | bytes 3391496 | tf_op jit(solution)/shard_map/ppermute | solution.py:476
  46.0 34.6 %collective-permute-start.4 = (bf16[23,64,384]{2,1,0:T(8,128)(2,1)}, bf16[23,64,384]{2,1,0:T(8,128)(2,1)}, u32[]{:S(2)}, u32[]{:S(2)}) collective-permute-start(bf16[23,64,384]{2,1,0:T(8,128)(2,1)} %broadcast_select_fusion.2), channel_id=1, source_target_pairs={{0,4},{2,6},{4,0},{6,2},{8,12},{10,14},{12,8},{14,10},{1,5},{3,7},... | collective-permute-start | bytes 3391496 | tf_op jit(solution)/shard_map/ppermute | solution.py:473
  52.4 1.5 copy-start.14
  53.8 1.0 copy-start.15
  54.9 2.8 %copy-start.6 = (bf16[23,64,384]{2,1,0:T(8,128)(2,1)S(1)}, bf16[23,64,384]{2,1,0:T(8,128)(2,1)}, u32[]{:S(2)}) copy-start(bf16[23,64,384]{2,1,0:T(8,128)(2,1)} %copy-done.5) | copy-start | bytes 3391492
  56.7 1.0 copy-start.9
  57.7 1.4 copy-start.7
  69.6 28.2 %collective-permute-start.7 = (bf16[23,64,384]{2,1,0:T(8,128)(2,1)S(1)}, bf16[23,64,384]{2,1,0:T(8,128)(2,1)S(1)}, u32[]{:S(2)}, u32[]{:S(2)}) collective-permute-start(bf16[23,64,384]{2,1,0:T(8,128)(2,1)S(1)} %broadcast_select_fusion.1), channel_id=1, source_target_pairs={{0,4},{2,6},{4,0},{6,2},{8,12},{10,14},{12,8},{14,10},{1,5},{3,7},... | collective-permute-start | bytes 3391496 | tf_op jit(solution)/shard_map/ppermute | solution.py:473
  74.9 24.0 %collective-permute-start.8 = (bf16[23,64,384]{2,1,0:T(8,128)(2,1)}, bf16[23,64,384]{2,1,0:T(8,128)(2,1)S(1)}, u32[]{:S(2)}, u32[]{:S(2)}) collective-permute-start(bf16[23,64,384]{2,1,0:T(8,128)(2,1)} %collective-permute-done.refs_0_.refs_4_), channel_id=1, source_target_pairs={{4,8},{6,10},{8,4},{10,6},{5,9},{7,11},{9,5},{11,7},{20,24},{22,26... | collective-permute-start | bytes 3391496 | tf_op jit(solution)/shard_map/ppermute | solution.py:473
  78.9 1.6 copy-start
  87.6 18.7 %collective-permute-start.5 = (bf16[64,96,128]{2,1,0:T(8,128)(2,1)}, bf16[64,96,128]{2,1,0:T(8,128)(2,1)}, u32[]{:S(2)}, u32[]{:S(2)}) collective-permute-start(bf16[64,96,128]{2,1,0:T(8,128)(2,1)} %triangle.4.refs_0_), channel_id=1, source_target_pairs={{5,4},{7,6},{8,9},{10,11},{21,20},{23,22},{24,25},{26,27}} | collective-permute-start | bytes 4718600 | tf_op jit(solution)/shard_map/ppermute | solution.py:483
  97.8 1.1 copy-start.3
  98.9 1.0 copy-start.11
  99.9 29.7 %collective-permute-start.9 = (bf16[23,64,384]{2,1,0:T(8,128)(2,1)}, bf16[23,64,384]{2,1,0:T(8,128)(2,1)}, u32[]{:S(2)}, u32[]{:S(2)}) collective-permute-start(bf16[23,64,384]{2,1,0:T(8,128)(2,1)} %broadcast_select_fusion), channel_id=1, source_target_pairs={{0,4},{2,6},{4,0},{6,2},{8,12},{10,14},{12,8},{14,10},{1,5},{3,7},... | collective-permute-start | bytes 3391496 | tf_op jit(solution)/shard_map/ppermute | solution.py:473
  104.7 24.9 %collective-permute-start.11 = (bf16[23,64,384]{2,1,0:T(8,128)(2,1)}, bf16[23,64,384]{2,1,0:T(8,128)(2,1)}, u32[]{:S(2)}, u32[]{:S(2)}) collective-permute-start(bf16[23,64,384]{2,1,0:T(8,128)(2,1)} %collective-permute-done.4.refs_1_.refs_2_), channel_id=1, source_target_pairs={{4,8},{6,10},{8,4},{10,6},{5,9},{7,11},{9,5},{11,7},{20,24},{22,26... | collective-permute-start | bytes 3391496 | tf_op jit(solution)/shard_map/ppermute | solution.py:473
  106.3 9.0 %copy-start.4 = (bf16[23,64,384]{2,1,0:T(8,128)(2,1)S(1)}, bf16[23,64,384]{2,1,0:T(8,128)(2,1)}, u32[]{:S(2)}) copy-start(bf16[23,64,384]{2,1,0:T(8,128)(2,1)} %copy-done.3) | copy-start | bytes 3391492
  110.6 12.4 %collective-permute-start.10 = (bf16[23,96,128]{2,1,0:T(8,128)(2,1)}, bf16[23,96,128]{2,1,0:T(8,128)(2,1)}, u32[]{:S(2)}, u32[]{:S(2)}) collective-permute-start(bf16[23,96,128]{2,1,0:T(8,128)(2,1)} %get-tuple-element.55), channel_id=1, source_target_pairs={{4,6},{6,4},{9,11},{11,9},{20,22},{22,20},{25,27},{27,25}} | collective-permute-start | bytes 1695752 | tf_op jit(solution)/shard_map/ppermute | solution.py:497
  112.1 17.4 %copy-start.12 = (bf16[23,64,384]{2,1,0:T(8,128)(2,1)S(1)}, bf16[23,64,384]{2,1,0:T(8,128)(2,1)}, u32[]{:S(2)}) copy-start(bf16[23,64,384]{2,1,0:T(8,128)(2,1)} %copy-done.11) | copy-start | bytes 3391492
  112.2 31.3 %collective-permute-start.18 = (bf16[64,96,128]{2,1,0:T(8,128)(2,1)S(1)}, bf16[64,96,128]{2,1,0:T(8,128)(2,1)S(1)}, u32[]{:S(2)}, u32[]{:S(2)}) collective-permute-start(bf16[64,96,128]{2,1,0:T(8,128)(2,1)S(1)} %triangle.5.refs_0_), channel_id=1, source_target_pairs={{1,0},{3,2},{5,4},{7,6},{8,9},{10,11},{12,13},{14,15},{17,16},{19,... | collective-permute-start | bytes 4718600 | tf_op jit(solution)/shard_map/ppermute | solution.py:483
  121.6 21.8 %collective-permute-start.19 = (bf16[64,96,128]{2,1,0:T(8,128)(2,1)S(1)}, bf16[64,96,128]{2,1,0:T(8,128)(2,1)}, u32[]{:S(2)}, u32[]{:S(2)}) collective-permute-start(bf16[64,96,128]{2,1,0:T(8,128)(2,1)S(1)} %triangle.7.refs_2_), channel_id=1, source_target_pairs={{0,1},{2,3},{4,5},{6,7},{9,8},{11,10},{13,12},{15,14},{16,17},{18,... | collective-permute-start | bytes 4718600 | tf_op jit(solution)/shard_map/ppermute | solution.py:483
  138.5 14.4 %collective-permute-start.12 = (bf16[64,96,128]{2,1,0:T(8,128)(2,1)}, bf16[64,96,128]{2,1,0:T(8,128)(2,1)S(1)}, u32[]{:S(2)}, u32[]{:S(2)}) collective-permute-start(bf16[64,96,128]{2,1,0:T(8,128)(2,1)} %get-tuple-element.58.refs_0_), channel_id=1, source_target_pairs={{1,0},{3,2},{4,5},{6,7},{9,8},{11,10},{12,13},{14,15},{17,16},{19,... | collective-permute-start | bytes 4718600 | tf_op jit(solution)/shard_map/ppermute | solution.py:483
  141.8 7.6 %collective-permute-start.13 = (bf16[64,48,128]{2,1,0:T(8,128)(2,1)S(1)}, bf16[64,48,128]{2,1,0:T(8,128)(2,1)S(1)}, u32[]{:S(2)}, u32[]{:S(2)}) collective-permute-start(bf16[64,48,128]{2,1,0:T(8,128)(2,1)S(1)} %get-tuple-element.60.refs_0_), channel_id=1, source_target_pairs={{5,4},{7,6},{8,9},{10,11},{21,20},{23,22},{24,25},{26,27}} | collective-permute-start | bytes 2359304 | tf_op jit(solution)/shard_map/ppermute | solution.py:483
  142.7 6.7 %collective-permute-start.14 = (bf16[64,48,128]{2,1,0:T(8,128)(2,1)S(1)}, bf16[64,48,128]{2,1,0:T(8,128)(2,1)S(1)}, u32[]{:S(2)}, u32[]{:S(2)}) collective-permute-start(bf16[64,48,128]{2,1,0:T(8,128)(2,1)S(1)} %get-tuple-element.61.refs_2_), channel_id=1, source_target_pairs={{4,5},{6,7},{9,8},{11,10},{20,21},{22,23},{25,24},{27,26}} | collective-permute-start | bytes 2359304 | tf_op jit(solution)/shard_map/ppermute | solution.py:483
  147.4 0.8 copy-start.17
  148.2 4.7 %copy-start.8 = (bf16[64,96,128]{2,1,0:T(8,128)(2,1)S(1)}, bf16[64,96,128]{2,1,0:T(8,128)(2,1)}, u32[]{:S(2)}) copy-start(bf16[64,96,128]{2,1,0:T(8,128)(2,1)} %get-tuple-element.58.refs_0_) | copy-start | bytes 4718596
  148.2 18.5 %collective-permute-start.20 = (bf16[23,96,128]{2,1,0:T(8,128)(2,1)}, bf16[23,96,128]{2,1,0:T(8,128)(2,1)}, u32[]{:S(2)}, u32[]{:S(2)}) collective-permute-start(bf16[23,96,128]{2,1,0:T(8,128)(2,1)} %get-tuple-element.66), channel_id=1, source_target_pairs={{0,2},{2,0},{4,6},{6,4},{8,10},{10,8},{12,14},{14,12},{1,3},{3,1},... | collective-permute-start | bytes 1695752 | tf_op jit(solution)/shard_map/ppermute | solution.py:476
  150.2 16.5 %copy-start.13 = (bf16[1024,128]{1,0:T(8,128)(2,1)S(1)}, bf16[1024,128]{1,0:T(8,128)(2,1)}, u32[]{:S(2)}) copy-start(bf16[1024,128]{1,0:T(8,128)(2,1)} %multiply_bitcast_fusion.refs_1_) | copy-start | bytes 786436
  150.2 16.5 %copy-start.16 = (bf16[12,128,384]{2,1,0:T(8,128)(2,1)S(1)}, bf16[12,128,384]{2,1,0:T(8,128)(2,1)}, u32[]{:S(2)}) copy-start(bf16[12,128,384]{2,1,0:T(8,128)(2,1)} %copy-done.15) | copy-start | bytes 3538948
  150.2 27.5 %collective-permute-start.15 = (bf16[23,96,128]{2,1,0:T(8,128)(2,1)S(1)}, bf16[23,96,128]{2,1,0:T(8,128)(2,1)}, u32[]{:S(2)}, u32[]{:S(2)}) collective-permute-start(bf16[23,96,128]{2,1,0:T(8,128)(2,1)S(1)} %fold.6), channel_id=1, source_target_pairs={{5,1},{7,3},{8,12},{10,14},{21,17},{23,19},{24,28},{26,30}} | collective-permute-start | bytes 1695752 | tf_op jit(solution)/shard_map/ppermute | solution.py:491
  151.6 27.3 %collective-permute-start.17 = (bf16[23,96,128]{2,1,0:T(8,128)(2,1)S(1)}, bf16[23,96,128]{2,1,0:T(8,128)(2,1)}, u32[]{:S(2)}, u32[]{:S(2)}) collective-permute-start(bf16[23,96,128]{2,1,0:T(8,128)(2,1)S(1)} %fold.6), channel_id=1, source_target_pairs={{4,3},{6,1},{9,14},{11,12},{20,19},{22,17},{25,30},{27,28}} | collective-permute-start | bytes 1695752 | tf_op jit(solution)/shard_map/ppermute | solution.py:491
  155.0 23.9 %collective-permute-start.16 = (bf16[23,96,128]{2,1,0:T(8,128)(2,1)}, bf16[23,96,128]{2,1,0:T(8,128)(2,1)}, u32[]{:S(2)}, u32[]{:S(2)}) collective-permute-start(bf16[23,96,128]{2,1,0:T(8,128)(2,1)} %get-tuple-element.62), channel_id=1, source_target_pairs={{0,2},{2,0},{5,7},{7,5},{8,10},{10,8},{13,15},{15,13},{16,18},{18,... | collective-permute-start | bytes 1695752 | tf_op jit(solution)/shard_map/ppermute | solution.py:497
  166.7 1.1 copy-start.18
  178.9 1.4 copy-start.10

commit v12 on v11

--- a/solution.py
+++ b/solution.py
@@ -17,7 +17,7 @@
 
 
 def params():
-    return pltpu.CompilerParams(vmem_limit_bytes=48 << 20)
+    return pltpu.CompilerParams(vmem_limit_bytes=20 << 20)
 
 
 def cost(flops, moved, transcendentals=0):
@@ -38,11 +38,28 @@
     return -(-count // unit) * unit
 
 
-def project_kernel(where_ref, pair_ref, weight_ref, own_ref, far_ref):
-    valid, row0, col0 = where_ref[0], where_ref[1], where_ref[2]
+def project_kernel(where_ref, pair_hbm, weight_ref, own_ref, far_ref, pair_ref, both_ref, sems, first):
+    valid, row0, col0, side = (where_ref[i] for i in range(4))
     _, half, cols, width = pair_ref.shape
     chans = width // 2
     tail = cols - width
+    count = sems.shape[0]
+    size = -(-half // count)
+    spans = [(k * size, min(size, half - k * size)) for k in range(count)]
+    loads = [
+        pltpu.make_async_copy(
+            pair_hbm.at[:, pl.ds(start, length)], pair_ref.at[:, pl.ds(start, length)], sems.at[k]
+        )
+        for k, (start, length) in enumerate(spans)
+    ]
+    for load in loads:
+        load.start()
+
+    for i in range(2):
+        block = weight_ref[:, (first + i) * width : (first + i + 1) * width].astype(F32)
+        block = jnp.where(side == 0, block, pltpu.roll(block, chans, 1))
+        both_ref[i * width : (i + 1) * width] = (block.T * 0.5).astype(BF16)
+
     lane = lax.broadcasted_iota(jnp.int32, (1, 3 * width), 1)
     in_tail = lane >= 2 * width
     ends = jnp.where(in_tail, 2 * width + chans, width)
@@ -56,7 +73,7 @@
             [first[:width], second[:width], first[width:], gap, second[width:], gap], axis=0
         )
         normed = norm_chans(tokens.T).astype(BF16)
-        both = jnp.dot(weight_ref[...], normed, preferred_element_type=F32)
+        both = jnp.dot(both_ref[...], normed, preferred_element_type=F32)
         limits = [jnp.where(row0 + h * half + r < valid, valid, 0) for h in range(2)]
         keep = jnp.where(token < limits[1] + is_first * (limits[0] - limits[1]), 1.0, 0.0)
         out = (twice_sigmoid(both[:width]) * both[width:] * keep).astype(BF16)
@@ -64,17 +81,28 @@
         far_ref[r] = out[chans:]
         return carry
 
-    lax.fori_loop(0, half, step, 0, unroll=4)
-
-
-def project(where, pair, weight):
+    for load, (start, length) in zip(loads, spans):
+        load.wait()
+        lax.fori_loop(start, start + length, step, 0, unroll=3)
+
+
+def project(where, pair, weight, first):
     _, half, cols, width = pair.shape
     piece = jax.ShapeDtypeStruct((half, width // 2, 3 * width), BF16)
     return pl.pallas_call(
-        project_kernel,
+        functools.partial(project_kernel, first=first),
         out_shape=(piece, piece),
-        in_specs=[pl.BlockSpec(memory_space=pltpu.SMEM)] + whole(2),
+        in_specs=[
+            pl.BlockSpec(memory_space=pltpu.SMEM),
+            pl.BlockSpec(memory_space=pl.ANY),
+            pl.BlockSpec(memory_space=VMEM),
+        ],
         out_specs=whole(2),
+        scratch_shapes=[
+            VMEM(pair.shape, BF16),
+            VMEM((2 * width, width), BF16),
+            pltpu.SemaphoreType.DMA((4,)),
+        ],
         compiler_params=params(),
         cost_estimate=cost(4 * pair.size * width, 4 * pair.size, pair.size),
         name="project",
@@ -499,12 +527,6 @@
     def by_side(block, axis):
         return jnp.where(side == 0, block, jnp.roll(block, width // 2, axis))
 
-    def gate_pair(first):
-        parts = [
-            by_side(in_weight[:, (first + i) * width : (first + i + 1) * width], 1) for i in range(2)
-        ]
-        return jnp.concatenate(parts, axis=1).T * BF16(0.5)
-
     def after(value, *others):
         return lax.optimization_barrier((value, *others))[0]
 
@@ -513,7 +535,7 @@
 
     is_keeper = core == keeper
     inner = (place == 1) | (place == 2)
-    where = scalars(valid_count, row_id * tile_rows, core * tile_cols)
+    where = scalars(valid_count, row_id * tile_rows, core * tile_cols, side)
     folded = pair.reshape(2, half, tile_cols, width)
     cross = [(1, 2), (2, 1)]
     everyone, inners = range(4), (1, 2)
@@ -529,7 +551,7 @@
         return jnp.where(inner, at_inner, at_end)
 
     swap = hop([(0, 1), (1, 0), (2, 3), (3, 2)])
-    right_own, right_far = project(where, folded, gate_pair(2))
+    right_own, right_far = project(where, folded, in_weight, 2)
     one = phase([(swap, right_own), (hop(cross), right_own), (across, right_far)], ())
     mate_own, near_own, right_beside = one
     order = jnp.where(is_keeper, place % 2, place // 2)
@@ -540,7 +562,7 @@
         trans_out.T,
     ]
     gate_weight = in_weight[:, 4 * width :].T * BF16(0.5)
-    left_own, left_far = project(where, folded, gate_pair(0))
+    left_own, left_far = project(where, folded, in_weight, 0)
     two = phase(
         [(swap, either(near_own, right_beside)), (hop(cross), right_beside), (across, left_far)],
         one + weights + [gate_weight],
@@ -548,7 +570,8 @@
     prepared = [prepare(scalars(f), after(folded, *one), gate_weight) for f in (order, 1 - order)]
     mate_beside, near_beside, left_beside = two
     three = phase(
-        [(swap, either(near_beside, left_own)), (hop(cross), mate_own)], (near_beside, left_beside, *prepared[0], *prepared[1]),
+        [(swap, either(near_beside, left_own)), (hop(cross), mate_own)],
+        (near_beside, left_beside, *prepared[0], *prepared[1]),
     )
     guest_own, far_own = three
 

time: 193 us -> 184 us (0.953)
  local copies, waits for them, and re-layouts: 23.2 us -> 16.3 us
  Pallas kernels: 78.5 us -> 73.9 us
  starting transfers between devices: 42.9 us -> 45.6 us
    ppermute x6, starting transfers between devices: 11.1 us -> 15.9 us  [to_core(): return lax.ppermute(value, ('row', 'col'), perm)]
    ppermute x3, waiting for transfers between devices: 29.4 us -> 34.2 us  [across(): return lax.ppermute(value, 'row', [(i, i ^ 1) for i in range(8)])]
    unnamed x56 -> x60, local copies, waits for them, and re-layouts: 19.4 us -> 14.9 us
    ppermute x8, waiting for transfers between devices: 6.65 us -> 2.63 us  [among(): lax.ppermute(value, 'row', [(2 * s + b, 2 * t + b) for s, t in moves for...]
    pallas_call x2, Pallas kernels: 21.4 us -> 19 us  [finish(): pl.pallas_call(functools.partial(finish_kernel, cols=cols), out_shape=jax...]
    pallas_call x4, Pallas kernels: 28.3 us -> 26.1 us  [triangle(): pl.pallas_call(functools.partial(triangle_kernel, counts=[len(piece) for...]
  transfers between devices with their start and end apart: 21 -> 21, of which waited for: 4 -> 5; matrix products, arithmetic and copies ran while one was open for 8% -> 4% of each run, Pallas kernels for 32% -> 32%
where the time goes in v12:
time: 184 us; the launch traced here: 182 us
  Pallas kernels  73.9 us (40%)
  starting transfers between devices  45.6 us (25%)
  waiting for transfers between devices  36.8 us (20%)
  local copies, waits for them, and re-layouts  16.3 us (9%)
  other arithmetic  8.2 us (4%)
    ppermute x3, waiting for transfers between devices, across(): return lax.ppermute(value, 'row', [(i, i ^ 1) for i in range(8)])  34.2 us
    pallas_call x4, Pallas kernels, triangle(): pl.pallas_call(functools.partial(triangle_kernel, counts=[len(piece) for...  26.1 us
    ppermute x8, starting transfers between devices, among(): lax.ppermute(value, 'row', [(2 * s + b, 2 * t + b) for s, t in moves for...  20.5 us
    pallas_call x2, Pallas kernels, finish(): pl.pallas_call(functools.partial(finish_kernel, cols=cols), out_shape=jax...  19 us
    ppermute x6, starting transfers between devices, to_core(): return lax.ppermute(value, ('row', 'col'), perm)  15.9 us
    unnamed x60, local copies, waits for them, and re-layouts  14.9 us
    pallas_call x2, Pallas kernels, project(): pl.pallas_call(functools.partial(project_kernel, first=first), out_shape=...  12.8 us
    pallas_call x4, Pallas kernels, fold(): pl.pallas_call(functools.partial(fold_kernel, outputs=outputs, half=half)...  9.23 us
  transfers between devices with their start and end apart: 21, of which 5 were waited for; matrix products, arithmetic and copies ran while one was open for 4% of the time, Pallas kernels for 32%

profile of v12, /device:TPU:1, one launch (start us, length us, event | category | flops | bytes accessed | tf_op | source)
XLA Modules:
  0.0 181.9 jit_solution(149663890289021406)
XLA Ops:
  0.0 1.2 slice.14
  1.9 1.6 copy-done
  3.5 0.9 copy-done.18
  4.4 6.7 %project.2 = (bf16[23,64,384]{2,1,0:T(8,128)(2,1)}, bf16[23,64,384]{2,1,0:T(8,128)(2,1)}) custom-call(s32[4]{0:T(128)S(1)} %pad_add_fusion.where_ref, bf16[2,23,184,128]{3,2,1,0:T(8,128)(2,1)S(1)} %bitcast.16, bf16[128,640]{1,0:T(8,128)(2,1)S(1)} %copy-done.18), custom_call_target="tpu_custom_call" | custom-call | flops 554696704 | bytes 4333568 | tf_op jit(solution)/shard_map/project/pallas_call | solution.py:92
  11.1 1.9 %collective-permute-start.1 = (bf16[23,64,384]{2,1,0:T(8,128)(2,1)}, bf16[23,64,384]{2,1,0:T(8,128)(2,1)}, u32[]{:S(2)}, u32[]{:S(2)}) collective-permute-start(bf16[23,64,384]{2,1,0:T(8,128)(2,1)} %get-tuple-element.39.refs_0_), channel_id=1, source_target_pairs={{4,8},{6,10},{8,4},{10,6},{5,9},{7,11},{9,5},{11,7},{20,24},{22,26... | collective-permute-start | bytes 3391496 | tf_op jit(solution)/shard_map/ppermute | solution.py:501
  13.0 2.0 %collective-permute-start.2 = (bf16[23,64,384]{2,1,0:T(8,128)(2,1)}, bf16[23,64,384]{2,1,0:T(8,128)(2,1)S(1)}, u32[]{:S(2)}, u32[]{:S(2)}) collective-permute-start(bf16[23,64,384]{2,1,0:T(8,128)(2,1)} %get-tuple-element.40), channel_id=1, source_target_pairs={{0,2},{2,0},{4,6},{6,4},{8,10},{10,8},{12,14},{14,12},{1,3},{3,1},... | collective-permute-start | bytes 3391496 | tf_op jit(solution)/shard_map/ppermute | solution.py:504
  15.0 2.8 %collective-permute-start = (bf16[23,64,384]{2,1,0:T(8,128)(2,1)}, bf16[23,64,384]{2,1,0:T(8,128)(2,1)}, u32[]{:S(2)}, u32[]{:S(2)}) collective-permute-start(bf16[23,64,384]{2,1,0:T(8,128)(2,1)} %get-tuple-element.39.refs_0_), channel_id=1, source_target_pairs={{0,4},{2,6},{4,0},{6,2},{8,12},{10,14},{12,8},{14,10},{1,5},{3,7},... | collective-permute-start | bytes 3391496 | tf_op jit(solution)/shard_map/ppermute | solution.py:501
  17.9 6.2 %project.3 = (bf16[23,64,384]{2,1,0:T(8,128)(2,1)S(1)}, bf16[23,64,384]{2,1,0:T(8,128)(2,1)}) custom-call(s32[4]{0:T(128)S(1)} %pad_add_fusion.where_ref, bf16[2,23,184,128]{3,2,1,0:T(8,128)(2,1)S(1)} %bitcast.17, bf16[128,640]{1,0:T(8,128)(2,1)S(1)} %copy-done.18), custom_call_target="tpu_custom_call" | custom-call | flops 554696704 | bytes 4333568 | tf_op jit(solution)/shard_map/project/pallas_call | solution.py:92
  24.1 1.0 copy-done.9
  25.2 0.1 copy.13
  25.3 0.1 copy.12
  25.4 0.2 copy.11
  25.8 0.9 multiply_bitcast_fusion.refs_1_
  26.7 13.3 %collective-permute-done.2.refs_1_ = bf16[23,64,384]{2,1,0:T(8,128)(2,1)S(1)} collective-permute-done((bf16[23,64,384]{2,1,0:T(8,128)(2,1)}, bf16[23,64,384]{2,1,0:T(8,128)(2,1)S(1)}, u32[]{:S(2)}, u32[]{:S(2)}) %collective-permute-start.2) | collective-permute-done | bytes 1130528 | tf_op jit(solution)/shard_map/ppermute | solution.py:504
  40.0 1.3 broadcast_select_fusion.2
  41.3 0.9 collective-permute-done.refs_0_.refs_4_
  42.2 1.7 collective-permute-start.6
  43.9 0.3 collective-permute-start.3
  44.2 4.5 %collective-permute-start.4 = (bf16[23,64,384]{2,1,0:T(8,128)(2,1)}, bf16[23,64,384]{2,1,0:T(8,128)(2,1)}, u32[]{:S(2)}, u32[]{:S(2)}) collective-permute-start(bf16[23,64,384]{2,1,0:T(8,128)(2,1)} %broadcast_select_fusion.2), channel_id=1, source_target_pairs={{0,4},{2,6},{4,0},{6,2},{8,12},{10,14},{12,8},{14,10},{1,5},{3,7},... | collective-permute-start | bytes 3391496 | tf_op jit(solution)/shard_map/ppermute | solution.py:501
  48.7 1.8 prepare.3
  50.5 1.5 copy-done.21
  52.0 1.0 copy-done.23
  53.0 1.8 prepare.2
  54.8 1.1 copy-done.13
  55.9 0.1 broadcast_select_fusion.1
  56.0 1.2 copy-done.11
  57.3 11.5 %collective-permute-done.3.beside_ref = bf16[23,64,384]{2,1,0:T(8,128)(2,1)} collective-permute-done((bf16[23,64,384]{2,1,0:T(8,128)(2,1)}, bf16[23,64,384]{2,1,0:T(8,128)(2,1)}, u32[]{:S(2)}, u32[]{:S(2)}) %collective-permute-start.3) | collective-permute-done | bytes 1130528 | tf_op jit(solution)/shard_map/ppermute | solution.py:504
  68.7 4.7 %collective-permute-start.7 = (bf16[23,64,384]{2,1,0:T(8,128)(2,1)S(1)}, bf16[23,64,384]{2,1,0:T(8,128)(2,1)S(1)}, u32[]{:S(2)}, u32[]{:S(2)}) collective-permute-start(bf16[23,64,384]{2,1,0:T(8,128)(2,1)S(1)} %broadcast_select_fusion.1), channel_id=1, source_target_pairs={{0,4},{2,6},{4,0},{6,2},{8,12},{10,14},{12,8},{14,10},{1,5},{3,7},... | collective-permute-start | bytes 3391496 | tf_op jit(solution)/shard_map/ppermute | solution.py:501
  73.4 0.7 collective-permute-start.8
  74.2 3.2 %left_major.1.left_ref = bf16[64,96,256]{2,1,0:T(8,128)(2,1)S(1)} custom-call(bf16[23,64,384]{2,1,0:T(8,128)(2,1)S(1)} %copy-done.10, bf16[23,64,384]{2,1,0:T(8,128)(2,1)} %collective-permute-done.3.beside_ref), custom_call_target="tpu_custom_call" | custom-call | bytes 4521984 | tf_op jit(solution)/shard_map/left_major/pallas_call | solution.py:144
  77.4 6.5 %triangle.4.refs_0_ = bf16[64,96,128]{2,1,0:T(8,128)(2,1)} custom-call(s32[2]{0:T(128)S(1)} %pad_add_fusion.1.flag_ref, bf16[64,96,256]{2,1,0:T(8,128)(2,1)S(1)} %left_major.1.left_ref, bf16[23,64,384]{2,1,0:T(8,128)(2,1)} %collective-permute-done.refs_0_.refs_4_, bf16[23,64,384]{2,1,0:T(8,128)(2,1)} %collective-permute-done.4.refs_1_.refs_2_), custom_call_target="tpu_custom_call" | custom-call | flops 402653184 | bytes 5652480 | tf_op jit(solution)/shard_map/triangle/pallas_call | solution.py:223
  83.9 1.9 %collective-permute-start.5 = (bf16[64,96,128]{2,1,0:T(8,128)(2,1)}, bf16[64,96,128]{2,1,0:T(8,128)(2,1)}, u32[]{:S(2)}, u32[]{:S(2)}) collective-permute-start(bf16[64,96,128]{2,1,0:T(8,128)(2,1)} %triangle.4.refs_0_), channel_id=1, source_target_pairs={{5,4},{7,6},{8,9},{10,11},{21,20},{23,22},{24,25},{26,27}} | collective-permute-start | bytes 4718600 | tf_op jit(solution)/shard_map/ppermute | solution.py:511
  85.8 5.4 %triangle.5.refs_0_ = bf16[64,96,128]{2,1,0:T(8,128)(2,1)S(1)} custom-call(s32[2]{0:T(128)S(1)} %pad_add_fusion.1.flag_ref, bf16[64,96,256]{2,1,0:T(8,128)(2,1)S(1)} %left_major.1.left_ref, bf16[23,64,384]{2,1,0:T(8,128)(2,1)} %get-tuple-element.39.refs_0_, bf16[23,64,384]{2,1,0:T(8,128)(2,1)S(1)} %copy-done.3), custom_call_target="tpu_custom_call" | custom-call | flops 402653184 | bytes 5652480 | tf_op jit(solution)/shard_map/triangle/pallas_call | solution.py:223
  91.3 3.0 %broadcast_select_fusion = bf16[23,64,384]{2,1,0:T(8,128)(2,1)} fusion(bf16[23,64,384]{2,1,0:T(8,128)(2,1)S(1)} %copy-done.3, bf16[23,64,384]{2,1,0:T(8,128)(2,1)} %collective-permute-done.3.beside_ref, pred[]{:T(512)S(6)} %or.7), kind=kLoop, calls=%fused_computation | loop fusion | flops 565248 | bytes 3391489 | tf_op jit(solution)/shard_map/jit(_where)/select_n | solution.py:551
  94.3 1.7 collective-permute-done.7.refs_0_.refs_3_
  96.0 1.0 copy-done.6
  97.0 1.0 copy-done.15
  98.0 2.5 %collective-permute-start.9 = (bf16[23,64,384]{2,1,0:T(8,128)(2,1)}, bf16[23,64,384]{2,1,0:T(8,128)(2,1)}, u32[]{:S(2)}, u32[]{:S(2)}) collective-permute-start(bf16[23,64,384]{2,1,0:T(8,128)(2,1)} %broadcast_select_fusion), channel_id=1, source_target_pairs={{0,4},{2,6},{4,0},{6,2},{8,12},{10,14},{12,8},{14,10},{1,5},{3,7},... | collective-permute-start | bytes 3391496 | tf_op jit(solution)/shard_map/ppermute | solution.py:501
  100.5 1.7 collective-permute-start.11
  102.2 4.2 %fold.4 = (bf16[23,96,128]{2,1,0:T(8,128)(2,1)S(1)}, bf16[23,96,128]{2,1,0:T(8,128)(2,1)}) custom-call(s32[1]{0:T(128)} %bitcast.6.role_ref, bf16[64,96,128]{2,1,0:T(8,128)(2,1)} %triangle.4.refs_0_, bf16[64,96,128]{2,1,0:T(8,128)(2,1)} %collective-permute-done.5.refs_1_), custom_call_target="tpu_custom_call" | custom-call | bytes 4718592 | tf_op jit(solution)/shard_map/fold/pallas_call | solution.py:285
  106.4 0.8 copy-done.19
  107.2 1.5 collective-permute-start.10
  108.7 5.8 %collective-permute-start.18 = (bf16[64,96,128]{2,1,0:T(8,128)(2,1)}, bf16[64,96,128]{2,1,0:T(8,128)(2,1)S(1)}, u32[]{:S(2)}, u32[]{:S(2)}) collective-permute-start(bf16[64,96,128]{2,1,0:T(8,128)(2,1)} %copy-done.4), channel_id=1, source_target_pairs={{1,0},{3,2},{5,4},{7,6},{8,9},{10,11},{12,13},{14,15},{17,16},{19,... | collective-permute-start | bytes 4718600 | tf_op jit(solution)/shard_map/ppermute | solution.py:511
  114.5 1.2 copy-done.7
  115.8 6.0 %triangle.7.refs_2_ = bf16[64,96,128]{2,1,0:T(8,128)(2,1)S(1)} custom-call(s32[2]{0:T(128)S(1)} %pad_add_fusion.2.flag_ref, bf16[64,96,256]{2,1,0:T(8,128)(2,1)S(1)} %left_major.1.left_ref, bf16[23,64,384]{2,1,0:T(8,128)(2,1)} %collective-permute-done.1.refs_0_, bf16[23,64,384]{2,1,0:T(8,128)(2,1)} %collective-permute-done.6.refs_1_, ...), custom_call_target="tpu_custom_call" | custom-call | flops 402653184 | bytes 5652480 | tf_op jit(solution)/shard_map/triangle/pallas_call | solution.py:223
  121.8 1.4 collective-permute-start.19
  123.3 8.1 %triangle.6 = (bf16[64,96,128]{2,1,0:T(8,128)(2,1)S(1)}, bf16[64,48,128]{2,1,0:T(8,128)(2,1)S(1)}, bf16[64,48,128]{2,1,0:T(8,128)(2,1)S(1)}) custom-call(s32[2]{0:T(128)S(1)} %pad_add_fusion.2.flag_ref, bf16[64,96,256]{2,1,0:T(8,128)(2,1)S(1)} %left_major.1.left_ref, bf16[23,64,384]{2,1,0:T(8,128)(2,1)S(1)} %copy-done.8, ...), custom_call_target="tpu_custom_call" | custom-call | flops 805306368 | bytes 5652480 | tf_op jit(solution)/shard_map/triangle/pallas_call | solution.py:223
  131.5 5.4 %collective-permute-start.12 = (bf16[64,96,128]{2,1,0:T(8,128)(2,1)S(1)}, bf16[64,96,128]{2,1,0:T(8,128)(2,1)S(1)}, u32[]{:S(2)}, u32[]{:S(2)}) collective-permute-start(bf16[64,96,128]{2,1,0:T(8,128)(2,1)S(1)} %get-tuple-element.58.refs_0_), channel_id=1, source_target_pairs={{1,0},{3,2},{4,5},{6,7},{9,8},{11,10},{12,13},{14,15},{17,16},{19,... | collective-permute-start | bytes 4718600 | tf_op jit(solution)/shard_map/ppermute | solution.py:511
  136.9 0.7 collective-permute-start.13
  137.6 0.7 collective-permute-start.14
  138.4 2.2 %fold.7 = (bf16[23,96,128]{2,1,0:T(8,128)(2,1)S(1)}, bf16[23,96,128]{2,1,0:T(8,128)(2,1)}) custom-call(s32[1]{0:T(128)} %bitcast.6.role_ref, bf16[64,96,128]{2,1,0:T(8,128)(2,1)S(1)} %copy-done.5, bf16[64,96,128]{2,1,0:T(8,128)(2,1)S(1)} %collective-permute-done.18.refs_1_, bf16[64,96,128]{2,1,0:T(8,128)(2,1)S(1)} %triangle.7.refs_2_, ...), custom_call_target="tpu_custom_call" | custom-call | bytes 4718592 | tf_op jit(solution)/shard_map/fold/pallas_call | solution.py:285
  140.5 1.2 collective-permute-start.20
  141.8 0.7 fold.6
  142.5 1.4 collective-permute-start.15
  144.0 1.3 collective-permute-start.17
  145.3 2.1 %fold.5 = (bf16[23,96,128]{2,1,0:T(8,128)(2,1)S(1)}, bf16[23,96,128]{2,1,0:T(8,128)(2,1)}) custom-call(s32[1]{0:T(128)} %bitcast.6.role_ref, bf16[64,96,128]{2,1,0:T(8,128)(2,1)S(1)} %get-tuple-element.58.refs_0_, bf16[64,96,128]{2,1,0:T(8,128)(2,1)S(1)} %collective-permute-done.12.refs_1_), custom_call_target="tpu_custom_call" | custom-call | bytes 4718592 | tf_op jit(solution)/shard_map/fold/pallas_call | solution.py:285
  147.4 1.5 collective-permute-start.16
  148.8 9.4 %collective-permute-done.20.other_ref = bf16[23,96,128]{2,1,0:T(8,128)(2,1)} collective-permute-done((bf16[23,96,128]{2,1,0:T(8,128)(2,1)}, bf16[23,96,128]{2,1,0:T(8,128)(2,1)}, u32[]{:S(2)}, u32[]{:S(2)}) %collective-permute-start.20) | collective-permute-done | bytes 565280 | tf_op jit(solution)/shard_map/ppermute | solution.py:504
  158.3 1.7 copy-done.22
  160.0 9.2 %finish.2.refs_3_ = bf16[2,23,96,128]{3,2,1,0:T(8,128)(2,1)S(1)} custom-call(s32[1]{0:T(128)} %bitcast.11.flag_ref, bf16[12,128,384]{2,1,0:T(8,128)(2,1)S(1)} %copy-done.24, f32[12,128,384]{2,1,0:T(8,128)S(1)} %copy-done.22, bf16[23,96,128]{2,1,0:T(8,128)(2,1)S(1)} %get-tuple-element.65.own_ref, bf16[23,96,128]{2,1,0:T(8,128)(2,1)} %collective-permute-done.20.other_ref, ...), custom_call_target="tpu_custom_call" | custom-call | flops 1881145344 | bytes 5652480 | tf_op jit(solution)/shard_map/finish/pallas_call | solution.py:382
  169.2 1.4 select_select_fusion.1.own_ref
  170.6 1.2 select_select_fusion.other_ref
  171.9 0.3 copy-done.14
  172.1 9.8 %finish.3 = bf16[2,23,184,128]{3,2,1,0:T(8,128)(2,1)} custom-call(s32[1]{0:T(128)} %bitcast.flag_ref, bf16[12,128,384]{2,1,0:T(8,128)(2,1)S(1)} %copy-done.14, f32[12,128,384]{2,1,0:T(8,128)S(1)} %copy-done.12, bf16[23,96,128]{2,1,0:T(8,128)(2,1)S(1)} %select_select_fusion.1.own_ref, bf16[23,96,128]{2,1,0:T(8,128)(2,1)S(1)} %select_select_fusion.other_ref, ...), custom_call_target="tpu_custom_call" | custom-call | flops 1881145344 | bytes 5652480 | tf_op jit(solution)/shard_map/finish/pallas_call | solution.py:382
  (68 shorter events, 0.7 us)
Async XLA Ops:
  1.9 1.6 copy-start
  3.5 0.9 copy-start.18
  11.1 14.0 %copy-start.27 = (bf16[128,128]{1,0:T(8,128)(2,1)S(1)}, bf16[128,128]{1,0:T(8,128)(2,1)}, u32[]{:S(2)}) copy-start(bf16[128,128]{1,0:T(8,128)(2,1)} %param.9) | copy-start | bytes 98308
  11.1 14.1 %slice-start = ((bf16[128,640]{1,0:T(8,128)(2,1)}), bf16[128,128]{1,0:T(8,128)(2,1)S(1)}, s32[]{:S(2)}) async-start(bf16[128,640]{1,0:T(8,128)(2,1)} %weight_ref.3), calls=%async_computation | async-start | bytes 65536 | tf_op jit(solution)/shard_map/slice | solution.py:564
  11.1 14.2 %copy-start.26 = (bf16[512,128]{1,0:T(8,128)(2,1)S(1)}, bf16[512,128]{1,0:T(8,128)(2,1)}, u32[]{:S(2)}) copy-start(bf16[512,128]{1,0:T(8,128)(2,1)} %param.11) | copy-start | bytes 393220
  11.1 14.3 %copy-start.25 = (bf16[128,1024]{1,0:T(8,128)(2,1)S(1)}, bf16[128,1024]{1,0:T(8,128)(2,1)}, u32[]{:S(2)}) copy-start(bf16[128,1024]{1,0:T(8,128)(2,1)} %param.10) | copy-start | bytes 786436
  11.1 15.6 %collective-permute-start.1 = (bf16[23,64,384]{2,1,0:T(8,128)(2,1)}, bf16[23,64,384]{2,1,0:T(8,128)(2,1)}, u32[]{:S(2)}, u32[]{:S(2)}) collective-permute-start(bf16[23,64,384]{2,1,0:T(8,128)(2,1)} %get-tuple-element.39.refs_0_), channel_id=1, source_target_pairs={{4,8},{6,10},{8,4},{10,6},{5,9},{7,11},{9,5},{11,7},{20,24},{22,26... | collective-permute-start | bytes 3391496 | tf_op jit(solution)/shard_map/ppermute | solution.py:501
  13.0 27.0 %collective-permute-start.2 = (bf16[23,64,384]{2,1,0:T(8,128)(2,1)}, bf16[23,64,384]{2,1,0:T(8,128)(2,1)S(1)}, u32[]{:S(2)}, u32[]{:S(2)}) collective-permute-start(bf16[23,64,384]{2,1,0:T(8,128)(2,1)} %get-tuple-element.40), channel_id=1, source_target_pairs={{0,2},{2,0},{4,6},{6,4},{8,10},{10,8},{12,14},{14,12},{1,3},{3,1},... | collective-permute-start | bytes 3391496 | tf_op jit(solution)/shard_map/ppermute | solution.py:504
  15.0 27.1 %collective-permute-start = (bf16[23,64,384]{2,1,0:T(8,128)(2,1)}, bf16[23,64,384]{2,1,0:T(8,128)(2,1)}, u32[]{:S(2)}, u32[]{:S(2)}) collective-permute-start(bf16[23,64,384]{2,1,0:T(8,128)(2,1)} %get-tuple-element.39.refs_0_), channel_id=1, source_target_pairs={{0,4},{2,6},{4,0},{6,2},{8,12},{10,14},{12,8},{14,10},{1,5},{3,7},... | collective-permute-start | bytes 3391496 | tf_op jit(solution)/shard_map/ppermute | solution.py:501
  24.1 1.0 copy-start.9
  26.7 22.0 %copy-start.1 = (bf16[46,184,128]{2,1,0:T(8,128)(2,1)S(1)}, bf16[46,184,128]{2,1,0:T(8,128)(2,1)}, u32[]{:S(2)}) copy-start(bf16[46,184,128]{2,1,0:T(8,128)(2,1)} %param.6) | copy-start | bytes 6500356
  40.0 2.2 %copy-start.2 = (bf16[23,64,384]{2,1,0:T(8,128)(2,1)}, bf16[23,64,384]{2,1,0:T(8,128)(2,1)S(1)}, u32[]{:S(2)}) copy-start(bf16[23,64,384]{2,1,0:T(8,128)(2,1)S(1)} %collective-permute-done.2.refs_1_) | copy-start | bytes 3391492
  42.2 13.7 %collective-permute-start.6 = (bf16[23,64,384]{2,1,0:T(8,128)(2,1)S(1)}, bf16[23,64,384]{2,1,0:T(8,128)(2,1)}, u32[]{:S(2)}, u32[]{:S(2)}) collective-permute-start(bf16[23,64,384]{2,1,0:T(8,128)(2,1)S(1)} %collective-permute-done.2.refs_1_), channel_id=1, source_target_pairs={{4,8},{6,10},{8,4},{10,6},{5,9},{7,11},{9,5},{11,7},{20,24},{22,26... | collective-permute-start | bytes 3391496 | tf_op jit(solution)/shard_map/ppermute | solution.py:501
  43.9 24.9 %collective-permute-start.3 = (bf16[23,64,384]{2,1,0:T(8,128)(2,1)}, bf16[23,64,384]{2,1,0:T(8,128)(2,1)}, u32[]{:S(2)}, u32[]{:S(2)}) collective-permute-start(bf16[23,64,384]{2,1,0:T(8,128)(2,1)} %get-tuple-element.46), channel_id=1, source_target_pairs={{0,2},{2,0},{4,6},{6,4},{8,10},{10,8},{12,14},{14,12},{1,3},{3,1},... | collective-permute-start | bytes 3391496 | tf_op jit(solution)/shard_map/ppermute | solution.py:504
  44.2 33.2 %collective-permute-start.4 = (bf16[23,64,384]{2,1,0:T(8,128)(2,1)}, bf16[23,64,384]{2,1,0:T(8,128)(2,1)}, u32[]{:S(2)}, u32[]{:S(2)}) collective-permute-start(bf16[23,64,384]{2,1,0:T(8,128)(2,1)} %broadcast_select_fusion.2), channel_id=1, source_target_pairs={{0,4},{2,6},{4,0},{6,2},{8,12},{10,14},{12,8},{14,10},{1,5},{3,7},... | collective-permute-start | bytes 3391496 | tf_op jit(solution)/shard_map/ppermute | solution.py:501
  50.5 1.5 copy-start.21
  52.0 1.0 copy-start.23
  53.0 2.9 %copy-start.10 = (bf16[23,64,384]{2,1,0:T(8,128)(2,1)S(1)}, bf16[23,64,384]{2,1,0:T(8,128)(2,1)}, u32[]{:S(2)}) copy-start(bf16[23,64,384]{2,1,0:T(8,128)(2,1)} %copy-done.9) | copy-start | bytes 3391492
  54.8 1.1 copy-start.13
  55.9 1.4 copy-start.11
  68.7 27.2 %collective-permute-start.7 = (bf16[23,64,384]{2,1,0:T(8,128)(2,1)S(1)}, bf16[23,64,384]{2,1,0:T(8,128)(2,1)S(1)}, u32[]{:S(2)}, u32[]{:S(2)}) collective-permute-start(bf16[23,64,384]{2,1,0:T(8,128)(2,1)S(1)} %broadcast_select_fusion.1), channel_id=1, source_target_pairs={{0,4},{2,6},{4,0},{6,2},{8,12},{10,14},{12,8},{14,10},{1,5},{3,7},... | collective-permute-start | bytes 3391496 | tf_op jit(solution)/shard_map/ppermute | solution.py:501
  73.4 23.6 %collective-permute-start.8 = (bf16[23,64,384]{2,1,0:T(8,128)(2,1)}, bf16[23,64,384]{2,1,0:T(8,128)(2,1)S(1)}, u32[]{:S(2)}, u32[]{:S(2)}) collective-permute-start(bf16[23,64,384]{2,1,0:T(8,128)(2,1)} %collective-permute-done.refs_0_.refs_4_), channel_id=1, source_target_pairs={{4,8},{6,10},{8,4},{10,6},{5,9},{7,11},{9,5},{11,7},{20,24},{22,26... | collective-permute-start | bytes 3391496 | tf_op jit(solution)/shard_map/ppermute | solution.py:501
  77.4 8.4 %copy-start.3 = (bf16[23,64,384]{2,1,0:T(8,128)(2,1)S(1)}, bf16[23,64,384]{2,1,0:T(8,128)(2,1)}, u32[]{:S(2)}) copy-start(bf16[23,64,384]{2,1,0:T(8,128)(2,1)} %copy-done.2) | copy-start | bytes 3391492
  83.9 18.3 %collective-permute-start.5 = (bf16[64,96,128]{2,1,0:T(8,128)(2,1)}, bf16[64,96,128]{2,1,0:T(8,128)(2,1)}, u32[]{:S(2)}, u32[]{:S(2)}) collective-permute-start(bf16[64,96,128]{2,1,0:T(8,128)(2,1)} %triangle.4.refs_0_), channel_id=1, source_target_pairs={{5,4},{7,6},{8,9},{10,11},{21,20},{23,22},{24,25},{26,27}} | collective-permute-start | bytes 4718600 | tf_op jit(solution)/shard_map/ppermute | solution.py:511
  91.3 3.0 %copy-start.4 = (bf16[64,96,128]{2,1,0:T(8,128)(2,1)}, bf16[64,96,128]{2,1,0:T(8,128)(2,1)S(1)}, u32[]{:S(2)}) copy-start(bf16[64,96,128]{2,1,0:T(8,128)(2,1)S(1)} %triangle.5.refs_0_) | copy-start | bytes 4718596
  95.9 1.0 copy-start.6
  97.0 1.0 copy-start.15
  98.0 25.3 %collective-permute-start.9 = (bf16[23,64,384]{2,1,0:T(8,128)(2,1)}, bf16[23,64,384]{2,1,0:T(8,128)(2,1)}, u32[]{:S(2)}, u32[]{:S(2)}) collective-permute-start(bf16[23,64,384]{2,1,0:T(8,128)(2,1)} %broadcast_select_fusion), channel_id=1, source_target_pairs={{0,4},{2,6},{4,0},{6,2},{8,12},{10,14},{12,8},{14,10},{1,5},{3,7},... | collective-permute-start | bytes 3391496 | tf_op jit(solution)/shard_map/ppermute | solution.py:501
  100.5 22.8 %collective-permute-start.11 = (bf16[23,64,384]{2,1,0:T(8,128)(2,1)}, bf16[23,64,384]{2,1,0:T(8,128)(2,1)}, u32[]{:S(2)}, u32[]{:S(2)}) collective-permute-start(bf16[23,64,384]{2,1,0:T(8,128)(2,1)} %collective-permute-done.4.refs_1_.refs_2_), channel_id=1, source_target_pairs={{4,8},{6,10},{8,4},{10,6},{5,9},{7,11},{9,5},{11,7},{20,24},{22,26... | collective-permute-start | bytes 3391496 | tf_op jit(solution)/shard_map/ppermute | solution.py:501
  106.4 0.8 copy-start.19
  107.2 16.1 %collective-permute-start.10 = (bf16[23,96,128]{2,1,0:T(8,128)(2,1)}, bf16[23,96,128]{2,1,0:T(8,128)(2,1)}, u32[]{:S(2)}, u32[]{:S(2)}) collective-permute-start(bf16[23,96,128]{2,1,0:T(8,128)(2,1)} %get-tuple-element.55), channel_id=1, source_target_pairs={{4,6},{6,4},{9,11},{11,9},{20,22},{22,20},{25,27},{27,25}} | collective-permute-start | bytes 1695752 | tf_op jit(solution)/shard_map/ppermute | solution.py:525
  108.7 29.6 %collective-permute-start.18 = (bf16[64,96,128]{2,1,0:T(8,128)(2,1)}, bf16[64,96,128]{2,1,0:T(8,128)(2,1)S(1)}, u32[]{:S(2)}, u32[]{:S(2)}) collective-permute-start(bf16[64,96,128]{2,1,0:T(8,128)(2,1)} %copy-done.4), channel_id=1, source_target_pairs={{1,0},{3,2},{5,4},{7,6},{8,9},{10,11},{12,13},{14,15},{17,16},{19,... | collective-permute-start | bytes 4718600 | tf_op jit(solution)/shard_map/ppermute | solution.py:511
  114.5 1.3 copy-start.7
  115.8 7.5 %copy-start.8 = (bf16[23,64,384]{2,1,0:T(8,128)(2,1)S(1)}, bf16[23,64,384]{2,1,0:T(8,128)(2,1)}, u32[]{:S(2)}) copy-start(bf16[23,64,384]{2,1,0:T(8,128)(2,1)} %copy-done.6) | copy-start | bytes 3391492
  115.8 7.5 %copy-start.16 = (bf16[23,64,384]{2,1,0:T(8,128)(2,1)S(1)}, bf16[23,64,384]{2,1,0:T(8,128)(2,1)}, u32[]{:S(2)}) copy-start(bf16[23,64,384]{2,1,0:T(8,128)(2,1)} %copy-done.15) | copy-start | bytes 3391492
  121.8 16.5 %copy-start.5 = (bf16[64,96,128]{2,1,0:T(8,128)(2,1)S(1)}, bf16[64,96,128]{2,1,0:T(8,128)(2,1)}, u32[]{:S(2)}) copy-start(bf16[64,96,128]{2,1,0:T(8,128)(2,1)} %copy-done.4) | copy-start | bytes 4718596
  121.8 16.5 %collective-permute-start.19 = (bf16[64,96,128]{2,1,0:T(8,128)(2,1)S(1)}, bf16[64,96,128]{2,1,0:T(8,128)(2,1)S(1)}, u32[]{:S(2)}, u32[]{:S(2)}) collective-permute-start(bf16[64,96,128]{2,1,0:T(8,128)(2,1)S(1)} %triangle.7.refs_2_), channel_id=1, source_target_pairs={{0,1},{2,3},{4,5},{6,7},{9,8},{11,10},{13,12},{15,14},{16,17},{18,... | collective-permute-start | bytes 4718600 | tf_op jit(solution)/shard_map/ppermute | solution.py:511
  131.5 13.8 %collective-permute-start.12 = (bf16[64,96,128]{2,1,0:T(8,128)(2,1)S(1)}, bf16[64,96,128]{2,1,0:T(8,128)(2,1)S(1)}, u32[]{:S(2)}, u32[]{:S(2)}) collective-permute-start(bf16[64,96,128]{2,1,0:T(8,128)(2,1)S(1)} %get-tuple-element.58.refs_0_), channel_id=1, source_target_pairs={{1,0},{3,2},{4,5},{6,7},{9,8},{11,10},{12,13},{14,15},{17,16},{19,... | collective-permute-start | bytes 4718600 | tf_op jit(solution)/shard_map/ppermute | solution.py:511
  136.9 4.9 %collective-permute-start.13 = (bf16[64,48,128]{2,1,0:T(8,128)(2,1)S(1)}, bf16[64,48,128]{2,1,0:T(8,128)(2,1)S(1)}, u32[]{:S(2)}, u32[]{:S(2)}) collective-permute-start(bf16[64,48,128]{2,1,0:T(8,128)(2,1)S(1)} %get-tuple-element.60.refs_0_), channel_id=1, source_target_pairs={{5,4},{7,6},{8,9},{10,11},{21,20},{23,22},{24,25},{26,27}} | collective-permute-start | bytes 2359304 | tf_op jit(solution)/shard_map/ppermute | solution.py:511
  137.6 4.1 %collective-permute-start.14 = (bf16[64,48,128]{2,1,0:T(8,128)(2,1)S(1)}, bf16[64,48,128]{2,1,0:T(8,128)(2,1)S(1)}, u32[]{:S(2)}, u32[]{:S(2)}) collective-permute-start(bf16[64,48,128]{2,1,0:T(8,128)(2,1)S(1)} %get-tuple-element.61.refs_2_), channel_id=1, source_target_pairs={{4,5},{6,7},{9,8},{11,10},{20,21},{22,23},{25,24},{27,26}} | collective-permute-start | bytes 2359304 | tf_op jit(solution)/shard_map/ppermute | solution.py:511
  140.5 17.7 %collective-permute-start.20 = (bf16[23,96,128]{2,1,0:T(8,128)(2,1)}, bf16[23,96,128]{2,1,0:T(8,128)(2,1)}, u32[]{:S(2)}, u32[]{:S(2)}) collective-permute-start(bf16[23,96,128]{2,1,0:T(8,128)(2,1)} %get-tuple-element.66), channel_id=1, source_target_pairs={{0,2},{2,0},{4,6},{6,4},{8,10},{10,8},{12,14},{14,12},{1,3},{3,1},... | collective-permute-start | bytes 1695752 | tf_op jit(solution)/shard_map/ppermute | solution.py:504
  142.5 15.8 %copy-start.17 = (bf16[1024,128]{1,0:T(8,128)(2,1)S(1)}, bf16[1024,128]{1,0:T(8,128)(2,1)}, u32[]{:S(2)}) copy-start(bf16[1024,128]{1,0:T(8,128)(2,1)} %multiply_bitcast_fusion.refs_1_) | copy-start | bytes 786436
  142.5 15.8 %copy-start.24 = (bf16[12,128,384]{2,1,0:T(8,128)(2,1)S(1)}, bf16[12,128,384]{2,1,0:T(8,128)(2,1)}, u32[]{:S(2)}) copy-start(bf16[12,128,384]{2,1,0:T(8,128)(2,1)} %copy-done.23) | copy-start | bytes 3538948
  142.5 26.7 %collective-permute-start.15 = (bf16[23,96,128]{2,1,0:T(8,128)(2,1)S(1)}, bf16[23,96,128]{2,1,0:T(8,128)(2,1)}, u32[]{:S(2)}, u32[]{:S(2)}) collective-permute-start(bf16[23,96,128]{2,1,0:T(8,128)(2,1)S(1)} %fold.6), channel_id=1, source_target_pairs={{5,1},{7,3},{8,12},{10,14},{21,17},{23,19},{24,28},{26,30}} | collective-permute-start | bytes 1695752 | tf_op jit(solution)/shard_map/ppermute | solution.py:519
  144.0 26.6 %collective-permute-start.17 = (bf16[23,96,128]{2,1,0:T(8,128)(2,1)S(1)}, bf16[23,96,128]{2,1,0:T(8,128)(2,1)}, u32[]{:S(2)}, u32[]{:S(2)}) collective-permute-start(bf16[23,96,128]{2,1,0:T(8,128)(2,1)S(1)} %fold.6), channel_id=1, source_target_pairs={{4,3},{6,1},{9,14},{11,12},{20,19},{22,17},{25,30},{27,28}} | collective-permute-start | bytes 1695752 | tf_op jit(solution)/shard_map/ppermute | solution.py:519
  147.4 23.2 %collective-permute-start.16 = (bf16[23,96,128]{2,1,0:T(8,128)(2,1)}, bf16[23,96,128]{2,1,0:T(8,128)(2,1)}, u32[]{:S(2)}, u32[]{:S(2)}) collective-permute-start(bf16[23,96,128]{2,1,0:T(8,128)(2,1)} %get-tuple-element.62), channel_id=1, source_target_pairs={{0,2},{2,0},{5,7},{7,5},{8,10},{10,8},{13,15},{15,13},{16,18},{18,... | collective-permute-start | bytes 1695752 | tf_op jit(solution)/shard_map/ppermute | solution.py:525
  148.8 20.3 %copy-start.20 = (bf16[23,96,128]{2,1,0:T(8,128)(2,1)S(1)}, bf16[23,96,128]{2,1,0:T(8,128)(2,1)}, u32[]{:S(2)}) copy-start(bf16[23,96,128]{2,1,0:T(8,128)(2,1)} %copy-done.19) | copy-start | bytes 1695748
  158.3 1.7 copy-start.22
  169.2 2.6 %copy-start.12 = (f32[12,128,384]{2,1,0:T(8,128)S(1)}, f32[12,128,384]{2,1,0:T(8,128)}, u32[]{:S(2)}) copy-start(f32[12,128,384]{2,1,0:T(8,128)} %copy-done.11) | copy-start | bytes 7077892
  170.6 1.6 copy-start.14

commit v13 on v12

--- a/solution.py
+++ b/solution.py
@@ -333,7 +333,8 @@
     )(flag, pair, gate_w)
 
 
-def finish_kernel(flag_ref, pair_ref, gate_ref, own_ref, other_ref, *refs, cols):
+def finish_kernel(flag_ref, pair_ref, gate_ref, own_ref, *refs, cols, sources):
+    other_refs, refs = refs[:sources], refs[sources:]
     out_w_ref, in_ref, back_ref = refs[:3]
     earlier_ref, out_ref = refs[3] if len(refs) == 5 else None, refs[-1]
     steps, width, _ = pair_ref.shape
@@ -345,7 +346,8 @@
     def step(i, carry):
         first = jnp.minimum(2 * i, half - 2)
         rows = [(h, first + e) for h in range(2) for e in range(2)]
-        turned = [[ref[first + e].T[:, :block] for ref in (own_ref, other_ref)] for e in range(2)]
+        others = [sum(ref[first + e] for ref in other_refs) for e in range(2)]
+        turned = [[v.T[:, :block] for v in (own_ref[first + e], others[e])] for e in range(2)]
         tri = [
             jnp.concatenate([t[h * chans : (h + 1) * chans] for t in turned[e]], axis=0)
             for h in range(2)
@@ -371,23 +373,23 @@
                 out_ref[h, r] = jnp.concatenate(parts, axis=0).astype(BF16)
         return carry
 
-    lax.fori_loop(0, steps, step, 0, unroll=4)
-
-
-def finish(flag, cols, prepared, own, other, weights, earlier=None):
+    lax.fori_loop(0, steps, step, 0, unroll=6)
+
+
+def finish(flag, cols, prepared, own, others, weights, earlier=None):
     half, _, width = own.shape
     shape = (2, half, padded(cols // 2, 16) if earlier is None else cols, width)
     extra = [] if earlier is None else [earlier]
     size = own.size * 2
     return pl.pallas_call(
-        functools.partial(finish_kernel, cols=cols),
+        functools.partial(finish_kernel, cols=cols, sources=len(others)),
         out_shape=jax.ShapeDtypeStruct(shape, BF16),
-        in_specs=[pl.BlockSpec(memory_space=pltpu.SMEM)] + whole(7 + len(extra)),
+        in_specs=[pl.BlockSpec(memory_space=pltpu.SMEM)] + whole(6 + len(others) + len(extra)),
         out_specs=pl.BlockSpec(memory_space=VMEM),
         compiler_params=params(),
         cost_estimate=cost(26 * size * width, 10 * size, 5 * size),
         name="finish",
-    )(flag, *prepared, own, other, *weights, *extra)
+    )(flag, *prepared, own, *others, *weights, *extra)
 
 
 def layer_norm(values):
@@ -612,13 +614,13 @@
     late_other = side_to_side(late_block[1], everyone, (0, 1, 0, 1))
 
     earlier = finish(
-        scalars(order), tile_cols, prepared[0], after(first[0], lent), first_other, weights
-    )
-    own, other = (
-        jnp.where(inner & is_keeper, early, jnp.where(inner | is_keeper, end, back))
-        for early, end, back in zip((mate_block[0], mate_other), (late_block[0], late_other), given)
-    )
-    result = finish(scalars(1 - order), tile_cols, prepared[1], own, other, weights, earlier)
+        scalars(order), tile_cols, prepared[0], after(first[0], lent), [first_other], weights
+    )
+    own = jnp.where(
+        inner & is_keeper, mate_block[0], jnp.where(inner | is_keeper, late_block[0], given[0])
+    )
+    others = [mate_other, late_other, given[1]]
+    result = finish(scalars(1 - order), tile_cols, prepared[1], own, others, weights, earlier)
     return result.reshape(tile_rows, tile_cols, width)
 
 

time: 184 us -> 184 us (level)
  transfers between devices with their start and end apart: 21 -> 21, of which waited for: 5 -> 5; matrix products, arithmetic and copies ran while one was open for 4% -> 4% of each run, Pallas kernels for 32% -> 31%
where the time goes in v13:
time: 184 us; the launch traced here: 182 us
  Pallas kernels  74 us (40%)
  starting transfers between devices  45.1 us (25%)
  waiting for transfers between devices  37.3 us (20%)
  local copies, waits for them, and re-layouts  17.4 us (9%)
  other arithmetic  6.9 us (4%)
    ppermute x3, waiting for transfers between devices, across(): return lax.ppermute(value, 'row', [(i, i ^ 1) for i in range(8)])  34.6 us
    pallas_call x4, Pallas kernels, triangle(): pl.pallas_call(functools.partial(triangle_kernel, counts=[len(piece) for...  26.1 us
    ppermute x8, starting transfers between devices, among(): lax.ppermute(value, 'row', [(2 * s + b, 2 * t + b) for s, t in moves for...  20.5 us
    pallas_call x2, Pallas kernels, finish(): pl.pallas_call(functools.partial(finish_kernel, cols=cols, sources=len(ot...  19 us
    unnamed x60, local copies, waits for them, and re-layouts  16 us
    ppermute x6, starting transfers between devices, to_core(): return lax.ppermute(value, ('row', 'col'), perm)  15.9 us
    pallas_call x2, Pallas kernels, project(): pl.pallas_call(functools.partial(project_kernel, first=first), out_shape=...  12.8 us
    pallas_call x4, Pallas kernels, fold(): pl.pallas_call(functools.partial(fold_kernel, outputs=outputs, half=half)...  9.25 us
  transfers between devices with their start and end apart: 21, of which 5 were waited for; matrix products, arithmetic and copies ran while one was open for 4% of the time, Pallas kernels for 31%

profile of v13, /device:TPU:1, one launch (start us, length us, event | category | flops | bytes accessed | tf_op | source)
XLA Modules:
  0.0 181.6 jit_solution(5692048370082111022)
XLA Ops:
  0.0 1.2 slice.14
  1.9 1.6 copy-done
  3.5 0.9 copy-done.18
  4.4 6.7 %project.2 = (bf16[23,64,384]{2,1,0:T(8,128)(2,1)}, bf16[23,64,384]{2,1,0:T(8,128)(2,1)}) custom-call(s32[4]{0:T(128)S(1)} %pad_add_fusion.where_ref, bf16[2,23,184,128]{3,2,1,0:T(8,128)(2,1)S(1)} %bitcast.16, bf16[128,640]{1,0:T(8,128)(2,1)S(1)} %copy-done.18), custom_call_target="tpu_custom_call" | custom-call | flops 554696704 | bytes 4333568 | tf_op jit(solution)/shard_map/project/pallas_call | solution.py:92
  11.1 1.9 %collective-permute-start.1 = (bf16[23,64,384]{2,1,0:T(8,128)(2,1)}, bf16[23,64,384]{2,1,0:T(8,128)(2,1)}, u32[]{:S(2)}, u32[]{:S(2)}) collective-permute-start(bf16[23,64,384]{2,1,0:T(8,128)(2,1)} %get-tuple-element.39.refs_0_), channel_id=1, source_target_pairs={{4,8},{6,10},{8,4},{10,6},{5,9},{7,11},{9,5},{11,7},{20,24},{22,26... | collective-permute-start | bytes 3391496 | tf_op jit(solution)/shard_map/ppermute | solution.py:503
  13.0 2.0 %collective-permute-start.2 = (bf16[23,64,384]{2,1,0:T(8,128)(2,1)}, bf16[23,64,384]{2,1,0:T(8,128)(2,1)S(1)}, u32[]{:S(2)}, u32[]{:S(2)}) collective-permute-start(bf16[23,64,384]{2,1,0:T(8,128)(2,1)} %get-tuple-element.40), channel_id=1, source_target_pairs={{0,2},{2,0},{4,6},{6,4},{8,10},{10,8},{12,14},{14,12},{1,3},{3,1},... | collective-permute-start | bytes 3391496 | tf_op jit(solution)/shard_map/ppermute | solution.py:506
  15.0 2.8 %collective-permute-start = (bf16[23,64,384]{2,1,0:T(8,128)(2,1)}, bf16[23,64,384]{2,1,0:T(8,128)(2,1)}, u32[]{:S(2)}, u32[]{:S(2)}) collective-permute-start(bf16[23,64,384]{2,1,0:T(8,128)(2,1)} %get-tuple-element.39.refs_0_), channel_id=1, source_target_pairs={{0,4},{2,6},{4,0},{6,2},{8,12},{10,14},{12,8},{14,10},{1,5},{3,7},... | collective-permute-start | bytes 3391496 | tf_op jit(solution)/shard_map/ppermute | solution.py:503
  17.9 6.2 %project.3 = (bf16[23,64,384]{2,1,0:T(8,128)(2,1)S(1)}, bf16[23,64,384]{2,1,0:T(8,128)(2,1)}) custom-call(s32[4]{0:T(128)S(1)} %pad_add_fusion.where_ref, bf16[2,23,184,128]{3,2,1,0:T(8,128)(2,1)S(1)} %bitcast.17, bf16[128,640]{1,0:T(8,128)(2,1)S(1)} %copy-done.18), custom_call_target="tpu_custom_call" | custom-call | flops 554696704 | bytes 4333568 | tf_op jit(solution)/shard_map/project/pallas_call | solution.py:92
  24.1 1.0 copy-done.9
  25.1 0.1 copy.10
  25.2 0.1 copy.13
  25.3 0.1 copy.12
  25.4 0.2 copy.11
  25.8 0.9 multiply_bitcast_fusion.refs_2_.refs_4_
  26.7 13.3 %collective-permute-done.2.refs_1_ = bf16[23,64,384]{2,1,0:T(8,128)(2,1)S(1)} collective-permute-done((bf16[23,64,384]{2,1,0:T(8,128)(2,1)}, bf16[23,64,384]{2,1,0:T(8,128)(2,1)S(1)}, u32[]{:S(2)}, u32[]{:S(2)}) %collective-permute-start.2) | collective-permute-done | bytes 1130528 | tf_op jit(solution)/shard_map/ppermute | solution.py:506
  40.0 1.3 broadcast_select_fusion.2
  41.3 0.9 collective-permute-done.refs_0_.refs_4_
  42.2 1.7 collective-permute-start.6
  43.9 0.3 collective-permute-start.3
  44.2 4.5 %collective-permute-start.4 = (bf16[23,64,384]{2,1,0:T(8,128)(2,1)}, bf16[23,64,384]{2,1,0:T(8,128)(2,1)}, u32[]{:S(2)}, u32[]{:S(2)}) collective-permute-start(bf16[23,64,384]{2,1,0:T(8,128)(2,1)} %broadcast_select_fusion.2), channel_id=1, source_target_pairs={{0,4},{2,6},{4,0},{6,2},{8,12},{10,14},{12,8},{14,10},{1,5},{3,7},... | collective-permute-start | bytes 3391496 | tf_op jit(solution)/shard_map/ppermute | solution.py:503
  48.7 1.8 prepare.3
  50.5 1.5 copy-done.21
  52.0 1.0 copy-done.23
  53.0 1.8 prepare.2
  54.8 1.1 copy-done.13
  55.9 0.1 broadcast_select_fusion.1
  56.0 1.2 copy-done.11
  57.3 11.5 %collective-permute-done.3.beside_ref = bf16[23,64,384]{2,1,0:T(8,128)(2,1)} collective-permute-done((bf16[23,64,384]{2,1,0:T(8,128)(2,1)}, bf16[23,64,384]{2,1,0:T(8,128)(2,1)}, u32[]{:S(2)}, u32[]{:S(2)}) %collective-permute-start.3) | collective-permute-done | bytes 1130528 | tf_op jit(solution)/shard_map/ppermute | solution.py:506
  68.7 4.7 %collective-permute-start.7 = (bf16[23,64,384]{2,1,0:T(8,128)(2,1)S(1)}, bf16[23,64,384]{2,1,0:T(8,128)(2,1)S(1)}, u32[]{:S(2)}, u32[]{:S(2)}) collective-permute-start(bf16[23,64,384]{2,1,0:T(8,128)(2,1)S(1)} %broadcast_select_fusion.1), channel_id=1, source_target_pairs={{0,4},{2,6},{4,0},{6,2},{8,12},{10,14},{12,8},{14,10},{1,5},{3,7},... | collective-permute-start | bytes 3391496 | tf_op jit(solution)/shard_map/ppermute | solution.py:503
  73.4 0.7 collective-permute-start.8
  74.2 3.2 %left_major.1.left_ref = bf16[64,96,256]{2,1,0:T(8,128)(2,1)S(1)} custom-call(bf16[23,64,384]{2,1,0:T(8,128)(2,1)S(1)} %copy-done.10, bf16[23,64,384]{2,1,0:T(8,128)(2,1)} %collective-permute-done.3.beside_ref), custom_call_target="tpu_custom_call" | custom-call | bytes 4521984 | tf_op jit(solution)/shard_map/left_major/pallas_call | solution.py:144
  77.4 6.5 %triangle.4.refs_0_ = bf16[64,96,128]{2,1,0:T(8,128)(2,1)} custom-call(s32[2]{0:T(128)S(1)} %pad_add_fusion.1.flag_ref, bf16[64,96,256]{2,1,0:T(8,128)(2,1)S(1)} %left_major.1.left_ref, bf16[23,64,384]{2,1,0:T(8,128)(2,1)} %collective-permute-done.refs_0_.refs_4_, bf16[23,64,384]{2,1,0:T(8,128)(2,1)} %collective-permute-done.4.refs_1_.refs_2_), custom_call_target="tpu_custom_call" | custom-call | flops 402653184 | bytes 5652480 | tf_op jit(solution)/shard_map/triangle/pallas_call | solution.py:223
  83.9 1.9 %collective-permute-start.5 = (bf16[64,96,128]{2,1,0:T(8,128)(2,1)}, bf16[64,96,128]{2,1,0:T(8,128)(2,1)}, u32[]{:S(2)}, u32[]{:S(2)}) collective-permute-start(bf16[64,96,128]{2,1,0:T(8,128)(2,1)} %triangle.4.refs_0_), channel_id=1, source_target_pairs={{5,4},{7,6},{8,9},{10,11},{21,20},{23,22},{24,25},{26,27}} | collective-permute-start | bytes 4718600 | tf_op jit(solution)/shard_map/ppermute | solution.py:513
  85.8 5.4 %triangle.5.refs_0_ = bf16[64,96,128]{2,1,0:T(8,128)(2,1)S(1)} custom-call(s32[2]{0:T(128)S(1)} %pad_add_fusion.1.flag_ref, bf16[64,96,256]{2,1,0:T(8,128)(2,1)S(1)} %left_major.1.left_ref, bf16[23,64,384]{2,1,0:T(8,128)(2,1)} %get-tuple-element.39.refs_0_, bf16[23,64,384]{2,1,0:T(8,128)(2,1)S(1)} %copy-done.3), custom_call_target="tpu_custom_call" | custom-call | flops 402653184 | bytes 5652480 | tf_op jit(solution)/shard_map/triangle/pallas_call | solution.py:223
  91.3 3.0 %broadcast_select_fusion = bf16[23,64,384]{2,1,0:T(8,128)(2,1)} fusion(bf16[23,64,384]{2,1,0:T(8,128)(2,1)S(1)} %copy-done.3, bf16[23,64,384]{2,1,0:T(8,128)(2,1)} %collective-permute-done.3.beside_ref, pred[]{:T(512)S(6)} %or.6), kind=kLoop, calls=%fused_computation | loop fusion | flops 565248 | bytes 3391489 | tf_op jit(solution)/shard_map/jit(_where)/select_n | solution.py:553
  94.3 1.7 collective-permute-done.7.refs_0_.refs_3_
  96.0 1.0 copy-done.6
  97.0 1.0 copy-done.15
  98.0 2.5 %collective-permute-start.9 = (bf16[23,64,384]{2,1,0:T(8,128)(2,1)}, bf16[23,64,384]{2,1,0:T(8,128)(2,1)}, u32[]{:S(2)}, u32[]{:S(2)}) collective-permute-start(bf16[23,64,384]{2,1,0:T(8,128)(2,1)} %broadcast_select_fusion), channel_id=1, source_target_pairs={{0,4},{2,6},{4,0},{6,2},{8,12},{10,14},{12,8},{14,10},{1,5},{3,7},... | collective-permute-start | bytes 3391496 | tf_op jit(solution)/shard_map/ppermute | solution.py:503
  100.5 1.7 collective-permute-start.11
  102.2 4.2 %fold.4 = (bf16[23,96,128]{2,1,0:T(8,128)(2,1)S(1)}, bf16[23,96,128]{2,1,0:T(8,128)(2,1)}) custom-call(s32[1]{0:T(128)} %bitcast.6.role_ref, bf16[64,96,128]{2,1,0:T(8,128)(2,1)} %triangle.4.refs_0_, bf16[64,96,128]{2,1,0:T(8,128)(2,1)} %collective-permute-done.5.refs_1_), custom_call_target="tpu_custom_call" | custom-call | bytes 4718592 | tf_op jit(solution)/shard_map/fold/pallas_call | solution.py:285
  106.4 0.8 copy-done.19
  107.2 1.5 collective-permute-start.10
  108.7 5.8 %collective-permute-start.18 = (bf16[64,96,128]{2,1,0:T(8,128)(2,1)}, bf16[64,96,128]{2,1,0:T(8,128)(2,1)S(1)}, u32[]{:S(2)}, u32[]{:S(2)}) collective-permute-start(bf16[64,96,128]{2,1,0:T(8,128)(2,1)} %copy-done.4), channel_id=1, source_target_pairs={{1,0},{3,2},{5,4},{7,6},{8,9},{10,11},{12,13},{14,15},{17,16},{19,... | collective-permute-start | bytes 4718600 | tf_op jit(solution)/shard_map/ppermute | solution.py:513
  114.5 1.2 copy-done.7
  115.8 6.0 %triangle.7.refs_2_ = bf16[64,96,128]{2,1,0:T(8,128)(2,1)S(1)} custom-call(s32[2]{0:T(128)S(1)} %pad_add_fusion.2.flag_ref, bf16[64,96,256]{2,1,0:T(8,128)(2,1)S(1)} %left_major.1.left_ref, bf16[23,64,384]{2,1,0:T(8,128)(2,1)} %collective-permute-done.1.refs_0_, bf16[23,64,384]{2,1,0:T(8,128)(2,1)} %collective-permute-done.6.refs_1_, ...), custom_call_target="tpu_custom_call" | custom-call | flops 402653184 | bytes 5652480 | tf_op jit(solution)/shard_map/triangle/pallas_call | solution.py:223
  121.8 1.4 collective-permute-start.19
  123.3 8.1 %triangle.6 = (bf16[64,96,128]{2,1,0:T(8,128)(2,1)S(1)}, bf16[64,48,128]{2,1,0:T(8,128)(2,1)S(1)}, bf16[64,48,128]{2,1,0:T(8,128)(2,1)S(1)}) custom-call(s32[2]{0:T(128)S(1)} %pad_add_fusion.2.flag_ref, bf16[64,96,256]{2,1,0:T(8,128)(2,1)S(1)} %left_major.1.left_ref, bf16[23,64,384]{2,1,0:T(8,128)(2,1)S(1)} %copy-done.8, ...), custom_call_target="tpu_custom_call" | custom-call | flops 805306368 | bytes 5652480 | tf_op jit(solution)/shard_map/triangle/pallas_call | solution.py:223
  131.5 5.4 %collective-permute-start.12 = (bf16[64,96,128]{2,1,0:T(8,128)(2,1)S(1)}, bf16[64,96,128]{2,1,0:T(8,128)(2,1)S(1)}, u32[]{:S(2)}, u32[]{:S(2)}) collective-permute-start(bf16[64,96,128]{2,1,0:T(8,128)(2,1)S(1)} %get-tuple-element.58.refs_0_), channel_id=1, source_target_pairs={{1,0},{3,2},{4,5},{6,7},{9,8},{11,10},{12,13},{14,15},{17,16},{19,... | collective-permute-start | bytes 4718600 | tf_op jit(solution)/shard_map/ppermute | solution.py:513
  136.9 0.7 collective-permute-start.13
  137.6 0.7 collective-permute-start.14
  138.4 2.2 %fold.7 = (bf16[23,96,128]{2,1,0:T(8,128)(2,1)S(1)}, bf16[23,96,128]{2,1,0:T(8,128)(2,1)}) custom-call(s32[1]{0:T(128)} %bitcast.6.role_ref, bf16[64,96,128]{2,1,0:T(8,128)(2,1)S(1)} %copy-done.5, bf16[64,96,128]{2,1,0:T(8,128)(2,1)S(1)} %collective-permute-done.18.refs_1_, bf16[64,96,128]{2,1,0:T(8,128)(2,1)S(1)} %triangle.7.refs_2_, ...), custom_call_target="tpu_custom_call" | custom-call | bytes 4718592 | tf_op jit(solution)/shard_map/fold/pallas_call | solution.py:285
  140.5 1.2 collective-permute-start.20
  141.7 0.7 fold.6
  142.5 1.4 collective-permute-start.15
  143.9 1.3 collective-permute-start.17
  145.2 2.1 %fold.5 = (bf16[23,96,128]{2,1,0:T(8,128)(2,1)S(1)}, bf16[23,96,128]{2,1,0:T(8,128)(2,1)}) custom-call(s32[1]{0:T(128)} %bitcast.6.role_ref, bf16[64,96,128]{2,1,0:T(8,128)(2,1)S(1)} %get-tuple-element.58.refs_0_, bf16[64,96,128]{2,1,0:T(8,128)(2,1)S(1)} %collective-permute-done.12.refs_1_), custom_call_target="tpu_custom_call" | custom-call | bytes 4718592 | tf_op jit(solution)/shard_map/fold/pallas_call | solution.py:285
  147.4 0.9 collective-permute-start.16
  148.3 9.9 %collective-permute-done.20.refs_0_ = bf16[23,96,128]{2,1,0:T(8,128)(2,1)} collective-permute-done((bf16[23,96,128]{2,1,0:T(8,128)(2,1)}, bf16[23,96,128]{2,1,0:T(8,128)(2,1)}, u32[]{:S(2)}, u32[]{:S(2)}) %collective-permute-start.20) | collective-permute-done | bytes 565280 | tf_op jit(solution)/shard_map/ppermute | solution.py:506
  158.2 1.7 copy-done.22
  159.9 1.3 copy-done.24
  161.1 8.8 %finish.2.refs_6_ = bf16[2,23,96,128]{3,2,1,0:T(8,128)(2,1)S(1)} custom-call(s32[1]{0:T(128)} %bitcast.11.flag_ref, bf16[12,128,384]{2,1,0:T(8,128)(2,1)S(1)} %copy-done.24, f32[12,128,384]{2,1,0:T(8,128)S(1)} %copy-done.22, bf16[23,96,128]{2,1,0:T(8,128)(2,1)S(1)} %get-tuple-element.65.own_ref, bf16[23,96,128]{2,1,0:T(8,128)(2,1)} %collective-permute-done.20.refs_0_, ...), custom_call_target="tpu_custom_call" | custom-call | flops 1881145344 | bytes 5652480 | tf_op jit(solution)/shard_map/finish/pallas_call | solution.py:384
  169.9 1.3 select_select_fusion.own_ref
  171.4 10.3 %finish.3 = bf16[2,23,184,128]{3,2,1,0:T(8,128)(2,1)} custom-call(s32[1]{0:T(128)} %bitcast.flag_ref, bf16[12,128,384]{2,1,0:T(8,128)(2,1)S(1)} %copy-done.14, f32[12,128,384]{2,1,0:T(8,128)S(1)} %copy-done.12, bf16[23,96,128]{2,1,0:T(8,128)(2,1)S(1)} %select_select_fusion.own_ref, bf16[23,96,128]{2,1,0:T(8,128)(2,1)} %collective-permute-done.10.refs_0_, ...), custom_call_target="tpu_custom_call" | custom-call | flops 1881145344 | bytes 5652480 | tf_op jit(solution)/shard_map/finish/pallas_call | solution.py:384
  (67 shorter events, 0.6 us)
Async XLA Ops:
  1.9 1.6 copy-start
  3.5 0.9 copy-start.18
  11.1 14.0 %copy-start.27 = (bf16[128,128]{1,0:T(8,128)(2,1)S(1)}, bf16[128,128]{1,0:T(8,128)(2,1)}, u32[]{:S(2)}) copy-start(bf16[128,128]{1,0:T(8,128)(2,1)} %param.9) | copy-start | bytes 98308
  11.1 14.1 %slice-start = ((bf16[128,640]{1,0:T(8,128)(2,1)}), bf16[128,128]{1,0:T(8,128)(2,1)S(1)}, s32[]{:S(2)}) async-start(bf16[128,640]{1,0:T(8,128)(2,1)} %weight_ref.3), calls=%async_computation | async-start | bytes 65536 | tf_op jit(solution)/shard_map/slice | solution.py:566
  11.1 14.2 %copy-start.26 = (bf16[512,128]{1,0:T(8,128)(2,1)S(1)}, bf16[512,128]{1,0:T(8,128)(2,1)}, u32[]{:S(2)}) copy-start(bf16[512,128]{1,0:T(8,128)(2,1)} %param.11) | copy-start | bytes 393220
  11.1 14.3 %copy-start.25 = (bf16[128,1024]{1,0:T(8,128)(2,1)S(1)}, bf16[128,1024]{1,0:T(8,128)(2,1)}, u32[]{:S(2)}) copy-start(bf16[128,1024]{1,0:T(8,128)(2,1)} %param.10) | copy-start | bytes 786436
  11.1 15.6 %collective-permute-start.1 = (bf16[23,64,384]{2,1,0:T(8,128)(2,1)}, bf16[23,64,384]{2,1,0:T(8,128)(2,1)}, u32[]{:S(2)}, u32[]{:S(2)}) collective-permute-start(bf16[23,64,384]{2,1,0:T(8,128)(2,1)} %get-tuple-element.39.refs_0_), channel_id=1, source_target_pairs={{4,8},{6,10},{8,4},{10,6},{5,9},{7,11},{9,5},{11,7},{20,24},{22,26... | collective-permute-start | bytes 3391496 | tf_op jit(solution)/shard_map/ppermute | solution.py:503
  13.0 27.0 %collective-permute-start.2 = (bf16[23,64,384]{2,1,0:T(8,128)(2,1)}, bf16[23,64,384]{2,1,0:T(8,128)(2,1)S(1)}, u32[]{:S(2)}, u32[]{:S(2)}) collective-permute-start(bf16[23,64,384]{2,1,0:T(8,128)(2,1)} %get-tuple-element.40), channel_id=1, source_target_pairs={{0,2},{2,0},{4,6},{6,4},{8,10},{10,8},{12,14},{14,12},{1,3},{3,1},... | collective-permute-start | bytes 3391496 | tf_op jit(solution)/shard_map/ppermute | solution.py:506
  15.0 27.1 %collective-permute-start = (bf16[23,64,384]{2,1,0:T(8,128)(2,1)}, bf16[23,64,384]{2,1,0:T(8,128)(2,1)}, u32[]{:S(2)}, u32[]{:S(2)}) collective-permute-start(bf16[23,64,384]{2,1,0:T(8,128)(2,1)} %get-tuple-element.39.refs_0_), channel_id=1, source_target_pairs={{0,4},{2,6},{4,0},{6,2},{8,12},{10,14},{12,8},{14,10},{1,5},{3,7},... | collective-permute-start | bytes 3391496 | tf_op jit(solution)/shard_map/ppermute | solution.py:503
  24.1 1.0 copy-start.9
  26.7 22.0 %copy-start.1 = (bf16[46,184,128]{2,1,0:T(8,128)(2,1)S(1)}, bf16[46,184,128]{2,1,0:T(8,128)(2,1)}, u32[]{:S(2)}) copy-start(bf16[46,184,128]{2,1,0:T(8,128)(2,1)} %param.6) | copy-start | bytes 6500356
  40.0 2.2 %copy-start.2 = (bf16[23,64,384]{2,1,0:T(8,128)(2,1)}, bf16[23,64,384]{2,1,0:T(8,128)(2,1)S(1)}, u32[]{:S(2)}) copy-start(bf16[23,64,384]{2,1,0:T(8,128)(2,1)S(1)} %collective-permute-done.2.refs_1_) | copy-start | bytes 3391492
  42.2 13.7 %collective-permute-start.6 = (bf16[23,64,384]{2,1,0:T(8,128)(2,1)S(1)}, bf16[23,64,384]{2,1,0:T(8,128)(2,1)}, u32[]{:S(2)}, u32[]{:S(2)}) collective-permute-start(bf16[23,64,384]{2,1,0:T(8,128)(2,1)S(1)} %collective-permute-done.2.refs_1_), channel_id=1, source_target_pairs={{4,8},{6,10},{8,4},{10,6},{5,9},{7,11},{9,5},{11,7},{20,24},{22,26... | collective-permute-start | bytes 3391496 | tf_op jit(solution)/shard_map/ppermute | solution.py:503
  43.9 24.9 %collective-permute-start.3 = (bf16[23,64,384]{2,1,0:T(8,128)(2,1)}, bf16[23,64,384]{2,1,0:T(8,128)(2,1)}, u32[]{:S(2)}, u32[]{:S(2)}) collective-permute-start(bf16[23,64,384]{2,1,0:T(8,128)(2,1)} %get-tuple-element.46), channel_id=1, source_target_pairs={{0,2},{2,0},{4,6},{6,4},{8,10},{10,8},{12,14},{14,12},{1,3},{3,1},... | collective-permute-start | bytes 3391496 | tf_op jit(solution)/shard_map/ppermute | solution.py:506
  44.2 33.2 %collective-permute-start.4 = (bf16[23,64,384]{2,1,0:T(8,128)(2,1)}, bf16[23,64,384]{2,1,0:T(8,128)(2,1)}, u32[]{:S(2)}, u32[]{:S(2)}) collective-permute-start(bf16[23,64,384]{2,1,0:T(8,128)(2,1)} %broadcast_select_fusion.2), channel_id=1, source_target_pairs={{0,4},{2,6},{4,0},{6,2},{8,12},{10,14},{12,8},{14,10},{1,5},{3,7},... | collective-permute-start | bytes 3391496 | tf_op jit(solution)/shard_map/ppermute | solution.py:503
  50.5 1.5 copy-start.21
  52.0 1.0 copy-start.23
  53.0 2.9 %copy-start.10 = (bf16[23,64,384]{2,1,0:T(8,128)(2,1)S(1)}, bf16[23,64,384]{2,1,0:T(8,128)(2,1)}, u32[]{:S(2)}) copy-start(bf16[23,64,384]{2,1,0:T(8,128)(2,1)} %copy-done.9) | copy-start | bytes 3391492
  54.8 1.1 copy-start.13
  55.9 1.4 copy-start.11
  68.7 27.2 %collective-permute-start.7 = (bf16[23,64,384]{2,1,0:T(8,128)(2,1)S(1)}, bf16[23,64,384]{2,1,0:T(8,128)(2,1)S(1)}, u32[]{:S(2)}, u32[]{:S(2)}) collective-permute-start(bf16[23,64,384]{2,1,0:T(8,128)(2,1)S(1)} %broadcast_select_fusion.1), channel_id=1, source_target_pairs={{0,4},{2,6},{4,0},{6,2},{8,12},{10,14},{12,8},{14,10},{1,5},{3,7},... | collective-permute-start | bytes 3391496 | tf_op jit(solution)/shard_map/ppermute | solution.py:503
  73.4 23.6 %collective-permute-start.8 = (bf16[23,64,384]{2,1,0:T(8,128)(2,1)}, bf16[23,64,384]{2,1,0:T(8,128)(2,1)S(1)}, u32[]{:S(2)}, u32[]{:S(2)}) collective-permute-start(bf16[23,64,384]{2,1,0:T(8,128)(2,1)} %collective-permute-done.refs_0_.refs_4_), channel_id=1, source_target_pairs={{4,8},{6,10},{8,4},{10,6},{5,9},{7,11},{9,5},{11,7},{20,24},{22,26... | collective-permute-start | bytes 3391496 | tf_op jit(solution)/shard_map/ppermute | solution.py:503
  77.4 8.4 %copy-start.3 = (bf16[23,64,384]{2,1,0:T(8,128)(2,1)S(1)}, bf16[23,64,384]{2,1,0:T(8,128)(2,1)}, u32[]{:S(2)}) copy-start(bf16[23,64,384]{2,1,0:T(8,128)(2,1)} %copy-done.2) | copy-start | bytes 3391492
  83.9 18.3 %collective-permute-start.5 = (bf16[64,96,128]{2,1,0:T(8,128)(2,1)}, bf16[64,96,128]{2,1,0:T(8,128)(2,1)}, u32[]{:S(2)}, u32[]{:S(2)}) collective-permute-start(bf16[64,96,128]{2,1,0:T(8,128)(2,1)} %triangle.4.refs_0_), channel_id=1, source_target_pairs={{5,4},{7,6},{8,9},{10,11},{21,20},{23,22},{24,25},{26,27}} | collective-permute-start | bytes 4718600 | tf_op jit(solution)/shard_map/ppermute | solution.py:513
  91.3 3.0 %copy-start.4 = (bf16[64,96,128]{2,1,0:T(8,128)(2,1)}, bf16[64,96,128]{2,1,0:T(8,128)(2,1)S(1)}, u32[]{:S(2)}) copy-start(bf16[64,96,128]{2,1,0:T(8,128)(2,1)S(1)} %triangle.5.refs_0_) | copy-start | bytes 4718596
  95.9 1.0 copy-start.6
  97.0 1.0 copy-start.15
  98.0 25.3 %collective-permute-start.9 = (bf16[23,64,384]{2,1,0:T(8,128)(2,1)}, bf16[23,64,384]{2,1,0:T(8,128)(2,1)}, u32[]{:S(2)}, u32[]{:S(2)}) collective-permute-start(bf16[23,64,384]{2,1,0:T(8,128)(2,1)} %broadcast_select_fusion), channel_id=1, source_target_pairs={{0,4},{2,6},{4,0},{6,2},{8,12},{10,14},{12,8},{14,10},{1,5},{3,7},... | collective-permute-start | bytes 3391496 | tf_op jit(solution)/shard_map/ppermute | solution.py:503
  100.5 22.8 %collective-permute-start.11 = (bf16[23,64,384]{2,1,0:T(8,128)(2,1)}, bf16[23,64,384]{2,1,0:T(8,128)(2,1)}, u32[]{:S(2)}, u32[]{:S(2)}) collective-permute-start(bf16[23,64,384]{2,1,0:T(8,128)(2,1)} %collective-permute-done.4.refs_1_.refs_2_), channel_id=1, source_target_pairs={{4,8},{6,10},{8,4},{10,6},{5,9},{7,11},{9,5},{11,7},{20,24},{22,26... | collective-permute-start | bytes 3391496 | tf_op jit(solution)/shard_map/ppermute | solution.py:503
  106.4 0.8 copy-start.19
  107.2 16.1 %collective-permute-start.10 = (bf16[23,96,128]{2,1,0:T(8,128)(2,1)}, bf16[23,96,128]{2,1,0:T(8,128)(2,1)}, u32[]{:S(2)}, u32[]{:S(2)}) collective-permute-start(bf16[23,96,128]{2,1,0:T(8,128)(2,1)} %get-tuple-element.55), channel_id=1, source_target_pairs={{4,6},{6,4},{9,11},{11,9},{20,22},{22,20},{25,27},{27,25}} | collective-permute-start | bytes 1695752 | tf_op jit(solution)/shard_map/ppermute | solution.py:527
  108.7 29.6 %collective-permute-start.18 = (bf16[64,96,128]{2,1,0:T(8,128)(2,1)}, bf16[64,96,128]{2,1,0:T(8,128)(2,1)S(1)}, u32[]{:S(2)}, u32[]{:S(2)}) collective-permute-start(bf16[64,96,128]{2,1,0:T(8,128)(2,1)} %copy-done.4), channel_id=1, source_target_pairs={{1,0},{3,2},{5,4},{7,6},{8,9},{10,11},{12,13},{14,15},{17,16},{19,... | collective-permute-start | bytes 4718600 | tf_op jit(solution)/shard_map/ppermute | solution.py:513
  114.5 1.3 copy-start.7
  115.8 7.5 %copy-start.8 = (bf16[23,64,384]{2,1,0:T(8,128)(2,1)S(1)}, bf16[23,64,384]{2,1,0:T(8,128)(2,1)}, u32[]{:S(2)}) copy-start(bf16[23,64,384]{2,1,0:T(8,128)(2,1)} %copy-done.6) | copy-start | bytes 3391492
  115.8 7.5 %copy-start.16 = (bf16[23,64,384]{2,1,0:T(8,128)(2,1)S(1)}, bf16[23,64,384]{2,1,0:T(8,128)(2,1)}, u32[]{:S(2)}) copy-start(bf16[23,64,384]{2,1,0:T(8,128)(2,1)} %copy-done.15) | copy-start | bytes 3391492
  121.8 16.5 %copy-start.5 = (bf16[64,96,128]{2,1,0:T(8,128)(2,1)S(1)}, bf16[64,96,128]{2,1,0:T(8,128)(2,1)}, u32[]{:S(2)}) copy-start(bf16[64,96,128]{2,1,0:T(8,128)(2,1)} %copy-done.4) | copy-start | bytes 4718596
  121.8 16.5 %collective-permute-start.19 = (bf16[64,96,128]{2,1,0:T(8,128)(2,1)S(1)}, bf16[64,96,128]{2,1,0:T(8,128)(2,1)S(1)}, u32[]{:S(2)}, u32[]{:S(2)}) collective-permute-start(bf16[64,96,128]{2,1,0:T(8,128)(2,1)S(1)} %triangle.7.refs_2_), channel_id=1, source_target_pairs={{0,1},{2,3},{4,5},{6,7},{9,8},{11,10},{13,12},{15,14},{16,17},{18,... | collective-permute-start | bytes 4718600 | tf_op jit(solution)/shard_map/ppermute | solution.py:513
  131.5 13.8 %collective-permute-start.12 = (bf16[64,96,128]{2,1,0:T(8,128)(2,1)S(1)}, bf16[64,96,128]{2,1,0:T(8,128)(2,1)S(1)}, u32[]{:S(2)}, u32[]{:S(2)}) collective-permute-start(bf16[64,96,128]{2,1,0:T(8,128)(2,1)S(1)} %get-tuple-element.58.refs_0_), channel_id=1, source_target_pairs={{1,0},{3,2},{4,5},{6,7},{9,8},{11,10},{12,13},{14,15},{17,16},{19,... | collective-permute-start | bytes 4718600 | tf_op jit(solution)/shard_map/ppermute | solution.py:513
  136.9 4.8 %collective-permute-start.13 = (bf16[64,48,128]{2,1,0:T(8,128)(2,1)S(1)}, bf16[64,48,128]{2,1,0:T(8,128)(2,1)S(1)}, u32[]{:S(2)}, u32[]{:S(2)}) collective-permute-start(bf16[64,48,128]{2,1,0:T(8,128)(2,1)S(1)} %get-tuple-element.60.refs_0_), channel_id=1, source_target_pairs={{5,4},{7,6},{8,9},{10,11},{21,20},{23,22},{24,25},{26,27}} | collective-permute-start | bytes 2359304 | tf_op jit(solution)/shard_map/ppermute | solution.py:513
  137.6 4.1 %collective-permute-start.14 = (bf16[64,48,128]{2,1,0:T(8,128)(2,1)S(1)}, bf16[64,48,128]{2,1,0:T(8,128)(2,1)S(1)}, u32[]{:S(2)}, u32[]{:S(2)}) collective-permute-start(bf16[64,48,128]{2,1,0:T(8,128)(2,1)S(1)} %get-tuple-element.61.refs_2_), channel_id=1, source_target_pairs={{4,5},{6,7},{9,8},{11,10},{20,21},{22,23},{25,24},{27,26}} | collective-permute-start | bytes 2359304 | tf_op jit(solution)/shard_map/ppermute | solution.py:513
  140.5 17.7 %collective-permute-start.20 = (bf16[23,96,128]{2,1,0:T(8,128)(2,1)}, bf16[23,96,128]{2,1,0:T(8,128)(2,1)}, u32[]{:S(2)}, u32[]{:S(2)}) collective-permute-start(bf16[23,96,128]{2,1,0:T(8,128)(2,1)} %get-tuple-element.66), channel_id=1, source_target_pairs={{0,2},{2,0},{4,6},{6,4},{8,10},{10,8},{12,14},{14,12},{1,3},{3,1},... | collective-permute-start | bytes 1695752 | tf_op jit(solution)/shard_map/ppermute | solution.py:506
  142.5 15.7 %copy-start.17 = (bf16[1024,128]{1,0:T(8,128)(2,1)S(1)}, bf16[1024,128]{1,0:T(8,128)(2,1)}, u32[]{:S(2)}) copy-start(bf16[1024,128]{1,0:T(8,128)(2,1)} %multiply_bitcast_fusion.refs_2_.refs_4_) | copy-start | bytes 786436
  142.5 27.4 %collective-permute-start.15 = (bf16[23,96,128]{2,1,0:T(8,128)(2,1)S(1)}, bf16[23,96,128]{2,1,0:T(8,128)(2,1)}, u32[]{:S(2)}, u32[]{:S(2)}) collective-permute-start(bf16[23,96,128]{2,1,0:T(8,128)(2,1)S(1)} %fold.6), channel_id=1, source_target_pairs={{5,1},{7,3},{8,12},{10,14},{21,17},{23,19},{24,28},{26,30}} | collective-permute-start | bytes 1695752 | tf_op jit(solution)/shard_map/ppermute | solution.py:521
  143.9 27.3 %collective-permute-start.17 = (bf16[23,96,128]{2,1,0:T(8,128)(2,1)S(1)}, bf16[23,96,128]{2,1,0:T(8,128)(2,1)S(1)}, u32[]{:S(2)}, u32[]{:S(2)}) collective-permute-start(bf16[23,96,128]{2,1,0:T(8,128)(2,1)S(1)} %fold.6), channel_id=1, source_target_pairs={{4,3},{6,1},{9,14},{11,12},{20,19},{22,17},{25,30},{27,28}} | collective-permute-start | bytes 1695752 | tf_op jit(solution)/shard_map/ppermute | solution.py:521
  147.4 23.9 %collective-permute-start.16 = (bf16[23,96,128]{2,1,0:T(8,128)(2,1)}, bf16[23,96,128]{2,1,0:T(8,128)(2,1)S(1)}, u32[]{:S(2)}, u32[]{:S(2)}) collective-permute-start(bf16[23,96,128]{2,1,0:T(8,128)(2,1)} %get-tuple-element.62), channel_id=1, source_target_pairs={{0,2},{2,0},{5,7},{7,5},{8,10},{10,8},{13,15},{15,13},{16,18},{18,... | collective-permute-start | bytes 1695752 | tf_op jit(solution)/shard_map/ppermute | solution.py:527
  148.3 21.6 %copy-start.20 = (bf16[23,96,128]{2,1,0:T(8,128)(2,1)S(1)}, bf16[23,96,128]{2,1,0:T(8,128)(2,1)}, u32[]{:S(2)}) copy-start(bf16[23,96,128]{2,1,0:T(8,128)(2,1)} %copy-done.19) | copy-start | bytes 1695748
  158.2 1.7 copy-start.22
  159.9 1.3 copy-start.24
  161.1 10.1 %copy-start.12 = (f32[12,128,384]{2,1,0:T(8,128)S(1)}, f32[12,128,384]{2,1,0:T(8,128)}, u32[]{:S(2)}) copy-start(f32[12,128,384]{2,1,0:T(8,128)} %copy-done.11) | copy-start | bytes 7077892
  169.9 1.4 copy-start.14

commit v14 on v13

--- a/solution.py
+++ b/solution.py
@@ -609,7 +609,7 @@
     lent_rest = to_core(lent_own, inners, [False] * 2), to_core(lent_beside, inners, [True] * 2)
     late_rest = to_core(late, everyone, [True, False, False, True])
     (lent,) = fold(half, role, lent_beside, lent_rest[1], lent_own, lent_rest[0])
-    given = give_back(lent, 0), give_back(lent, 1)
+    given = give_back(lent, 0), give_back(after(lent, first_other), 1)
     late_block = fold(half, role, late, late_rest)
     late_other = side_to_side(late_block[1], everyone, (0, 1, 0, 1))
 

time: 184 us -> 186 us (1.011)
  the two profiles are of different devices: /device:TPU:1 before, /device:TPU:16 now
where the time goes in v14:
time: 186 us; the launch traced here: 185 us
  Pallas kernels  70 us (38%)
  waiting for transfers between devices  53.7 us (29%)
  starting transfers between devices  35.7 us (19%)
  local copies, waits for them, and re-layouts  18 us (10%)
  other arithmetic  6.87 us (4%)
    ppermute x8, waiting for transfers between devices, among(): lax.ppermute(value, 'row', [(2 * s + b, 2 * t + b) for s, t in moves for...  42 us
    pallas_call x4, Pallas kernels, triangle(): pl.pallas_call(functools.partial(triangle_kernel, counts=[len(piece) for...  26 us
    pallas_call x2, Pallas kernels, finish(): pl.pallas_call(functools.partial(finish_kernel, cols=cols, sources=len(ot...  16.8 us
    unnamed x66, local copies, waits for them, and re-layouts  16.7 us
    ppermute x8, starting transfers between devices, among(): lax.ppermute(value, 'row', [(2 * s + b, 2 * t + b) for s, t in moves for...  13.6 us
    pallas_call x2, Pallas kernels, project(): pl.pallas_call(functools.partial(project_kernel, first=first), out_shape=...  12.7 us
    ppermute x3, waiting for transfers between devices, across(): return lax.ppermute(value, 'row', [(i, i ^ 1) for i in range(8)])  11.3 us
    ppermute x6, starting transfers between devices, to_core(): return lax.ppermute(value, ('row', 'col'), perm)  11.2 us
  transfers between devices with their start and end apart: 21, of which 10 were waited for; matrix products, arithmetic and copies ran while one was open for 4% of the time, Pallas kernels for 29%

profile of v14, /device:TPU:16, one launch (start us, length us, event | category | flops | bytes accessed | tf_op | source)
XLA Modules:
  0.0 185.4 jit_solution(12280554896336704569)
XLA Ops:
  0.0 1.2 slice.14
  1.9 1.6 copy-done
  3.5 0.9 copy-done.17
  4.4 6.5 %project.2 = (bf16[23,64,384]{2,1,0:T(8,128)(2,1)}, bf16[23,64,384]{2,1,0:T(8,128)(2,1)}) custom-call(s32[4]{0:T(128)S(1)} %pad_add_fusion.where_ref, bf16[2,23,184,128]{3,2,1,0:T(8,128)(2,1)S(1)} %bitcast.16, bf16[128,640]{1,0:T(8,128)(2,1)S(1)} %copy-done.17), custom_call_target="tpu_custom_call" | custom-call | flops 554696704 | bytes 4333568 | tf_op jit(solution)/shard_map/project/pallas_call | solution.py:92
  11.0 2.5 %collective-permute-start.1 = (bf16[23,64,384]{2,1,0:T(8,128)(2,1)}, bf16[23,64,384]{2,1,0:T(8,128)(2,1)}, u32[]{:S(2)}, u32[]{:S(2)}) collective-permute-start(bf16[23,64,384]{2,1,0:T(8,128)(2,1)} %get-tuple-element.40.refs_0_), channel_id=1, source_target_pairs={{4,8},{6,10},{8,4},{10,6},{5,9},{7,11},{9,5},{11,7},{20,24},{22,26... | collective-permute-start | bytes 3391496 | tf_op jit(solution)/shard_map/ppermute | solution.py:503
  13.5 1.6 collective-permute-start.2
  15.0 0.9 collective-permute-start
  15.9 6.2 %project.3 = (bf16[23,64,384]{2,1,0:T(8,128)(2,1)S(1)}, bf16[23,64,384]{2,1,0:T(8,128)(2,1)}) custom-call(s32[4]{0:T(128)S(1)} %pad_add_fusion.where_ref, bf16[2,23,184,128]{3,2,1,0:T(8,128)(2,1)S(1)} %bitcast.17, bf16[128,640]{1,0:T(8,128)(2,1)S(1)} %copy-done.17), custom_call_target="tpu_custom_call" | custom-call | flops 554696704 | bytes 4333568 | tf_op jit(solution)/shard_map/project/pallas_call | solution.py:92
  22.1 1.0 copy-done.8
  23.5 0.2 copy.11
  23.9 0.9 multiply_bitcast_fusion.refs_2_.refs_4_
  24.8 15.2 %collective-permute-done.1.refs_0_ = bf16[23,64,384]{2,1,0:T(8,128)(2,1)} collective-permute-done((bf16[23,64,384]{2,1,0:T(8,128)(2,1)}, bf16[23,64,384]{2,1,0:T(8,128)(2,1)}, u32[]{:S(2)}, u32[]{:S(2)}) %collective-permute-start.1) | collective-permute-done | bytes 1130528 | tf_op jit(solution)/shard_map/ppermute | solution.py:503
  40.0 0.2 collective-permute-done.2.refs_1_
  40.1 2.8 %broadcast_select_fusion.2 = bf16[23,64,384]{2,1,0:T(8,128)(2,1)} fusion(bf16[23,64,384]{2,1,0:T(8,128)(2,1)} %collective-permute-done.1.refs_0_, bf16[23,64,384]{2,1,0:T(8,128)(2,1)S(1)} %collective-permute-done.2.refs_1_, pred[]{:T(512)S(6)} %or.6), kind=kLoop, calls=%fused_computation.2 | loop fusion | flops 565248 | bytes 3391489 | tf_op jit(solution)/shard_map/jit(_where)/select_n | solution.py:553
  43.0 3.5 %collective-permute-start.6 = (bf16[23,64,384]{2,1,0:T(8,128)(2,1)S(1)}, bf16[23,64,384]{2,1,0:T(8,128)(2,1)}, u32[]{:S(2)}, u32[]{:S(2)}) collective-permute-start(bf16[23,64,384]{2,1,0:T(8,128)(2,1)S(1)} %collective-permute-done.2.refs_1_), channel_id=1, source_target_pairs={{4,8},{6,10},{8,4},{10,6},{5,9},{7,11},{9,5},{11,7},{20,24},{22,26... | collective-permute-start | bytes 3391496 | tf_op jit(solution)/shard_map/ppermute | solution.py:503
  46.4 1.6 collective-permute-start.3
  48.0 1.8 prepare.3
  49.8 1.4 copy-done.22
  51.3 1.0 copy-done.24
  52.3 1.8 prepare.2
  54.1 1.1 copy-done.12
  55.1 15.5 %collective-permute-done.6.refs_1_ = bf16[23,64,384]{2,1,0:T(8,128)(2,1)} collective-permute-done((bf16[23,64,384]{2,1,0:T(8,128)(2,1)S(1)}, bf16[23,64,384]{2,1,0:T(8,128)(2,1)}, u32[]{:S(2)}, u32[]{:S(2)}) %collective-permute-start.6) | collective-permute-done | bytes 1130528 | tf_op jit(solution)/shard_map/ppermute | solution.py:503
  70.6 1.4 broadcast_select_fusion.1
  72.1 3.4 %collective-permute-start.8 = (bf16[23,64,384]{2,1,0:T(8,128)(2,1)}, bf16[23,64,384]{2,1,0:T(8,128)(2,1)S(1)}, u32[]{:S(2)}, u32[]{:S(2)}) collective-permute-start(bf16[23,64,384]{2,1,0:T(8,128)(2,1)} %collective-permute-done.refs_0_.refs_4_), channel_id=1, source_target_pairs={{4,8},{6,10},{8,4},{10,6},{5,9},{7,11},{9,5},{11,7},{20,24},{22,26... | collective-permute-start | bytes 3391496 | tf_op jit(solution)/shard_map/ppermute | solution.py:503
  75.6 3.2 %left_major.1.left_ref = bf16[64,96,256]{2,1,0:T(8,128)(2,1)S(1)} custom-call(bf16[23,64,384]{2,1,0:T(8,128)(2,1)S(1)} %copy-done.9, bf16[23,64,384]{2,1,0:T(8,128)(2,1)} %collective-permute-done.3.beside_ref), custom_call_target="tpu_custom_call" | custom-call | bytes 4521984 | tf_op jit(solution)/shard_map/left_major/pallas_call | solution.py:144
  78.8 6.5 %triangle.4.refs_0_ = bf16[64,96,128]{2,1,0:T(8,128)(2,1)} custom-call(s32[2]{0:T(128)S(1)} %pad_add_fusion.1.flag_ref, bf16[64,96,256]{2,1,0:T(8,128)(2,1)S(1)} %left_major.1.left_ref, bf16[23,64,384]{2,1,0:T(8,128)(2,1)} %collective-permute-done.refs_0_.refs_4_, bf16[23,64,384]{2,1,0:T(8,128)(2,1)} %collective-permute-done.4.refs_1_.refs_2_), custom_call_target="tpu_custom_call" | custom-call | flops 402653184 | bytes 5652480 | tf_op jit(solution)/shard_map/triangle/pallas_call | solution.py:223
  85.3 2.5 %collective-permute-start.5 = (bf16[64,96,128]{2,1,0:T(8,128)(2,1)}, bf16[64,96,128]{2,1,0:T(8,128)(2,1)}, u32[]{:S(2)}, u32[]{:S(2)}) collective-permute-start(bf16[64,96,128]{2,1,0:T(8,128)(2,1)} %triangle.4.refs_0_), channel_id=1, source_target_pairs={{5,4},{7,6},{8,9},{10,11},{21,20},{23,22},{24,25},{26,27}} | collective-permute-start | bytes 4718600 | tf_op jit(solution)/shard_map/ppermute | solution.py:513
  87.8 5.4 %triangle.5.refs_0_ = bf16[64,96,128]{2,1,0:T(8,128)(2,1)S(1)} custom-call(s32[2]{0:T(128)S(1)} %pad_add_fusion.1.flag_ref, bf16[64,96,256]{2,1,0:T(8,128)(2,1)S(1)} %left_major.1.left_ref, bf16[23,64,384]{2,1,0:T(8,128)(2,1)} %get-tuple-element.40.refs_0_, bf16[23,64,384]{2,1,0:T(8,128)(2,1)S(1)} %copy-done.3), custom_call_target="tpu_custom_call" | custom-call | flops 402653184 | bytes 5652480 | tf_op jit(solution)/shard_map/triangle/pallas_call | solution.py:223
  93.2 1.3 broadcast_select_fusion
  94.5 0.3 copy-done.4
  94.8 2.7 %collective-permute-done.7.refs_0_.refs_3_ = bf16[23,64,384]{2,1,0:T(8,128)(2,1)S(1)} collective-permute-done((bf16[23,64,384]{2,1,0:T(8,128)(2,1)S(1)}, bf16[23,64,384]{2,1,0:T(8,128)(2,1)S(1)}, u32[]{:S(2)}, u32[]{:S(2)}) %collective-permute-start.7) | collective-permute-done | bytes 1130528 | tf_op jit(solution)/shard_map/ppermute | solution.py:503
  97.4 1.0 copy-done.6
  98.4 0.5 collective-permute-done.8.refs_2_
  98.9 1.0 copy-done.14
  99.9 3.3 %collective-permute-start.11 = (bf16[23,64,384]{2,1,0:T(8,128)(2,1)}, bf16[23,64,384]{2,1,0:T(8,128)(2,1)}, u32[]{:S(2)}, u32[]{:S(2)}) collective-permute-start(bf16[23,64,384]{2,1,0:T(8,128)(2,1)} %collective-permute-done.4.refs_1_.refs_2_), channel_id=1, source_target_pairs={{4,8},{6,10},{8,4},{10,6},{5,9},{7,11},{9,5},{11,7},{20,24},{22,26... | collective-permute-start | bytes 3391496 | tf_op jit(solution)/shard_map/ppermute | solution.py:503
  103.3 3.5 %fold.4 = (bf16[23,96,128]{2,1,0:T(8,128)(2,1)S(1)}, bf16[23,96,128]{2,1,0:T(8,128)(2,1)S(1)}) custom-call(s32[1]{0:T(128)} %bitcast.6.role_ref, bf16[64,96,128]{2,1,0:T(8,128)(2,1)} %triangle.4.refs_0_, bf16[64,96,128]{2,1,0:T(8,128)(2,1)} %collective-permute-done.5.refs_1_), custom_call_target="tpu_custom_call" | custom-call | bytes 4718592 | tf_op jit(solution)/shard_map/fold/pallas_call | solution.py:285
  106.9 0.8 copy-done.18
  107.7 0.7 collective-permute-start.10
  108.4 1.7 collective-permute-start.17
  110.2 5.9 %triangle.7.refs_2_ = bf16[64,96,128]{2,1,0:T(8,128)(2,1)S(1)} custom-call(s32[2]{0:T(128)S(1)} %pad_add_fusion.2.flag_ref, bf16[64,96,256]{2,1,0:T(8,128)(2,1)S(1)} %left_major.1.left_ref, bf16[23,64,384]{2,1,0:T(8,128)(2,1)} %collective-permute-done.1.refs_0_, bf16[23,64,384]{2,1,0:T(8,128)(2,1)} %collective-permute-done.6.refs_1_, ...), custom_call_target="tpu_custom_call" | custom-call | flops 402653184 | bytes 5652480 | tf_op jit(solution)/shard_map/triangle/pallas_call | solution.py:223
  116.0 1.3 collective-permute-start.18
  117.3 0.8 copy-done.20
  118.2 6.0 %collective-permute-done.9.refs_1_.refs_5_ = bf16[23,64,384]{2,1,0:T(8,128)(2,1)} collective-permute-done((bf16[23,64,384]{2,1,0:T(8,128)(2,1)}, bf16[23,64,384]{2,1,0:T(8,128)(2,1)}, u32[]{:S(2)}, u32[]{:S(2)}) %collective-permute-start.9) | collective-permute-done | bytes 1130528 | tf_op jit(solution)/shard_map/ppermute | solution.py:503
  124.2 2.2 %collective-permute-done.11.refs_3_ = bf16[23,64,384]{2,1,0:T(8,128)(2,1)} collective-permute-done((bf16[23,64,384]{2,1,0:T(8,128)(2,1)}, bf16[23,64,384]{2,1,0:T(8,128)(2,1)}, u32[]{:S(2)}, u32[]{:S(2)}) %collective-permute-start.11) | collective-permute-done | bytes 1130528 | tf_op jit(solution)/shard_map/ppermute | solution.py:503
  126.3 8.2 %triangle.6 = (bf16[64,96,128]{2,1,0:T(8,128)(2,1)S(1)}, bf16[64,48,128]{2,1,0:T(8,128)(2,1)S(1)}, bf16[64,48,128]{2,1,0:T(8,128)(2,1)S(1)}) custom-call(s32[2]{0:T(128)S(1)} %pad_add_fusion.2.flag_ref, bf16[64,96,256]{2,1,0:T(8,128)(2,1)S(1)} %left_major.1.left_ref, bf16[23,64,384]{2,1,0:T(8,128)(2,1)S(1)} %copy-done.7, ...), custom_call_target="tpu_custom_call" | custom-call | flops 805306368 | bytes 5652480 | tf_op jit(solution)/shard_map/triangle/pallas_call | solution.py:223
  134.5 1.3 collective-permute-start.12
  135.8 3.2 %collective-permute-start.13 = (bf16[64,48,128]{2,1,0:T(8,128)(2,1)S(1)}, bf16[64,48,128]{2,1,0:T(8,128)(2,1)S(1)}, u32[]{:S(2)}, u32[]{:S(2)}) collective-permute-start(bf16[64,48,128]{2,1,0:T(8,128)(2,1)S(1)} %get-tuple-element.61.refs_0_), channel_id=1, source_target_pairs={{5,4},{7,6},{8,9},{10,11},{21,20},{23,22},{24,25},{26,27}} | collective-permute-start | bytes 2359304 | tf_op jit(solution)/shard_map/ppermute | solution.py:513
  139.0 1.3 collective-permute-start.14
  140.3 1.4 fold.7
  141.7 1.1 collective-permute-start.19
  142.8 0.4 collective-permute-done.14.refs_3_
  143.2 0.7 fold.6
  144.0 2.2 %collective-permute-start.15 = (bf16[23,96,128]{2,1,0:T(8,128)(2,1)S(1)}, bf16[23,96,128]{2,1,0:T(8,128)(2,1)}, u32[]{:S(2)}, u32[]{:S(2)}) collective-permute-start(bf16[23,96,128]{2,1,0:T(8,128)(2,1)S(1)} %fold.6), channel_id=1, source_target_pairs={{5,1},{7,3},{8,12},{10,14},{21,17},{23,19},{24,28},{26,30}} | collective-permute-start | bytes 1695752 | tf_op jit(solution)/shard_map/ppermute | solution.py:521
  146.2 11.0 %collective-permute-done.19.refs_0_ = bf16[23,96,128]{2,1,0:T(8,128)(2,1)S(1)} collective-permute-done((bf16[23,96,128]{2,1,0:T(8,128)(2,1)S(1)}, bf16[23,96,128]{2,1,0:T(8,128)(2,1)S(1)}, u32[]{:S(2)}, u32[]{:S(2)}) %collective-permute-start.19) | collective-permute-done | bytes 565280 | tf_op jit(solution)/shard_map/ppermute | solution.py:506
  157.2 0.7 collective-permute-start.20
  158.0 2.1 %fold.5 = (bf16[23,96,128]{2,1,0:T(8,128)(2,1)S(1)}, bf16[23,96,128]{2,1,0:T(8,128)(2,1)}) custom-call(s32[1]{0:T(128)} %bitcast.6.role_ref, bf16[64,96,128]{2,1,0:T(8,128)(2,1)S(1)} %get-tuple-element.59.refs_0_, bf16[64,96,128]{2,1,0:T(8,128)(2,1)S(1)} %collective-permute-done.12.refs_1_), custom_call_target="tpu_custom_call" | custom-call | bytes 4718592 | tf_op jit(solution)/shard_map/fold/pallas_call | solution.py:285
  160.1 3.1 %collective-permute-start.16 = (bf16[23,96,128]{2,1,0:T(8,128)(2,1)}, bf16[23,96,128]{2,1,0:T(8,128)(2,1)S(1)}, u32[]{:S(2)}, u32[]{:S(2)}) collective-permute-start(bf16[23,96,128]{2,1,0:T(8,128)(2,1)} %get-tuple-element.63), channel_id=1, source_target_pairs={{0,2},{2,0},{5,7},{7,5},{8,10},{10,8},{13,15},{15,13},{16,18},{18,... | collective-permute-start | bytes 1695752 | tf_op jit(solution)/shard_map/ppermute | solution.py:527
  163.2 1.7 copy-done.23
  164.9 1.3 copy-done.25
  166.1 1.1 copy-done.27
  167.2 7.6 %finish.2.refs_6_ = bf16[2,23,96,128]{3,2,1,0:T(8,128)(2,1)S(1)} custom-call(s32[1]{0:T(128)} %bitcast.11.flag_ref, bf16[12,128,384]{2,1,0:T(8,128)(2,1)S(1)} %copy-done.25, f32[12,128,384]{2,1,0:T(8,128)S(1)} %copy-done.23, bf16[23,96,128]{2,1,0:T(8,128)(2,1)S(1)} %get-tuple-element.68.own_ref, bf16[23,96,128]{2,1,0:T(8,128)(2,1)S(1)} %copy-done.27, ...), custom_call_target="tpu_custom_call" | custom-call | flops 1881145344 | bytes 5652480 | tf_op jit(solution)/shard_map/finish/pallas_call | solution.py:384
  174.8 0.2 select_select_fusion.own_ref
  175.0 1.1 copy-done.13
  176.2 9.2 %finish.3 = bf16[2,23,184,128]{3,2,1,0:T(8,128)(2,1)} custom-call(s32[1]{0:T(128)} %bitcast.flag_ref, bf16[12,128,384]{2,1,0:T(8,128)(2,1)S(1)} %copy-done.13, f32[12,128,384]{2,1,0:T(8,128)S(1)} %copy-done.11, bf16[23,96,128]{2,1,0:T(8,128)(2,1)S(1)} %select_select_fusion.own_ref, bf16[23,96,128]{2,1,0:T(8,128)(2,1)S(1)} %copy-done.21, ...), custom_call_target="tpu_custom_call" | custom-call | flops 1881145344 | bytes 5652480 | tf_op jit(solution)/shard_map/finish/pallas_call | solution.py:384
  (73 shorter events, 1.2 us)
Async XLA Ops:
  1.9 1.6 copy-start
  3.5 0.9 copy-start.17
  10.9 12.2 %copy-start.30 = (bf16[128,128]{1,0:T(8,128)(2,1)S(1)}, bf16[128,128]{1,0:T(8,128)(2,1)}, u32[]{:S(2)}) copy-start(bf16[128,128]{1,0:T(8,128)(2,1)} %param.9) | copy-start | bytes 98308
  10.9 12.3 %slice-start = ((bf16[128,640]{1,0:T(8,128)(2,1)}), bf16[128,128]{1,0:T(8,128)(2,1)S(1)}, s32[]{:S(2)}) async-start(bf16[128,640]{1,0:T(8,128)(2,1)} %weight_ref.3), calls=%async_computation | async-start | bytes 65536 | tf_op jit(solution)/shard_map/slice | solution.py:566
  11.0 12.4 %copy-start.29 = (bf16[512,128]{1,0:T(8,128)(2,1)S(1)}, bf16[512,128]{1,0:T(8,128)(2,1)}, u32[]{:S(2)}) copy-start(bf16[512,128]{1,0:T(8,128)(2,1)} %param.11) | copy-start | bytes 393220
  11.0 12.5 %copy-start.28 = (bf16[128,1024]{1,0:T(8,128)(2,1)S(1)}, bf16[128,1024]{1,0:T(8,128)(2,1)}, u32[]{:S(2)}) copy-start(bf16[128,1024]{1,0:T(8,128)(2,1)} %param.10) | copy-start | bytes 786436
  11.0 29.0 %collective-permute-start.1 = (bf16[23,64,384]{2,1,0:T(8,128)(2,1)}, bf16[23,64,384]{2,1,0:T(8,128)(2,1)}, u32[]{:S(2)}, u32[]{:S(2)}) collective-permute-start(bf16[23,64,384]{2,1,0:T(8,128)(2,1)} %get-tuple-element.40.refs_0_), channel_id=1, source_target_pairs={{4,8},{6,10},{8,4},{10,6},{5,9},{7,11},{9,5},{11,7},{20,24},{22,26... | collective-permute-start | bytes 3391496 | tf_op jit(solution)/shard_map/ppermute | solution.py:503
  13.5 26.6 %collective-permute-start.2 = (bf16[23,64,384]{2,1,0:T(8,128)(2,1)}, bf16[23,64,384]{2,1,0:T(8,128)(2,1)S(1)}, u32[]{:S(2)}, u32[]{:S(2)}) collective-permute-start(bf16[23,64,384]{2,1,0:T(8,128)(2,1)} %get-tuple-element.41), channel_id=1, source_target_pairs={{0,2},{2,0},{4,6},{6,4},{8,10},{10,8},{12,14},{14,12},{1,3},{3,1},... | collective-permute-start | bytes 3391496 | tf_op jit(solution)/shard_map/ppermute | solution.py:506
  15.0 27.9 %collective-permute-start = (bf16[23,64,384]{2,1,0:T(8,128)(2,1)}, bf16[23,64,384]{2,1,0:T(8,128)(2,1)}, u32[]{:S(2)}, u32[]{:S(2)}) collective-permute-start(bf16[23,64,384]{2,1,0:T(8,128)(2,1)} %get-tuple-element.40.refs_0_), channel_id=1, source_target_pairs={{0,4},{2,6},{4,0},{6,2},{8,12},{10,14},{12,8},{14,10},{1,5},{3,7},... | collective-permute-start | bytes 3391496 | tf_op jit(solution)/shard_map/ppermute | solution.py:503
  22.1 1.0 copy-start.8
  24.8 23.2 %copy-start.1 = (bf16[46,184,128]{2,1,0:T(8,128)(2,1)S(1)}, bf16[46,184,128]{2,1,0:T(8,128)(2,1)}, u32[]{:S(2)}) copy-start(bf16[46,184,128]{2,1,0:T(8,128)(2,1)} %param.6) | copy-start | bytes 6500356
  40.1 2.8 %copy-start.2 = (bf16[23,64,384]{2,1,0:T(8,128)(2,1)}, bf16[23,64,384]{2,1,0:T(8,128)(2,1)S(1)}, u32[]{:S(2)}) copy-start(bf16[23,64,384]{2,1,0:T(8,128)(2,1)S(1)} %collective-permute-done.2.refs_1_) | copy-start | bytes 3391492
  43.0 27.6 %collective-permute-start.6 = (bf16[23,64,384]{2,1,0:T(8,128)(2,1)S(1)}, bf16[23,64,384]{2,1,0:T(8,128)(2,1)}, u32[]{:S(2)}, u32[]{:S(2)}) collective-permute-start(bf16[23,64,384]{2,1,0:T(8,128)(2,1)S(1)} %collective-permute-done.2.refs_1_), channel_id=1, source_target_pairs={{4,8},{6,10},{8,4},{10,6},{5,9},{7,11},{9,5},{11,7},{20,24},{22,26... | collective-permute-start | bytes 3391496 | tf_op jit(solution)/shard_map/ppermute | solution.py:503
  46.4 25.7 %collective-permute-start.3 = (bf16[23,64,384]{2,1,0:T(8,128)(2,1)}, bf16[23,64,384]{2,1,0:T(8,128)(2,1)}, u32[]{:S(2)}, u32[]{:S(2)}) collective-permute-start(bf16[23,64,384]{2,1,0:T(8,128)(2,1)} %get-tuple-element.47), channel_id=1, source_target_pairs={{0,2},{2,0},{4,6},{6,4},{8,10},{10,8},{12,14},{14,12},{1,3},{3,1},... | collective-permute-start | bytes 3391496 | tf_op jit(solution)/shard_map/ppermute | solution.py:506
  48.0 30.8 %collective-permute-start.4 = (bf16[23,64,384]{2,1,0:T(8,128)(2,1)}, bf16[23,64,384]{2,1,0:T(8,128)(2,1)}, u32[]{:S(2)}, u32[]{:S(2)}) collective-permute-start(bf16[23,64,384]{2,1,0:T(8,128)(2,1)} %broadcast_select_fusion.2), channel_id=1, source_target_pairs={{0,4},{2,6},{4,0},{6,2},{8,12},{10,14},{12,8},{14,10},{1,5},{3,7},... | collective-permute-start | bytes 3391496 | tf_op jit(solution)/shard_map/ppermute | solution.py:503
  49.8 1.5 copy-start.22
  51.3 1.0 copy-start.24
  52.3 18.3 %copy-start.9 = (bf16[23,64,384]{2,1,0:T(8,128)(2,1)S(1)}, bf16[23,64,384]{2,1,0:T(8,128)(2,1)}, u32[]{:S(2)}) copy-start(bf16[23,64,384]{2,1,0:T(8,128)(2,1)} %copy-done.8) | copy-start | bytes 3391492
  54.0 1.1 copy-start.12
  55.1 16.9 %copy-start.10 = (f32[12,128,384]{2,1,0:T(8,128)}, f32[12,128,384]{2,1,0:T(8,128)S(1)}, u32[]{:S(2)}) copy-start(f32[12,128,384]{2,1,0:T(8,128)S(1)} %get-tuple-element.44.gate_ref) | copy-start | bytes 7077892
  72.1 25.3 %collective-permute-start.7 = (bf16[23,64,384]{2,1,0:T(8,128)(2,1)S(1)}, bf16[23,64,384]{2,1,0:T(8,128)(2,1)S(1)}, u32[]{:S(2)}, u32[]{:S(2)}) collective-permute-start(bf16[23,64,384]{2,1,0:T(8,128)(2,1)S(1)} %broadcast_select_fusion.1), channel_id=1, source_target_pairs={{0,4},{2,6},{4,0},{6,2},{8,12},{10,14},{12,8},{14,10},{1,5},{3,7},... | collective-permute-start | bytes 3391496 | tf_op jit(solution)/shard_map/ppermute | solution.py:503
  72.1 26.8 %collective-permute-start.8 = (bf16[23,64,384]{2,1,0:T(8,128)(2,1)}, bf16[23,64,384]{2,1,0:T(8,128)(2,1)S(1)}, u32[]{:S(2)}, u32[]{:S(2)}) collective-permute-start(bf16[23,64,384]{2,1,0:T(8,128)(2,1)} %collective-permute-done.refs_0_.refs_4_), channel_id=1, source_target_pairs={{4,8},{6,10},{8,4},{10,6},{5,9},{7,11},{9,5},{11,7},{20,24},{22,26... | collective-permute-start | bytes 3391496 | tf_op jit(solution)/shard_map/ppermute | solution.py:503
  78.8 9.0 %copy-start.3 = (bf16[23,64,384]{2,1,0:T(8,128)(2,1)S(1)}, bf16[23,64,384]{2,1,0:T(8,128)(2,1)}, u32[]{:S(2)}) copy-start(bf16[23,64,384]{2,1,0:T(8,128)(2,1)} %copy-done.2) | copy-start | bytes 3391492
  85.3 18.0 %collective-permute-start.5 = (bf16[64,96,128]{2,1,0:T(8,128)(2,1)}, bf16[64,96,128]{2,1,0:T(8,128)(2,1)}, u32[]{:S(2)}, u32[]{:S(2)}) collective-permute-start(bf16[64,96,128]{2,1,0:T(8,128)(2,1)} %triangle.4.refs_0_), channel_id=1, source_target_pairs={{5,4},{7,6},{8,9},{10,11},{21,20},{23,22},{24,25},{26,27}} | collective-permute-start | bytes 4718600 | tf_op jit(solution)/shard_map/ppermute | solution.py:513
  93.2 1.5 copy-start.4
  97.4 1.0 copy-start.6
  98.9 1.0 copy-start.14
  99.9 24.3 %collective-permute-start.9 = (bf16[23,64,384]{2,1,0:T(8,128)(2,1)}, bf16[23,64,384]{2,1,0:T(8,128)(2,1)}, u32[]{:S(2)}, u32[]{:S(2)}) collective-permute-start(bf16[23,64,384]{2,1,0:T(8,128)(2,1)} %broadcast_select_fusion), channel_id=1, source_target_pairs={{0,4},{2,6},{4,0},{6,2},{8,12},{10,14},{12,8},{14,10},{1,5},{3,7},... | collective-permute-start | bytes 3391496 | tf_op jit(solution)/shard_map/ppermute | solution.py:503
  99.9 26.4 %collective-permute-start.11 = (bf16[23,64,384]{2,1,0:T(8,128)(2,1)}, bf16[23,64,384]{2,1,0:T(8,128)(2,1)}, u32[]{:S(2)}, u32[]{:S(2)}) collective-permute-start(bf16[23,64,384]{2,1,0:T(8,128)(2,1)} %collective-permute-done.4.refs_1_.refs_2_), channel_id=1, source_target_pairs={{4,8},{6,10},{8,4},{10,6},{5,9},{7,11},{9,5},{11,7},{20,24},{22,26... | collective-permute-start | bytes 3391496 | tf_op jit(solution)/shard_map/ppermute | solution.py:503
  103.3 5.2 %copy-start.5 = (bf16[64,96,128]{2,1,0:T(8,128)(2,1)S(1)}, bf16[64,96,128]{2,1,0:T(8,128)(2,1)}, u32[]{:S(2)}) copy-start(bf16[64,96,128]{2,1,0:T(8,128)(2,1)} %copy-done.4) | copy-start | bytes 4718596
  103.3 6.8 %copy-start.7 = (bf16[23,64,384]{2,1,0:T(8,128)(2,1)S(1)}, bf16[23,64,384]{2,1,0:T(8,128)(2,1)}, u32[]{:S(2)}) copy-start(bf16[23,64,384]{2,1,0:T(8,128)(2,1)} %copy-done.6) | copy-start | bytes 3391492
  106.9 0.8 copy-start.18
  107.7 9.7 %collective-permute-start.10 = (bf16[23,96,128]{2,1,0:T(8,128)(2,1)S(1)}, bf16[23,96,128]{2,1,0:T(8,128)(2,1)S(1)}, u32[]{:S(2)}, u32[]{:S(2)}) collective-permute-start(bf16[23,96,128]{2,1,0:T(8,128)(2,1)S(1)} %get-tuple-element.56), channel_id=1, source_target_pairs={{4,6},{6,4},{9,11},{11,9},{20,22},{22,20},{25,27},{27,25}} | collective-permute-start | bytes 1695752 | tf_op jit(solution)/shard_map/ppermute | solution.py:527
  108.4 17.9 %copy-start.15 = (bf16[23,64,384]{2,1,0:T(8,128)(2,1)S(1)}, bf16[23,64,384]{2,1,0:T(8,128)(2,1)}, u32[]{:S(2)}) copy-start(bf16[23,64,384]{2,1,0:T(8,128)(2,1)} %copy-done.14) | copy-start | bytes 3391492
  108.4 31.9 %collective-permute-start.17 = (bf16[64,96,128]{2,1,0:T(8,128)(2,1)S(1)}, bf16[64,96,128]{2,1,0:T(8,128)(2,1)S(1)}, u32[]{:S(2)}, u32[]{:S(2)}) collective-permute-start(bf16[64,96,128]{2,1,0:T(8,128)(2,1)S(1)} %copy-done.5), channel_id=1, source_target_pairs={{1,0},{3,2},{5,4},{7,6},{8,9},{10,11},{12,13},{14,15},{17,16},{19,... | collective-permute-start | bytes 4718600 | tf_op jit(solution)/shard_map/ppermute | solution.py:513
  116.0 24.3 %collective-permute-start.18 = (bf16[64,96,128]{2,1,0:T(8,128)(2,1)S(1)}, bf16[64,96,128]{2,1,0:T(8,128)(2,1)S(1)}, u32[]{:S(2)}, u32[]{:S(2)}) collective-permute-start(bf16[64,96,128]{2,1,0:T(8,128)(2,1)S(1)} %triangle.7.refs_2_), channel_id=1, source_target_pairs={{0,1},{2,3},{4,5},{6,7},{9,8},{11,10},{13,12},{15,14},{16,17},{18,... | collective-permute-start | bytes 4718600 | tf_op jit(solution)/shard_map/ppermute | solution.py:513
  117.3 0.8 copy-start.20
  134.5 23.4 %collective-permute-start.12 = (bf16[64,96,128]{2,1,0:T(8,128)(2,1)S(1)}, bf16[64,96,128]{2,1,0:T(8,128)(2,1)S(1)}, u32[]{:S(2)}, u32[]{:S(2)}) collective-permute-start(bf16[64,96,128]{2,1,0:T(8,128)(2,1)S(1)} %get-tuple-element.59.refs_0_), channel_id=1, source_target_pairs={{1,0},{3,2},{4,5},{6,7},{9,8},{11,10},{12,13},{14,15},{17,16},{19,... | collective-permute-start | bytes 4718600 | tf_op jit(solution)/shard_map/ppermute | solution.py:513
  135.8 6.9 %collective-permute-start.13 = (bf16[64,48,128]{2,1,0:T(8,128)(2,1)S(1)}, bf16[64,48,128]{2,1,0:T(8,128)(2,1)S(1)}, u32[]{:S(2)}, u32[]{:S(2)}) collective-permute-start(bf16[64,48,128]{2,1,0:T(8,128)(2,1)S(1)} %get-tuple-element.61.refs_0_), channel_id=1, source_target_pairs={{5,4},{7,6},{8,9},{10,11},{21,20},{23,22},{24,25},{26,27}} | collective-permute-start | bytes 2359304 | tf_op jit(solution)/shard_map/ppermute | solution.py:513
  139.0 4.2 %collective-permute-start.14 = (bf16[64,48,128]{2,1,0:T(8,128)(2,1)S(1)}, bf16[64,48,128]{2,1,0:T(8,128)(2,1)S(1)}, u32[]{:S(2)}, u32[]{:S(2)}) collective-permute-start(bf16[64,48,128]{2,1,0:T(8,128)(2,1)S(1)} %get-tuple-element.62.refs_2_), channel_id=1, source_target_pairs={{4,5},{6,7},{9,8},{11,10},{20,21},{22,23},{25,24},{27,26}} | collective-permute-start | bytes 2359304 | tf_op jit(solution)/shard_map/ppermute | solution.py:513
  141.7 15.5 %collective-permute-start.19 = (bf16[23,96,128]{2,1,0:T(8,128)(2,1)S(1)}, bf16[23,96,128]{2,1,0:T(8,128)(2,1)S(1)}, u32[]{:S(2)}, u32[]{:S(2)}) collective-permute-start(bf16[23,96,128]{2,1,0:T(8,128)(2,1)S(1)} %get-tuple-element.65), channel_id=1, source_target_pairs={{0,2},{2,0},{4,6},{6,4},{8,10},{10,8},{12,14},{14,12},{1,3},{3,1},... | collective-permute-start | bytes 1695752 | tf_op jit(solution)/shard_map/ppermute | solution.py:506
  144.0 19.2 %copy-start.16 = (bf16[1024,128]{1,0:T(8,128)(2,1)S(1)}, bf16[1024,128]{1,0:T(8,128)(2,1)}, u32[]{:S(2)}) copy-start(bf16[1024,128]{1,0:T(8,128)(2,1)} %multiply_bitcast_fusion.refs_2_.refs_4_) | copy-start | bytes 786436
  144.0 30.8 %collective-permute-start.15 = (bf16[23,96,128]{2,1,0:T(8,128)(2,1)S(1)}, bf16[23,96,128]{2,1,0:T(8,128)(2,1)}, u32[]{:S(2)}, u32[]{:S(2)}) collective-permute-start(bf16[23,96,128]{2,1,0:T(8,128)(2,1)S(1)} %fold.6), channel_id=1, source_target_pairs={{5,1},{7,3},{8,12},{10,14},{21,17},{23,19},{24,28},{26,30}} | collective-permute-start | bytes 1695752 | tf_op jit(solution)/shard_map/ppermute | solution.py:521
  157.2 2.8 %copy-start.26 = (bf16[23,96,128]{2,1,0:T(8,128)(2,1)}, bf16[23,96,128]{2,1,0:T(8,128)(2,1)S(1)}, u32[]{:S(2)}) copy-start(bf16[23,96,128]{2,1,0:T(8,128)(2,1)S(1)} %collective-permute-done.19.refs_0_) | copy-start | bytes 1695748
  157.2 17.7 %collective-permute-start.20 = (bf16[23,96,128]{2,1,0:T(8,128)(2,1)S(1)}, bf16[23,96,128]{2,1,0:T(8,128)(2,1)S(1)}, u32[]{:S(2)}, u32[]{:S(2)}) collective-permute-start(bf16[23,96,128]{2,1,0:T(8,128)(2,1)S(1)} %fold.6), channel_id=1, source_target_pairs={{4,3},{6,1},{9,14},{11,12},{20,19},{22,17},{25,30},{27,28}} | collective-permute-start | bytes 1695752 | tf_op jit(solution)/shard_map/ppermute | solution.py:521
  160.1 14.9 %collective-permute-start.16 = (bf16[23,96,128]{2,1,0:T(8,128)(2,1)}, bf16[23,96,128]{2,1,0:T(8,128)(2,1)S(1)}, u32[]{:S(2)}, u32[]{:S(2)}) collective-permute-start(bf16[23,96,128]{2,1,0:T(8,128)(2,1)} %get-tuple-element.63), channel_id=1, source_target_pairs={{0,2},{2,0},{5,7},{7,5},{8,10},{10,8},{13,15},{15,13},{16,18},{18,... | collective-permute-start | bytes 1695752 | tf_op jit(solution)/shard_map/ppermute | solution.py:527
  163.2 1.7 copy-start.23
  164.9 1.3 copy-start.25
  166.1 1.1 copy-start.27
  167.2 7.6 %copy-start.19 = (bf16[23,96,128]{2,1,0:T(8,128)(2,1)S(1)}, bf16[23,96,128]{2,1,0:T(8,128)(2,1)}, u32[]{:S(2)}) copy-start(bf16[23,96,128]{2,1,0:T(8,128)(2,1)} %copy-done.18) | copy-start | bytes 1695748
  167.2 7.8 %copy-start.11 = (f32[12,128,384]{2,1,0:T(8,128)S(1)}, f32[12,128,384]{2,1,0:T(8,128)}, u32[]{:S(2)}) copy-start(f32[12,128,384]{2,1,0:T(8,128)} %copy-done.10) | copy-start | bytes 7077892
  174.8 1.3 copy-start.13
  174.8 1.4 copy-start.21

commit v15 on v12

--- a/solution.py
+++ b/solution.py
@@ -371,7 +371,7 @@
                 out_ref[h, r] = jnp.concatenate(parts, axis=0).astype(BF16)
         return carry
 
-    lax.fori_loop(0, steps, step, 0, unroll=4)
+    lax.fori_loop(0, steps, step, 0, unroll=6)
 
 
 def finish(flag, cols, prepared, own, other, weights, earlier=None):

time: 184 us -> 182 us (0.989)
  transfers between devices with their start and end apart: 21 -> 21, of which waited for: 5 -> 5; matrix products, arithmetic and copies ran while one was open for 4% -> 4% of each run, Pallas kernels for 32% -> 31%
where the time goes in v15:
time: 182 us; the launch traced here: 181 us
  Pallas kernels  72.8 us (40%)
  starting transfers between devices  45.6 us (25%)
  waiting for transfers between devices  36.8 us (20%)
  local copies, waits for them, and re-layouts  16.3 us (9%)
  other arithmetic  8.2 us (5%)
    ppermute x3, waiting for transfers between devices, across(): return lax.ppermute(value, 'row', [(i, i ^ 1) for i in range(8)])  34.2 us
    pallas_call x4, Pallas kernels, triangle(): pl.pallas_call(functools.partial(triangle_kernel, counts=[len(piece) for...  26.1 us
    ppermute x8, starting transfers between devices, among(): lax.ppermute(value, 'row', [(2 * s + b, 2 * t + b) for s, t in moves for...  20.5 us
    pallas_call x2, Pallas kernels, finish(): pl.pallas_call(functools.partial(finish_kernel, cols=cols), out_shape=jax...  17.9 us
    ppermute x6, starting transfers between devices, to_core(): return lax.ppermute(value, ('row', 'col'), perm)  15.9 us
    unnamed x60, local copies, waits for them, and re-layouts  14.9 us
    pallas_call x2, Pallas kernels, project(): pl.pallas_call(functools.partial(project_kernel, first=first), out_shape=...  12.8 us
    pallas_call x4, Pallas kernels, fold(): pl.pallas_call(functools.partial(fold_kernel, outputs=outputs, half=half)...  9.23 us
  transfers between devices with their start and end apart: 21, of which 5 were waited for; matrix products, arithmetic and copies ran while one was open for 4% of the time, Pallas kernels for 31%

profile of v15, /device:TPU:1, one launch (start us, length us, event | category | flops | bytes accessed | tf_op | source)
XLA Modules:
  0.0 180.8 jit_solution(5347277611774231607)
XLA Ops:
  0.0 1.2 slice.14
  1.9 1.6 copy-done
  3.5 0.9 copy-done.18
  4.4 6.7 %project.2 = (bf16[23,64,384]{2,1,0:T(8,128)(2,1)}, bf16[23,64,384]{2,1,0:T(8,128)(2,1)}) custom-call(s32[4]{0:T(128)S(1)} %pad_add_fusion.where_ref, bf16[2,23,184,128]{3,2,1,0:T(8,128)(2,1)S(1)} %bitcast.16, bf16[128,640]{1,0:T(8,128)(2,1)S(1)} %copy-done.18), custom_call_target="tpu_custom_call" | custom-call | flops 554696704 | bytes 4333568 | tf_op jit(solution)/shard_map/project/pallas_call | solution.py:92
  11.1 1.9 %collective-permute-start.1 = (bf16[23,64,384]{2,1,0:T(8,128)(2,1)}, bf16[23,64,384]{2,1,0:T(8,128)(2,1)}, u32[]{:S(2)}, u32[]{:S(2)}) collective-permute-start(bf16[23,64,384]{2,1,0:T(8,128)(2,1)} %get-tuple-element.39.refs_0_), channel_id=1, source_target_pairs={{4,8},{6,10},{8,4},{10,6},{5,9},{7,11},{9,5},{11,7},{20,24},{22,26... | collective-permute-start | bytes 3391496 | tf_op jit(solution)/shard_map/ppermute | solution.py:501
  13.0 2.0 %collective-permute-start.2 = (bf16[23,64,384]{2,1,0:T(8,128)(2,1)}, bf16[23,64,384]{2,1,0:T(8,128)(2,1)S(1)}, u32[]{:S(2)}, u32[]{:S(2)}) collective-permute-start(bf16[23,64,384]{2,1,0:T(8,128)(2,1)} %get-tuple-element.40), channel_id=1, source_target_pairs={{0,2},{2,0},{4,6},{6,4},{8,10},{10,8},{12,14},{14,12},{1,3},{3,1},... | collective-permute-start | bytes 3391496 | tf_op jit(solution)/shard_map/ppermute | solution.py:504
  15.0 2.8 %collective-permute-start = (bf16[23,64,384]{2,1,0:T(8,128)(2,1)}, bf16[23,64,384]{2,1,0:T(8,128)(2,1)}, u32[]{:S(2)}, u32[]{:S(2)}) collective-permute-start(bf16[23,64,384]{2,1,0:T(8,128)(2,1)} %get-tuple-element.39.refs_0_), channel_id=1, source_target_pairs={{0,4},{2,6},{4,0},{6,2},{8,12},{10,14},{12,8},{14,10},{1,5},{3,7},... | collective-permute-start | bytes 3391496 | tf_op jit(solution)/shard_map/ppermute | solution.py:501
  17.9 6.2 %project.3 = (bf16[23,64,384]{2,1,0:T(8,128)(2,1)S(1)}, bf16[23,64,384]{2,1,0:T(8,128)(2,1)}) custom-call(s32[4]{0:T(128)S(1)} %pad_add_fusion.where_ref, bf16[2,23,184,128]{3,2,1,0:T(8,128)(2,1)S(1)} %bitcast.17, bf16[128,640]{1,0:T(8,128)(2,1)S(1)} %copy-done.18), custom_call_target="tpu_custom_call" | custom-call | flops 554696704 | bytes 4333568 | tf_op jit(solution)/shard_map/project/pallas_call | solution.py:92
  24.1 1.0 copy-done.9
  25.2 0.1 copy.13
  25.3 0.1 copy.12
  25.4 0.2 copy.11
  25.8 0.9 multiply_bitcast_fusion.refs_1_
  26.7 13.3 %collective-permute-done.2.refs_1_ = bf16[23,64,384]{2,1,0:T(8,128)(2,1)S(1)} collective-permute-done((bf16[23,64,384]{2,1,0:T(8,128)(2,1)}, bf16[23,64,384]{2,1,0:T(8,128)(2,1)S(1)}, u32[]{:S(2)}, u32[]{:S(2)}) %collective-permute-start.2) | collective-permute-done | bytes 1130528 | tf_op jit(solution)/shard_map/ppermute | solution.py:504
  40.0 1.3 broadcast_select_fusion.2
  41.3 0.9 collective-permute-done.refs_0_.refs_4_
  42.2 1.7 collective-permute-start.6
  43.9 0.3 collective-permute-start.3
  44.2 4.5 %collective-permute-start.4 = (bf16[23,64,384]{2,1,0:T(8,128)(2,1)}, bf16[23,64,384]{2,1,0:T(8,128)(2,1)}, u32[]{:S(2)}, u32[]{:S(2)}) collective-permute-start(bf16[23,64,384]{2,1,0:T(8,128)(2,1)} %broadcast_select_fusion.2), channel_id=1, source_target_pairs={{0,4},{2,6},{4,0},{6,2},{8,12},{10,14},{12,8},{14,10},{1,5},{3,7},... | collective-permute-start | bytes 3391496 | tf_op jit(solution)/shard_map/ppermute | solution.py:501
  48.7 1.8 prepare.3
  50.5 1.5 copy-done.21
  52.0 1.0 copy-done.23
  53.0 1.8 prepare.2
  54.8 1.1 copy-done.13
  55.9 0.1 broadcast_select_fusion.1
  56.0 1.2 copy-done.11
  57.3 11.5 %collective-permute-done.3.beside_ref = bf16[23,64,384]{2,1,0:T(8,128)(2,1)} collective-permute-done((bf16[23,64,384]{2,1,0:T(8,128)(2,1)}, bf16[23,64,384]{2,1,0:T(8,128)(2,1)}, u32[]{:S(2)}, u32[]{:S(2)}) %collective-permute-start.3) | collective-permute-done | bytes 1130528 | tf_op jit(solution)/shard_map/ppermute | solution.py:504
  68.7 4.7 %collective-permute-start.7 = (bf16[23,64,384]{2,1,0:T(8,128)(2,1)S(1)}, bf16[23,64,384]{2,1,0:T(8,128)(2,1)S(1)}, u32[]{:S(2)}, u32[]{:S(2)}) collective-permute-start(bf16[23,64,384]{2,1,0:T(8,128)(2,1)S(1)} %broadcast_select_fusion.1), channel_id=1, source_target_pairs={{0,4},{2,6},{4,0},{6,2},{8,12},{10,14},{12,8},{14,10},{1,5},{3,7},... | collective-permute-start | bytes 3391496 | tf_op jit(solution)/shard_map/ppermute | solution.py:501
  73.4 0.7 collective-permute-start.8
  74.2 3.2 %left_major.1.left_ref = bf16[64,96,256]{2,1,0:T(8,128)(2,1)S(1)} custom-call(bf16[23,64,384]{2,1,0:T(8,128)(2,1)S(1)} %copy-done.10, bf16[23,64,384]{2,1,0:T(8,128)(2,1)} %collective-permute-done.3.beside_ref), custom_call_target="tpu_custom_call" | custom-call | bytes 4521984 | tf_op jit(solution)/shard_map/left_major/pallas_call | solution.py:144
  77.4 6.5 %triangle.4.refs_0_ = bf16[64,96,128]{2,1,0:T(8,128)(2,1)} custom-call(s32[2]{0:T(128)S(1)} %pad_add_fusion.1.flag_ref, bf16[64,96,256]{2,1,0:T(8,128)(2,1)S(1)} %left_major.1.left_ref, bf16[23,64,384]{2,1,0:T(8,128)(2,1)} %collective-permute-done.refs_0_.refs_4_, bf16[23,64,384]{2,1,0:T(8,128)(2,1)} %collective-permute-done.4.refs_1_.refs_2_), custom_call_target="tpu_custom_call" | custom-call | flops 402653184 | bytes 5652480 | tf_op jit(solution)/shard_map/triangle/pallas_call | solution.py:223
  83.9 1.9 %collective-permute-start.5 = (bf16[64,96,128]{2,1,0:T(8,128)(2,1)}, bf16[64,96,128]{2,1,0:T(8,128)(2,1)}, u32[]{:S(2)}, u32[]{:S(2)}) collective-permute-start(bf16[64,96,128]{2,1,0:T(8,128)(2,1)} %triangle.4.refs_0_), channel_id=1, source_target_pairs={{5,4},{7,6},{8,9},{10,11},{21,20},{23,22},{24,25},{26,27}} | collective-permute-start | bytes 4718600 | tf_op jit(solution)/shard_map/ppermute | solution.py:511
  85.8 5.4 %triangle.5.refs_0_ = bf16[64,96,128]{2,1,0:T(8,128)(2,1)S(1)} custom-call(s32[2]{0:T(128)S(1)} %pad_add_fusion.1.flag_ref, bf16[64,96,256]{2,1,0:T(8,128)(2,1)S(1)} %left_major.1.left_ref, bf16[23,64,384]{2,1,0:T(8,128)(2,1)} %get-tuple-element.39.refs_0_, bf16[23,64,384]{2,1,0:T(8,128)(2,1)S(1)} %copy-done.3), custom_call_target="tpu_custom_call" | custom-call | flops 402653184 | bytes 5652480 | tf_op jit(solution)/shard_map/triangle/pallas_call | solution.py:223
  91.3 3.0 %broadcast_select_fusion = bf16[23,64,384]{2,1,0:T(8,128)(2,1)} fusion(bf16[23,64,384]{2,1,0:T(8,128)(2,1)S(1)} %copy-done.3, bf16[23,64,384]{2,1,0:T(8,128)(2,1)} %collective-permute-done.3.beside_ref, pred[]{:T(512)S(6)} %or.7), kind=kLoop, calls=%fused_computation | loop fusion | flops 565248 | bytes 3391489 | tf_op jit(solution)/shard_map/jit(_where)/select_n | solution.py:551
  94.3 1.7 collective-permute-done.7.refs_0_.refs_3_
  96.0 1.0 copy-done.6
  97.0 1.0 copy-done.15
  98.0 2.5 %collective-permute-start.9 = (bf16[23,64,384]{2,1,0:T(8,128)(2,1)}, bf16[23,64,384]{2,1,0:T(8,128)(2,1)}, u32[]{:S(2)}, u32[]{:S(2)}) collective-permute-start(bf16[23,64,384]{2,1,0:T(8,128)(2,1)} %broadcast_select_fusion), channel_id=1, source_target_pairs={{0,4},{2,6},{4,0},{6,2},{8,12},{10,14},{12,8},{14,10},{1,5},{3,7},... | collective-permute-start | bytes 3391496 | tf_op jit(solution)/shard_map/ppermute | solution.py:501
  100.5 1.7 collective-permute-start.11
  102.2 4.2 %fold.4 = (bf16[23,96,128]{2,1,0:T(8,128)(2,1)S(1)}, bf16[23,96,128]{2,1,0:T(8,128)(2,1)}) custom-call(s32[1]{0:T(128)} %bitcast.6.role_ref, bf16[64,96,128]{2,1,0:T(8,128)(2,1)} %triangle.4.refs_0_, bf16[64,96,128]{2,1,0:T(8,128)(2,1)} %collective-permute-done.5.refs_1_), custom_call_target="tpu_custom_call" | custom-call | bytes 4718592 | tf_op jit(solution)/shard_map/fold/pallas_call | solution.py:285
  106.4 0.8 copy-done.19
  107.2 1.5 collective-permute-start.10
  108.7 5.8 %collective-permute-start.18 = (bf16[64,96,128]{2,1,0:T(8,128)(2,1)}, bf16[64,96,128]{2,1,0:T(8,128)(2,1)S(1)}, u32[]{:S(2)}, u32[]{:S(2)}) collective-permute-start(bf16[64,96,128]{2,1,0:T(8,128)(2,1)} %copy-done.4), channel_id=1, source_target_pairs={{1,0},{3,2},{5,4},{7,6},{8,9},{10,11},{12,13},{14,15},{17,16},{19,... | collective-permute-start | bytes 4718600 | tf_op jit(solution)/shard_map/ppermute | solution.py:511
  114.5 1.2 copy-done.7
  115.8 6.0 %triangle.7.refs_2_ = bf16[64,96,128]{2,1,0:T(8,128)(2,1)S(1)} custom-call(s32[2]{0:T(128)S(1)} %pad_add_fusion.2.flag_ref, bf16[64,96,256]{2,1,0:T(8,128)(2,1)S(1)} %left_major.1.left_ref, bf16[23,64,384]{2,1,0:T(8,128)(2,1)} %collective-permute-done.1.refs_0_, bf16[23,64,384]{2,1,0:T(8,128)(2,1)} %collective-permute-done.6.refs_1_, ...), custom_call_target="tpu_custom_call" | custom-call | flops 402653184 | bytes 5652480 | tf_op jit(solution)/shard_map/triangle/pallas_call | solution.py:223
  121.8 1.4 collective-permute-start.19
  123.3 8.1 %triangle.6 = (bf16[64,96,128]{2,1,0:T(8,128)(2,1)S(1)}, bf16[64,48,128]{2,1,0:T(8,128)(2,1)S(1)}, bf16[64,48,128]{2,1,0:T(8,128)(2,1)S(1)}) custom-call(s32[2]{0:T(128)S(1)} %pad_add_fusion.2.flag_ref, bf16[64,96,256]{2,1,0:T(8,128)(2,1)S(1)} %left_major.1.left_ref, bf16[23,64,384]{2,1,0:T(8,128)(2,1)S(1)} %copy-done.8, ...), custom_call_target="tpu_custom_call" | custom-call | flops 805306368 | bytes 5652480 | tf_op jit(solution)/shard_map/triangle/pallas_call | solution.py:223
  131.5 5.4 %collective-permute-start.12 = (bf16[64,96,128]{2,1,0:T(8,128)(2,1)S(1)}, bf16[64,96,128]{2,1,0:T(8,128)(2,1)S(1)}, u32[]{:S(2)}, u32[]{:S(2)}) collective-permute-start(bf16[64,96,128]{2,1,0:T(8,128)(2,1)S(1)} %get-tuple-element.58.refs_0_), channel_id=1, source_target_pairs={{1,0},{3,2},{4,5},{6,7},{9,8},{11,10},{12,13},{14,15},{17,16},{19,... | collective-permute-start | bytes 4718600 | tf_op jit(solution)/shard_map/ppermute | solution.py:511
  136.9 0.7 collective-permute-start.13
  137.6 0.7 collective-permute-start.14
  138.4 2.2 %fold.7 = (bf16[23,96,128]{2,1,0:T(8,128)(2,1)S(1)}, bf16[23,96,128]{2,1,0:T(8,128)(2,1)}) custom-call(s32[1]{0:T(128)} %bitcast.6.role_ref, bf16[64,96,128]{2,1,0:T(8,128)(2,1)S(1)} %copy-done.5, bf16[64,96,128]{2,1,0:T(8,128)(2,1)S(1)} %collective-permute-done.18.refs_1_, bf16[64,96,128]{2,1,0:T(8,128)(2,1)S(1)} %triangle.7.refs_2_, ...), custom_call_target="tpu_custom_call" | custom-call | bytes 4718592 | tf_op jit(solution)/shard_map/fold/pallas_call | solution.py:285
  140.5 1.2 collective-permute-start.20
  141.8 0.7 fold.6
  142.5 1.4 collective-permute-start.15
  144.0 1.3 collective-permute-start.17
  145.3 2.1 %fold.5 = (bf16[23,96,128]{2,1,0:T(8,128)(2,1)S(1)}, bf16[23,96,128]{2,1,0:T(8,128)(2,1)}) custom-call(s32[1]{0:T(128)} %bitcast.6.role_ref, bf16[64,96,128]{2,1,0:T(8,128)(2,1)S(1)} %get-tuple-element.58.refs_0_, bf16[64,96,128]{2,1,0:T(8,128)(2,1)S(1)} %collective-permute-done.12.refs_1_), custom_call_target="tpu_custom_call" | custom-call | bytes 4718592 | tf_op jit(solution)/shard_map/fold/pallas_call | solution.py:285
  147.4 1.5 collective-permute-start.16
  148.8 9.4 %collective-permute-done.20.other_ref = bf16[23,96,128]{2,1,0:T(8,128)(2,1)} collective-permute-done((bf16[23,96,128]{2,1,0:T(8,128)(2,1)}, bf16[23,96,128]{2,1,0:T(8,128)(2,1)}, u32[]{:S(2)}, u32[]{:S(2)}) %collective-permute-start.20) | collective-permute-done | bytes 565280 | tf_op jit(solution)/shard_map/ppermute | solution.py:504
  158.3 1.7 copy-done.22
  160.0 8.6 %finish.2.refs_3_ = bf16[2,23,96,128]{3,2,1,0:T(8,128)(2,1)S(1)} custom-call(s32[1]{0:T(128)} %bitcast.11.flag_ref, bf16[12,128,384]{2,1,0:T(8,128)(2,1)S(1)} %copy-done.24, f32[12,128,384]{2,1,0:T(8,128)S(1)} %copy-done.22, bf16[23,96,128]{2,1,0:T(8,128)(2,1)S(1)} %get-tuple-element.65.own_ref, bf16[23,96,128]{2,1,0:T(8,128)(2,1)} %collective-permute-done.20.other_ref, ...), custom_call_target="tpu_custom_call" | custom-call | flops 1881145344 | bytes 5652480 | tf_op jit(solution)/shard_map/finish/pallas_call | solution.py:382
  168.6 1.4 select_select_fusion.1.own_ref
  170.0 1.2 select_select_fusion.other_ref
  171.3 0.3 copy-done.14
  171.6 9.2 %finish.3 = bf16[2,23,184,128]{3,2,1,0:T(8,128)(2,1)} custom-call(s32[1]{0:T(128)} %bitcast.flag_ref, bf16[12,128,384]{2,1,0:T(8,128)(2,1)S(1)} %copy-done.14, f32[12,128,384]{2,1,0:T(8,128)S(1)} %copy-done.12, bf16[23,96,128]{2,1,0:T(8,128)(2,1)S(1)} %select_select_fusion.1.own_ref, bf16[23,96,128]{2,1,0:T(8,128)(2,1)S(1)} %select_select_fusion.other_ref, ...), custom_call_target="tpu_custom_call" | custom-call | flops 1881145344 | bytes 5652480 | tf_op jit(solution)/shard_map/finish/pallas_call | solution.py:382
  (68 shorter events, 0.7 us)
Async XLA Ops:
  1.9 1.6 copy-start
  3.5 0.9 copy-start.18
  11.1 14.0 %copy-start.27 = (bf16[128,128]{1,0:T(8,128)(2,1)S(1)}, bf16[128,128]{1,0:T(8,128)(2,1)}, u32[]{:S(2)}) copy-start(bf16[128,128]{1,0:T(8,128)(2,1)} %param.9) | copy-start | bytes 98308
  11.1 14.1 %slice-start = ((bf16[128,640]{1,0:T(8,128)(2,1)}), bf16[128,128]{1,0:T(8,128)(2,1)S(1)}, s32[]{:S(2)}) async-start(bf16[128,640]{1,0:T(8,128)(2,1)} %weight_ref.3), calls=%async_computation | async-start | bytes 65536 | tf_op jit(solution)/shard_map/slice | solution.py:564
  11.1 14.2 %copy-start.26 = (bf16[512,128]{1,0:T(8,128)(2,1)S(1)}, bf16[512,128]{1,0:T(8,128)(2,1)}, u32[]{:S(2)}) copy-start(bf16[512,128]{1,0:T(8,128)(2,1)} %param.11) | copy-start | bytes 393220
  11.1 14.3 %copy-start.25 = (bf16[128,1024]{1,0:T(8,128)(2,1)S(1)}, bf16[128,1024]{1,0:T(8,128)(2,1)}, u32[]{:S(2)}) copy-start(bf16[128,1024]{1,0:T(8,128)(2,1)} %param.10) | copy-start | bytes 786436
  11.1 15.6 %collective-permute-start.1 = (bf16[23,64,384]{2,1,0:T(8,128)(2,1)}, bf16[23,64,384]{2,1,0:T(8,128)(2,1)}, u32[]{:S(2)}, u32[]{:S(2)}) collective-permute-start(bf16[23,64,384]{2,1,0:T(8,128)(2,1)} %get-tuple-element.39.refs_0_), channel_id=1, source_target_pairs={{4,8},{6,10},{8,4},{10,6},{5,9},{7,11},{9,5},{11,7},{20,24},{22,26... | collective-permute-start | bytes 3391496 | tf_op jit(solution)/shard_map/ppermute | solution.py:501
  13.0 27.0 %collective-permute-start.2 = (bf16[23,64,384]{2,1,0:T(8,128)(2,1)}, bf16[23,64,384]{2,1,0:T(8,128)(2,1)S(1)}, u32[]{:S(2)}, u32[]{:S(2)}) collective-permute-start(bf16[23,64,384]{2,1,0:T(8,128)(2,1)} %get-tuple-element.40), channel_id=1, source_target_pairs={{0,2},{2,0},{4,6},{6,4},{8,10},{10,8},{12,14},{14,12},{1,3},{3,1},... | collective-permute-start | bytes 3391496 | tf_op jit(solution)/shard_map/ppermute | solution.py:504
  15.0 27.1 %collective-permute-start = (bf16[23,64,384]{2,1,0:T(8,128)(2,1)}, bf16[23,64,384]{2,1,0:T(8,128)(2,1)}, u32[]{:S(2)}, u32[]{:S(2)}) collective-permute-start(bf16[23,64,384]{2,1,0:T(8,128)(2,1)} %get-tuple-element.39.refs_0_), channel_id=1, source_target_pairs={{0,4},{2,6},{4,0},{6,2},{8,12},{10,14},{12,8},{14,10},{1,5},{3,7},... | collective-permute-start | bytes 3391496 | tf_op jit(solution)/shard_map/ppermute | solution.py:501
  24.1 1.0 copy-start.9
  26.7 22.0 %copy-start.1 = (bf16[46,184,128]{2,1,0:T(8,128)(2,1)S(1)}, bf16[46,184,128]{2,1,0:T(8,128)(2,1)}, u32[]{:S(2)}) copy-start(bf16[46,184,128]{2,1,0:T(8,128)(2,1)} %param.6) | copy-start | bytes 6500356
  40.0 2.2 %copy-start.2 = (bf16[23,64,384]{2,1,0:T(8,128)(2,1)}, bf16[23,64,384]{2,1,0:T(8,128)(2,1)S(1)}, u32[]{:S(2)}) copy-start(bf16[23,64,384]{2,1,0:T(8,128)(2,1)S(1)} %collective-permute-done.2.refs_1_) | copy-start | bytes 3391492
  42.2 13.7 %collective-permute-start.6 = (bf16[23,64,384]{2,1,0:T(8,128)(2,1)S(1)}, bf16[23,64,384]{2,1,0:T(8,128)(2,1)}, u32[]{:S(2)}, u32[]{:S(2)}) collective-permute-start(bf16[23,64,384]{2,1,0:T(8,128)(2,1)S(1)} %collective-permute-done.2.refs_1_), channel_id=1, source_target_pairs={{4,8},{6,10},{8,4},{10,6},{5,9},{7,11},{9,5},{11,7},{20,24},{22,26... | collective-permute-start | bytes 3391496 | tf_op jit(solution)/shard_map/ppermute | solution.py:501
  43.9 24.9 %collective-permute-start.3 = (bf16[23,64,384]{2,1,0:T(8,128)(2,1)}, bf16[23,64,384]{2,1,0:T(8,128)(2,1)}, u32[]{:S(2)}, u32[]{:S(2)}) collective-permute-start(bf16[23,64,384]{2,1,0:T(8,128)(2,1)} %get-tuple-element.46), channel_id=1, source_target_pairs={{0,2},{2,0},{4,6},{6,4},{8,10},{10,8},{12,14},{14,12},{1,3},{3,1},... | collective-permute-start | bytes 3391496 | tf_op jit(solution)/shard_map/ppermute | solution.py:504
  44.2 33.2 %collective-permute-start.4 = (bf16[23,64,384]{2,1,0:T(8,128)(2,1)}, bf16[23,64,384]{2,1,0:T(8,128)(2,1)}, u32[]{:S(2)}, u32[]{:S(2)}) collective-permute-start(bf16[23,64,384]{2,1,0:T(8,128)(2,1)} %broadcast_select_fusion.2), channel_id=1, source_target_pairs={{0,4},{2,6},{4,0},{6,2},{8,12},{10,14},{12,8},{14,10},{1,5},{3,7},... | collective-permute-start | bytes 3391496 | tf_op jit(solution)/shard_map/ppermute | solution.py:501
  50.5 1.5 copy-start.21
  52.0 1.0 copy-start.23
  53.0 2.9 %copy-start.10 = (bf16[23,64,384]{2,1,0:T(8,128)(2,1)S(1)}, bf16[23,64,384]{2,1,0:T(8,128)(2,1)}, u32[]{:S(2)}) copy-start(bf16[23,64,384]{2,1,0:T(8,128)(2,1)} %copy-done.9) | copy-start | bytes 3391492
  54.8 1.1 copy-start.13
  55.9 1.4 copy-start.11
  68.7 27.2 %collective-permute-start.7 = (bf16[23,64,384]{2,1,0:T(8,128)(2,1)S(1)}, bf16[23,64,384]{2,1,0:T(8,128)(2,1)S(1)}, u32[]{:S(2)}, u32[]{:S(2)}) collective-permute-start(bf16[23,64,384]{2,1,0:T(8,128)(2,1)S(1)} %broadcast_select_fusion.1), channel_id=1, source_target_pairs={{0,4},{2,6},{4,0},{6,2},{8,12},{10,14},{12,8},{14,10},{1,5},{3,7},... | collective-permute-start | bytes 3391496 | tf_op jit(solution)/shard_map/ppermute | solution.py:501
  73.4 23.6 %collective-permute-start.8 = (bf16[23,64,384]{2,1,0:T(8,128)(2,1)}, bf16[23,64,384]{2,1,0:T(8,128)(2,1)S(1)}, u32[]{:S(2)}, u32[]{:S(2)}) collective-permute-start(bf16[23,64,384]{2,1,0:T(8,128)(2,1)} %collective-permute-done.refs_0_.refs_4_), channel_id=1, source_target_pairs={{4,8},{6,10},{8,4},{10,6},{5,9},{7,11},{9,5},{11,7},{20,24},{22,26... | collective-permute-start | bytes 3391496 | tf_op jit(solution)/shard_map/ppermute | solution.py:501
  77.4 8.4 %copy-start.3 = (bf16[23,64,384]{2,1,0:T(8,128)(2,1)S(1)}, bf16[23,64,384]{2,1,0:T(8,128)(2,1)}, u32[]{:S(2)}) copy-start(bf16[23,64,384]{2,1,0:T(8,128)(2,1)} %copy-done.2) | copy-start | bytes 3391492
  83.9 18.3 %collective-permute-start.5 = (bf16[64,96,128]{2,1,0:T(8,128)(2,1)}, bf16[64,96,128]{2,1,0:T(8,128)(2,1)}, u32[]{:S(2)}, u32[]{:S(2)}) collective-permute-start(bf16[64,96,128]{2,1,0:T(8,128)(2,1)} %triangle.4.refs_0_), channel_id=1, source_target_pairs={{5,4},{7,6},{8,9},{10,11},{21,20},{23,22},{24,25},{26,27}} | collective-permute-start | bytes 4718600 | tf_op jit(solution)/shard_map/ppermute | solution.py:511
  91.3 3.0 %copy-start.4 = (bf16[64,96,128]{2,1,0:T(8,128)(2,1)}, bf16[64,96,128]{2,1,0:T(8,128)(2,1)S(1)}, u32[]{:S(2)}) copy-start(bf16[64,96,128]{2,1,0:T(8,128)(2,1)S(1)} %triangle.5.refs_0_) | copy-start | bytes 4718596
  95.9 1.0 copy-start.6
  97.0 1.0 copy-start.15
  98.0 25.3 %collective-permute-start.9 = (bf16[23,64,384]{2,1,0:T(8,128)(2,1)}, bf16[23,64,384]{2,1,0:T(8,128)(2,1)}, u32[]{:S(2)}, u32[]{:S(2)}) collective-permute-start(bf16[23,64,384]{2,1,0:T(8,128)(2,1)} %broadcast_select_fusion), channel_id=1, source_target_pairs={{0,4},{2,6},{4,0},{6,2},{8,12},{10,14},{12,8},{14,10},{1,5},{3,7},... | collective-permute-start | bytes 3391496 | tf_op jit(solution)/shard_map/ppermute | solution.py:501
  100.5 22.8 %collective-permute-start.11 = (bf16[23,64,384]{2,1,0:T(8,128)(2,1)}, bf16[23,64,384]{2,1,0:T(8,128)(2,1)}, u32[]{:S(2)}, u32[]{:S(2)}) collective-permute-start(bf16[23,64,384]{2,1,0:T(8,128)(2,1)} %collective-permute-done.4.refs_1_.refs_2_), channel_id=1, source_target_pairs={{4,8},{6,10},{8,4},{10,6},{5,9},{7,11},{9,5},{11,7},{20,24},{22,26... | collective-permute-start | bytes 3391496 | tf_op jit(solution)/shard_map/ppermute | solution.py:501
  106.4 0.8 copy-start.19
  107.2 16.1 %collective-permute-start.10 = (bf16[23,96,128]{2,1,0:T(8,128)(2,1)}, bf16[23,96,128]{2,1,0:T(8,128)(2,1)}, u32[]{:S(2)}, u32[]{:S(2)}) collective-permute-start(bf16[23,96,128]{2,1,0:T(8,128)(2,1)} %get-tuple-element.55), channel_id=1, source_target_pairs={{4,6},{6,4},{9,11},{11,9},{20,22},{22,20},{25,27},{27,25}} | collective-permute-start | bytes 1695752 | tf_op jit(solution)/shard_map/ppermute | solution.py:525
  108.7 29.6 %collective-permute-start.18 = (bf16[64,96,128]{2,1,0:T(8,128)(2,1)}, bf16[64,96,128]{2,1,0:T(8,128)(2,1)S(1)}, u32[]{:S(2)}, u32[]{:S(2)}) collective-permute-start(bf16[64,96,128]{2,1,0:T(8,128)(2,1)} %copy-done.4), channel_id=1, source_target_pairs={{1,0},{3,2},{5,4},{7,6},{8,9},{10,11},{12,13},{14,15},{17,16},{19,... | collective-permute-start | bytes 4718600 | tf_op jit(solution)/shard_map/ppermute | solution.py:511
  114.5 1.3 copy-start.7
  115.8 7.5 %copy-start.8 = (bf16[23,64,384]{2,1,0:T(8,128)(2,1)S(1)}, bf16[23,64,384]{2,1,0:T(8,128)(2,1)}, u32[]{:S(2)}) copy-start(bf16[23,64,384]{2,1,0:T(8,128)(2,1)} %copy-done.6) | copy-start | bytes 3391492
  115.8 7.5 %copy-start.16 = (bf16[23,64,384]{2,1,0:T(8,128)(2,1)S(1)}, bf16[23,64,384]{2,1,0:T(8,128)(2,1)}, u32[]{:S(2)}) copy-start(bf16[23,64,384]{2,1,0:T(8,128)(2,1)} %copy-done.15) | copy-start | bytes 3391492
  121.8 16.5 %copy-start.5 = (bf16[64,96,128]{2,1,0:T(8,128)(2,1)S(1)}, bf16[64,96,128]{2,1,0:T(8,128)(2,1)}, u32[]{:S(2)}) copy-start(bf16[64,96,128]{2,1,0:T(8,128)(2,1)} %copy-done.4) | copy-start | bytes 4718596
  121.8 16.5 %collective-permute-start.19 = (bf16[64,96,128]{2,1,0:T(8,128)(2,1)S(1)}, bf16[64,96,128]{2,1,0:T(8,128)(2,1)S(1)}, u32[]{:S(2)}, u32[]{:S(2)}) collective-permute-start(bf16[64,96,128]{2,1,0:T(8,128)(2,1)S(1)} %triangle.7.refs_2_), channel_id=1, source_target_pairs={{0,1},{2,3},{4,5},{6,7},{9,8},{11,10},{13,12},{15,14},{16,17},{18,... | collective-permute-start | bytes 4718600 | tf_op jit(solution)/shard_map/ppermute | solution.py:511
  131.5 13.8 %collective-permute-start.12 = (bf16[64,96,128]{2,1,0:T(8,128)(2,1)S(1)}, bf16[64,96,128]{2,1,0:T(8,128)(2,1)S(1)}, u32[]{:S(2)}, u32[]{:S(2)}) collective-permute-start(bf16[64,96,128]{2,1,0:T(8,128)(2,1)S(1)} %get-tuple-element.58.refs_0_), channel_id=1, source_target_pairs={{1,0},{3,2},{4,5},{6,7},{9,8},{11,10},{12,13},{14,15},{17,16},{19,... | collective-permute-start | bytes 4718600 | tf_op jit(solution)/shard_map/ppermute | solution.py:511
  136.9 4.9 %collective-permute-start.13 = (bf16[64,48,128]{2,1,0:T(8,128)(2,1)S(1)}, bf16[64,48,128]{2,1,0:T(8,128)(2,1)S(1)}, u32[]{:S(2)}, u32[]{:S(2)}) collective-permute-start(bf16[64,48,128]{2,1,0:T(8,128)(2,1)S(1)} %get-tuple-element.60.refs_0_), channel_id=1, source_target_pairs={{5,4},{7,6},{8,9},{10,11},{21,20},{23,22},{24,25},{26,27}} | collective-permute-start | bytes 2359304 | tf_op jit(solution)/shard_map/ppermute | solution.py:511
  137.6 4.1 %collective-permute-start.14 = (bf16[64,48,128]{2,1,0:T(8,128)(2,1)S(1)}, bf16[64,48,128]{2,1,0:T(8,128)(2,1)S(1)}, u32[]{:S(2)}, u32[]{:S(2)}) collective-permute-start(bf16[64,48,128]{2,1,0:T(8,128)(2,1)S(1)} %get-tuple-element.61.refs_2_), channel_id=1, source_target_pairs={{4,5},{6,7},{9,8},{11,10},{20,21},{22,23},{25,24},{27,26}} | collective-permute-start | bytes 2359304 | tf_op jit(solution)/shard_map/ppermute | solution.py:511
  140.5 17.7 %collective-permute-start.20 = (bf16[23,96,128]{2,1,0:T(8,128)(2,1)}, bf16[23,96,128]{2,1,0:T(8,128)(2,1)}, u32[]{:S(2)}, u32[]{:S(2)}) collective-permute-start(bf16[23,96,128]{2,1,0:T(8,128)(2,1)} %get-tuple-element.66), channel_id=1, source_target_pairs={{0,2},{2,0},{4,6},{6,4},{8,10},{10,8},{12,14},{14,12},{1,3},{3,1},... | collective-permute-start | bytes 1695752 | tf_op jit(solution)/shard_map/ppermute | solution.py:504
  142.5 15.8 %copy-start.17 = (bf16[1024,128]{1,0:T(8,128)(2,1)S(1)}, bf16[1024,128]{1,0:T(8,128)(2,1)}, u32[]{:S(2)}) copy-start(bf16[1024,128]{1,0:T(8,128)(2,1)} %multiply_bitcast_fusion.refs_1_) | copy-start | bytes 786436
  142.5 15.8 %copy-start.24 = (bf16[12,128,384]{2,1,0:T(8,128)(2,1)S(1)}, bf16[12,128,384]{2,1,0:T(8,128)(2,1)}, u32[]{:S(2)}) copy-start(bf16[12,128,384]{2,1,0:T(8,128)(2,1)} %copy-done.23) | copy-start | bytes 3538948
  142.5 26.1 %collective-permute-start.15 = (bf16[23,96,128]{2,1,0:T(8,128)(2,1)S(1)}, bf16[23,96,128]{2,1,0:T(8,128)(2,1)}, u32[]{:S(2)}, u32[]{:S(2)}) collective-permute-start(bf16[23,96,128]{2,1,0:T(8,128)(2,1)S(1)} %fold.6), channel_id=1, source_target_pairs={{5,1},{7,3},{8,12},{10,14},{21,17},{23,19},{24,28},{26,30}} | collective-permute-start | bytes 1695752 | tf_op jit(solution)/shard_map/ppermute | solution.py:519
  144.0 26.1 %collective-permute-start.17 = (bf16[23,96,128]{2,1,0:T(8,128)(2,1)S(1)}, bf16[23,96,128]{2,1,0:T(8,128)(2,1)}, u32[]{:S(2)}, u32[]{:S(2)}) collective-permute-start(bf16[23,96,128]{2,1,0:T(8,128)(2,1)S(1)} %fold.6), channel_id=1, source_target_pairs={{4,3},{6,1},{9,14},{11,12},{20,19},{22,17},{25,30},{27,28}} | collective-permute-start | bytes 1695752 | tf_op jit(solution)/shard_map/ppermute | solution.py:519
  147.4 22.6 %collective-permute-start.16 = (bf16[23,96,128]{2,1,0:T(8,128)(2,1)}, bf16[23,96,128]{2,1,0:T(8,128)(2,1)}, u32[]{:S(2)}, u32[]{:S(2)}) collective-permute-start(bf16[23,96,128]{2,1,0:T(8,128)(2,1)} %get-tuple-element.62), channel_id=1, source_target_pairs={{0,2},{2,0},{5,7},{7,5},{8,10},{10,8},{13,15},{15,13},{16,18},{18,... | collective-permute-start | bytes 1695752 | tf_op jit(solution)/shard_map/ppermute | solution.py:525
  148.8 19.8 %copy-start.20 = (bf16[23,96,128]{2,1,0:T(8,128)(2,1)S(1)}, bf16[23,96,128]{2,1,0:T(8,128)(2,1)}, u32[]{:S(2)}) copy-start(bf16[23,96,128]{2,1,0:T(8,128)(2,1)} %copy-done.19) | copy-start | bytes 1695748
  158.3 1.7 copy-start.22
  168.6 2.6 %copy-start.12 = (f32[12,128,384]{2,1,0:T(8,128)S(1)}, f32[12,128,384]{2,1,0:T(8,128)}, u32[]{:S(2)}) copy-start(f32[12,128,384]{2,1,0:T(8,128)} %copy-done.11) | copy-start | bytes 7077892
  170.0 1.6 copy-start.14
